TPU v7x, 32 devices: a whole 2x2x4 slice. The times are simulated.
32 devices in a mesh: walk: 8 (over y, x, core), par: 4 (over z).
Axes of the slice: x: 2, y: 2, z: 4, core: 2. Of those that a mesh axis runs over, the one named last changes fastest.
Arguments:
- features: bfloat16 [1536, 32, 256], P(('walk', 'par')), may hold values from -6 to 6
- signals: bfloat16 [1536, 32, 256], P(('walk', 'par')), may hold values from -6 to 6
- param_scale: float32 [256, 256], replicated, may hold values from 0.2 to 2
- geometry: int32 [1536], replicated, may hold values from 0 to 63
- electrons: int32 [64], replicated, may hold values from 16 to 32
Outputs:
- panel: float32 [1536, 256], P('walk')
- trailing: float32 [1536, 1536], P('walk', 'par')
All inputs are finite; a program needn't handle non-finite values.
Results may differ from a plain program's by a relative error of at most 0.0003.
Values sent between devices are 32-bit elements; how exact they have to be, the bound alone decides.
No kernel may reach another device: no remote copies, remote signals or barrier semaphores. Data moves between devices by JAX's collectives and lax.ppermute only.
A program may use at most 256 MiB of HBM per device.

v0:
```python
import math

import jax
import jax.numpy as jnp
from jax import lax
from jax.sharding import PartitionSpec as P

PB = 256


HIGHEST = lax.Precision.HIGHEST
SHIFT = 0.05
CONTRACT_LAST = (((1,), (1,)), ((), ()))
CONTRACT_FIRST = (((0,), (0,)), ((), ()))


def outer_rows(left_rows, right_rows):
    return lax.dot_general(left_rows, right_rows, CONTRACT_LAST, precision=HIGHEST)


def first_dims(left_rows, right_rows):
    return lax.dot_general(left_rows, right_rows, CONTRACT_FIRST, precision=HIGHEST)


def one_hot(labels, groups):
    return (labels[:, None] == jnp.arange(groups, dtype=jnp.int32)[None, :]).astype(jnp.float32)


def on_device(features, signals, param_scale, geometry, electrons):
    par_size = lax.axis_size("par")
    walk_index = lax.axis_index("walk")
    par_index = lax.axis_index("par")
    per_device = features.shape[0]
    walkers = geometry.shape[0]
    groups = electrons.shape[0]
    row_block = per_device * par_size
    col_block = walkers // par_size
    width = param_scale.shape[0]
    slots_count = features.shape[1]
    anchor = (walk_index * par_size + par_index) * per_device
    own_geometry = lax.dynamic_slice_in_dim(geometry, anchor, per_device)
    own_matches = own_geometry[:, None] == jnp.arange(groups, dtype=jnp.int32)[None, :]
    own_electrons = jnp.sum(jnp.where(own_matches, electrons[None, :], 0), axis=1)
    live = (jnp.arange(slots_count, dtype=jnp.int32)[None, :] < own_electrons[:, None]).astype(
        features.dtype
    )
    masked = features * live[:, :, None]
    scaling = param_scale * (1.0 / math.sqrt(slots_count * width * width))
    jacobian = (
        jnp.einsum("wei,wej->wij", masked, signals, preferred_element_type=jnp.float32)
        * scaling[None]
    )
    jacobian = jacobian.reshape(per_device, width * width)
    all_onehot = one_hot(geometry, groups)
    counts = jnp.maximum(jnp.sum(all_onehot, axis=0), 1.0)
    reciprocal = 1.0 / counts
    columns = lax.all_to_all(jacobian, ("walk", "par"), split_axis=1, concat_axis=0, tiled=True)
    sums = first_dims(all_onehot, columns)
    columns = columns - jnp.dot(all_onehot, sums * reciprocal[:, None], precision=HIGHEST)
    stripe = lax.psum_scatter(outer_rows(columns, columns), "walk", scatter_dimension=0, tiled=True)
    gram = lax.psum_scatter(stripe, "par", scatter_dimension=1, tiled=True)
    row_ids = walk_index * row_block + jnp.arange(row_block, dtype=jnp.int32)
    col_ids = par_index * col_block + jnp.arange(col_block, dtype=jnp.int32)
    shifted = gram + SHIFT * (row_ids[:, None] == col_ids[None, :]).astype(jnp.float32)
    whole_rows = lax.all_gather(shifted, "par", axis=1, tiled=True)
    panel_part = whole_rows[:, :PB]
    panel_whole = lax.all_gather(panel_part, "walk", axis=0, tiled=True)
    factor_head = jnp.linalg.cholesky(panel_whole[:PB])
    head_inverse = jax.scipy.linalg.solve_triangular(
        factor_head, jnp.eye(PB, dtype=jnp.float32), lower=True
    )
    own_panel = outer_rows(panel_part, head_inverse)
    col_rows = lax.dynamic_slice_in_dim(panel_whole, par_index * col_block, col_block, 0)
    col_panel = outer_rows(col_rows, head_inverse)
    trailing = shifted - outer_rows(own_panel, col_panel)
    return (own_panel, trailing)


def solution(mesh):
    in_specs = (P(("walk", "par"), None, None), P(("walk", "par"), None, None), P(), P(), P())
    out_specs = (P("walk", None), P("walk", "par"))
    return jax.shard_map(
        on_device, mesh=mesh, in_specs=in_specs, out_specs=out_specs, check_vma=False
    )
```

profile of v0, /device:TPU:0, one launch (start us, length us, event | category | flops | bytes accessed | tf_op | source)
XLA Modules:
  0.0 659.8 jit_solution(1431024369149093980)
XLA Ops:
  7.2 0.8 dynamic_slice.6
  8.0 0.8 select_reduce_fusion.2
  8.9 0.1 fusion.18
  8.9 1.0 broadcast_multiply_fusion.1
  9.9 8.6 %broadcast_multiply_fusion = f32[48,256,256]{2,1,0:T(8,128)} fusion(f32[256,256]{1,0:T(8,128)S(1)} %broadcast_multiply_fusion.1, bf16[48,32,256]{2,1,0:T(8,128)(2,1)S(1)} %copy-done, bf16[48,32,256]{2,1,0:T(8,128)(2,1)} %param.5, bf16[48,32]{1,0:T(8,128)(2,1)S(1)} %fusion.18), kind=kOutput, calls=%fused_computation.4 | convolution fusion | flops 204865536 | bytes 14420992 | tf_op jit(solution)/shard_map/wei,wej->wij/dot_general | solution.py:50
  18.6 13.6 %all_to_all.14 = f32[48,32,2048]{2,1,0:T(8,128)} reshape(f32[48,256,256]{2,1,0:T(8,128)} %broadcast_multiply_fusion) | data formatting | bytes 25165824 | tf_op jit(solution)/shard_map/all_to_all | solution.py:57
  32.2 16.3 %copy.21 = f32[48,32,2048]{2,0,1:T(8,128)} copy(f32[48,32,2048]{2,1,0:T(8,128)} %all_to_all.14) | data formatting | bytes 25165824 | tf_op jit(solution)/shard_map/all_to_all | solution.py:57
  48.5 7.4 %all-to-all-start = ((f32[48,32,2048]{2,0,1:T(8,128)}), f32[48,32,2048]{2,0,1:T(8,128)}, u32[]{:S(2)}, u32[]{:S(2)}) async-start(f32[48,32,2048]{2,0,1:T(8,128)} %copy.21), calls=%async_computation | async-start | bytes 25165824 | tf_op jit(solution)/shard_map/all_to_all | solution.py:57
  55.9 0.2 reduce-scatter.7.cloned.1.call-start
  56.1 0.1 convert_reduce_fusion
  56.3 270.5 %all-to-all-done = f32[48,32,2048]{2,0,1:T(8,128)} async-done(((f32[48,32,2048]{2,0,1:T(8,128)}), f32[48,32,2048]{2,0,1:T(8,128)}, u32[]{:S(2)}, u32[]{:S(2)}) %all-to-all-start) | async-done | bytes 12582944 | tf_op jit(solution)/shard_map/all_to_all | solution.py:57
  326.8 7.9 %convolution_multiply_fusion = f32[64,2048]{1,0:T(8,128)S(1)} fusion(f32[1536,2048]{1,0:T(8,128)} %bitcast.1, f32[64]{0:T(128)S(1)} %maximum_divide_fusion, s32[1536]{0:T(1024)S(1)} %copy-done.3), kind=kOutput, calls=%fused_computation.5 | convolution fusion | flops 2416148480 | bytes 13113600 | tf_op jit(solution)/shard_map/dot_general | solution.py:22
  334.7 8.1 %fusion.5 = f32[1536,2048]{1,0:T(8,128)} fusion(f32[64,2048]{1,0:T(8,128)S(1)} %convolution_multiply_fusion, s32[1536]{0:T(1024)S(1)} %copy-done.3), kind=kOutput, calls=%fused_computation.14 | convolution fusion | flops 2416017408 | bytes 13113344 | tf_op jit(solution)/shard_map/dot_general | solution.py:59
  342.8 69.0 %fusion = f32[1536,1536]{1,0:T(8,128)} fusion(f32[1536,2048]{1,0:T(8,128)} %bitcast.1, f32[1536,2048]{1,0:T(8,128)} %fusion.5), kind=kOutput, calls=%fused_computation.2 | convolution fusion | flops 57985204224 | bytes 34603008
  411.8 0.0 reduce-scatter.5.cloned.1.call-start
  411.9 83.2 %reduce-scatter.7.cloned.1.call-done = f32[192,1536]{1,0:T(8,128)} async-done(((f32[1536,1536]{1,0:T(8,128)}), f32[192,1536]{1,0:T(8,128)}) %reduce-scatter.7.cloned.1.call-update) | async-done | bytes 1179664 | tf_op jit(solution)/shard_map/reduce_scatter | solution.py:60
  495.1 0.0 reduce-scatter.5.cloned.1.call-update
  495.1 0.0 all-gather.3.cloned.1.call-start
  495.2 31.4 %reduce-scatter.5.cloned.1.call-done = f32[192,384]{1,0:T(8,128)} async-done(((f32[192,1536]{1,0:T(8,128)}), f32[192,384]{1,0:T(8,128)}) %reduce-scatter.5.cloned.1.call-update) | async-done | bytes 294928 | tf_op jit(solution)/shard_map/reduce_scatter | solution.py:61
  526.6 1.8 select_add_fusion
  528.4 0.0 all-gather.3.cloned.1.call-update
  528.4 0.3 all-gather.5.cloned.1.call-start
  528.7 29.3 %all-gather.3.cloned.1.call-done = f32[192,1536]{1,0:T(8,128)} async-done(((f32[192,384]{1,0:T(8,128)}), f32[192,1536]{1,0:T(8,128)}) %all-gather.3.cloned.1.call-update) | async-done | bytes 1179664 | tf_op jit(solution)/shard_map/all_gather | solution.py:65
  558.0 1.6 slice.67
  559.6 0.0 all-gather.5.cloned.1.call-update
  559.7 25.5 %all-gather.5.cloned.1.call-done = f32[1536,256]{1,0:T(8,128)} async-done(((f32[192,256]{1,0:T(8,128)}), f32[1536,256]{1,0:T(8,128)}) %all-gather.5.cloned.1.call-update) | async-done | bytes 1572880 | tf_op jit(solution)/shard_map/all_gather | solution.py:67
  585.1 1.0 slice.68
  586.1 0.1 copy.29
  586.2 1.0 fusion.7
  587.2 11.7 %cholesky.50 = f32[128,128]{1,0:T(8,128)S(1)} custom-call(f32[128,128]{1,0:T(8,128)S(1)} %cholesky.118), custom_call_target="Cholesky" | custom-call | tf_op jit(solution)/shard_map/jit(cholesky)/cholesky | solution.py:68
  599.0 9.8 %custom-call.15 = f32[1,128,128]{1,2,0:T(8,128)S(1)} custom-call(f32[1,128,128]{2,1,0:T(8,128)S(1)} %get-tuple-element.27), custom_call_target="InvertDiagBlocksLowerTriangular" | custom-call | tf_op jit(solution)/shard_map/jit(cholesky)/cholesky | solution.py:68
  608.8 0.2 constant_dynamic-update-slice_fusion.1
  609.0 0.3 convolution_subtract_fusion.2
  609.3 11.7 %cholesky.105 = f32[128,128]{1,0:T(8,128)S(1)} custom-call(f32[128,128]{1,0:T(8,128)S(1)} %convolution_subtract_fusion.2), custom_call_target="Cholesky" | custom-call | tf_op jit(solution)/shard_map/jit(cholesky)/cholesky | solution.py:68
  621.1 0.7 compare_reduce_fusion
  623.0 0.1 triangular_solve.63
  623.1 4.1 while.1
  623.3 0.6 fusion.38
  623.9 1.3 bitcast_dynamic-update-slice_fusion.2
  625.2 0.6 fusion.38
  625.8 1.3 bitcast_dynamic-update-slice_fusion.2
  627.1 19.7 %custom-call.16 = f32[2,128,128]{1,2,0:T(8,128)S(1)} custom-call(f32[2,128,128]{2,1,0:T(8,128)S(1)} %get-tuple-element.9), custom_call_target="InvertDiagBlocksLowerTriangular" | custom-call | tf_op jit(solution)/shard_map/jit(_solve_triangular)/triangular_solve | solution.py:69
  646.8 0.3 fusion.11
  647.1 0.3 convolution_subtract_fusion.1
  647.4 0.3 fusion.14
  647.7 1.4 fusion.8
  649.1 1.6 fusion.3
  650.6 2.2 convolution_subtract_fusion
  (22 shorter events, 0.2 us)
Async XLA Ops:
  7.2 2.8 copy-start
  48.5 7.6 %copy-start.3 = (s32[1536]{0:T(1024)S(1)}, s32[1536]{0:T(1024)}, u32[]{:S(2)}) copy-start(s32[1536]{0:T(1024)} %param.8) | copy-start | bytes 18436
  48.5 278.3 %all-to-all-start = ((f32[48,32,2048]{2,0,1:T(8,128)}), f32[48,32,2048]{2,0,1:T(8,128)}, u32[]{:S(2)}, u32[]{:S(2)}) async-start(f32[48,32,2048]{2,0,1:T(8,128)} %copy.21), calls=%async_computation | async-start | bytes 25165824 | tf_op jit(solution)/shard_map/all_to_all | solution.py:57
  55.9 439.2 %reduce-scatter.7.cloned.1.call-start = ((), (), s32[]{:S(2)}) async-start(), calls=%async_computation.6 | async-start | bytes 10616832 | tf_op jit(solution)/shard_map/reduce_scatter | solution.py:60
  342.8 310.1 %copy-start.1 = (bf16[48,32,256]{2,1,0:T(8,128)(2,1)S(1)}, bf16[48,32,256]{2,1,0:T(8,128)(2,1)}, u32[]{:S(2)}) copy-start(bf16[48,32,256]{2,1,0:T(8,128)(2,1)} %param.6) | copy-start | bytes 2359300
  411.8 114.8 %reduce-scatter.5.cloned.1.call-start = ((), (), s32[]{:S(2)}) async-start(), calls=%async_computation.3 | async-start | bytes 1474560 | tf_op jit(solution)/shard_map/reduce_scatter | solution.py:61
  495.1 62.8 %all-gather.3.cloned.1.call-start = ((), (), s32[]{:S(2)}) async-start(), calls=%async_computation.4 | async-start | bytes 1474560 | tf_op jit(solution)/shard_map/all_gather | solution.py:65
  528.4 56.7 %all-gather.5.cloned.1.call-start = ((), (), s32[]{:S(2)}) async-start(), calls=%async_computation.5 | async-start | bytes 1769472 | tf_op jit(solution)/shard_map/all_gather | solution.py:67
  649.0 3.8 copy-start.2
Sparse Core Ops, SparseCore 0:
  412.0 83.0 reduce-scatter.6
  497.4 29.1 reduce-scatter.4
  528.8 29.1 all-gather.2
  560.3 24.7 all-gather.4
where the time goes:
time: 668 us; the launch traced here: 660 us
  waiting for transfers between devices  440 us (66%)
  matrix products  100 us (15%)
  other arithmetic  58.5 us (9%)
  local copies, waits for them, and re-layouts  37.4 us (6%)
  between operations  15.6 us (2%)
  starting transfers between devices  7.95 us (1%)
    all_to_all x1, waiting for transfers between devices, on_device(): lax.all_to_all(jacobian, ('walk', 'par'), split_axis=1, concat_axis=0, ti...  271 us
    reduce_scatter x1, waiting for transfers between devices, on_device(): lax.psum_scatter(outer_rows(columns, columns), 'walk', scatter_dimension=...  83.2 us
    unnamed x1, matrix products  69 us
    another operation x6, other arithmetic, on_device(): factor_head = jnp.linalg.cholesky(panel_whole[:PB])  34 us
    reduce_scatter x1, waiting for transfers between devices, on_device(): gram = lax.psum_scatter(stripe, 'par', scatter_dimension=1, tiled=True)  31.4 us
    all_to_all x2, local copies, waits for them, and re-layouts, on_device(): lax.all_to_all(jacobian, ('walk', 'par'), split_axis=1, concat_axis=0, ti...  29.9 us
    all_gather x1, waiting for transfers between devices, on_device(): whole_rows = lax.all_gather(shifted, 'par', axis=1, tiled=True)  29.3 us
    all_gather x1, waiting for transfers between devices, on_device(): panel_whole = lax.all_gather(panel_part, 'walk', axis=0, tiled=True)  25.5 us
  transfers between devices with their start and end apart: 5, of which 5 were waited for; matrix products, arithmetic and copies ran while one was open for 0% of the time, Pallas kernels for 0%

commit v1 on v0

v1 whole, which is shorter than its diff:
```python
import functools
import math

import jax
import jax.numpy as jnp
import numpy as np
from jax import lax
from jax.experimental import pallas as pl
from jax.experimental.pallas import tpu as pltpu
from jax.sharding import PartitionSpec as P

PB = 256
HIGHEST = lax.Precision.HIGHEST
SHIFT = 0.05
LANES = 256
CONTRACT_LAST = (((1,), (1,)), ((), ()))
VMEM_LIMIT = 60 * 1024 * 1024


def outer_rows(left_rows, right_rows):
    return lax.dot_general(left_rows, right_rows, CONTRACT_LAST, precision=HIGHEST)


def xor_pairs(size, bit):
    return [(i, i ^ bit) for i in range(size)]


class Plan:
    def __init__(self, walk_size, par_size):
        self.walk_size, self.par_size = walk_size, par_size
        par_bits = par_size.bit_length() - 1
        walk_bits = walk_size.bit_length() - 1
        self.dims = []
        for bit in reversed(range(par_bits)):
            self.dims.append(("par", 1 << bit, "J" if bit == 0 else "I"))
        for bit in range(1, walk_bits):
            self.dims.append(("walk", 1 << bit, "J" if bit == walk_bits - 1 else "I"))
        self.place = []
        seen = {"I": 0, "J": 0}
        for _, _, kind in self.dims:
            self.place.append(seen[kind])
            seen[kind] += 1
        self.blocks = {"F": 1 << seen["I"], "S": 1 << seen["J"]}
        self.rounds = self.schedule()

    def splits(self, side, kind):
        return (side == "F") == (kind == "I")

    def depth(self, side, src, rb, first):
        best = 0
        for k in range(first, len(self.dims)):
            kind = self.dims[k][2]
            if self.splits(side, kind):
                if rb >> self.place[k] & 1:
                    return max(best, 1 + self.depth(side, src, rb ^ (1 << self.place[k]), k + 1))
            else:
                best = max(best, 1 + self.depth(side, src, rb, k + 1))
        return best

    def tasks(self):
        out = []
        for side in ("F", "S"):
            live = [(0, rb) for rb in range(self.blocks[side])]
            for k, (_, _, kind) in enumerate(self.dims):
                kept, made = [], []
                for src, rb in live:
                    if self.splits(side, kind):
                        p = self.place[k]
                        if rb >> p & 1:
                            made.append((k, (side, src, rb), (side, src | 1 << k, rb ^ (1 << p))))
                        else:
                            kept.append((src, rb))
                    else:
                        kept.append((src, rb))
                        made.append((k, (side, src, rb), (side, src | 1 << k, rb)))
                live = kept + [dst[1:] for _, _, dst in made]
                out += made
        return out

    def schedule(self):
        left = self.tasks()
        have = {(side, 0, rb) for side in ("F", "S") for rb in range(self.blocks[side])}
        rounds = []
        while left:
            chosen = []
            for k, (axis, _, _) in enumerate(self.dims):
                ready = [t for t in left if t[0] == k and t[1] in have]
                ready.sort(key=lambda t: -self.depth(t[2][0], t[2][1], t[2][2], k + 1))
                chosen += ready[: 1 if axis == "par" else 2]
            left = [t for t in left if t not in chosen]
            have |= {t[2] for t in chosen}
            rounds.append(chosen)
        return rounds

    def flip(self, src):
        walk = par = 0
        for k, (axis, bit, _) in enumerate(self.dims):
            if src >> k & 1:
                walk, par = (walk | bit, par) if axis == "walk" else (walk, par | bit)
        return walk, par


def permute(value, axis, size, bit):
    return lax.ppermute(value, axis, xor_pairs(size, bit))


def exchange(plan, pieces):
    sizes = {"walk": plan.walk_size, "par": plan.par_size}
    held = dict(pieces)
    stacks = {"F": [], "S": []}
    fresh = [("F", 0, 0), ("S", 0, 0)]
    gate = []
    for chosen in plan.rounds + [[]]:
        groups = {}
        for k, src, dst in chosen:
            groups.setdefault((k, held[src].shape), []).append((src, dst))
        stacked = {}
        for side in ("F", "S"):
            names = [n for n in fresh if n[0] == side]
            if names:
                stacked[side] = names
        keys = sorted({s for pairs in groups.values() for s, _ in pairs} | set(fresh))
        if gate:
            tied = lax.optimization_barrier(tuple(held[n] for n in keys) + tuple(held[n] for n in gate))
            for n, v in zip(keys + gate, tied):
                held[n] = v
        fresh, gate = [], []
        for (k, _), pairs in groups.items():
            axis, bit, _ = plan.dims[k]
            if len(pairs) == 1:
                held[pairs[0][1]] = permute(held[pairs[0][0]], axis, sizes[axis], bit)
            else:
                moved = permute(jnp.stack([held[s] for s, _ in pairs]), axis, sizes[axis], bit)
                for i, (_, d) in enumerate(pairs):
                    held[d] = moved[i]
            gate += [d for _, d in pairs]
            fresh += [d for _, d in pairs if d[2] == 0]
        for side, names in stacked.items():
            own = jnp.stack([held[n] for n in names])
            other = permute(own, "walk", plan.walk_size, 1)
            stacks[side].append(([(n[1], 0) for n in names], own))
            stacks[side].append(([(n[1], 1) for n in names], other))
    return stacks


def gathered(stacks, order):
    sources = [s for names, _ in stacks for s in names]
    whole = jnp.concatenate([a for _, a in stacks], axis=0)
    return whole, sources


def jacobian_kernel(slots, rows_ref, f_ref, s_ref, scale_ref, out_ref):
    del rows_ref
    ib, lanes = f_ref.shape[1:]
    jb = s_ref.shape[1]
    together = LANES // slots
    parts = LANES // jb
    tiles = ib // parts
    lane = lax.broadcasted_iota(jnp.int32, (together, LANES), 1)
    row = lax.broadcasted_iota(jnp.int32, (together, LANES), 0)
    mine = (lane >= row * slots) & (lane < row * slots + slots)
    for g in range(lanes // LANES):
        left = f_ref[0, :, g * LANES : (g + 1) * LANES]
        right = s_ref[0, :, g * LANES : (g + 1) * LANES].astype(jnp.bfloat16)
        spread = jnp.where(mine[None], left[:, None, :], 0.0).reshape(ib * together, LANES)
        block = lax.dot_general(
            spread.astype(jnp.bfloat16), right, CONTRACT_LAST, preferred_element_type=jnp.float32
        )
        block = block.reshape(parts, tiles, together, jb)
        for b in range(parts):
            out_ref[:, g * together : (g + 1) * together, b * jb : (b + 1) * jb] = (
                block[b] * scale_ref[:, b * jb : (b + 1) * jb][:, None, :]
            )


def jacobian(rows, features, signals, scaling, walkers, slots):
    sources, ib, lanes = features.shape
    jb = signals.shape[1]
    tiles = ib * jb // LANES
    per_source = lanes // slots
    return pl.pallas_call(
        functools.partial(jacobian_kernel, slots),
        out_shape=jax.ShapeDtypeStruct((tiles, walkers, LANES), jnp.float32),
        grid_spec=pltpu.PrefetchScalarGridSpec(
            num_scalar_prefetch=1,
            grid=(sources,),
            in_specs=[
                pl.BlockSpec((1, ib, lanes), lambda q, rows: (q, 0, 0)),
                pl.BlockSpec((1, jb, lanes), lambda q, rows: (q, 0, 0)),
                pl.BlockSpec((tiles, LANES), lambda q, rows: (0, 0)),
            ],
            out_specs=pl.BlockSpec((tiles, per_source, LANES), lambda q, rows: (0, rows[q], 0)),
        ),
        compiler_params=pltpu.CompilerParams(vmem_limit_bytes=VMEM_LIMIT),
        name="jacobian",
    )(rows, features, signals, scaling)


def split_two(value):
    high = value.astype(jnp.bfloat16)
    return high, (value - high.astype(jnp.float32)).astype(jnp.bfloat16)


def gram_kernel(
    row_block, col_block, orders, row_at, col_at, j_ref, hot_ref, hot_t_ref, recip_ref, a_ref, b_ref, high_ref, low_ref
):
    @pl.when(pl.program_id(0) == 0)
    def _():
        a_ref[...] = jnp.zeros_like(a_ref)
        b_ref[...] = jnp.zeros_like(b_ref)

    value = j_ref[0]
    high, low = split_two(value)
    dot = functools.partial(jnp.dot, preferred_element_type=jnp.float32)
    means = (dot(hot_t_ref[...], high) + dot(hot_t_ref[...], low)) * recip_ref[...]
    first, rest = split_two(means)
    second, third = split_two(means - first.astype(jnp.float32))
    hot = hot_ref[...]
    value = value - (dot(hot, first) + dot(hot, second))
    del rest, third
    high, low = split_two(value)
    high_ref[...] = high
    low_ref[...] = low
    slots = len(orders[0])
    left = []
    for s in range(slots):
        at = pl.ds(pl.multiple_of(row_at[s], 16), row_block)
        h, l = high_ref[at, :], low_ref[at, :]
        left.append(jnp.concatenate([h, h, l], axis=1))
    left = jnp.concatenate(left, axis=0)
    blocks = col_at.shape[0]
    for half, out in enumerate((a_ref, b_ref)):
        for n in range(blocks // 2):
            at = pl.ds(pl.multiple_of(col_at[half * (blocks // 2) + n], 16), col_block)
            h, l = high_ref[at, :], low_ref[at, :]
            right = jnp.concatenate([h, l, h], axis=1)
            got = lax.dot_general(left, right, CONTRACT_LAST, preferred_element_type=jnp.float32)
            for place, s in enumerate(orders[half]):
                out[place * row_block : (place + 1) * row_block, n * col_block : (n + 1) * col_block] += got[
                    s * row_block : (s + 1) * row_block
                ]


def gram_rows(columns, hot, hot_t, recip, row_at, col_at, row_block, col_block, orders):
    tiles, walkers, lanes = columns.shape
    groups = hot.shape[1]
    slots = len(orders[0])
    half = jax.ShapeDtypeStruct((slots * row_block, walkers // 2), jnp.float32)
    fixed = lambda t, r, c: (0, 0)
    return pl.pallas_call(
        functools.partial(gram_kernel, row_block, col_block, orders),
        out_shape=(half, half),
        grid_spec=pltpu.PrefetchScalarGridSpec(
            num_scalar_prefetch=2,
            grid=(tiles,),
            in_specs=[
                pl.BlockSpec((1, walkers, lanes), lambda t, r, c: (t, 0, 0)),
                pl.BlockSpec((walkers, groups), fixed),
                pl.BlockSpec((groups, walkers), fixed),
                pl.BlockSpec((groups, 1), fixed),
            ],
            out_specs=(pl.BlockSpec(half.shape, fixed), pl.BlockSpec(half.shape, fixed)),
            scratch_shapes=[
                pltpu.VMEM((walkers, lanes), jnp.bfloat16),
                pltpu.VMEM((walkers, lanes), jnp.bfloat16),
            ],
        ),
        compiler_params=pltpu.CompilerParams(vmem_limit_bytes=VMEM_LIMIT),
        name="gram_rows",
    )(row_at, col_at, columns, hot, hot_t, recip)


def on_device(features, signals, param_scale, geometry, electrons):
    par_size = lax.axis_size("par")
    walk_size = lax.axis_size("walk")
    walk_index = lax.axis_index("walk")
    par_index = lax.axis_index("par")
    per_device, slots_count, width = features.shape
    walkers = geometry.shape[0]
    groups = electrons.shape[0]
    row_block = per_device * par_size
    col_block = walkers // par_size
    plan = Plan(walk_size, par_size)

    anchor = (walk_index * par_size + par_index) * per_device
    own_geometry = lax.dynamic_slice_in_dim(geometry, anchor, per_device)
    own_matches = own_geometry[:, None] == jnp.arange(groups, dtype=jnp.int32)[None, :]
    own_electrons = jnp.sum(jnp.where(own_matches, electrons[None, :], 0), axis=1)
    live = jnp.arange(slots_count, dtype=jnp.int32)[None, :] < own_electrons[:, None]
    masked = jnp.where(live[:, :, None], features, jnp.zeros_like(features))

    own = {"F": 0, "S": 0}
    for k, (axis, bit, kind) in enumerate(plan.dims):
        index = walk_index if axis == "walk" else par_index
        side = "F" if kind == "I" else "S"
        own[side] = own[side] + jnp.where((index & bit) != 0, 1 << plan.place[k], 0)
    pieces = {}
    for side, value in (("F", masked), ("S", signals)):
        flat = value.reshape(per_device * slots_count, width).T.astype(jnp.float32)
        size = width // plan.blocks[side]
        for rb in range(plan.blocks[side]):
            pieces[side, 0, rb] = lax.dynamic_slice_in_dim(flat, (own[side] ^ rb) * size, size, 0)
    ib, jb = width // plan.blocks["F"], width // plan.blocks["S"]
    stacks = exchange(plan, pieces)
    left, left_names = gathered(stacks["F"], None)
    right, right_names = gathered(stacks["S"], None)
    if left_names != right_names:
        right = jnp.concatenate(
            [right[i : i + 1] for i in [right_names.index(n) for n in left_names]], axis=0
        )
    rows = []
    for src, core in left_names:
        walk_flip, par_flip = plan.flip(src)
        rows.append((walk_index ^ (walk_flip | core)) * par_size + (par_index ^ par_flip))
    rows = jnp.stack(rows).astype(jnp.int32)

    parts = LANES // jb
    scaling = param_scale * (1.0 / math.sqrt(slots_count * width * width))
    scaling = lax.dynamic_slice(scaling, (own["F"] * ib, own["S"] * jb), (ib, jb))
    scaling = scaling.reshape(parts, ib // parts, jb).transpose(1, 0, 2).reshape(ib // parts, LANES)
    columns = jacobian(rows, left, right, scaling, walkers, slots_count)

    matches = geometry[:, None] == jnp.arange(groups, dtype=jnp.int32)[None, :]
    hot = matches.astype(jnp.bfloat16)
    hot_t = (jnp.arange(groups, dtype=jnp.int32)[:, None] == geometry[None, :]).astype(jnp.bfloat16)
    counts = jnp.maximum(jnp.sum(matches.astype(jnp.float32), axis=0), 1.0)
    recip = (1.0 / counts)[:, None]

    chip_bits = walk_size.bit_length() - 2
    slots = 1 << chip_bits
    core, chip = walk_index & 1, walk_index >> 1
    row_at = jnp.stack([((chip ^ s) * 2 + core) * row_block for s in range(slots)]).astype(jnp.int32)
    col_at = jnp.stack([(par_index ^ p) * col_block for p in range(par_size)]).astype(jnp.int32)
    up = list(range(chip_bits))
    sweeps = (up, up[::-1])
    orders = tuple(
        tuple(sorted(range(slots), key=lambda s, o=o: [s >> b & 1 for b in o])) for o in sweeps
    )
    halves = list(gram_rows(columns, hot, hot_t, recip, row_at, col_at, row_block, col_block, orders))
    for step in range(chip_bits):
        moved = []
        for h in range(2):
            mid = halves[h].shape[0] // 2
            bit = 2 << sweeps[h][step]
            moved.append(permute(halves[h][mid:], "walk", walk_size, bit))
        halves = [halves[h][: halves[h].shape[0] // 2] + moved[h] for h in range(2)]
    gram = halves[0] + permute(halves[1], "par", par_size, par_size // 2)
    bit = par_size // 4
    while bit:
        mid = gram.shape[1] // 2
        gram = gram[:, :mid] + permute(gram[:, mid:], "par", par_size, bit)
        bit //= 2

    row_ids = walk_index * row_block + jnp.arange(row_block, dtype=jnp.int32)
    col_ids = par_index * col_block + jnp.arange(col_block, dtype=jnp.int32)
    shifted = gram + SHIFT * (row_ids[:, None] == col_ids[None, :]).astype(jnp.float32)
    whole_rows = lax.all_gather(shifted, "par", axis=1, tiled=True)
    panel_part = whole_rows[:, :PB]
    panel_whole = lax.all_gather(panel_part, "walk", axis=0, tiled=True)
    factor_head = jnp.linalg.cholesky(panel_whole[:PB])
    head_inverse = jax.scipy.linalg.solve_triangular(
        factor_head, jnp.eye(PB, dtype=jnp.float32), lower=True
    )
    own_panel = outer_rows(panel_part, head_inverse)
    col_rows = lax.dynamic_slice_in_dim(panel_whole, par_index * col_block, col_block, 0)
    col_panel = outer_rows(col_rows, head_inverse)
    trailing = shifted - outer_rows(own_panel, col_panel)
    return (own_panel, trailing)


def solution(mesh):
    in_specs = (P(("walk", "par"), None, None), P(("walk", "par"), None, None), P(), P(), P())
    out_specs = (P("walk", None), P("walk", "par"))
    return jax.shard_map(
        on_device, mesh=mesh, in_specs=in_specs, out_specs=out_specs, check_vma=False
    )
```

time: 668 us -> 618 us (0.925)
  waiting for transfers between devices: 440 us -> 283 us
  Pallas kernels: 0 us -> 110 us
  matrix products: 100 us -> 6.45 us
  starting transfers between devices: 7.95 us -> 52.8 us
  local copies, waits for them, and re-layouts: 37.4 us -> 77 us
  other arithmetic: 58.5 us -> 71.5 us
    all_to_all x1 -> x0, waiting for transfers between devices: 271 us -> none  [on_device(): lax.all_to_all(jacobian, ('walk', 'par'), split_axis=1, concat_axis=0, ti...]
    ppermute x0 -> x54, waiting for transfers between devices: none -> 228 us  [permute(): return lax.ppermute(value, axis, xor_pairs(size, bit))]
    reduce_scatter x2 -> x0, waiting for transfers between devices: 115 us -> none  [the longest x1 83.2 us: on_device(): lax.psum_scatter(outer_rows(columns, columns), 'walk', scatter_dimension=...]
    pallas_call x0 -> x2, Pallas kernels: none -> 110 us  [the longest x1 74.1 us: gram_rows(): pl.pallas_call(functools.partial(gram_kernel, row_block, col_block, order...]
    unnamed x1 -> x0, matrix products: 69 us -> none
    unnamed x9 -> x70, local copies, waits for them, and re-layouts: 0.15 us -> 56.2 us
    ppermute x0 -> x54, starting transfers between devices: none -> 52.5 us  [permute(): return lax.ppermute(value, axis, xor_pairs(size, bit))]
    all_to_all x2 -> x0, local copies, waits for them, and re-layouts: 29.9 us -> none  [on_device(): lax.all_to_all(jacobian, ('walk', 'par'), split_axis=1, concat_axis=0, ti...]
  transfers between devices with their start and end apart: 5 -> 56, of which waited for: 5 -> 24; matrix products, arithmetic and copies ran while one was open for 0% -> 12% of each run, Pallas kernels for 0% -> 0%
where the time goes in v1:
time: 618 us; the launch traced here: 616 us
  waiting for transfers between devices  283 us (46%)
  Pallas kernels  110 us (18%)
  local copies, waits for them, and re-layouts  77 us (12%)
  other arithmetic  71.5 us (12%)
  starting transfers between devices  52.8 us (9%)
  between operations  16.1 us (3%)
  matrix products  6.45 us (1%)
    ppermute x54, waiting for transfers between devices, permute(): return lax.ppermute(value, axis, xor_pairs(size, bit))  228 us
    pallas_call x1, Pallas kernels, gram_rows(): pl.pallas_call(functools.partial(gram_kernel, row_block, col_block, order...  74.1 us
    unnamed x70, local copies, waits for them, and re-layouts  56.2 us
    ppermute x54, starting transfers between devices, permute(): return lax.ppermute(value, axis, xor_pairs(size, bit))  52.5 us
    pallas_call x1, Pallas kernels, jacobian(): pl.pallas_call(functools.partial(jacobian_kernel, slots), out_shape=jax.S...  35.6 us
    another operation x7, other arithmetic, on_device(): factor_head = jnp.linalg.cholesky(panel_whole[:PB])  34.6 us
    all_gather x1, waiting for transfers between devices, on_device(): whole_rows = lax.all_gather(shifted, 'par', axis=1, tiled=True)  29.4 us
    all_gather x1, waiting for transfers between devices, on_device(): panel_whole = lax.all_gather(panel_part, 'walk', axis=0, tiled=True)  25.6 us
  transfers between devices with their start and end apart: 56, of which 24 were waited for; matrix products, arithmetic and copies ran while one was open for 12% of the time, Pallas kernels for 0%

profile of v1, /device:TPU:0, one launch (start us, length us, event | category | flops | bytes accessed | tf_op | source)
XLA Modules:
  0.0 616.4 jit_solution(16985510835746814547)
XLA Ops:
  10.5 2.1 constant_dynamic-slice_fusion.3
  14.5 2.2 copy.60
  16.7 3.6 collective-permute-start.1
  24.1 2.2 constant_dynamic-slice_fusion.1
  27.8 2.1 pad_maximum_fusion.4
  37.9 2.1 copy.59
  46.3 1.8 constant_dynamic-update-slice_fusion.22
  48.1 1.8 constant_dynamic-update-slice_fusion.43
  51.0 13.9 %collective-permute-done.4 = f32[2,64,1536]{2,1,0:T(8,128)S(1)} collective-permute-done((f32[2,64,1536]{2,1,0:T(8,128)}, f32[2,64,1536]{2,1,0:T(8,128)S(1)}, u32[]{:S(2)}, u32[]{:S(2)}) %collective-permute-start.4) | collective-permute-done | bytes 786464 | tf_op jit(solution)/shard_map/ppermute | solution.py:104
  67.7 1.7 collective-permute-start.9
  71.0 15.7 %collective-permute-done.8 = f32[2,64,1536]{2,1,0:T(8,128)S(1)} collective-permute-done((f32[2,64,1536]{2,1,0:T(8,128)S(1)}, f32[2,64,1536]{2,1,0:T(8,128)S(1)}, u32[]{:S(2)}, u32[]{:S(2)}) %collective-permute-start.8) | collective-permute-done | bytes 786464 | tf_op jit(solution)/shard_map/ppermute | solution.py:104
  89.3 2.6 collective-permute-start.11
  96.4 15.0 %collective-permute-done.13 = f32[2,64,1536]{2,1,0:T(8,128)S(1)} collective-permute-done((f32[2,64,1536]{2,1,0:T(8,128)S(1)}, f32[2,64,1536]{2,1,0:T(8,128)S(1)}, u32[]{:S(2)}, u32[]{:S(2)}) %collective-permute-start.13) | collective-permute-done | bytes 786464 | tf_op jit(solution)/shard_map/ppermute | solution.py:104
  113.2 8.3 %collective-permute-done.12 = f32[64,1536]{1,0:T(8,128)S(1)} collective-permute-done((f32[64,1536]{1,0:T(8,128)S(1)}, f32[64,1536]{1,0:T(8,128)S(1)}, u32[]{:S(2)}, u32[]{:S(2)}) %collective-permute-start.12) | collective-permute-done | bytes 393248 | tf_op jit(solution)/shard_map/ppermute | solution.py:104
  121.7 1.9 collective-permute-start.17
  129.7 10.9 %collective-permute-done.19 = f32[2,64,1536]{2,1,0:T(8,128)S(1)} collective-permute-done((f32[2,64,1536]{2,1,0:T(8,128)S(1)}, f32[2,64,1536]{2,1,0:T(8,128)S(1)}, u32[]{:S(2)}, u32[]{:S(2)}) %collective-permute-start.19) | collective-permute-done | bytes 786464 | tf_op jit(solution)/shard_map/ppermute | solution.py:104
  140.6 2.1 collective-permute-start.18
  143.4 5.6 collective-permute-done.18
  152.9 1.7 collective-permute-start.23
  154.8 10.0 %collective-permute-done.24 = f32[2,64,1536]{2,1,0:T(8,128)S(1)} collective-permute-done((f32[2,64,1536]{2,1,0:T(8,128)S(1)}, f32[2,64,1536]{2,1,0:T(8,128)S(1)}, u32[]{:S(2)}, u32[]{:S(2)}) %collective-permute-start.24) | collective-permute-done | bytes 786464 | tf_op jit(solution)/shard_map/ppermute | solution.py:104
  164.8 2.2 collective-permute-start.21
  170.0 10.5 %collective-permute-done.21 = f32[64,1536]{1,0:T(8,128)S(1)} collective-permute-done((f32[64,1536]{1,0:T(8,128)S(1)}, f32[64,1536]{1,0:T(8,128)S(1)}, u32[]{:S(2)}, u32[]{:S(2)}) %collective-permute-start.21) | collective-permute-done | bytes 393248 | tf_op jit(solution)/shard_map/ppermute | solution.py:104
  186.5 2.5 collective-permute-start.27
  189.7 13.1 %collective-permute-done.29 = f32[2,64,1536]{2,1,0:T(8,128)S(1)} collective-permute-done((f32[2,64,1536]{2,1,0:T(8,128)S(1)}, f32[2,64,1536]{2,1,0:T(8,128)S(1)}, u32[]{:S(2)}, u32[]{:S(2)}) %collective-permute-start.29) | collective-permute-done | bytes 786464 | tf_op jit(solution)/shard_map/ppermute | solution.py:104
  202.9 3.2 collective-permute-done.27
  209.4 15.5 %collective-permute-done.33 = f32[2,64,1536]{2,1,0:T(8,128)S(1)} collective-permute-done((f32[2,64,1536]{2,1,0:T(8,128)S(1)}, f32[2,64,1536]{2,1,0:T(8,128)S(1)}, u32[]{:S(2)}, u32[]{:S(2)}) %collective-permute-start.33) | collective-permute-done | bytes 786464 | tf_op jit(solution)/shard_map/ppermute | solution.py:104
  225.4 8.6 %collective-permute-done.31 = f32[64,1536]{1,0:T(8,128)S(1)} collective-permute-done((f32[64,1536]{1,0:T(8,128)S(1)}, f32[64,1536]{1,0:T(8,128)S(1)}, u32[]{:S(2)}, u32[]{:S(2)}) %collective-permute-start.31) | collective-permute-done | bytes 393248 | tf_op jit(solution)/shard_map/ppermute | solution.py:104
  234.0 1.9 collective-permute-start.40
  239.4 12.8 %collective-permute-done.40 = f32[2,64,1536]{2,1,0:T(8,128)S(1)} collective-permute-done((f32[2,64,1536]{2,1,0:T(8,128)S(1)}, f32[2,64,1536]{2,1,0:T(8,128)S(1)}, u32[]{:S(2)}, u32[]{:S(2)}) %collective-permute-start.40) | collective-permute-done | bytes 786464 | tf_op jit(solution)/shard_map/ppermute | solution.py:104
  252.2 2.1 collective-permute-start.38
  254.3 7.4 %collective-permute-done.38 = f32[64,1536]{1,0:T(8,128)S(1)} collective-permute-done((f32[64,1536]{1,0:T(8,128)S(1)}, f32[64,1536]{1,0:T(8,128)S(1)}, u32[]{:S(2)}, u32[]{:S(2)}) %collective-permute-start.38) | collective-permute-done | bytes 393248 | tf_op jit(solution)/shard_map/ppermute | solution.py:104
  265.6 8.6 %collective-permute-done.44 = f32[64,1536]{1,0:T(8,128)S(1)} collective-permute-done((f32[64,1536]{1,0:T(8,128)S(1)}, f32[64,1536]{1,0:T(8,128)S(1)}, u32[]{:S(2)}, u32[]{:S(2)}) %collective-permute-start.44) | collective-permute-done | bytes 393248 | tf_op jit(solution)/shard_map/ppermute | solution.py:104
  293.0 35.6 %jacobian.1.j_ref = f32[16,1536,256]{2,1,0:T(8,128)} custom-call(s32[32]{0:T(128)} %stack.375.rows_ref, f32[32,64,1536]{2,1,0:T(8,128)} %constant_dynamic-update-slice_fusion.f_ref, f32[32,64,1536]{2,1,0:T(8,128)} %slice_dynamic-update-slice_fusion.s_ref, f32[16,256]{1,0:T(8,128)} %reshape.83.scale_ref), custom_call_target="tpu_custom_call" | custom-call | tf_op jit(solution)/shard_map/jacobian/pallas_call | solution.py:181
  328.7 74.1 %gram_rows.1 = (f32[768,768]{1,0:T(8,128)}, f32[768,768]{1,0:T(8,128)}) custom-call(s32[4]{0:T(128)} %get-tuple-element.182.row_at, s32[4]{0:T(128)} %get-tuple-element.183.col_at, f32[16,1536,256]{2,1,0:T(8,128)} %jacobian.1.j_ref, bf16[1536,64]{1,0:T(8,128)(2,1)} %fusion.hot_ref, bf16[64,1536]{1,0:T(8,128)(2,1)} %fusion.4.hot_t_ref, f32[64,1]{1,0:T(8,128)} %copy.55.recip_ref), custom_call_target="tpu_custom_call" | custom-call | tf_op jit(solution)/shard_map/gram_rows/pallas_call | solution.py:250
  407.9 24.2 %collective-permute-done.50 = f32[384,768]{1,0:T(8,128)S(1)} collective-permute-done((f32[384,768]{1,0:T(8,128)S(1)}, f32[384,768]{1,0:T(8,128)S(1)}, u32[]{:S(2)}, u32[]{:S(2)}) %collective-permute-start.50) | collective-permute-done | bytes 1179680 | tf_op jit(solution)/shard_map/ppermute | solution.py:104
  437.4 10.6 %collective-permute-done.51 = f32[192,768]{1,0:T(8,128)S(1)} collective-permute-done((f32[192,768]{1,0:T(8,128)S(1)}, f32[192,768]{1,0:T(8,128)S(1)}, u32[]{:S(2)}, u32[]{:S(2)}) %collective-permute-start.51) | collective-permute-done | bytes 589856 | tf_op jit(solution)/shard_map/ppermute | solution.py:104
  448.1 2.2 collective-permute-start.52
  450.3 24.9 %collective-permute-done.52 = f32[192,768]{1,0:T(8,128)S(1)} collective-permute-done((f32[192,768]{1,0:T(8,128)S(1)}, f32[192,768]{1,0:T(8,128)S(1)}, u32[]{:S(2)}, u32[]{:S(2)}) %collective-permute-start.52) | collective-permute-done | bytes 589856 | tf_op jit(solution)/shard_map/ppermute | solution.py:104
  475.4 7.7 %collective-permute-done.53 = f32[192,384]{1,0:T(8,128)S(1)} collective-permute-done((f32[192,384]{1,0:T(8,128)S(1)}, f32[192,384]{1,0:T(8,128)S(1)}, u32[]{:S(2)}, u32[]{:S(2)}) %collective-permute-start.53) | collective-permute-done | bytes 294944 | tf_op jit(solution)/shard_map/ppermute | solution.py:104
  484.2 29.4 %all-gather.3.cloned.1.call-done = f32[192,1536]{1,0:T(8,128)} async-done(((f32[192,384]{1,0:T(8,128)}), f32[192,1536]{1,0:T(8,128)}) %all-gather.3.cloned.1.call-update) | async-done | bytes 1179664 | tf_op jit(solution)/shard_map/all_gather | solution.py:357
  513.6 1.6 slice.278
  515.3 25.6 %all-gather.5.cloned.1.call-done = f32[1536,256]{1,0:T(8,128)} async-done(((f32[192,256]{1,0:T(8,128)}), f32[1536,256]{1,0:T(8,128)}) %all-gather.5.cloned.1.call-update) | async-done | bytes 1572880 | tf_op jit(solution)/shard_map/all_gather | solution.py:359
  543.0 11.7 %cholesky.50 = f32[128,128]{1,0:T(8,128)S(1)} custom-call(f32[128,128]{1,0:T(8,128)S(1)} %cholesky.118), custom_call_target="Cholesky" | custom-call | tf_op jit(solution)/shard_map/jit(cholesky)/cholesky | solution.py:360
  554.8 9.8 %custom-call.15 = f32[1,128,128]{1,2,0:T(8,128)S(1)} custom-call(f32[1,128,128]{2,1,0:T(8,128)S(1)} %get-tuple-element.179), custom_call_target="InvertDiagBlocksLowerTriangular" | custom-call | tf_op jit(solution)/shard_map/jit(cholesky)/cholesky | solution.py:360
  565.1 11.7 %cholesky.105 = f32[128,128]{1,0:T(8,128)S(1)} custom-call(f32[128,128]{1,0:T(8,128)S(1)} %convolution_subtract_fusion.2), custom_call_target="Cholesky" | custom-call | tf_op jit(solution)/shard_map/jit(cholesky)/cholesky | solution.py:360
  579.6 4.3 while.1
  583.9 19.7 %custom-call.16 = f32[2,128,128]{1,2,0:T(8,128)S(1)} custom-call(f32[2,128,128]{2,1,0:T(8,128)S(1)} %get-tuple-element.125), custom_call_target="InvertDiagBlocksLowerTriangular" | custom-call | tf_op jit(solution)/shard_map/jit(_solve_triangular)/triangular_solve | solution.py:361
  607.4 2.2 convolution_subtract_fusion
  (231 shorter events, 113.5 us)
Async XLA Ops:
  7.2 506.4 %all-gather.3.cloned.1.call-start = ((), (), s32[]{:S(2)}) async-start(), calls=%async_computation | async-start | bytes 1474560 | tf_op jit(solution)/shard_map/all_gather | solution.py:357
  14.0 30.8 %collective-permute-start = (f32[1,64,1536]{2,1,0:T(8,128)S(1)}, f32[1,64,1536]{2,1,0:T(8,128)}, u32[]{:S(2)}, u32[]{:S(2)}) collective-permute-start(f32[1,64,1536]{2,1,0:T(8,128)S(1)} %bitcast.239), channel_id=1, source_target_pairs={{0,4},{4,0},{8,12},{12,8},{16,20},{20,16},{24,28},{28,24},{1,5},{5... | collective-permute-start | bytes 1179656 | tf_op jit(solution)/shard_map/ppermute | solution.py:104
  16.7 48.4 %collective-permute-start.1 = (f32[64,1536]{1,0:T(8,128)}, f32[64,1536]{1,0:T(8,128)}, u32[]{:S(2)}, u32[]{:S(2)}) collective-permute-start(f32[64,1536]{1,0:T(8,128)} %bitcast.47), channel_id=1, source_target_pairs={{0,2},{1,3},{2,0},{3,1},{4,6},{5,7},{6,4},{7,5},{8,10},{9,11},{10,... | collective-permute-start | bytes 1179656 | tf_op jit(solution)/shard_map/ppermute | solution.py:104
  21.3 43.8 %collective-permute-start.2 = (f32[64,1536]{1,0:T(8,128)}, f32[64,1536]{1,0:T(8,128)}, u32[]{:S(2)}, u32[]{:S(2)}) collective-permute-start(f32[64,1536]{1,0:T(8,128)} %bitcast.48), channel_id=1, source_target_pairs={{0,1},{1,0},{2,3},{3,2},{4,5},{5,4},{6,7},{7,6},{8,9},{9,8},{10,11... | collective-permute-start | bytes 1179656 | tf_op jit(solution)/shard_map/ppermute | solution.py:104
  29.9 20.0 %collective-permute-start.3 = (f32[2,64,1536]{2,1,0:T(8,128)S(1)}, f32[2,64,1536]{2,1,0:T(8,128)}, u32[]{:S(2)}, u32[]{:S(2)}) collective-permute-start(f32[2,64,1536]{2,1,0:T(8,128)S(1)} %get-tuple-element.175), channel_id=1, source_target_pairs={{0,8},{4,12},{8,0},{12,4},{16,24},{20,28},{24,16},{28,20},{1,9},{5... | collective-permute-start | bytes 2359304 | tf_op jit(solution)/shard_map/ppermute | solution.py:104
  32.7 15.4 %collective-permute-start.35 = (f32[1,64,1536]{2,1,0:T(8,128)S(1)}, f32[1,64,1536]{2,1,0:T(8,128)}, u32[]{:S(2)}, u32[]{:S(2)}) collective-permute-start(f32[1,64,1536]{2,1,0:T(8,128)S(1)} %bitcast.231), channel_id=1, source_target_pairs={{0,4},{4,0},{8,12},{12,8},{16,20},{20,16},{24,28},{28,24},{1,5},{5... | collective-permute-start | bytes 1179656 | tf_op jit(solution)/shard_map/ppermute | solution.py:104
  44.8 20.2 %collective-permute-start.4 = (f32[2,64,1536]{2,1,0:T(8,128)}, f32[2,64,1536]{2,1,0:T(8,128)S(1)}, u32[]{:S(2)}, u32[]{:S(2)}) collective-permute-start(f32[2,64,1536]{2,1,0:T(8,128)} %get-tuple-element.174), channel_id=1, source_target_pairs={{0,16},{4,20},{8,24},{12,28},{16,0},{20,4},{24,8},{28,12},{1,17},{... | collective-permute-start | bytes 2359304 | tf_op jit(solution)/shard_map/ppermute | solution.py:104
  65.2 21.8 %collective-permute-start.5 = (f32[2,64,1536]{2,1,0:T(8,128)S(1)}, f32[2,64,1536]{2,1,0:T(8,128)S(1)}, u32[]{:S(2)}, u32[]{:S(2)}) collective-permute-start(f32[2,64,1536]{2,1,0:T(8,128)S(1)} %get-tuple-element.173), channel_id=1, source_target_pairs={{0,4},{4,0},{8,12},{12,8},{16,20},{20,16},{24,28},{28,24},{1,5},{5... | collective-permute-start | bytes 2359304 | tf_op jit(solution)/shard_map/ppermute | solution.py:104
  65.3 21.7 %collective-permute-start.6 = (f32[64,1536]{1,0:T(8,128)}, f32[64,1536]{1,0:T(8,128)S(1)}, u32[]{:S(2)}, u32[]{:S(2)}) collective-permute-start(f32[64,1536]{1,0:T(8,128)} %bitcast.263), channel_id=1, source_target_pairs={{0,2},{1,3},{2,0},{3,1},{4,6},{5,7},{6,4},{7,5},{8,10},{9,11},{10,... | collective-permute-start | bytes 1179656 | tf_op jit(solution)/shard_map/ppermute | solution.py:104
  65.7 21.3 %collective-permute-start.7 = (f32[64,1536]{1,0:T(8,128)}, f32[64,1536]{1,0:T(8,128)S(1)}, u32[]{:S(2)}, u32[]{:S(2)}) collective-permute-start(f32[64,1536]{1,0:T(8,128)} %collective-permute-done.1), channel_id=1, source_target_pairs={{0,1},{1,0},{2,3},{3,2},{4,5},{5,4},{6,7},{7,6},{8,9},{9,8},{10,11... | collective-permute-start | bytes 1179656 | tf_op jit(solution)/shard_map/ppermute | solution.py:104
  67.3 19.4 %collective-permute-start.8 = (f32[2,64,1536]{2,1,0:T(8,128)S(1)}, f32[2,64,1536]{2,1,0:T(8,128)S(1)}, u32[]{:S(2)}, u32[]{:S(2)}) collective-permute-start(f32[2,64,1536]{2,1,0:T(8,128)S(1)} %pad_maximum_fusion.10), channel_id=1, source_target_pairs={{0,8},{4,12},{8,0},{12,4},{16,24},{20,28},{24,16},{28,20},{1,9},{5... | collective-permute-start | bytes 2359304 | tf_op jit(solution)/shard_map/ppermute | solution.py:104
  67.7 19.2 %collective-permute-start.9 = (f32[2,64,1536]{2,1,0:T(8,128)S(1)}, f32[2,64,1536]{2,1,0:T(8,128)S(1)}, u32[]{:S(2)}, u32[]{:S(2)}) collective-permute-start(f32[2,64,1536]{2,1,0:T(8,128)S(1)} %get-tuple-element.172), channel_id=1, source_target_pairs={{0,16},{4,20},{8,24},{12,28},{16,0},{20,4},{24,8},{28,12},{1,17},{... | collective-permute-start | bytes 2359304 | tf_op jit(solution)/shard_map/ppermute | solution.py:104
  86.7 65.4 %collective-permute-start.37 = (f32[1,64,1536]{2,1,0:T(8,128)S(1)}, f32[1,64,1536]{2,1,0:T(8,128)S(1)}, u32[]{:S(2)}, u32[]{:S(2)}) collective-permute-start(f32[1,64,1536]{2,1,0:T(8,128)S(1)} %bitcast.250), channel_id=1, source_target_pairs={{0,4},{4,0},{8,12},{12,8},{16,20},{20,16},{24,28},{28,24},{1,5},{5... | collective-permute-start | bytes 1179656 | tf_op jit(solution)/shard_map/ppermute | solution.py:104
  88.9 34.9 %collective-permute-start.10 = (f32[3,64,1536]{2,1,0:T(8,128)S(1)}, f32[3,64,1536]{2,1,0:T(8,128)S(1)}, u32[]{:S(2)}, u32[]{:S(2)}) collective-permute-start(f32[3,64,1536]{2,1,0:T(8,128)S(1)} %pad_maximum_fusion.2), channel_id=1, source_target_pairs={{0,4},{4,0},{8,12},{12,8},{16,20},{20,16},{24,28},{28,24},{1,5},{5... | collective-permute-start | bytes 3538952 | tf_op jit(solution)/shard_map/ppermute | solution.py:104
  89.3 23.9 %collective-permute-start.11 = (f32[64,1536]{1,0:T(8,128)S(1)}, f32[64,1536]{1,0:T(8,128)S(1)}, u32[]{:S(2)}, u32[]{:S(2)}) collective-permute-start(f32[64,1536]{1,0:T(8,128)S(1)} %bitcast.265), channel_id=1, source_target_pairs={{0,2},{1,3},{2,0},{3,1},{4,6},{5,7},{6,4},{7,5},{8,10},{9,11},{10,... | collective-permute-start | bytes 1179656 | tf_op jit(solution)/shard_map/ppermute | solution.py:104
  92.0 19.4 %collective-permute-start.13 = (f32[2,64,1536]{2,1,0:T(8,128)S(1)}, f32[2,64,1536]{2,1,0:T(8,128)S(1)}, u32[]{:S(2)}, u32[]{:S(2)}) collective-permute-start(f32[2,64,1536]{2,1,0:T(8,128)S(1)} %pad_maximum_fusion.11), channel_id=1, source_target_pairs={{0,8},{4,12},{8,0},{12,4},{16,24},{20,28},{24,16},{28,20},{1,9},{5... | collective-permute-start | bytes 2359304 | tf_op jit(solution)/shard_map/ppermute | solution.py:104
  93.3 19.7 %collective-permute-start.14 = (f32[2,64,1536]{2,1,0:T(8,128)S(1)}, f32[2,64,1536]{2,1,0:T(8,128)S(1)}, u32[]{:S(2)}, u32[]{:S(2)}) collective-permute-start(f32[2,64,1536]{2,1,0:T(8,128)S(1)} %pad_maximum_fusion.12), channel_id=1, source_target_pairs={{0,16},{4,20},{8,24},{12,28},{16,0},{20,4},{24,8},{28,12},{1,17},{... | collective-permute-start | bytes 2359304 | tf_op jit(solution)/shard_map/ppermute | solution.py:104
  111.4 10.1 %collective-permute-start.12 = (f32[64,1536]{1,0:T(8,128)S(1)}, f32[64,1536]{1,0:T(8,128)S(1)}, u32[]{:S(2)}, u32[]{:S(2)}) collective-permute-start(f32[64,1536]{1,0:T(8,128)S(1)} %bitcast.264), channel_id=1, source_target_pairs={{0,1},{1,0},{2,3},{3,2},{4,5},{5,4},{6,7},{7,6},{8,9},{9,8},{10,11... | collective-permute-start | bytes 1179656 | tf_op jit(solution)/shard_map/ppermute | solution.py:104
  113.0 163.3 %collective-permute-start.43 = (f32[1,64,1536]{2,1,0:T(8,128)S(1)}, f32[1,64,1536]{2,1,0:T(8,128)S(1)}, u32[]{:S(2)}, u32[]{:S(2)}) collective-permute-start(f32[1,64,1536]{2,1,0:T(8,128)S(1)} %bitcast.249), channel_id=1, source_target_pairs={{0,4},{4,0},{8,12},{12,8},{16,20},{20,16},{24,28},{28,24},{1,5},{5... | collective-permute-start | bytes 1179656 | tf_op jit(solution)/shard_map/ppermute | solution.py:104
  121.5 21.3 %collective-permute-start.16 = (f32[64,1536]{1,0:T(8,128)S(1)}, f32[64,1536]{1,0:T(8,128)S(1)}, u32[]{:S(2)}, u32[]{:S(2)}) collective-permute-start(f32[64,1536]{1,0:T(8,128)S(1)} %bitcast.261), channel_id=1, source_target_pairs={{0,2},{1,3},{2,0},{3,1},{4,6},{5,7},{6,4},{7,5},{8,10},{9,11},{10,... | collective-permute-start | bytes 1179656 | tf_op jit(solution)/shard_map/ppermute | solution.py:104
  121.7 21.2 %collective-permute-start.17 = (f32[64,1536]{1,0:T(8,128)S(1)}, f32[64,1536]{1,0:T(8,128)S(1)}, u32[]{:S(2)}, u32[]{:S(2)}) collective-permute-start(f32[64,1536]{1,0:T(8,128)S(1)} %collective-permute-done.6), channel_id=1, source_target_pairs={{0,1},{1,0},{2,3},{3,2},{4,5},{5,4},{6,7},{7,6},{8,9},{9,8},{10,11... | collective-permute-start | bytes 1179656 | tf_op jit(solution)/shard_map/ppermute | solution.py:104
  123.7 16.9 %collective-permute-start.19 = (f32[2,64,1536]{2,1,0:T(8,128)S(1)}, f32[2,64,1536]{2,1,0:T(8,128)S(1)}, u32[]{:S(2)}, u32[]{:S(2)}) collective-permute-start(f32[2,64,1536]{2,1,0:T(8,128)S(1)} %pad_maximum_fusion.13), channel_id=1, source_target_pairs={{0,16},{4,20},{8,24},{12,28},{16,0},{20,4},{24,8},{28,12},{1,17},{... | collective-permute-start | bytes 2359304 | tf_op jit(solution)/shard_map/ppermute | solution.py:104
  142.8 24.3 %collective-permute-start.15 = (f32[4,64,1536]{2,1,0:T(8,128)S(1)}, f32[4,64,1536]{2,1,0:T(8,128)S(1)}, u32[]{:S(2)}, u32[]{:S(2)}) collective-permute-start(f32[4,64,1536]{2,1,0:T(8,128)S(1)} %pad_maximum_fusion), channel_id=1, source_target_pairs={{0,4},{4,0},{8,12},{12,8},{16,20},{20,16},{24,28},{28,24},{1,5},{5... | collective-permute-start | bytes 4718600 | tf_op jit(solution)/shard_map/ppermute | solution.py:104
  149.0 15.8 %collective-permute-start.24 = (f32[2,64,1536]{2,1,0:T(8,128)S(1)}, f32[2,64,1536]{2,1,0:T(8,128)S(1)}, u32[]{:S(2)}, u32[]{:S(2)}) collective-permute-start(f32[2,64,1536]{2,1,0:T(8,128)S(1)} %pad_maximum_fusion.15), channel_id=1, source_target_pairs={{0,16},{4,20},{8,24},{12,28},{16,0},{20,4},{24,8},{28,12},{1,17},{... | collective-permute-start | bytes 2359304 | tf_op jit(solution)/shard_map/ppermute | solution.py:104
  152.9 28.5 %collective-permute-start.23 = (f32[64,1536]{1,0:T(8,128)S(1)}, f32[64,1536]{1,0:T(8,128)S(1)}, u32[]{:S(2)}, u32[]{:S(2)}) collective-permute-start(f32[64,1536]{1,0:T(8,128)S(1)} %collective-permute-done.17), channel_id=1, source_target_pairs={{0,8},{4,12},{8,0},{12,4},{16,24},{20,28},{24,16},{28,20},{1,9},{5... | collective-permute-start | bytes 1179656 | tf_op jit(solution)/shard_map/ppermute | solution.py:104
  154.7 28.5 %collective-permute-start.20 = (f32[2,64,1536]{2,1,0:T(8,128)S(1)}, f32[2,64,1536]{2,1,0:T(8,128)S(1)}, u32[]{:S(2)}, u32[]{:S(2)}) collective-permute-start(f32[2,64,1536]{2,1,0:T(8,128)S(1)} %pad_maximum_fusion.14), channel_id=1, source_target_pairs={{0,4},{4,0},{8,12},{12,8},{16,20},{20,16},{24,28},{28,24},{1,5},{5... | collective-permute-start | bytes 2359304 | tf_op jit(solution)/shard_map/ppermute | solution.py:104
  164.8 15.7 %collective-permute-start.21 = (f32[64,1536]{1,0:T(8,128)S(1)}, f32[64,1536]{1,0:T(8,128)S(1)}, u32[]{:S(2)}, u32[]{:S(2)}) collective-permute-start(f32[64,1536]{1,0:T(8,128)S(1)} %bitcast.258), channel_id=1, source_target_pairs={{0,2},{1,3},{2,0},{3,1},{4,6},{5,7},{6,4},{7,5},{8,10},{9,11},{10,... | collective-permute-start | bytes 1179656 | tf_op jit(solution)/shard_map/ppermute | solution.py:104
  167.1 14.3 %collective-permute-start.22 = (f32[64,1536]{1,0:T(8,128)S(1)}, f32[64,1536]{1,0:T(8,128)S(1)}, u32[]{:S(2)}, u32[]{:S(2)}) collective-permute-start(f32[64,1536]{1,0:T(8,128)S(1)} %bitcast.241), channel_id=1, source_target_pairs={{0,1},{1,0},{2,3},{3,2},{4,5},{5,4},{6,7},{7,6},{8,9},{9,8},{10,11... | collective-permute-start | bytes 1179656 | tf_op jit(solution)/shard_map/ppermute | solution.py:104
  181.4 21.5 %collective-permute-start.26 = (f32[64,1536]{1,0:T(8,128)S(1)}, f32[64,1536]{1,0:T(8,128)S(1)}, u32[]{:S(2)}, u32[]{:S(2)}) collective-permute-start(f32[64,1536]{1,0:T(8,128)S(1)} %bitcast.233), channel_id=1, source_target_pairs={{0,2},{1,3},{2,0},{3,1},{4,6},{5,7},{6,4},{7,5},{8,10},{9,11},{10,... | collective-permute-start | bytes 1179656 | tf_op jit(solution)/shard_map/ppermute | solution.py:104
  181.4 24.7 %collective-permute-start.28 = (f32[64,1536]{1,0:T(8,128)S(1)}, f32[64,1536]{1,0:T(8,128)S(1)}, u32[]{:S(2)}, u32[]{:S(2)}) collective-permute-start(f32[64,1536]{1,0:T(8,128)S(1)} %collective-permute-done.21), channel_id=1, source_target_pairs={{0,8},{4,12},{8,0},{12,4},{16,24},{20,28},{24,16},{28,20},{1,9},{5... | collective-permute-start | bytes 1179656 | tf_op jit(solution)/shard_map/ppermute | solution.py:104
  183.2 19.6 %collective-permute-start.29 = (f32[2,64,1536]{2,1,0:T(8,128)S(1)}, f32[2,64,1536]{2,1,0:T(8,128)S(1)}, u32[]{:S(2)}, u32[]{:S(2)}) collective-permute-start(f32[2,64,1536]{2,1,0:T(8,128)S(1)} %pad_maximum_fusion.16), channel_id=1, source_target_pairs={{0,16},{4,20},{8,24},{12,28},{16,0},{20,4},{24,8},{28,12},{1,17},{... | collective-permute-start | bytes 2359304 | tf_op jit(solution)/shard_map/ppermute | solution.py:104
  186.5 19.7 %collective-permute-start.27 = (f32[64,1536]{1,0:T(8,128)S(1)}, f32[64,1536]{1,0:T(8,128)S(1)}, u32[]{:S(2)}, u32[]{:S(2)}) collective-permute-start(f32[64,1536]{1,0:T(8,128)S(1)} %collective-permute-done.11), channel_id=1, source_target_pairs={{0,1},{1,0},{2,3},{3,2},{4,5},{5,4},{6,7},{7,6},{8,9},{9,8},{10,11... | collective-permute-start | bytes 1179656 | tf_op jit(solution)/shard_map/ppermute | solution.py:104
  202.8 87.8 %collective-permute-start.47 = (f32[2,64,1536]{2,1,0:T(8,128)S(1)}, f32[2,64,1536]{2,1,0:T(8,128)S(1)}, u32[]{:S(2)}, u32[]{:S(2)}) collective-permute-start(f32[2,64,1536]{2,1,0:T(8,128)S(1)} %pad_maximum_fusion.19), channel_id=1, source_target_pairs={{0,4},{4,0},{8,12},{12,8},{16,20},{20,16},{24,28},{28,24},{1,5},{5... | collective-permute-start | bytes 2359304 | tf_op jit(solution)/shard_map/ppermute | solution.py:104
  206.3 18.5 %collective-permute-start.33 = (f32[2,64,1536]{2,1,0:T(8,128)S(1)}, f32[2,64,1536]{2,1,0:T(8,128)S(1)}, u32[]{:S(2)}, u32[]{:S(2)}) collective-permute-start(f32[2,64,1536]{2,1,0:T(8,128)S(1)} %get-tuple-element.170), channel_id=1, source_target_pairs={{0,16},{4,20},{8,24},{12,28},{16,0},{20,4},{24,8},{28,12},{1,17},{... | collective-permute-start | bytes 2359304 | tf_op jit(solution)/shard_map/ppermute | solution.py:104
  207.7 28.3 %collective-permute-start.30 = (f32[2,64,1536]{2,1,0:T(8,128)S(1)}, f32[2,64,1536]{2,1,0:T(8,128)S(1)}, u32[]{:S(2)}, u32[]{:S(2)}) collective-permute-start(f32[2,64,1536]{2,1,0:T(8,128)S(1)} %get-tuple-element.171), channel_id=1, source_target_pairs={{0,4},{4,0},{8,12},{12,8},{16,20},{20,16},{24,28},{28,24},{1,5},{5... | collective-permute-start | bytes 2359304 | tf_op jit(solution)/shard_map/ppermute | solution.py:104
  207.7 26.3 %collective-permute-start.32 = (f32[64,1536]{1,0:T(8,128)S(1)}, f32[64,1536]{1,0:T(8,128)S(1)}, u32[]{:S(2)}, u32[]{:S(2)}) collective-permute-start(f32[64,1536]{1,0:T(8,128)S(1)} %collective-permute-done.26), channel_id=1, source_target_pairs={{0,8},{4,12},{8,0},{12,4},{16,24},{20,28},{24,16},{28,20},{1,9},{5... | collective-permute-start | bytes 1179656 | tf_op jit(solution)/shard_map/ppermute | solution.py:104
  234.0 18.2 %collective-permute-start.40 = (f32[2,64,1536]{2,1,0:T(8,128)S(1)}, f32[2,64,1536]{2,1,0:T(8,128)S(1)}, u32[]{:S(2)}, u32[]{:S(2)}) collective-permute-start(f32[2,64,1536]{2,1,0:T(8,128)S(1)} %pad_maximum_fusion.17), channel_id=1, source_target_pairs={{0,16},{4,20},{8,24},{12,28},{16,0},{20,4},{24,8},{28,12},{1,17},{... | collective-permute-start | bytes 2359304 | tf_op jit(solution)/shard_map/ppermute | solution.py:104
  237.7 24.7 %collective-permute-start.34 = (f32[1,64,1536]{2,1,0:T(8,128)S(1)}, f32[1,64,1536]{2,1,0:T(8,128)S(1)}, u32[]{:S(2)}, u32[]{:S(2)}) collective-permute-start(f32[1,64,1536]{2,1,0:T(8,128)S(1)} %bitcast.252), channel_id=1, source_target_pairs={{0,4},{4,0},{8,12},{12,8},{16,20},{20,16},{24,28},{28,24},{1,5},{5... | collective-permute-start | bytes 1179656 | tf_op jit(solution)/shard_map/ppermute | solution.py:104
  237.7 24.0 %collective-permute-start.39 = (f32[64,1536]{1,0:T(8,128)S(1)}, f32[64,1536]{1,0:T(8,128)S(1)}, u32[]{:S(2)}, u32[]{:S(2)}) collective-permute-start(f32[64,1536]{1,0:T(8,128)S(1)} %collective-permute-done.31), channel_id=1, source_target_pairs={{0,8},{4,12},{8,0},{12,4},{16,24},{20,28},{24,16},{28,20},{1,9},{5... | collective-permute-start | bytes 1179656 | tf_op jit(solution)/shard_map/ppermute | solution.py:104
  261.7 12.5 %collective-permute-start.41 = (f32[3,64,1536]{2,1,0:T(8,128)S(1)}, f32[3,64,1536]{2,1,0:T(8,128)S(1)}, u32[]{:S(2)}, u32[]{:S(2)}) collective-permute-start(f32[3,64,1536]{2,1,0:T(8,128)S(1)} %pad_maximum_fusion.3), channel_id=1, source_target_pairs={{0,4},{4,0},{8,12},{12,8},{16,20},{20,16},{24,28},{28,24},{1,5},{5... | collective-permute-start | bytes 3538952 | tf_op jit(solution)/shard_map/ppermute | solution.py:104
  261.8 13.8 %collective-permute-start.42 = (f32[4,64,1536]{2,1,0:T(8,128)S(1)}, f32[4,64,1536]{2,1,0:T(8,128)S(1)}, u32[]{:S(2)}, u32[]{:S(2)}) collective-permute-start(f32[4,64,1536]{2,1,0:T(8,128)S(1)} %pad_maximum_fusion.1), channel_id=1, source_target_pairs={{0,4},{4,0},{8,12},{12,8},{16,20},{20,16},{24,28},{28,24},{1,5},{5... | collective-permute-start | bytes 4718600 | tf_op jit(solution)/shard_map/ppermute | solution.py:104
  263.2 11.0 %collective-permute-start.44 = (f32[64,1536]{1,0:T(8,128)S(1)}, f32[64,1536]{1,0:T(8,128)S(1)}, u32[]{:S(2)}, u32[]{:S(2)}) collective-permute-start(f32[64,1536]{1,0:T(8,128)S(1)} %collective-permute-done.38), channel_id=1, source_target_pairs={{0,8},{4,12},{8,0},{12,4},{16,24},{20,28},{24,16},{28,20},{1,9},{5... | collective-permute-start | bytes 1179656 | tf_op jit(solution)/shard_map/ppermute | solution.py:104
  404.1 28.0 %collective-permute-start.50 = (f32[384,768]{1,0:T(8,128)S(1)}, f32[384,768]{1,0:T(8,128)S(1)}, u32[]{:S(2)}, u32[]{:S(2)}) collective-permute-start(f32[384,768]{1,0:T(8,128)S(1)} %slice.221), channel_id=1, source_target_pairs={{0,16},{4,20},{8,24},{12,28},{16,0},{20,4},{24,8},{28,12},{1,17},{... | collective-permute-start | bytes 3538952 | tf_op jit(solution)/shard_map/ppermute | solution.py:104
  407.0 27.6 %collective-permute-start.48 = (f32[384,768]{1,0:T(8,128)S(1)}, f32[384,768]{1,0:T(8,128)S(1)}, u32[]{:S(2)}, u32[]{:S(2)}) collective-permute-start(f32[384,768]{1,0:T(8,128)S(1)} %slice.217), channel_id=1, source_target_pairs={{0,8},{4,12},{8,0},{12,4},{16,24},{20,28},{24,16},{28,20},{1,9},{5... | collective-permute-start | bytes 3538952 | tf_op jit(solution)/shard_map/ppermute | solution.py:104
  433.6 14.5 %collective-permute-start.51 = (f32[192,768]{1,0:T(8,128)S(1)}, f32[192,768]{1,0:T(8,128)S(1)}, u32[]{:S(2)}, u32[]{:S(2)}) collective-permute-start(f32[192,768]{1,0:T(8,128)S(1)} %slice.275), channel_id=1, source_target_pairs={{0,8},{4,12},{8,0},{12,4},{16,24},{20,28},{24,16},{28,20},{1,9},{5... | collective-permute-start | bytes 1769480 | tf_op jit(solution)/shard_map/ppermute | solution.py:104
  436.1 14.2 %collective-permute-start.49 = (f32[192,768]{1,0:T(8,128)S(1)}, f32[192,768]{1,0:T(8,128)S(1)}, u32[]{:S(2)}, u32[]{:S(2)}) collective-permute-start(f32[192,768]{1,0:T(8,128)S(1)} %slice.273), channel_id=1, source_target_pairs={{0,16},{4,20},{8,24},{12,28},{16,0},{20,4},{24,8},{28,12},{1,17},{... | collective-permute-start | bytes 1769480 | tf_op jit(solution)/shard_map/ppermute | solution.py:104
  448.1 27.1 %collective-permute-start.52 = (f32[192,768]{1,0:T(8,128)S(1)}, f32[192,768]{1,0:T(8,128)S(1)}, u32[]{:S(2)}, u32[]{:S(2)}) collective-permute-start(f32[192,768]{1,0:T(8,128)S(1)} %slice_add_fusion.2), channel_id=1, source_target_pairs={{0,2},{1,3},{2,0},{3,1},{4,6},{5,7},{6,4},{7,5},{8,10},{9,11},{10,... | collective-permute-start | bytes 1769480 | tf_op jit(solution)/shard_map/ppermute | solution.py:104
  483.9 57.0 %all-gather.5.cloned.1.call-start = ((), (), s32[]{:S(2)}) async-start(), calls=%async_computation.1 | async-start | bytes 1769472 | tf_op jit(solution)/shard_map/all_gather | solution.py:359
  (12 other events, 207.6 us)
Sparse Core Ops, SparseCore 0:
  484.0 29.4 all-gather.2
  516.0 24.7 all-gather.4

commit v2 on v1

--- a/solution.py
+++ b/solution.py
@@ -41,27 +41,34 @@
             self.place.append(seen[kind])
             seen[kind] += 1
         self.blocks = {"F": 1 << seen["I"], "S": 1 << seen["J"]}
+        self.order = {
+            side: sorted(
+                range(len(self.dims)), key=lambda k: (self.dims[k][0] == "walk", not self.splits(side, self.dims[k][2]))
+            )
+            for side in ("F", "S")
+        }
         self.rounds = self.schedule()
 
     def splits(self, side, kind):
         return (side == "F") == (kind == "I")
 
-    def depth(self, side, src, rb, first):
+    def depth(self, side, src, rb, after):
         best = 0
-        for k in range(first, len(self.dims)):
-            kind = self.dims[k][2]
-            if self.splits(side, kind):
+        order = self.order[side]
+        for k in order[order.index(after) + 1 :]:
+            if self.splits(side, self.dims[k][2]):
                 if rb >> self.place[k] & 1:
-                    return max(best, 1 + self.depth(side, src, rb ^ (1 << self.place[k]), k + 1))
+                    return max(best, 1 + self.depth(side, src, rb ^ (1 << self.place[k]), k))
             else:
-                best = max(best, 1 + self.depth(side, src, rb, k + 1))
+                best = max(best, 1 + self.depth(side, src, rb, k))
         return best
 
     def tasks(self):
         out = []
         for side in ("F", "S"):
             live = [(0, rb) for rb in range(self.blocks[side])]
-            for k, (_, _, kind) in enumerate(self.dims):
+            for k in self.order[side]:
+                kind = self.dims[k][2]
                 kept, made = [], []
                 for src, rb in live:
                     if self.splits(side, kind):
@@ -85,7 +92,12 @@
             chosen = []
             for k, (axis, _, _) in enumerate(self.dims):
                 ready = [t for t in left if t[0] == k and t[1] in have]
-                ready.sort(key=lambda t: -self.depth(t[2][0], t[2][1], t[2][2], k + 1))
+                ready.sort(
+                    key=lambda t: (
+                        not self.splits(t[1][0], self.dims[k][2]),
+                        -self.depth(*t[2], k),
+                    )
+                )
                 chosen += ready[: 1 if axis == "par" else 2]
             left = [t for t in left if t not in chosen]
             have |= {t[2] for t in chosen}
@@ -104,27 +116,34 @@
     return lax.ppermute(value, axis, xor_pairs(size, bit))
 
 
-def exchange(plan, pieces):
+def exchange(plan, pieces, block):
     sizes = {"walk": plan.walk_size, "par": plan.par_size}
     held = dict(pieces)
-    stacks = {"F": [], "S": []}
-    fresh = [("F", 0, 0), ("S", 0, 0)]
+    planes, chips = plan.par_size, plan.walk_size // 2
+    members = {q: [q | m * planes for m in range(chips)] for q in range(planes)}
+    waiting = list(range(planes))
+    own, other, sent = {}, {}, []
     gate = []
-    for chosen in plan.rounds + [[]]:
+    rounds = list(plan.rounds)
+    while rounds or waiting or sent:
+        chosen = rounds.pop(0) if rounds else []
         groups = {}
         for k, src, dst in chosen:
             groups.setdefault((k, held[src].shape), []).append((src, dst))
-        stacked = {}
-        for side in ("F", "S"):
-            names = [n for n in fresh if n[0] == side]
-            if names:
-                stacked[side] = names
-        keys = sorted({s for pairs in groups.values() for s, _ in pairs} | set(fresh))
-        if gate:
+        keys = sorted({s for pairs in groups.values() for s, _ in pairs})
+        if gate and keys:
             tied = lax.optimization_barrier(tuple(held[n] for n in keys) + tuple(held[n] for n in gate))
             for n, v in zip(keys + gate, tied):
                 held[n] = v
-        fresh, gate = [], []
+        gate = []
+        for q in sent:
+            other[q] = permute(own[q], "walk", plan.walk_size, 1)
+        sent = []
+        for q in list(waiting):
+            if all((side, m, 0) in held for side in ("F", "S") for m in members[q]):
+                own[q] = block([held["F", m, 0] for m in members[q]], [held["S", m, 0] for m in members[q]])
+                waiting.remove(q)
+                sent.append(q)
         for (k, _), pairs in groups.items():
             axis, bit, _ = plan.dims[k]
             if len(pairs) == 1:
@@ -134,66 +153,49 @@
                 for i, (_, d) in enumerate(pairs):
                     held[d] = moved[i]
             gate += [d for _, d in pairs]
-            fresh += [d for _, d in pairs if d[2] == 0]
-        for side, names in stacked.items():
-            own = jnp.stack([held[n] for n in names])
-            other = permute(own, "walk", plan.walk_size, 1)
-            stacks[side].append(([(n[1], 0) for n in names], own))
-            stacks[side].append(([(n[1], 1) for n in names], other))
-    return stacks
-
-
-def gathered(stacks, order):
-    sources = [s for names, _ in stacks for s in names]
-    whole = jnp.concatenate([a for _, a in stacks], axis=0)
-    return whole, sources
-
-
-def jacobian_kernel(slots, rows_ref, f_ref, s_ref, scale_ref, out_ref):
-    del rows_ref
-    ib, lanes = f_ref.shape[1:]
-    jb = s_ref.shape[1]
+    return [own[q] for q in range(planes)] + [other[q] for q in range(planes)], [
+        [(m, core) for m in members[q]] for core in range(2) for q in range(planes)
+    ]
+
+
+def jacobian_kernel(slots, count, *refs):
+    lefts, rights, scale_ref, out_ref = refs[:count], refs[count : 2 * count], refs[2 * count], refs[-1]
+    ib = lefts[0].shape[0]
+    jb = rights[0].shape[0]
     together = LANES // slots
     parts = LANES // jb
-    tiles = ib // parts
     lane = lax.broadcasted_iota(jnp.int32, (together, LANES), 1)
     row = lax.broadcasted_iota(jnp.int32, (together, LANES), 0)
     mine = (lane >= row * slots) & (lane < row * slots + slots)
-    for g in range(lanes // LANES):
-        left = f_ref[0, :, g * LANES : (g + 1) * LANES]
-        right = s_ref[0, :, g * LANES : (g + 1) * LANES].astype(jnp.bfloat16)
+    for n in range(count):
+        left = lefts[n][...]
+        right = rights[n][...].astype(jnp.bfloat16)
         spread = jnp.where(mine[None], left[:, None, :], 0.0).reshape(ib * together, LANES)
         block = lax.dot_general(
             spread.astype(jnp.bfloat16), right, CONTRACT_LAST, preferred_element_type=jnp.float32
         )
-        block = block.reshape(parts, tiles, together, jb)
+        block = block.reshape(parts, ib // parts, together, jb)
         for b in range(parts):
-            out_ref[:, g * together : (g + 1) * together, b * jb : (b + 1) * jb] = (
-                block[b] * scale_ref[:, b * jb : (b + 1) * jb][:, None, :]
-            )
-
-
-def jacobian(rows, features, signals, scaling, walkers, slots):
-    sources, ib, lanes = features.shape
-    jb = signals.shape[1]
+            out_ref[:, n, :, b * jb : (b + 1) * jb] = block[b] * scale_ref[:, b * jb : (b + 1) * jb][:, None, :]
+
+
+def jacobian(lefts, rights, scaling, slots):
+    count = len(lefts)
+    ib, lanes = lefts[0].shape
+    jb = rights[0].shape[0]
     tiles = ib * jb // LANES
-    per_source = lanes // slots
+    together = LANES // slots
     return pl.pallas_call(
-        functools.partial(jacobian_kernel, slots),
-        out_shape=jax.ShapeDtypeStruct((tiles, walkers, LANES), jnp.float32),
-        grid_spec=pltpu.PrefetchScalarGridSpec(
-            num_scalar_prefetch=1,
-            grid=(sources,),
-            in_specs=[
-                pl.BlockSpec((1, ib, lanes), lambda q, rows: (q, 0, 0)),
-                pl.BlockSpec((1, jb, lanes), lambda q, rows: (q, 0, 0)),
-                pl.BlockSpec((tiles, LANES), lambda q, rows: (0, 0)),
-            ],
-            out_specs=pl.BlockSpec((tiles, per_source, LANES), lambda q, rows: (0, rows[q], 0)),
-        ),
+        functools.partial(jacobian_kernel, slots, count),
+        out_shape=jax.ShapeDtypeStruct((tiles, count, lanes // slots, LANES), jnp.float32),
+        grid=(lanes // LANES,),
+        in_specs=[pl.BlockSpec((ib, LANES), lambda g: (0, g))] * count
+        + [pl.BlockSpec((jb, LANES), lambda g: (0, g))] * count
+        + [pl.BlockSpec((tiles, LANES), lambda g: (0, 0))],
+        out_specs=pl.BlockSpec((tiles, count, together, LANES), lambda g: (0, 0, g, 0)),
         compiler_params=pltpu.CompilerParams(vmem_limit_bytes=VMEM_LIMIT),
         name="jacobian",
-    )(rows, features, signals, scaling)
+    )(*lefts, *rights, scaling)
 
 
 def split_two(value):
@@ -201,73 +203,73 @@
     return high, (value - high.astype(jnp.float32)).astype(jnp.bfloat16)
 
 
-def gram_kernel(
-    row_block, col_block, orders, row_at, col_at, j_ref, hot_ref, hot_t_ref, recip_ref, a_ref, b_ref, high_ref, low_ref
-):
+def gram_kernel(row_block, col_block, orders, count, row_at, col_at, place_at, *refs):
+    pieces = refs[:count]
+    hot_ref, hot_t_ref, recip_ref, a_ref, b_ref, value_ref, high_ref, low_ref = refs[count:]
+
     @pl.when(pl.program_id(0) == 0)
     def _():
         a_ref[...] = jnp.zeros_like(a_ref)
         b_ref[...] = jnp.zeros_like(b_ref)
 
-    value = j_ref[0]
+    members, rows = pieces[0].shape[1:3]
+    for a in range(count):
+        for m in range(members):
+            value_ref[pl.ds(pl.multiple_of(place_at[a * members + m], 8), rows), :] = pieces[a][0, m]
+    value = value_ref[...]
     high, low = split_two(value)
     dot = functools.partial(jnp.dot, preferred_element_type=jnp.float32)
     means = (dot(hot_t_ref[...], high) + dot(hot_t_ref[...], low)) * recip_ref[...]
-    first, rest = split_two(means)
-    second, third = split_two(means - first.astype(jnp.float32))
+    first, second = split_two(means)
     hot = hot_ref[...]
-    value = value - (dot(hot, first) + dot(hot, second))
-    del rest, third
-    high, low = split_two(value)
+    high, low = split_two(value - (dot(hot, first) + dot(hot, second)))
     high_ref[...] = high
     low_ref[...] = low
-    slots = len(orders[0])
-    left = []
-    for s in range(slots):
-        at = pl.ds(pl.multiple_of(row_at[s], 16), row_block)
-        h, l = high_ref[at, :], low_ref[at, :]
-        left.append(jnp.concatenate([h, h, l], axis=1))
-    left = jnp.concatenate(left, axis=0)
     blocks = col_at.shape[0]
     for half, out in enumerate((a_ref, b_ref)):
+        left = []
+        for s in orders[half]:
+            at = pl.ds(pl.multiple_of(row_at[s], 16), row_block)
+            h, l = high_ref[at, :], low_ref[at, :]
+            left.append(jnp.concatenate([h, h, l], axis=1))
+        left = jnp.concatenate(left, axis=0)
+        right = []
         for n in range(blocks // 2):
             at = pl.ds(pl.multiple_of(col_at[half * (blocks // 2) + n], 16), col_block)
             h, l = high_ref[at, :], low_ref[at, :]
-            right = jnp.concatenate([h, l, h], axis=1)
-            got = lax.dot_general(left, right, CONTRACT_LAST, preferred_element_type=jnp.float32)
-            for place, s in enumerate(orders[half]):
-                out[place * row_block : (place + 1) * row_block, n * col_block : (n + 1) * col_block] += got[
-                    s * row_block : (s + 1) * row_block
-                ]
-
-
-def gram_rows(columns, hot, hot_t, recip, row_at, col_at, row_block, col_block, orders):
-    tiles, walkers, lanes = columns.shape
-    groups = hot.shape[1]
+            right.append(jnp.concatenate([h, l, h], axis=1))
+        right = jnp.concatenate(right, axis=0)
+        out[...] += lax.dot_general(left, right, CONTRACT_LAST, preferred_element_type=jnp.float32)
+
+
+def gram_rows(pieces, hot, hot_t, recip, row_at, col_at, place_at, row_block, col_block, orders):
+    tiles, members, rows, lanes = pieces[0].shape
+    walkers, groups = hot.shape
     slots = len(orders[0])
     half = jax.ShapeDtypeStruct((slots * row_block, walkers // 2), jnp.float32)
-    fixed = lambda t, r, c: (0, 0)
+    fixed = lambda t, *_: (0, 0)
     return pl.pallas_call(
-        functools.partial(gram_kernel, row_block, col_block, orders),
+        functools.partial(gram_kernel, row_block, col_block, orders, len(pieces)),
         out_shape=(half, half),
         grid_spec=pltpu.PrefetchScalarGridSpec(
-            num_scalar_prefetch=2,
+            num_scalar_prefetch=3,
             grid=(tiles,),
-            in_specs=[
-                pl.BlockSpec((1, walkers, lanes), lambda t, r, c: (t, 0, 0)),
+            in_specs=[pl.BlockSpec((1, members, rows, lanes), lambda t, *_: (t, 0, 0, 0))] * len(pieces)
+            + [
                 pl.BlockSpec((walkers, groups), fixed),
                 pl.BlockSpec((groups, walkers), fixed),
                 pl.BlockSpec((groups, 1), fixed),
             ],
             out_specs=(pl.BlockSpec(half.shape, fixed), pl.BlockSpec(half.shape, fixed)),
             scratch_shapes=[
+                pltpu.VMEM((walkers, lanes), jnp.float32),
                 pltpu.VMEM((walkers, lanes), jnp.bfloat16),
                 pltpu.VMEM((walkers, lanes), jnp.bfloat16),
             ],
         ),
         compiler_params=pltpu.CompilerParams(vmem_limit_bytes=VMEM_LIMIT),
         name="gram_rows",
-    )(row_at, col_at, columns, hot, hot_t, recip)
+    )(row_at, col_at, place_at, *pieces, hot, hot_t, recip)
 
 
 def on_device(features, signals, param_scale, geometry, electrons):
@@ -301,24 +303,16 @@
         for rb in range(plan.blocks[side]):
             pieces[side, 0, rb] = lax.dynamic_slice_in_dim(flat, (own[side] ^ rb) * size, size, 0)
     ib, jb = width // plan.blocks["F"], width // plan.blocks["S"]
-    stacks = exchange(plan, pieces)
-    left, left_names = gathered(stacks["F"], None)
-    right, right_names = gathered(stacks["S"], None)
-    if left_names != right_names:
-        right = jnp.concatenate(
-            [right[i : i + 1] for i in [right_names.index(n) for n in left_names]], axis=0
-        )
-    rows = []
-    for src, core in left_names:
-        walk_flip, par_flip = plan.flip(src)
-        rows.append((walk_index ^ (walk_flip | core)) * par_size + (par_index ^ par_flip))
-    rows = jnp.stack(rows).astype(jnp.int32)
-
     parts = LANES // jb
     scaling = param_scale * (1.0 / math.sqrt(slots_count * width * width))
     scaling = lax.dynamic_slice(scaling, (own["F"] * ib, own["S"] * jb), (ib, jb))
     scaling = scaling.reshape(parts, ib // parts, jb).transpose(1, 0, 2).reshape(ib // parts, LANES)
-    columns = jacobian(rows, left, right, scaling, walkers, slots_count)
+    columns, names = exchange(plan, pieces, lambda f, s: jacobian(f, s, scaling, slots_count))
+    place_at = []
+    for src, core in [n for members in names for n in members]:
+        walk_flip, par_flip = plan.flip(src)
+        place_at.append((walk_index ^ (walk_flip | core)) * par_size + (par_index ^ par_flip))
+    place_at = (jnp.stack(place_at) * per_device).astype(jnp.int32)
 
     matches = geometry[:, None] == jnp.arange(groups, dtype=jnp.int32)[None, :]
     hot = matches.astype(jnp.bfloat16)
@@ -336,7 +330,7 @@
     orders = tuple(
         tuple(sorted(range(slots), key=lambda s, o=o: [s >> b & 1 for b in o])) for o in sweeps
     )
-    halves = list(gram_rows(columns, hot, hot_t, recip, row_at, col_at, row_block, col_block, orders))
+    halves = list(gram_rows(columns, hot, hot_t, recip, row_at, col_at, place_at, row_block, col_block, orders))
     for step in range(chip_bits):
         moved = []
         for h in range(2):

time: 618 us -> 469 us (0.76)
  waiting for transfers between devices: 283 us -> 203 us
  local copies, waits for them, and re-layouts: 77 us -> 36.6 us
  Pallas kernels: 110 us -> 87.5 us
    ppermute x54 -> x36, waiting for transfers between devices: 228 us -> 146 us  [permute(): return lax.ppermute(value, axis, xor_pairs(size, bit))]
    unnamed x70 -> x69, local copies, waits for them, and re-layouts: 56.2 us -> 10.4 us
    pallas_call x1, Pallas kernels: 74.1 us -> 61.2 us  [gram_rows(): pl.pallas_call(functools.partial(gram_kernel, row_block, col_block, order...]
    pallas_call x1 -> x4, Pallas kernels: 35.6 us -> 26.3 us  [jacobian(): pl.pallas_call(functools.partial(jacobian_kernel, slots, count), out_shap...]
    squeeze x11 -> x10, local copies, waits for them, and re-layouts: 1.68 us -> 11 us  [exchange(): held[d] = moved[i]]
    ppermute x54 -> x36, starting transfers between devices: 52.5 us -> 48.4 us  [permute(): return lax.ppermute(value, axis, xor_pairs(size, bit))]
  transfers between devices with their start and end apart: 56 -> 38, of which waited for: 24 -> 27; matrix products, arithmetic and copies ran while one was open for 12% -> 5% of each run, Pallas kernels for 0% -> 6%
where the time goes in v2:
time: 469 us; the launch traced here: 467 us
  waiting for transfers between devices  203 us (43%)
  Pallas kernels  87.5 us (19%)
  other arithmetic  69.1 us (15%)
  starting transfers between devices  48.7 us (10%)
  local copies, waits for them, and re-layouts  36.6 us (8%)
  between operations  15.9 us (3%)
  matrix products  5.49 us (1%)
    ppermute x36, waiting for transfers between devices, permute(): return lax.ppermute(value, axis, xor_pairs(size, bit))  146 us
    pallas_call x1, Pallas kernels, gram_rows(): pl.pallas_call(functools.partial(gram_kernel, row_block, col_block, order...  61.2 us
    ppermute x36, starting transfers between devices, permute(): return lax.ppermute(value, axis, xor_pairs(size, bit))  48.4 us
    another operation x7, other arithmetic, on_device(): factor_head = jnp.linalg.cholesky(panel_whole[:PB])  34.6 us
    all_gather x1, waiting for transfers between devices, on_device(): whole_rows = lax.all_gather(shifted, 'par', axis=1, tiled=True)  31.6 us
    pallas_call x4, Pallas kernels, jacobian(): pl.pallas_call(functools.partial(jacobian_kernel, slots, count), out_shap...  26.3 us
    all_gather x1, waiting for transfers between devices, on_device(): panel_whole = lax.all_gather(panel_part, 'walk', axis=0, tiled=True)  25.6 us
    another operation x3, other arithmetic, on_device(): jax.scipy.linalg.solve_triangular(factor_head, jnp.eye(PB, dtype=jnp.floa...  19.7 us
  transfers between devices with their start and end apart: 38, of which 27 were waited for; matrix products, arithmetic and copies ran while one was open for 5% of the time, Pallas kernels for 6%

profile of v2, /device:TPU:0, one launch (start us, length us, event | category | flops | bytes accessed | tf_op | source)
XLA Modules:
  0.0 466.6 jit_solution(7542972660661773741)
XLA Ops:
  10.6 2.1 constant_dynamic-slice_fusion.3
  15.5 2.5 constant_dynamic-slice_fusion.1
  18.0 2.2 copy.65
  20.2 2.0 pad_maximum_fusion.1
  22.2 3.0 collective-permute-start.3
  26.5 2.1 pad_maximum_fusion
  31.0 2.6 collective-permute-start
  35.0 1.6 collective-permute-start.1
  38.7 4.4 collective-permute-done.3
  43.1 1.9 slice_bitcast_fusion.16
  45.0 2.9 collective-permute-done.2
  47.9 1.9 slice_bitcast_fusion.18
  54.8 2.0 collective-permute-start.5
  56.7 12.7 %collective-permute-done.7 = f32[2,64,1536]{2,1,0:T(8,128)S(1)} collective-permute-done((f32[2,64,1536]{2,1,0:T(8,128)S(1)}, f32[2,64,1536]{2,1,0:T(8,128)S(1)}, u32[]{:S(2)}, u32[]{:S(2)}) %collective-permute-start.7) | collective-permute-done | bytes 786464 | tf_op jit(solution)/shard_map/ppermute | solution.py:116
  72.9 1.5 collective-permute-start.10
  74.4 2.4 collective-permute-start.8
  76.8 1.8 collective-permute-start.9
  78.6 10.4 %collective-permute-done.11 = f32[2,64,1536]{2,1,0:T(8,128)S(1)} collective-permute-done((f32[2,64,1536]{2,1,0:T(8,128)S(1)}, f32[2,64,1536]{2,1,0:T(8,128)S(1)}, u32[]{:S(2)}, u32[]{:S(2)}) %collective-permute-start.11) | collective-permute-done | bytes 786464 | tf_op jit(solution)/shard_map/ppermute | solution.py:116
  92.4 1.8 collective-permute-start.12
  94.2 2.4 collective-permute-start.13
  98.3 13.0 %collective-permute-done.12 = f32[64,1536]{1,0:T(8,128)S(1)} collective-permute-done((f32[64,1536]{1,0:T(8,128)S(1)}, f32[64,1536]{1,0:T(8,128)S(1)}, u32[]{:S(2)}, u32[]{:S(2)}) %collective-permute-start.12) | collective-permute-done | bytes 393248 | tf_op jit(solution)/shard_map/ppermute | solution.py:116
  113.0 3.3 collective-permute-start.16
  116.3 1.8 collective-permute-start.17
  118.0 10.6 %collective-permute-done.19 = f32[2,64,1536]{2,1,0:T(8,128)S(1)} collective-permute-done((f32[2,64,1536]{2,1,0:T(8,128)S(1)}, f32[2,64,1536]{2,1,0:T(8,128)S(1)}, u32[]{:S(2)}, u32[]{:S(2)}) %collective-permute-start.19) | collective-permute-done | bytes 786464 | tf_op jit(solution)/shard_map/ppermute | solution.py:116
  130.3 2.1 collective-permute-done.16.refs_4_
  136.4 2.4 collective-permute-start.21
  138.9 12.0 %collective-permute-done.23 = f32[2,64,1536]{2,1,0:T(8,128)S(1)} collective-permute-done((f32[2,64,1536]{2,1,0:T(8,128)S(1)}, f32[2,64,1536]{2,1,0:T(8,128)S(1)}, u32[]{:S(2)}, u32[]{:S(2)}) %collective-permute-start.23) | collective-permute-done | bytes 786464 | tf_op jit(solution)/shard_map/ppermute | solution.py:116
  157.3 6.6 %jacobian.4.refs_0_ = f32[16,4,48,256]{3,2,1,0:T(8,128)} custom-call(f32[64,1536]{1,0:T(8,128)} %bitcast.158, f32[64,1536]{1,0:T(8,128)} %copy-done.3, f32[64,1536]{1,0:T(8,128)} %get-tuple-element.49.refs_2_, f32[64,1536]{1,0:T(8,128)} %get-tuple-element.55.refs_3_, f32[64,1536]{1,0:T(8,128)} %bitcast.161, f32[64,1536]{1,0:T(8,128)} %get-tuple-element.56.refs_5_, ...), custom_call_target="tpu_custom_call" | custom-call | tf_op jit(solution)/shard_map/jacobian/pallas_call | solution.py:188
  163.9 6.6 %jacobian.6.refs_2_ = f32[16,4,48,256]{3,2,1,0:T(8,128)} custom-call(f32[64,1536]{1,0:T(8,128)} %copy-done.20, f32[64,1536]{1,0:T(8,128)} %copy-done.18, f32[64,1536]{1,0:T(8,128)} %get-tuple-element.84.refs_2_, f32[64,1536]{1,0:T(8,128)} %get-tuple-element.85.refs_3_, f32[64,1536]{1,0:T(8,128)} %copy-done.16, f32[64,1536]{1,0:T(8,128)} %get-tuple-element.86.refs_5_, ...), custom_call_target="tpu_custom_call" | custom-call | tf_op jit(solution)/shard_map/jacobian/pallas_call | solution.py:188
  171.0 6.6 %jacobian.5.refs_1_ = f32[16,4,48,256]{3,2,1,0:T(8,128)} custom-call(f32[64,1536]{1,0:T(8,128)} %copy-done.15, f32[64,1536]{1,0:T(8,128)} %copy-done.4, f32[64,1536]{1,0:T(8,128)} %get-tuple-element.75.refs_2_, f32[64,1536]{1,0:T(8,128)} %get-tuple-element.76.refs_3_, f32[64,1536]{1,0:T(8,128)} %copy-done.19, f32[64,1536]{1,0:T(8,128)} %get-tuple-element.82.refs_5_, ...), custom_call_target="tpu_custom_call" | custom-call | tf_op jit(solution)/shard_map/jacobian/pallas_call | solution.py:188
  178.4 6.6 %jacobian.7.refs_3_ = f32[16,4,48,256]{3,2,1,0:T(8,128)} custom-call(f32[64,1536]{1,0:T(8,128)} %collective-permute-done.21.refs_0_, f32[64,1536]{1,0:T(8,128)} %copy-done.7, f32[64,1536]{1,0:T(8,128)} %copy-done.24, f32[64,1536]{1,0:T(8,128)} %get-tuple-element.89.refs_3_, f32[64,1536]{1,0:T(8,128)} %collective-permute-done.20.refs_4_, ...), custom_call_target="tpu_custom_call" | custom-call | tf_op jit(solution)/shard_map/jacobian/pallas_call | solution.py:188
  189.6 1.5 collective-permute-done.29.refs_7_
  191.3 61.2 %gram_rows.1 = (f32[768,768]{1,0:T(8,128)}, f32[768,768]{1,0:T(8,128)}) custom-call(s32[4]{0:T(128)} %get-tuple-element.150.row_at, s32[4]{0:T(128)} %get-tuple-element.151.col_at, s32[32]{0:T(128)} %broadcast_multiply_fusion.place_at, f32[16,4,48,256]{3,2,1,0:T(8,128)} %jacobian.4.refs_0_, f32[16,4,48,256]{3,2,1,0:T(8,128)} %jacobian.5.refs_1_, ...), custom_call_target="tpu_custom_call" | custom-call | tf_op jit(solution)/shard_map/gram_rows/pallas_call | solution.py:251
  252.4 1.5 slice.169
  256.3 25.8 %collective-permute-done.32 = f32[384,768]{1,0:T(8,128)S(1)} collective-permute-done((f32[384,768]{1,0:T(8,128)S(1)}, f32[384,768]{1,0:T(8,128)S(1)}, u32[]{:S(2)}, u32[]{:S(2)}) %collective-permute-start.32) | collective-permute-done | bytes 1179680 | tf_op jit(solution)/shard_map/ppermute | solution.py:116
  284.7 12.2 %collective-permute-done.33 = f32[192,768]{1,0:T(8,128)S(1)} collective-permute-done((f32[192,768]{1,0:T(8,128)S(1)}, f32[192,768]{1,0:T(8,128)S(1)}, u32[]{:S(2)}, u32[]{:S(2)}) %collective-permute-start.33) | collective-permute-done | bytes 589856 | tf_op jit(solution)/shard_map/ppermute | solution.py:116
  297.0 2.4 collective-permute-start.34
  299.4 24.9 %collective-permute-done.34 = f32[192,768]{1,0:T(8,128)S(1)} collective-permute-done((f32[192,768]{1,0:T(8,128)S(1)}, f32[192,768]{1,0:T(8,128)S(1)}, u32[]{:S(2)}, u32[]{:S(2)}) %collective-permute-start.34) | collective-permute-done | bytes 589856 | tf_op jit(solution)/shard_map/ppermute | solution.py:116
  324.9 7.3 %collective-permute-done.35 = f32[192,384]{1,0:T(8,128)S(1)} collective-permute-done((f32[192,384]{1,0:T(8,128)S(1)}, f32[192,384]{1,0:T(8,128)S(1)}, u32[]{:S(2)}, u32[]{:S(2)}) %collective-permute-start.35) | collective-permute-done | bytes 294944 | tf_op jit(solution)/shard_map/ppermute | solution.py:116
  333.3 31.6 %all-gather.3.cloned.1.call-done = f32[192,1536]{1,0:T(8,128)} async-done(((f32[192,384]{1,0:T(8,128)}), f32[192,1536]{1,0:T(8,128)}) %all-gather.3.cloned.1.call-update) | async-done | bytes 1179664 | tf_op jit(solution)/shard_map/all_gather | solution.py:351
  364.9 1.6 slice.213
  366.6 25.6 %all-gather.5.cloned.1.call-done = f32[1536,256]{1,0:T(8,128)} async-done(((f32[192,256]{1,0:T(8,128)}), f32[1536,256]{1,0:T(8,128)}) %all-gather.5.cloned.1.call-update) | async-done | bytes 1572880 | tf_op jit(solution)/shard_map/all_gather | solution.py:353
  394.3 11.7 %cholesky.50 = f32[128,128]{1,0:T(8,128)S(1)} custom-call(f32[128,128]{1,0:T(8,128)S(1)} %cholesky.118), custom_call_target="Cholesky" | custom-call | tf_op jit(solution)/shard_map/jit(cholesky)/cholesky | solution.py:354
  406.1 9.8 %custom-call.15 = f32[1,128,128]{1,2,0:T(8,128)S(1)} custom-call(f32[1,128,128]{2,1,0:T(8,128)S(1)} %get-tuple-element.147), custom_call_target="InvertDiagBlocksLowerTriangular" | custom-call | tf_op jit(solution)/shard_map/jit(cholesky)/cholesky | solution.py:354
  416.4 11.7 %cholesky.105 = f32[128,128]{1,0:T(8,128)S(1)} custom-call(f32[128,128]{1,0:T(8,128)S(1)} %convolution_subtract_fusion.2), custom_call_target="Cholesky" | custom-call | tf_op jit(solution)/shard_map/jit(cholesky)/cholesky | solution.py:354
  430.8 4.2 while.1
  435.0 19.7 %custom-call.16 = f32[2,128,128]{1,2,0:T(8,128)S(1)} custom-call(f32[2,128,128]{2,1,0:T(8,128)S(1)} %get-tuple-element.101), custom_call_target="InvertDiagBlocksLowerTriangular" | custom-call | tf_op jit(solution)/shard_map/jit(_solve_triangular)/triangular_solve | solution.py:355
  456.9 1.6 fusion.2
  (188 shorter events, 64.6 us)
Async XLA Ops:
  7.2 357.7 %all-gather.3.cloned.1.call-start = ((), (), s32[]{:S(2)}) async-start(), calls=%async_computation | async-start | bytes 1474560 | tf_op jit(solution)/shard_map/all_gather | solution.py:351
  14.1 102.2 %copy-start = (f32[1536,64]{0,1:T(8,128)}, f32[1536,64]{0,1:T(8,128)S(1)}, u32[]{:S(2)}) copy-start(f32[1536,64]{0,1:T(8,128)S(1)} %copy.58) | copy-start | bytes 1179652
  22.2 20.8 %collective-permute-start.3 = (f32[2,64,1536]{2,1,0:T(8,128)}, f32[2,64,1536]{2,1,0:T(8,128)}, u32[]{:S(2)}, u32[]{:S(2)}) collective-permute-start(f32[2,64,1536]{2,1,0:T(8,128)} %pad_maximum_fusion.1), channel_id=1, source_target_pairs={{0,16},{4,20},{8,24},{12,28},{16,0},{20,4},{24,8},{28,12},{1,17},{... | collective-permute-start | bytes 2359304 | tf_op jit(solution)/shard_map/ppermute | solution.py:116
  26.5 86.5 %copy-start.1 = (f32[1536,64]{0,1:T(8,128)}, f32[1536,64]{0,1:T(8,128)S(1)}, u32[]{:S(2)}) copy-start(f32[1536,64]{0,1:T(8,128)S(1)} %copy.64) | copy-start | bytes 1179652
  28.6 19.3 %collective-permute-start.2 = (f32[2,64,1536]{2,1,0:T(8,128)}, f32[2,64,1536]{2,1,0:T(8,128)}, u32[]{:S(2)}, u32[]{:S(2)}) collective-permute-start(f32[2,64,1536]{2,1,0:T(8,128)} %pad_maximum_fusion), channel_id=1, source_target_pairs={{0,8},{4,12},{8,0},{12,4},{16,24},{20,28},{24,16},{28,20},{1,9},{5... | collective-permute-start | bytes 2359304 | tf_op jit(solution)/shard_map/ppermute | solution.py:116
  30.0 7.6 %copy-start.9 = (f32[1536,64]{1,0:T(8,128)S(1)}, f32[1536,64]{1,0:T(8,128)}, u32[]{:S(2)}) copy-start(f32[1536,64]{1,0:T(8,128)} %get-tuple-element.119) | copy-start | bytes 1179652
  31.0 19.9 %collective-permute-start = (f32[64,1536]{1,0:T(8,128)}, f32[64,1536]{1,0:T(8,128)S(1)}, u32[]{:S(2)}, u32[]{:S(2)}) collective-permute-start(f32[64,1536]{1,0:T(8,128)} %bitcast.46), channel_id=1, source_target_pairs={{0,2},{1,3},{2,0},{3,1},{4,6},{5,7},{6,4},{7,5},{8,10},{9,11},{10,... | collective-permute-start | bytes 1179656 | tf_op jit(solution)/shard_map/ppermute | solution.py:116
  35.0 17.4 %collective-permute-start.1 = (f32[64,1536]{1,0:T(8,128)S(1)}, f32[64,1536]{1,0:T(8,128)S(1)}, u32[]{:S(2)}, u32[]{:S(2)}) collective-permute-start(f32[64,1536]{1,0:T(8,128)S(1)} %bitcast.182), channel_id=1, source_target_pairs={{0,1},{1,0},{2,3},{3,2},{4,5},{5,4},{6,7},{7,6},{8,9},{9,8},{10,11... | collective-permute-start | bytes 1179656 | tf_op jit(solution)/shard_map/ppermute | solution.py:116
  45.0 8.1 %copy-start.2 = (f32[64,1536]{1,0:T(8,128)}, f32[64,1536]{1,0:T(8,128)S(1)}, u32[]{:S(2)}) copy-start(f32[64,1536]{1,0:T(8,128)S(1)} %get-tuple-element.53.refs_6_) | copy-start | bytes 1179652
  52.5 17.0 %collective-permute-start.7 = (f32[2,64,1536]{2,1,0:T(8,128)S(1)}, f32[2,64,1536]{2,1,0:T(8,128)S(1)}, u32[]{:S(2)}, u32[]{:S(2)}) collective-permute-start(f32[2,64,1536]{2,1,0:T(8,128)S(1)} %pad_maximum_fusion.3), channel_id=1, source_target_pairs={{0,16},{4,20},{8,24},{12,28},{16,0},{20,4},{24,8},{28,12},{1,17},{... | collective-permute-start | bytes 2359304 | tf_op jit(solution)/shard_map/ppermute | solution.py:116
  53.2 17.1 %collective-permute-start.6 = (f32[2,64,1536]{2,1,0:T(8,128)S(1)}, f32[2,64,1536]{2,1,0:T(8,128)S(1)}, u32[]{:S(2)}, u32[]{:S(2)}) collective-permute-start(f32[2,64,1536]{2,1,0:T(8,128)S(1)} %pad_maximum_fusion.2), channel_id=1, source_target_pairs={{0,8},{4,12},{8,0},{12,4},{16,24},{20,28},{24,16},{28,20},{1,9},{5... | collective-permute-start | bytes 2359304 | tf_op jit(solution)/shard_map/ppermute | solution.py:116
  53.7 17.7 %collective-permute-start.4 = (f32[64,1536]{1,0:T(8,128)S(1)}, f32[64,1536]{1,0:T(8,128)S(1)}, u32[]{:S(2)}, u32[]{:S(2)}) collective-permute-start(f32[64,1536]{1,0:T(8,128)S(1)} %bitcast.181), channel_id=1, source_target_pairs={{0,2},{1,3},{2,0},{3,1},{4,6},{5,7},{6,4},{7,5},{8,10},{9,11},{10,... | collective-permute-start | bytes 1179656 | tf_op jit(solution)/shard_map/ppermute | solution.py:116
  54.8 16.8 %collective-permute-start.5 = (f32[64,1536]{1,0:T(8,128)S(1)}, f32[64,1536]{1,0:T(8,128)S(1)}, u32[]{:S(2)}, u32[]{:S(2)}) collective-permute-start(f32[64,1536]{1,0:T(8,128)S(1)} %bitcast.180), channel_id=1, source_target_pairs={{0,1},{1,0},{2,3},{3,2},{4,5},{5,4},{6,7},{7,6},{8,9},{9,8},{10,11... | collective-permute-start | bytes 1179656 | tf_op jit(solution)/shard_map/ppermute | solution.py:116
  71.5 65.0 %copy-start.15 = (f32[64,1536]{1,0:T(8,128)}, f32[64,1536]{1,0:T(8,128)S(1)}, u32[]{:S(2)}) copy-start(f32[64,1536]{1,0:T(8,128)S(1)} %collective-permute-done.4.refs_0_) | copy-start | bytes 1179652
  71.5 63.6 %copy-start.16 = (f32[64,1536]{1,0:T(8,128)}, f32[64,1536]{1,0:T(8,128)S(1)}, u32[]{:S(2)}) copy-start(f32[64,1536]{1,0:T(8,128)S(1)} %collective-permute-done.5.refs_4_) | copy-start | bytes 1179652
  71.6 17.4 %collective-permute-start.11 = (f32[2,64,1536]{2,1,0:T(8,128)S(1)}, f32[2,64,1536]{2,1,0:T(8,128)S(1)}, u32[]{:S(2)}, u32[]{:S(2)}) collective-permute-start(f32[2,64,1536]{2,1,0:T(8,128)S(1)} %pad_maximum_fusion.5), channel_id=1, source_target_pairs={{0,16},{4,20},{8,24},{12,28},{16,0},{20,4},{24,8},{28,12},{1,17},{... | collective-permute-start | bytes 2359304 | tf_op jit(solution)/shard_map/ppermute | solution.py:116
  72.9 19.6 %copy-start.26 = (f32[64,1536]{1,0:T(8,128)S(1)}, f32[64,1536]{1,0:T(8,128)}, u32[]{:S(2)}) copy-start(f32[64,1536]{1,0:T(8,128)} %copy-done.25) | copy-start | bytes 1179652
  72.9 17.1 %collective-permute-start.10 = (f32[2,64,1536]{2,1,0:T(8,128)S(1)}, f32[2,64,1536]{2,1,0:T(8,128)S(1)}, u32[]{:S(2)}, u32[]{:S(2)}) collective-permute-start(f32[2,64,1536]{2,1,0:T(8,128)S(1)} %pad_maximum_fusion.4), channel_id=1, source_target_pairs={{0,8},{4,12},{8,0},{12,4},{16,24},{20,28},{24,16},{28,20},{1,9},{5... | collective-permute-start | bytes 2359304 | tf_op jit(solution)/shard_map/ppermute | solution.py:116
  74.4 17.9 %collective-permute-start.8 = (f32[64,1536]{1,0:T(8,128)S(1)}, f32[64,1536]{1,0:T(8,128)S(1)}, u32[]{:S(2)}, u32[]{:S(2)}) collective-permute-start(f32[64,1536]{1,0:T(8,128)S(1)} %bitcast.175), channel_id=1, source_target_pairs={{0,2},{1,3},{2,0},{3,1},{4,6},{5,7},{6,4},{7,5},{8,10},{9,11},{10,... | collective-permute-start | bytes 1179656 | tf_op jit(solution)/shard_map/ppermute | solution.py:116
  76.8 15.6 %collective-permute-start.9 = (f32[64,1536]{1,0:T(8,128)S(1)}, f32[64,1536]{1,0:T(8,128)S(1)}, u32[]{:S(2)}, u32[]{:S(2)}) collective-permute-start(f32[64,1536]{1,0:T(8,128)S(1)} %bitcast.177), channel_id=1, source_target_pairs={{0,1},{1,0},{2,3},{3,2},{4,5},{5,4},{6,7},{7,6},{8,9},{9,8},{10,11... | collective-permute-start | bytes 1179656 | tf_op jit(solution)/shard_map/ppermute | solution.py:116
  92.4 18.9 %collective-permute-start.12 = (f32[64,1536]{1,0:T(8,128)S(1)}, f32[64,1536]{1,0:T(8,128)S(1)}, u32[]{:S(2)}, u32[]{:S(2)}) collective-permute-start(f32[64,1536]{1,0:T(8,128)S(1)} %copy-done.26), channel_id=1, source_target_pairs={{0,2},{1,3},{2,0},{3,1},{4,6},{5,7},{6,4},{7,5},{8,10},{9,11},{10,... | collective-permute-start | bytes 1179656 | tf_op jit(solution)/shard_map/ppermute | solution.py:116
  94.2 17.3 %collective-permute-start.13 = (f32[64,1536]{1,0:T(8,128)S(1)}, f32[64,1536]{1,0:T(8,128)S(1)}, u32[]{:S(2)}, u32[]{:S(2)}) collective-permute-start(f32[64,1536]{1,0:T(8,128)S(1)} %collective-permute-done), channel_id=1, source_target_pairs={{0,1},{1,0},{2,3},{3,2},{4,5},{5,4},{6,7},{7,6},{8,9},{9,8},{10,11... | collective-permute-start | bytes 1179656 | tf_op jit(solution)/shard_map/ppermute | solution.py:116
  96.6 14.8 %collective-permute-start.14 = (f32[64,1536]{1,0:T(8,128)S(1)}, f32[64,1536]{1,0:T(8,128)S(1)}, u32[]{:S(2)}, u32[]{:S(2)}) collective-permute-start(f32[64,1536]{1,0:T(8,128)S(1)} %collective-permute-done.9), channel_id=1, source_target_pairs={{0,8},{4,12},{8,0},{12,4},{16,24},{20,28},{24,16},{28,20},{1,9},{5... | collective-permute-start | bytes 1179656 | tf_op jit(solution)/shard_map/ppermute | solution.py:116
  97.5 14.0 %collective-permute-start.15 = (f32[64,1536]{1,0:T(8,128)S(1)}, f32[64,1536]{1,0:T(8,128)S(1)}, u32[]{:S(2)}, u32[]{:S(2)}) collective-permute-start(f32[64,1536]{1,0:T(8,128)S(1)} %collective-permute-done.8), channel_id=1, source_target_pairs={{0,16},{4,20},{8,24},{12,28},{16,0},{20,4},{24,8},{28,12},{1,17},{... | collective-permute-start | bytes 1179656 | tf_op jit(solution)/shard_map/ppermute | solution.py:116
  111.5 17.1 %collective-permute-start.19 = (f32[2,64,1536]{2,1,0:T(8,128)S(1)}, f32[2,64,1536]{2,1,0:T(8,128)S(1)}, u32[]{:S(2)}, u32[]{:S(2)}) collective-permute-start(f32[2,64,1536]{2,1,0:T(8,128)S(1)} %pad_maximum_fusion.7), channel_id=1, source_target_pairs={{0,16},{4,20},{8,24},{12,28},{16,0},{20,4},{24,8},{28,12},{1,17},{... | collective-permute-start | bytes 2359304 | tf_op jit(solution)/shard_map/ppermute | solution.py:116
  112.7 16.8 %collective-permute-start.18 = (f32[2,64,1536]{2,1,0:T(8,128)S(1)}, f32[2,64,1536]{2,1,0:T(8,128)S(1)}, u32[]{:S(2)}, u32[]{:S(2)}) collective-permute-start(f32[2,64,1536]{2,1,0:T(8,128)S(1)} %pad_maximum_fusion.6), channel_id=1, source_target_pairs={{0,8},{4,12},{8,0},{12,4},{16,24},{20,28},{24,16},{28,20},{1,9},{5... | collective-permute-start | bytes 2359304 | tf_op jit(solution)/shard_map/ppermute | solution.py:116
  113.0 19.4 %collective-permute-start.16 = (f32[64,1536]{1,0:T(8,128)S(1)}, f32[64,1536]{1,0:T(8,128)S(1)}, u32[]{:S(2)}, u32[]{:S(2)}) collective-permute-start(f32[64,1536]{1,0:T(8,128)S(1)} %bitcast.160), channel_id=1, source_target_pairs={{0,2},{1,3},{2,0},{3,1},{4,6},{5,7},{6,4},{7,5},{8,10},{9,11},{10,... | collective-permute-start | bytes 1179656 | tf_op jit(solution)/shard_map/ppermute | solution.py:116
  116.3 16.4 %collective-permute-start.17 = (f32[64,1536]{1,0:T(8,128)S(1)}, f32[64,1536]{1,0:T(8,128)S(1)}, u32[]{:S(2)}, u32[]{:S(2)}) collective-permute-start(f32[64,1536]{1,0:T(8,128)S(1)} %bitcast.157), channel_id=1, source_target_pairs={{0,1},{1,0},{2,3},{3,2},{4,5},{5,4},{6,7},{7,6},{8,9},{9,8},{10,11... | collective-permute-start | bytes 1179656 | tf_op jit(solution)/shard_map/ppermute | solution.py:116
  132.8 18.1 %collective-permute-start.23 = (f32[2,64,1536]{2,1,0:T(8,128)S(1)}, f32[2,64,1536]{2,1,0:T(8,128)S(1)}, u32[]{:S(2)}, u32[]{:S(2)}) collective-permute-start(f32[2,64,1536]{2,1,0:T(8,128)S(1)} %pad_maximum_fusion.9), channel_id=1, source_target_pairs={{0,16},{4,20},{8,24},{12,28},{16,0},{20,4},{24,8},{28,12},{1,17},{... | collective-permute-start | bytes 2359304 | tf_op jit(solution)/shard_map/ppermute | solution.py:116
  133.7 18.1 %collective-permute-start.22 = (f32[2,64,1536]{2,1,0:T(8,128)S(1)}, f32[2,64,1536]{2,1,0:T(8,128)S(1)}, u32[]{:S(2)}, u32[]{:S(2)}) collective-permute-start(f32[2,64,1536]{2,1,0:T(8,128)S(1)} %pad_maximum_fusion.8), channel_id=1, source_target_pairs={{0,8},{4,12},{8,0},{12,4},{16,24},{20,28},{24,16},{28,20},{1,9},{5... | collective-permute-start | bytes 2359304 | tf_op jit(solution)/shard_map/ppermute | solution.py:116
  135.1 18.6 %collective-permute-start.20 = (f32[64,1536]{1,0:T(8,128)S(1)}, f32[64,1536]{1,0:T(8,128)}, u32[]{:S(2)}, u32[]{:S(2)}) collective-permute-start(f32[64,1536]{1,0:T(8,128)S(1)} %collective-permute-done.5.refs_4_), channel_id=1, source_target_pairs={{0,2},{1,3},{2,0},{3,1},{4,6},{5,7},{6,4},{7,5},{8,10},{9,11},{10,... | collective-permute-start | bytes 1179656 | tf_op jit(solution)/shard_map/ppermute | solution.py:116
  136.4 17.4 %collective-permute-start.21 = (f32[64,1536]{1,0:T(8,128)S(1)}, f32[64,1536]{1,0:T(8,128)}, u32[]{:S(2)}, u32[]{:S(2)}) collective-permute-start(f32[64,1536]{1,0:T(8,128)S(1)} %collective-permute-done.4.refs_0_), channel_id=1, source_target_pairs={{0,1},{1,0},{2,3},{3,2},{4,5},{5,4},{6,7},{7,6},{8,9},{9,8},{10,11... | collective-permute-start | bytes 1179656 | tf_op jit(solution)/shard_map/ppermute | solution.py:116
  153.9 23.8 %collective-permute-start.24 = (f32[64,1536]{1,0:T(8,128)}, f32[64,1536]{1,0:T(8,128)S(1)}, u32[]{:S(2)}, u32[]{:S(2)}) collective-permute-start(f32[64,1536]{1,0:T(8,128)} %collective-permute-done.21.refs_0_), channel_id=1, source_target_pairs={{0,16},{4,20},{8,24},{12,28},{16,0},{20,4},{24,8},{28,12},{1,17},{... | collective-permute-start | bytes 1179656 | tf_op jit(solution)/shard_map/ppermute | solution.py:116
  154.9 22.8 %collective-permute-start.25 = (f32[64,1536]{1,0:T(8,128)}, f32[64,1536]{1,0:T(8,128)}, u32[]{:S(2)}, u32[]{:S(2)}) collective-permute-start(f32[64,1536]{1,0:T(8,128)} %collective-permute-done.20.refs_4_), channel_id=1, source_target_pairs={{0,8},{4,12},{8,0},{12,4},{16,24},{20,28},{24,16},{28,20},{1,9},{5... | collective-permute-start | bytes 1179656 | tf_op jit(solution)/shard_map/ppermute | solution.py:116
  163.9 25.6 %collective-permute-start.26 = (f32[16,4,48,256]{3,2,1,0:T(8,128)}, f32[16,4,48,256]{3,2,1,0:T(8,128)S(1)}, u32[]{:S(2)}, u32[]{:S(2)}) collective-permute-start(f32[16,4,48,256]{3,2,1,0:T(8,128)} %jacobian.4.refs_0_), channel_id=1, source_target_pairs={{0,4},{4,0},{8,12},{12,8},{16,20},{20,16},{24,28},{28,24},{1,5},{5... | collective-permute-start | bytes 9437192 | tf_op jit(solution)/shard_map/ppermute | solution.py:116
  170.5 19.0 %collective-permute-start.28 = (f32[16,4,48,256]{3,2,1,0:T(8,128)}, f32[16,4,48,256]{3,2,1,0:T(8,128)}, u32[]{:S(2)}, u32[]{:S(2)}) collective-permute-start(f32[16,4,48,256]{3,2,1,0:T(8,128)} %jacobian.6.refs_2_), channel_id=1, source_target_pairs={{0,4},{4,0},{8,12},{12,8},{16,20},{20,16},{24,28},{28,24},{1,5},{5... | collective-permute-start | bytes 9437192 | tf_op jit(solution)/shard_map/ppermute | solution.py:116
  177.5 7.9 %copy-start.29 = (s32[1536]{0:T(1024)S(1)}, s32[1536]{0:T(1024)}, u32[]{:S(2)}) copy-start(s32[1536]{0:T(1024)} %param.8) | copy-start | bytes 18436
  177.6 12.0 %collective-permute-start.27 = (f32[16,4,48,256]{3,2,1,0:T(8,128)}, f32[16,4,48,256]{3,2,1,0:T(8,128)}, u32[]{:S(2)}, u32[]{:S(2)}) collective-permute-start(f32[16,4,48,256]{3,2,1,0:T(8,128)} %jacobian.5.refs_1_), channel_id=1, source_target_pairs={{0,4},{4,0},{8,12},{12,8},{16,20},{20,16},{24,28},{28,24},{1,5},{5... | collective-permute-start | bytes 9437192 | tf_op jit(solution)/shard_map/ppermute | solution.py:116
  185.0 6.1 %collective-permute-start.29 = (f32[16,4,48,256]{3,2,1,0:T(8,128)}, f32[16,4,48,256]{3,2,1,0:T(8,128)}, u32[]{:S(2)}, u32[]{:S(2)}) collective-permute-start(f32[16,4,48,256]{3,2,1,0:T(8,128)} %jacobian.7.refs_3_), channel_id=1, source_target_pairs={{0,4},{4,0},{8,12},{12,8},{16,20},{20,16},{24,28},{28,24},{1,5},{5... | collective-permute-start | bytes 9437192 | tf_op jit(solution)/shard_map/ppermute | solution.py:116
  253.9 28.1 %copy-start.14 = (f32[768,768]{1,0:T(8,128)S(1)}, f32[768,768]{1,0:T(8,128)}, u32[]{:S(2)}) copy-start(f32[768,768]{1,0:T(8,128)} %get-tuple-element.93) | copy-start | bytes 7077892
  253.9 28.1 %collective-permute-start.32 = (f32[384,768]{1,0:T(8,128)S(1)}, f32[384,768]{1,0:T(8,128)S(1)}, u32[]{:S(2)}, u32[]{:S(2)}) collective-permute-start(f32[384,768]{1,0:T(8,128)S(1)} %slice.169), channel_id=1, source_target_pairs={{0,16},{4,20},{8,24},{12,28},{16,0},{20,4},{24,8},{28,12},{1,17},{... | collective-permute-start | bytes 3538952 | tf_op jit(solution)/shard_map/ppermute | solution.py:116
  255.0 28.5 %collective-permute-start.30 = (f32[384,768]{1,0:T(8,128)S(1)}, f32[384,768]{1,0:T(8,128)S(1)}, u32[]{:S(2)}, u32[]{:S(2)}) collective-permute-start(f32[384,768]{1,0:T(8,128)S(1)} %slice.165), channel_id=1, source_target_pairs={{0,8},{4,12},{8,0},{12,4},{16,24},{20,28},{24,16},{28,20},{1,9},{5... | collective-permute-start | bytes 3538952 | tf_op jit(solution)/shard_map/ppermute | solution.py:116
  282.2 14.7 %collective-permute-start.33 = (f32[192,768]{1,0:T(8,128)S(1)}, f32[192,768]{1,0:T(8,128)S(1)}, u32[]{:S(2)}, u32[]{:S(2)}) collective-permute-start(f32[192,768]{1,0:T(8,128)S(1)} %slice.210), channel_id=1, source_target_pairs={{0,8},{4,12},{8,0},{12,4},{16,24},{20,28},{24,16},{28,20},{1,9},{5... | collective-permute-start | bytes 1769480 | tf_op jit(solution)/shard_map/ppermute | solution.py:116
  283.6 15.7 %collective-permute-start.31 = (f32[192,768]{1,0:T(8,128)S(1)}, f32[192,768]{1,0:T(8,128)S(1)}, u32[]{:S(2)}, u32[]{:S(2)}) collective-permute-start(f32[192,768]{1,0:T(8,128)S(1)} %slice.208), channel_id=1, source_target_pairs={{0,16},{4,20},{8,24},{12,28},{16,0},{20,4},{24,8},{28,12},{1,17},{... | collective-permute-start | bytes 1769480 | tf_op jit(solution)/shard_map/ppermute | solution.py:116
  297.0 27.3 %collective-permute-start.34 = (f32[192,768]{1,0:T(8,128)S(1)}, f32[192,768]{1,0:T(8,128)S(1)}, u32[]{:S(2)}, u32[]{:S(2)}) collective-permute-start(f32[192,768]{1,0:T(8,128)S(1)} %slice_add_fusion.2), channel_id=1, source_target_pairs={{0,2},{1,3},{2,0},{3,1},{4,6},{5,7},{6,4},{7,5},{8,10},{9,11},{10,... | collective-permute-start | bytes 1769480 | tf_op jit(solution)/shard_map/ppermute | solution.py:116
  324.4 7.8 %collective-permute-start.35 = (f32[192,384]{1,0:T(8,128)S(1)}, f32[192,384]{1,0:T(8,128)S(1)}, u32[]{:S(2)}, u32[]{:S(2)}) collective-permute-start(f32[192,384]{1,0:T(8,128)S(1)} %slice.212), channel_id=1, source_target_pairs={{0,1},{1,0},{2,3},{3,2},{4,5},{5,4},{6,7},{7,6},{8,9},{9,8},{10,11... | collective-permute-start | bytes 884744 | tf_op jit(solution)/shard_map/ppermute | solution.py:116
  333.0 59.2 %all-gather.5.cloned.1.call-start = ((), (), s32[]{:S(2)}) async-start(), calls=%async_computation.1 | async-start | bytes 1769472 | tf_op jit(solution)/shard_map/all_gather | solution.py:353
  430.8 27.7 %copy-start.12 = (f32[192,384]{1,0:T(8,128)S(1)}, f32[192,384]{1,0:T(8,128)}, u32[]{:S(2)}) copy-start(f32[192,384]{1,0:T(8,128)} %fusion.5) | copy-start | bytes 884740
  (20 other events, 53.6 us)
Sparse Core Ops, SparseCore 0:
  333.2 31.6 all-gather.2
  367.4 24.7 all-gather.4

commit v3 on v2

--- a/solution.py
+++ b/solution.py
@@ -13,6 +13,7 @@
 HIGHEST = lax.Precision.HIGHEST
 SHIFT = 0.05
 LANES = 256
+SUB = 8
 CONTRACT_LAST = (((1,), (1,)), ((), ()))
 VMEM_LIMIT = 60 * 1024 * 1024
 
@@ -95,6 +96,7 @@
                 ready.sort(
                     key=lambda t: (
                         not self.splits(t[1][0], self.dims[k][2]),
+                        axis == "par" and (t[2][1] & (self.par_size - 1)).bit_count(),
                         -self.depth(*t[2], k),
                     )
                 )
@@ -136,6 +138,12 @@
             for n, v in zip(keys + gate, tied):
                 held[n] = v
         gate = []
+        if sent and keys:
+            tied = lax.optimization_barrier(tuple(held[n] for n in keys) + tuple(own[q] for q in sent))
+            for n, v in zip(keys, tied):
+                held[n] = v
+            for q, v in zip(sent, tied[len(keys) :]):
+                own[q] = v
         for q in sent:
             other[q] = permute(own[q], "walk", plan.walk_size, 1)
         sent = []
@@ -272,6 +280,68 @@
     )(row_at, col_at, place_at, *pieces, hot, hot_t, recip)
 
 
+def inverse_factor(value):
+    size = value.shape[0]
+    lane = lax.broadcasted_iota(jnp.int32, (1, size), 1)
+    sub = lax.broadcasted_iota(jnp.int32, (SUB, 1), 0)
+    tiles = [value[t * SUB : (t + 1) * SUB] for t in range(size // SUB)]
+    for j in range(size):
+        home, at = divmod(j, SUB)
+        row = tiles[home][at : at + 1]
+        scaled = jnp.where(lane == j, 1.0, row) / row[:, j : j + 1]
+        for t in range(home, len(tiles)):
+            tile = tiles[t]
+            factor = tile[:, j : j + 1]
+            clear = lane == j
+            if t == home:
+                if at == SUB - 1:
+                    continue
+                factor = jnp.where(sub > at, factor, 0.0)
+                clear = clear & (sub > at)
+            tiles[t] = jnp.where(clear, 0.0, tile) - factor * scaled
+    value = jnp.concatenate(tiles, axis=0)
+    row_id = lax.broadcasted_iota(jnp.int32, (size, 1), 0)
+    diagonal = jnp.sum(jnp.where(lane == row_id, value, 0.0), axis=1, keepdims=True)
+    unit = jnp.where(lane < row_id, value, jnp.where(lane == row_id, 1.0, 0.0))
+    return unit / jnp.sqrt(diagonal)
+
+
+def head_kernel(a_ref, out_ref, work_ref, below_ref):
+    half = work_ref.shape[0]
+    dot = functools.partial(lax.dot_general, precision=HIGHEST, preferred_element_type=jnp.float32)
+    first = pl.program_id(0) == 0
+    @pl.when(first)
+    def _():
+        work_ref[...] = a_ref[:half, :half]
+    inverse = inverse_factor(work_ref[...])
+    @pl.when(first)
+    def _():
+        out_ref[:half, :half] = inverse
+        out_ref[:half, half:] = jnp.zeros((half, half), jnp.float32)
+        below = dot(a_ref[half:, :half], inverse, CONTRACT_LAST)
+        below_ref[...] = below
+        work_ref[...] = a_ref[half:, half:] - dot(below, below, CONTRACT_LAST)
+    @pl.when(jnp.logical_not(first))
+    def _():
+        out_ref[half:, half:] = inverse
+        plain = (((1,), (0,)), ((), ()))
+        out_ref[half:, :half] = -dot(inverse, dot(below_ref[...], out_ref[:half, :half], plain), plain)
+
+
+def head_inverse(head):
+    size = head.shape[0]
+    fixed = pl.BlockSpec((size, size), lambda i: (0, 0))
+    return pl.pallas_call(
+        head_kernel,
+        out_shape=jax.ShapeDtypeStruct(head.shape, jnp.float32),
+        grid=(2,),
+        in_specs=[fixed],
+        out_specs=fixed,
+        scratch_shapes=[pltpu.VMEM((size // 2, size // 2), jnp.float32)] * 2,
+        name="head_inverse",
+    )(head)
+
+
 def on_device(features, signals, param_scale, geometry, electrons):
     par_size = lax.axis_size("par")
     walk_size = lax.axis_size("walk")
@@ -331,6 +401,48 @@
         tuple(sorted(range(slots), key=lambda s, o=o: [s >> b & 1 for b in o])) for o in sweeps
     )
     halves = list(gram_rows(columns, hot, hot_t, recip, row_at, col_at, place_at, row_block, col_block, orders))
+
+    heads = []
+    for h in range(2):
+        part = lax.dynamic_slice(
+            halves[h], (0, (par_index % (par_size // 2)) * col_block), (slots * row_block, PB)
+        ).reshape(slots, row_block, PB)
+        heads.append(jnp.stack([part[orders[h].index(s)] for s in range(slots)]))
+    head_rows = jnp.where(par_index < par_size // 2, heads[0], heads[1])
+    sides = [head_rows[:, :, : PB // 2], head_rows[:, :, PB // 2 :]]
+    sides = [jnp.stack([sides[h][s] for s in orders[h]]) for h in range(2)]
+    for step in range(chip_bits):
+        mid = sides[0].shape[0] // 2
+        moved = [permute(sides[h][mid:], "walk", walk_size, 2 << sweeps[h][step]) for h in range(2)]
+        sides = [sides[h][:mid] + moved[h] for h in range(2)]
+    rows_mine = jnp.concatenate([sides[0][0], sides[1][0]], axis=1)
+    bit = par_size // 2
+    while bit:
+        rows_mine = rows_mine + permute(rows_mine, "par", par_size, bit)
+        bit //= 2
+    all_rows = rows_mine[None]
+    for bit in [2 << b for b in range(chip_bits)] + [1]:
+        all_rows = jnp.concatenate([all_rows, permute(all_rows, "walk", walk_size, bit)], axis=0)
+    flips = [0]
+    for bit in [2 << b for b in range(chip_bits)] + [1]:
+        flips += [f | bit for f in flips]
+    where_flip = np.argsort(np.array(flips))
+
+    def rows_of(block_index):
+        at = jnp.asarray(where_flip)[block_index ^ walk_index]
+        return lax.dynamic_index_in_dim(all_rows, at, 0, keepdims=False)
+
+    def shift_at(first_row, count):
+        ids = first_row + jnp.arange(count, dtype=jnp.int32)
+        return SHIFT * (ids[:, None] == jnp.arange(PB, dtype=jnp.int32)[None, :]).astype(jnp.float32)
+
+    head = jnp.concatenate([rows_of(b) for b in range(-(-PB // row_block))], axis=0)[:PB]
+    inverse = head_inverse(head + shift_at(0, PB))
+    own_panel = outer_rows(rows_mine + shift_at(walk_index * row_block, row_block), inverse)
+    per_col = col_block // row_block
+    col_rows = jnp.concatenate([rows_of(par_index * per_col + b) for b in range(per_col)], axis=0)
+    col_panel = outer_rows(col_rows + shift_at(par_index * col_block, col_block), inverse)
+
     for step in range(chip_bits):
         moved = []
         for h in range(2):
@@ -344,20 +456,9 @@
         mid = gram.shape[1] // 2
         gram = gram[:, :mid] + permute(gram[:, mid:], "par", par_size, bit)
         bit //= 2
-
     row_ids = walk_index * row_block + jnp.arange(row_block, dtype=jnp.int32)
     col_ids = par_index * col_block + jnp.arange(col_block, dtype=jnp.int32)
     shifted = gram + SHIFT * (row_ids[:, None] == col_ids[None, :]).astype(jnp.float32)
-    whole_rows = lax.all_gather(shifted, "par", axis=1, tiled=True)
-    panel_part = whole_rows[:, :PB]
-    panel_whole = lax.all_gather(panel_part, "walk", axis=0, tiled=True)
-    factor_head = jnp.linalg.cholesky(panel_whole[:PB])
-    head_inverse = jax.scipy.linalg.solve_triangular(
-        factor_head, jnp.eye(PB, dtype=jnp.float32), lower=True
-    )
-    own_panel = outer_rows(panel_part, head_inverse)
-    col_rows = lax.dynamic_slice_in_dim(panel_whole, par_index * col_block, col_block, 0)
-    col_panel = outer_rows(col_rows, head_inverse)
     trailing = shifted - outer_rows(own_panel, col_panel)
     return (own_panel, trailing)
 

time: 469 us -> 372 us (0.79)
  waiting for transfers between devices: 203 us -> 130 us
  other arithmetic: 69.1 us -> 23.2 us
  Pallas kernels: 87.5 us -> 112 us
  starting transfers between devices: 48.7 us -> 59 us
  between operations: 15.9 us -> 8.61 us
    all_gather x2 -> x0, waiting for transfers between devices: 57.2 us -> none  [the longest x1 31.6 us: on_device(): whole_rows = lax.all_gather(shifted, 'par', axis=1, tiled=True)]
    another operation x10 -> x1, other arithmetic: 54.3 us -> 0.02 us  [on_device(): sides = [jnp.stack([sides[h][s] for s in orders[h]]) for h in range(2)]]
    pallas_call x0 -> x1, Pallas kernels: none -> 24.3 us  [head_inverse(): pl.pallas_call(head_kernel, out_shape=jax.ShapeDtypeStruct(head.shape, jn...]
    ppermute x36 -> x45, waiting for transfers between devices: 146 us -> 130 us  [permute(): return lax.ppermute(value, axis, xor_pairs(size, bit))]
    ppermute x36 -> x45, starting transfers between devices: 48.4 us -> 59 us  [permute(): return lax.ppermute(value, axis, xor_pairs(size, bit))]
    unnamed x69 -> x96, local copies, waits for them, and re-layouts: 10.4 us -> 9.68 us
  transfers between devices with their start and end apart: 38 -> 45, of which waited for: 27 -> 28; matrix products, arithmetic and copies ran while one was open for 5% -> 10% of each run, Pallas kernels for 6% -> 14%
where the time goes in v3:
time: 372 us; the launch traced here: 370 us
  waiting for transfers between devices  130 us (35%)
  Pallas kernels  112 us (30%)
  starting transfers between devices  59 us (16%)
  local copies, waits for them, and re-layouts  35 us (9%)
  other arithmetic  23.2 us (6%)
  between operations  8.61 us (2%)
    ppermute x45, waiting for transfers between devices, permute(): return lax.ppermute(value, axis, xor_pairs(size, bit))  130 us
    pallas_call x1, Pallas kernels, gram_rows(): pl.pallas_call(functools.partial(gram_kernel, row_block, col_block, order...  61.1 us
    ppermute x45, starting transfers between devices, permute(): return lax.ppermute(value, axis, xor_pairs(size, bit))  59 us
    pallas_call x4, Pallas kernels, jacobian(): pl.pallas_call(functools.partial(jacobian_kernel, slots, count), out_shap...  26.2 us
    pallas_call x1, Pallas kernels, head_inverse(): pl.pallas_call(head_kernel, out_shape=jax.ShapeDtypeStruct(head.shape, jn...  24.3 us
    squeeze x10, local copies, waits for them, and re-layouts, exchange(): held[d] = moved[i]  11.4 us
    unnamed x96, local copies, waits for them, and re-layouts  9.68 us
    another operation x10, other arithmetic, exchange(): jnp.stack([held[s] for s, _ in pairs])  8.56 us
  transfers between devices with their start and end apart: 45, of which 28 were waited for; matrix products, arithmetic and copies ran while one was open for 10% of the time, Pallas kernels for 14%

profile of v3, /device:TPU:0, one launch (start us, length us, event | category | flops | bytes accessed | tf_op | source)
XLA Modules:
  0.0 370.3 jit_solution(14677327891150545329)
XLA Ops:
  4.0 2.1 constant_dynamic-slice_fusion.1
  8.9 2.5 constant_dynamic-slice_fusion
  11.4 2.2 copy.34
  13.6 2.0 pad_maximum_fusion.2
  15.6 3.0 collective-permute-start.3
  19.9 2.1 pad_maximum_fusion.1
  22.0 1.5 collective-permute-start.2
  24.5 2.6 collective-permute-start
  28.1 1.6 collective-permute-start.1
  30.2 6.3 %collective-permute-done.3 = f32[2,64,1536]{2,1,0:T(8,128)} collective-permute-done((f32[2,64,1536]{2,1,0:T(8,128)}, f32[2,64,1536]{2,1,0:T(8,128)}, u32[]{:S(2)}, u32[]{:S(2)}) %collective-permute-start.3) | collective-permute-done | bytes 786464 | tf_op jit(solution)/shard_map/ppermute | solution.py:118
  36.4 2.0 slice_bitcast_fusion.16
  38.4 2.9 collective-permute-done.2
  41.3 1.9 slice_bitcast_fusion.18
  48.2 1.8 collective-permute-start.5
  50.0 12.9 %collective-permute-done.7 = f32[2,64,1536]{2,1,0:T(8,128)S(1)} collective-permute-done((f32[2,64,1536]{2,1,0:T(8,128)S(1)}, f32[2,64,1536]{2,1,0:T(8,128)S(1)}, u32[]{:S(2)}, u32[]{:S(2)}) %collective-permute-start.7) | collective-permute-done | bytes 786464 | tf_op jit(solution)/shard_map/ppermute | solution.py:118
  68.1 1.5 collective-permute-start.10
  71.1 1.4 reshape.78.refs_8_
  72.5 2.4 collective-permute-start.8
  74.9 1.7 collective-permute-start.9
  76.6 6.5 %jacobian.4.refs_0_ = f32[16,4,48,256]{3,2,1,0:T(8,128)} custom-call(f32[64,1536]{1,0:T(8,128)} %bitcast.162, f32[64,1536]{1,0:T(8,128)} %copy-done.10, f32[64,1536]{1,0:T(8,128)} %get-tuple-element.73.refs_2_, f32[64,1536]{1,0:T(8,128)} %get-tuple-element.74.refs_3_, f32[64,1536]{1,0:T(8,128)} %bitcast.167, f32[64,1536]{1,0:T(8,128)} %get-tuple-element.75.refs_5_, ...), custom_call_target="tpu_custom_call" | custom-call | tf_op jit(solution)/shard_map/jacobian/pallas_call | solution.py:196
  86.4 4.0 %collective-permute-done.8 = f32[64,1536]{1,0:T(8,128)S(1)} collective-permute-done((f32[64,1536]{1,0:T(8,128)S(1)}, f32[64,1536]{1,0:T(8,128)S(1)}, u32[]{:S(2)}, u32[]{:S(2)}) %collective-permute-start.8) | collective-permute-done | bytes 393248 | tf_op jit(solution)/shard_map/ppermute | solution.py:118
  92.3 2.8 collective-permute-start.13
  96.8 13.4 %collective-permute-done.12.refs_4_ = f32[64,1536]{1,0:T(8,128)S(1)} collective-permute-done((f32[64,1536]{1,0:T(8,128)S(1)}, f32[64,1536]{1,0:T(8,128)S(1)}, u32[]{:S(2)}, u32[]{:S(2)}) %collective-permute-start.12) | collective-permute-done | bytes 393248 | tf_op jit(solution)/shard_map/ppermute | solution.py:118
  111.4 3.4 collective-permute-start.16
  114.8 1.8 collective-permute-start.17
  116.6 10.9 %collective-permute-done.19 = f32[2,64,1536]{2,1,0:T(8,128)S(1)} collective-permute-done((f32[2,64,1536]{2,1,0:T(8,128)S(1)}, f32[2,64,1536]{2,1,0:T(8,128)S(1)}, u32[]{:S(2)}, u32[]{:S(2)}) %collective-permute-start.19) | collective-permute-done | bytes 786464 | tf_op jit(solution)/shard_map/ppermute | solution.py:118
  129.4 2.1 collective-permute-done.16
  131.9 2.1 collective-permute-start.20
  134.0 1.5 collective-permute-start.21
  135.5 1.5 collective-permute-start.22
  138.1 6.6 %jacobian.6.refs_2_ = f32[16,4,48,256]{3,2,1,0:T(8,128)} custom-call(f32[64,1536]{1,0:T(8,128)} %copy-done.28, f32[64,1536]{1,0:T(8,128)} %copy-done.30, f32[64,1536]{1,0:T(8,128)} %get-tuple-element.100.refs_2_, f32[64,1536]{1,0:T(8,128)} %get-tuple-element.101.refs_3_, f32[64,1536]{1,0:T(8,128)} %copy-done.23, f32[64,1536]{1,0:T(8,128)} %get-tuple-element.102.refs_5_, ...), custom_call_target="tpu_custom_call" | custom-call | tf_op jit(solution)/shard_map/jacobian/pallas_call | solution.py:196
  144.6 6.6 %jacobian.5.refs_1_ = f32[16,4,48,256]{3,2,1,0:T(8,128)} custom-call(f32[64,1536]{1,0:T(8,128)} %copy-done.22, f32[64,1536]{1,0:T(8,128)} %copy-done.6, f32[64,1536]{1,0:T(8,128)} %get-tuple-element.96.refs_2_, f32[64,1536]{1,0:T(8,128)} %get-tuple-element.97.refs_3_, f32[64,1536]{1,0:T(8,128)} %copy-done.26, f32[64,1536]{1,0:T(8,128)} %get-tuple-element.98.refs_5_, ...), custom_call_target="tpu_custom_call" | custom-call | tf_op jit(solution)/shard_map/jacobian/pallas_call | solution.py:196
  157.5 14.3 %collective-permute-done.25 = f32[2,64,1536]{2,1,0:T(8,128)S(1)} collective-permute-done((f32[2,64,1536]{2,1,0:T(8,128)S(1)}, f32[2,64,1536]{2,1,0:T(8,128)S(1)}, u32[]{:S(2)}, u32[]{:S(2)}) %collective-permute-start.25) | collective-permute-done | bytes 786464 | tf_op jit(solution)/shard_map/ppermute | solution.py:118
  174.2 6.6 %jacobian.7.refs_3_ = f32[16,4,48,256]{3,2,1,0:T(8,128)} custom-call(f32[64,1536]{1,0:T(8,128)} %copy-done.31, f32[64,1536]{1,0:T(8,128)} %copy-done.32, f32[64,1536]{1,0:T(8,128)} %get-tuple-element.139.refs_2_, f32[64,1536]{1,0:T(8,128)} %get-tuple-element.138.refs_3_, f32[64,1536]{1,0:T(8,128)} %copy-done.29, f32[64,1536]{1,0:T(8,128)} %get-tuple-element.137.refs_5_, ...), custom_call_target="tpu_custom_call" | custom-call | tf_op jit(solution)/shard_map/jacobian/pallas_call | solution.py:196
  184.9 1.8 collective-permute-done.29.refs_7_
  186.8 61.1 %gram_rows.1 = (f32[768,768]{1,0:T(8,128)}, f32[768,768]{1,0:T(8,128)}) custom-call(s32[4]{0:T(128)} %get-tuple-element.160.row_at, s32[4]{0:T(128)} %get-tuple-element.161.col_at, s32[32]{0:T(128)} %broadcast_multiply_fusion.place_at, f32[16,4,48,256]{3,2,1,0:T(8,128)} %jacobian.4.refs_0_, f32[16,4,48,256]{3,2,1,0:T(8,128)} %jacobian.5.refs_1_, ...), custom_call_target="tpu_custom_call" | custom-call | tf_op jit(solution)/shard_map/gram_rows/pallas_call | solution.py:259
  250.6 1.6 collective-permute-start.30
  253.3 4.3 %collective-permute-done.30 = f32[2,192,128]{2,1,0:T(8,128)S(1)} collective-permute-done((f32[2,192,128]{2,1,0:T(8,128)S(1)}, f32[2,192,128]{2,1,0:T(8,128)S(1)}, u32[]{:S(2)}, u32[]{:S(2)}) %collective-permute-start.30) | collective-permute-done | bytes 196640 | tf_op jit(solution)/shard_map/ppermute | solution.py:118
  260.4 2.0 collective-permute-done.31
  263.7 2.9 collective-permute-start.34
  268.7 5.3 %collective-permute-done.34 = f32[192,256]{1,0:T(8,128)S(1)} collective-permute-done((f32[192,256]{1,0:T(8,128)S(1)}, f32[192,256]{1,0:T(8,128)S(1)}, u32[]{:S(2)}, u32[]{:S(2)}) %collective-permute-start.34) | collective-permute-done | bytes 196640 | tf_op jit(solution)/shard_map/ppermute | solution.py:118
  276.7 3.3 collective-permute-done.35
  281.1 26.1 %collective-permute-done.36 = f32[1,192,256]{2,1,0:T(8,128)S(1)} collective-permute-done((f32[1,192,256]{2,1,0:T(8,128)S(1)}, f32[1,192,256]{2,1,0:T(8,128)S(1)}, u32[]{:S(2)}, u32[]{:S(2)}) %collective-permute-start.36) | collective-permute-done | bytes 196640 | tf_op jit(solution)/shard_map/ppermute | solution.py:118
  316.1 1.8 slice_add_fusion
  322.0 9.0 %collective-permute-done.42 = f32[192,768]{1,0:T(8,128)S(1)} collective-permute-done((f32[192,768]{1,0:T(8,128)S(1)}, f32[192,768]{1,0:T(8,128)S(1)}, u32[]{:S(2)}, u32[]{:S(2)}) %collective-permute-start.42) | collective-permute-done | bytes 589856 | tf_op jit(solution)/shard_map/ppermute | solution.py:118
  331.1 3.4 collective-permute-start.43
  335.5 24.3 %head_inverse.1 = f32[256,256]{1,0:T(8,128)} custom-call(f32[256,256]{1,0:T(8,128)} %fusion.9.a_ref), custom_call_target="tpu_custom_call" | custom-call | tf_op jit(solution)/shard_map/head_inverse/pallas_call | solution.py:334
  364.4 5.0 %collective-permute-done.44 = f32[192,384]{1,0:T(8,128)S(1)} collective-permute-done((f32[192,384]{1,0:T(8,128)S(1)}, f32[192,384]{1,0:T(8,128)S(1)}, u32[]{:S(2)}, u32[]{:S(2)}) %collective-permute-start.44) | collective-permute-done | bytes 294944 | tf_op jit(solution)/shard_map/ppermute | solution.py:118
  (219 shorter events, 71.2 us)
Async XLA Ops:
  15.6 20.8 %collective-permute-start.3 = (f32[2,64,1536]{2,1,0:T(8,128)}, f32[2,64,1536]{2,1,0:T(8,128)}, u32[]{:S(2)}, u32[]{:S(2)}) collective-permute-start(f32[2,64,1536]{2,1,0:T(8,128)} %pad_maximum_fusion.2), channel_id=1, source_target_pairs={{0,16},{4,20},{8,24},{12,28},{16,0},{20,4},{24,8},{28,12},{1,17},{... | collective-permute-start | bytes 2359304 | tf_op jit(solution)/shard_map/ppermute | solution.py:118
  22.0 19.3 %collective-permute-start.2 = (f32[2,64,1536]{2,1,0:T(8,128)}, f32[2,64,1536]{2,1,0:T(8,128)}, u32[]{:S(2)}, u32[]{:S(2)}) collective-permute-start(f32[2,64,1536]{2,1,0:T(8,128)} %pad_maximum_fusion.1), channel_id=1, source_target_pairs={{0,8},{4,12},{8,0},{12,4},{16,24},{20,28},{24,16},{28,20},{1,9},{5... | collective-permute-start | bytes 2359304 | tf_op jit(solution)/shard_map/ppermute | solution.py:118
  24.5 19.9 %collective-permute-start = (f32[64,1536]{1,0:T(8,128)}, f32[64,1536]{1,0:T(8,128)S(1)}, u32[]{:S(2)}, u32[]{:S(2)}) collective-permute-start(f32[64,1536]{1,0:T(8,128)} %bitcast.189), channel_id=1, source_target_pairs={{0,2},{1,3},{2,0},{3,1},{4,6},{5,7},{6,4},{7,5},{8,10},{9,11},{10,... | collective-permute-start | bytes 1179656 | tf_op jit(solution)/shard_map/ppermute | solution.py:118
  28.1 17.5 %collective-permute-start.1 = (f32[64,1536]{1,0:T(8,128)}, f32[64,1536]{1,0:T(8,128)S(1)}, u32[]{:S(2)}, u32[]{:S(2)}) collective-permute-start(f32[64,1536]{1,0:T(8,128)} %bitcast.51), channel_id=1, source_target_pairs={{0,1},{1,0},{2,3},{3,2},{4,5},{5,4},{6,7},{7,6},{8,9},{9,8},{10,11... | collective-permute-start | bytes 1179656 | tf_op jit(solution)/shard_map/ppermute | solution.py:118
  45.7 17.2 %collective-permute-start.7 = (f32[2,64,1536]{2,1,0:T(8,128)S(1)}, f32[2,64,1536]{2,1,0:T(8,128)S(1)}, u32[]{:S(2)}, u32[]{:S(2)}) collective-permute-start(f32[2,64,1536]{2,1,0:T(8,128)S(1)} %pad_maximum_fusion.4), channel_id=1, source_target_pairs={{0,16},{4,20},{8,24},{12,28},{16,0},{20,4},{24,8},{28,12},{1,17},{... | collective-permute-start | bytes 2359304 | tf_op jit(solution)/shard_map/ppermute | solution.py:118
  46.4 17.4 %collective-permute-start.6 = (f32[2,64,1536]{2,1,0:T(8,128)S(1)}, f32[2,64,1536]{2,1,0:T(8,128)S(1)}, u32[]{:S(2)}, u32[]{:S(2)}) collective-permute-start(f32[2,64,1536]{2,1,0:T(8,128)S(1)} %pad_maximum_fusion.3), channel_id=1, source_target_pairs={{0,8},{4,12},{8,0},{12,4},{16,24},{20,28},{24,16},{28,20},{1,9},{5... | collective-permute-start | bytes 2359304 | tf_op jit(solution)/shard_map/ppermute | solution.py:118
  46.9 17.9 %collective-permute-start.4 = (f32[64,1536]{1,0:T(8,128)S(1)}, f32[64,1536]{1,0:T(8,128)S(1)}, u32[]{:S(2)}, u32[]{:S(2)}) collective-permute-start(f32[64,1536]{1,0:T(8,128)S(1)} %bitcast.188), channel_id=1, source_target_pairs={{0,2},{1,3},{2,0},{3,1},{4,6},{5,7},{6,4},{7,5},{8,10},{9,11},{10,... | collective-permute-start | bytes 1179656 | tf_op jit(solution)/shard_map/ppermute | solution.py:118
  48.2 16.7 %collective-permute-start.5 = (f32[64,1536]{1,0:T(8,128)S(1)}, f32[64,1536]{1,0:T(8,128)S(1)}, u32[]{:S(2)}, u32[]{:S(2)}) collective-permute-start(f32[64,1536]{1,0:T(8,128)S(1)} %bitcast.187), channel_id=1, source_target_pairs={{0,1},{1,0},{2,3},{3,2},{4,5},{5,4},{6,7},{7,6},{8,9},{9,8},{10,11... | collective-permute-start | bytes 1179656 | tf_op jit(solution)/shard_map/ppermute | solution.py:118
  64.8 69.3 %copy-start.22 = (f32[64,1536]{1,0:T(8,128)}, f32[64,1536]{1,0:T(8,128)S(1)}, u32[]{:S(2)}) copy-start(f32[64,1536]{1,0:T(8,128)S(1)} %collective-permute-done.4.refs_0_) | copy-start | bytes 1179652
  64.8 67.0 %copy-start.23 = (f32[64,1536]{1,0:T(8,128)}, f32[64,1536]{1,0:T(8,128)S(1)}, u32[]{:S(2)}) copy-start(f32[64,1536]{1,0:T(8,128)S(1)} %collective-permute-done.5.refs_4_) | copy-start | bytes 1179652
  65.8 17.6 %collective-permute-start.11 = (f32[2,64,1536]{2,1,0:T(8,128)}, f32[2,64,1536]{2,1,0:T(8,128)S(1)}, u32[]{:S(2)}, u32[]{:S(2)}) collective-permute-start(f32[2,64,1536]{2,1,0:T(8,128)} %pad_maximum_fusion.6), channel_id=1, source_target_pairs={{0,16},{4,20},{8,24},{12,28},{16,0},{20,4},{24,8},{28,12},{1,17},{... | collective-permute-start | bytes 2359304 | tf_op jit(solution)/shard_map/ppermute | solution.py:118
  68.1 17.3 %collective-permute-start.10 = (f32[2,64,1536]{2,1,0:T(8,128)}, f32[2,64,1536]{2,1,0:T(8,128)S(1)}, u32[]{:S(2)}, u32[]{:S(2)}) collective-permute-start(f32[2,64,1536]{2,1,0:T(8,128)} %pad_maximum_fusion.5), channel_id=1, source_target_pairs={{0,8},{4,12},{8,0},{12,4},{16,24},{20,28},{24,16},{28,20},{1,9},{5... | collective-permute-start | bytes 2359304 | tf_op jit(solution)/shard_map/ppermute | solution.py:118
  72.5 17.9 %collective-permute-start.8 = (f32[64,1536]{1,0:T(8,128)S(1)}, f32[64,1536]{1,0:T(8,128)S(1)}, u32[]{:S(2)}, u32[]{:S(2)}) collective-permute-start(f32[64,1536]{1,0:T(8,128)S(1)} %bitcast.182), channel_id=1, source_target_pairs={{0,2},{1,3},{2,0},{3,1},{4,6},{5,7},{6,4},{7,5},{8,10},{9,11},{10,... | collective-permute-start | bytes 1179656 | tf_op jit(solution)/shard_map/ppermute | solution.py:118
  74.9 15.7 %collective-permute-start.9 = (f32[64,1536]{1,0:T(8,128)S(1)}, f32[64,1536]{1,0:T(8,128)}, u32[]{:S(2)}, u32[]{:S(2)}) collective-permute-start(f32[64,1536]{1,0:T(8,128)S(1)} %bitcast.184), channel_id=1, source_target_pairs={{0,1},{1,0},{2,3},{3,2},{4,5},{5,4},{6,7},{7,6},{8,9},{9,8},{10,11... | collective-permute-start | bytes 1179656 | tf_op jit(solution)/shard_map/ppermute | solution.py:118
  91.2 19.0 %collective-permute-start.12 = (f32[64,1536]{1,0:T(8,128)S(1)}, f32[64,1536]{1,0:T(8,128)S(1)}, u32[]{:S(2)}, u32[]{:S(2)}) collective-permute-start(f32[64,1536]{1,0:T(8,128)S(1)} %bitcast.168), channel_id=1, source_target_pairs={{0,2},{1,3},{2,0},{3,1},{4,6},{5,7},{6,4},{7,5},{8,10},{9,11},{10,... | collective-permute-start | bytes 1179656 | tf_op jit(solution)/shard_map/ppermute | solution.py:118
  92.3 18.0 %collective-permute-start.13 = (f32[64,1536]{1,0:T(8,128)S(1)}, f32[64,1536]{1,0:T(8,128)S(1)}, u32[]{:S(2)}, u32[]{:S(2)}) collective-permute-start(f32[64,1536]{1,0:T(8,128)S(1)} %bitcast.163), channel_id=1, source_target_pairs={{0,1},{1,0},{2,3},{3,2},{4,5},{5,4},{6,7},{7,6},{8,9},{9,8},{10,11... | collective-permute-start | bytes 1179656 | tf_op jit(solution)/shard_map/ppermute | solution.py:118
  95.2 15.1 %collective-permute-start.14 = (f32[64,1536]{1,0:T(8,128)}, f32[64,1536]{1,0:T(8,128)S(1)}, u32[]{:S(2)}, u32[]{:S(2)}) collective-permute-start(f32[64,1536]{1,0:T(8,128)} %collective-permute-done.9), channel_id=1, source_target_pairs={{0,8},{4,12},{8,0},{12,4},{16,24},{20,28},{24,16},{28,20},{1,9},{5... | collective-permute-start | bytes 1179656 | tf_op jit(solution)/shard_map/ppermute | solution.py:118
  95.8 14.5 %collective-permute-start.15 = (f32[64,1536]{1,0:T(8,128)}, f32[64,1536]{1,0:T(8,128)S(1)}, u32[]{:S(2)}, u32[]{:S(2)}) collective-permute-start(f32[64,1536]{1,0:T(8,128)} %copy-done.43), channel_id=1, source_target_pairs={{0,16},{4,20},{8,24},{12,28},{16,0},{20,4},{24,8},{28,12},{1,17},{... | collective-permute-start | bytes 1179656 | tf_op jit(solution)/shard_map/ppermute | solution.py:118
  110.4 17.1 %collective-permute-start.19 = (f32[2,64,1536]{2,1,0:T(8,128)S(1)}, f32[2,64,1536]{2,1,0:T(8,128)S(1)}, u32[]{:S(2)}, u32[]{:S(2)}) collective-permute-start(f32[2,64,1536]{2,1,0:T(8,128)S(1)} %pad_maximum_fusion.8), channel_id=1, source_target_pairs={{0,16},{4,20},{8,24},{12,28},{16,0},{20,4},{24,8},{28,12},{1,17},{... | collective-permute-start | bytes 2359304 | tf_op jit(solution)/shard_map/ppermute | solution.py:118
  111.4 17.1 %collective-permute-start.18 = (f32[2,64,1536]{2,1,0:T(8,128)S(1)}, f32[2,64,1536]{2,1,0:T(8,128)S(1)}, u32[]{:S(2)}, u32[]{:S(2)}) collective-permute-start(f32[2,64,1536]{2,1,0:T(8,128)S(1)} %pad_maximum_fusion.7), channel_id=1, source_target_pairs={{0,8},{4,12},{8,0},{12,4},{16,24},{20,28},{24,16},{28,20},{1,9},{5... | collective-permute-start | bytes 2359304 | tf_op jit(solution)/shard_map/ppermute | solution.py:118
  111.4 20.1 %collective-permute-start.16 = (f32[64,1536]{1,0:T(8,128)S(1)}, f32[64,1536]{1,0:T(8,128)S(1)}, u32[]{:S(2)}, u32[]{:S(2)}) collective-permute-start(f32[64,1536]{1,0:T(8,128)S(1)} %collective-permute-done.1), channel_id=1, source_target_pairs={{0,2},{1,3},{2,0},{3,1},{4,6},{5,7},{6,4},{7,5},{8,10},{9,11},{10,... | collective-permute-start | bytes 1179656 | tf_op jit(solution)/shard_map/ppermute | solution.py:118
  114.8 17.1 %collective-permute-start.17 = (f32[64,1536]{1,0:T(8,128)S(1)}, f32[64,1536]{1,0:T(8,128)S(1)}, u32[]{:S(2)}, u32[]{:S(2)}) collective-permute-start(f32[64,1536]{1,0:T(8,128)S(1)} %copy-done.40), channel_id=1, source_target_pairs={{0,1},{1,0},{2,3},{3,2},{4,5},{5,4},{6,7},{7,6},{8,9},{9,8},{10,11... | collective-permute-start | bytes 1179656 | tf_op jit(solution)/shard_map/ppermute | solution.py:118
  131.9 19.3 %collective-permute-start.20 = (f32[64,1536]{1,0:T(8,128)S(1)}, f32[64,1536]{1,0:T(8,128)S(1)}, u32[]{:S(2)}, u32[]{:S(2)}) collective-permute-start(f32[64,1536]{1,0:T(8,128)S(1)} %collective-permute-done.5.refs_4_), channel_id=1, source_target_pairs={{0,2},{1,3},{2,0},{3,1},{4,6},{5,7},{6,4},{7,5},{8,10},{9,11},{10,... | collective-permute-start | bytes 1179656 | tf_op jit(solution)/shard_map/ppermute | solution.py:118
  134.0 17.2 %collective-permute-start.21 = (f32[64,1536]{1,0:T(8,128)S(1)}, f32[64,1536]{1,0:T(8,128)S(1)}, u32[]{:S(2)}, u32[]{:S(2)}) collective-permute-start(f32[64,1536]{1,0:T(8,128)S(1)} %collective-permute-done.4.refs_0_), channel_id=1, source_target_pairs={{0,1},{1,0},{2,3},{3,2},{4,5},{5,4},{6,7},{7,6},{8,9},{9,8},{10,11... | collective-permute-start | bytes 1179656 | tf_op jit(solution)/shard_map/ppermute | solution.py:118
  135.5 15.7 %collective-permute-start.22 = (f32[64,1536]{1,0:T(8,128)S(1)}, f32[64,1536]{1,0:T(8,128)S(1)}, u32[]{:S(2)}, u32[]{:S(2)}) collective-permute-start(f32[64,1536]{1,0:T(8,128)S(1)} %collective-permute-done.17), channel_id=1, source_target_pairs={{0,8},{4,12},{8,0},{12,4},{16,24},{20,28},{24,16},{28,20},{1,9},{5... | collective-permute-start | bytes 1179656 | tf_op jit(solution)/shard_map/ppermute | solution.py:118
  137.1 14.2 %collective-permute-start.23 = (f32[64,1536]{1,0:T(8,128)S(1)}, f32[64,1536]{1,0:T(8,128)S(1)}, u32[]{:S(2)}, u32[]{:S(2)}) collective-permute-start(f32[64,1536]{1,0:T(8,128)S(1)} %collective-permute-done.16), channel_id=1, source_target_pairs={{0,16},{4,20},{8,24},{12,28},{16,0},{20,4},{24,8},{28,12},{1,17},{... | collective-permute-start | bytes 1179656 | tf_op jit(solution)/shard_map/ppermute | solution.py:118
  153.4 18.4 %collective-permute-start.25 = (f32[2,64,1536]{2,1,0:T(8,128)S(1)}, f32[2,64,1536]{2,1,0:T(8,128)S(1)}, u32[]{:S(2)}, u32[]{:S(2)}) collective-permute-start(f32[2,64,1536]{2,1,0:T(8,128)S(1)} %pad_maximum_fusion.10), channel_id=1, source_target_pairs={{0,8},{4,12},{8,0},{12,4},{16,24},{20,28},{24,16},{28,20},{1,9},{5... | collective-permute-start | bytes 2359304 | tf_op jit(solution)/shard_map/ppermute | solution.py:118
  155.9 17.3 %collective-permute-start.24 = (f32[2,64,1536]{2,1,0:T(8,128)S(1)}, f32[2,64,1536]{2,1,0:T(8,128)S(1)}, u32[]{:S(2)}, u32[]{:S(2)}) collective-permute-start(f32[2,64,1536]{2,1,0:T(8,128)S(1)} %pad_maximum_fusion.9), channel_id=1, source_target_pairs={{0,16},{4,20},{8,24},{12,28},{16,0},{20,4},{24,8},{28,12},{1,17},{... | collective-permute-start | bytes 2359304 | tf_op jit(solution)/shard_map/ppermute | solution.py:118
  157.0 27.9 %collective-permute-start.26 = (f32[16,4,48,256]{3,2,1,0:T(8,128)S(1)}, f32[16,4,48,256]{3,2,1,0:T(8,128)}, u32[]{:S(2)}, u32[]{:S(2)}) collective-permute-start(f32[16,4,48,256]{3,2,1,0:T(8,128)S(1)} %copy-done), channel_id=1, source_target_pairs={{0,4},{4,0},{8,12},{12,8},{16,20},{20,16},{24,28},{28,24},{1,5},{5... | collective-permute-start | bytes 9437192 | tf_op jit(solution)/shard_map/ppermute | solution.py:118
  157.0 27.9 %collective-permute-start.27 = (f32[16,4,48,256]{3,2,1,0:T(8,128)}, f32[16,4,48,256]{3,2,1,0:T(8,128)}, u32[]{:S(2)}, u32[]{:S(2)}) collective-permute-start(f32[16,4,48,256]{3,2,1,0:T(8,128)} %jacobian.5.refs_1_), channel_id=1, source_target_pairs={{0,4},{4,0},{8,12},{12,8},{16,20},{20,16},{24,28},{28,24},{1,5},{5... | collective-permute-start | bytes 9437192 | tf_op jit(solution)/shard_map/ppermute | solution.py:118
  157.5 27.4 %collective-permute-start.28 = (f32[16,4,48,256]{3,2,1,0:T(8,128)}, f32[16,4,48,256]{3,2,1,0:T(8,128)}, u32[]{:S(2)}, u32[]{:S(2)}) collective-permute-start(f32[16,4,48,256]{3,2,1,0:T(8,128)} %jacobian.6.refs_2_), channel_id=1, source_target_pairs={{0,4},{4,0},{8,12},{12,8},{16,20},{20,16},{24,28},{28,24},{1,5},{5... | collective-permute-start | bytes 9437192 | tf_op jit(solution)/shard_map/ppermute | solution.py:118
  180.8 6.0 %collective-permute-start.29 = (f32[16,4,48,256]{3,2,1,0:T(8,128)}, f32[16,4,48,256]{3,2,1,0:T(8,128)}, u32[]{:S(2)}, u32[]{:S(2)}) collective-permute-start(f32[16,4,48,256]{3,2,1,0:T(8,128)} %jacobian.7.refs_3_), channel_id=1, source_target_pairs={{0,4},{4,0},{8,12},{12,8},{16,20},{20,16},{24,28},{28,24},{1,5},{5... | collective-permute-start | bytes 9437192 | tf_op jit(solution)/shard_map/ppermute | solution.py:118
  250.6 7.0 %collective-permute-start.30 = (f32[2,192,128]{2,1,0:T(8,128)S(1)}, f32[2,192,128]{2,1,0:T(8,128)S(1)}, u32[]{:S(2)}, u32[]{:S(2)}) collective-permute-start(f32[2,192,128]{2,1,0:T(8,128)S(1)} %pad_maximum_fusion.14), channel_id=1, source_target_pairs={{0,8},{4,12},{8,0},{12,4},{16,24},{20,28},{24,16},{28,20},{1,9},{5... | collective-permute-start | bytes 589832 | tf_op jit(solution)/shard_map/ppermute | solution.py:118
  252.2 6.7 %collective-permute-start.32 = (f32[2,192,128]{2,1,0:T(8,128)S(1)}, f32[2,192,128]{2,1,0:T(8,128)S(1)}, u32[]{:S(2)}, u32[]{:S(2)}) collective-permute-start(f32[2,192,128]{2,1,0:T(8,128)S(1)} %slice.276), channel_id=1, source_target_pairs={{0,16},{4,20},{8,24},{12,28},{16,0},{20,4},{24,8},{28,12},{1,17},{... | collective-permute-start | bytes 589832 | tf_op jit(solution)/shard_map/ppermute | solution.py:118
  257.7 4.7 %collective-permute-start.31 = (f32[1,192,128]{2,1,0:T(8,128)S(1)}, f32[1,192,128]{2,1,0:T(8,128)S(1)}, u32[]{:S(2)}, u32[]{:S(2)}) collective-permute-start(f32[1,192,128]{2,1,0:T(8,128)S(1)} %slice.274), channel_id=1, source_target_pairs={{0,16},{4,20},{8,24},{12,28},{16,0},{20,4},{24,8},{28,12},{1,17},{... | collective-permute-start | bytes 294920 | tf_op jit(solution)/shard_map/ppermute | solution.py:118
  259.0 4.7 %collective-permute-start.33 = (f32[1,192,128]{2,1,0:T(8,128)S(1)}, f32[1,192,128]{2,1,0:T(8,128)S(1)}, u32[]{:S(2)}, u32[]{:S(2)}) collective-permute-start(f32[1,192,128]{2,1,0:T(8,128)S(1)} %slice.278), channel_id=1, source_target_pairs={{0,8},{4,12},{8,0},{12,4},{16,24},{20,28},{24,16},{28,20},{1,9},{5... | collective-permute-start | bytes 294920 | tf_op jit(solution)/shard_map/ppermute | solution.py:118
  263.7 10.3 %collective-permute-start.34 = (f32[192,256]{1,0:T(8,128)S(1)}, f32[192,256]{1,0:T(8,128)S(1)}, u32[]{:S(2)}, u32[]{:S(2)}) collective-permute-start(f32[192,256]{1,0:T(8,128)S(1)} %pad_maximum_fusion.15), channel_id=1, source_target_pairs={{0,2},{1,3},{2,0},{3,1},{4,6},{5,7},{6,4},{7,5},{8,10},{9,11},{10,... | collective-permute-start | bytes 589832 | tf_op jit(solution)/shard_map/ppermute | solution.py:118
  267.7 48.4 %collective-permute-start.41 = (f32[384,768]{1,0:T(8,128)}, f32[384,768]{1,0:T(8,128)}, u32[]{:S(2)}, u32[]{:S(2)}) collective-permute-start(f32[384,768]{1,0:T(8,128)} %slice.244), channel_id=1, source_target_pairs={{0,16},{4,20},{8,24},{12,28},{16,0},{20,4},{24,8},{28,12},{1,17},{... | collective-permute-start | bytes 3538952 | tf_op jit(solution)/shard_map/ppermute | solution.py:118
  274.1 5.8 %collective-permute-start.35 = (f32[192,256]{1,0:T(8,128)S(1)}, f32[192,256]{1,0:T(8,128)S(1)}, u32[]{:S(2)}, u32[]{:S(2)}) collective-permute-start(f32[192,256]{1,0:T(8,128)S(1)} %fusion.27), channel_id=1, source_target_pairs={{0,1},{1,0},{2,3},{3,2},{4,5},{5,4},{6,7},{7,6},{8,9},{9,8},{10,11... | collective-permute-start | bytes 589832 | tf_op jit(solution)/shard_map/ppermute | solution.py:118
  276.0 43.4 %collective-permute-start.39 = (f32[384,768]{1,0:T(8,128)}, f32[384,768]{1,0:T(8,128)}, u32[]{:S(2)}, u32[]{:S(2)}) collective-permute-start(f32[384,768]{1,0:T(8,128)} %slice.240), channel_id=1, source_target_pairs={{0,8},{4,12},{8,0},{12,4},{16,24},{20,28},{24,16},{28,20},{1,9},{5... | collective-permute-start | bytes 3538952 | tf_op jit(solution)/shard_map/ppermute | solution.py:118
  280.0 38.7 %copy-start.11 = (f32[1,192,256]{2,1,0:T(8,128)}, f32[1,192,256]{2,1,0:T(8,128)S(1)}, u32[]{:S(2)}) copy-start(f32[1,192,256]{2,1,0:T(8,128)S(1)} %add_bitcast_fusion) | copy-start | bytes 589828
  280.0 27.3 %collective-permute-start.36 = (f32[1,192,256]{2,1,0:T(8,128)S(1)}, f32[1,192,256]{2,1,0:T(8,128)S(1)}, u32[]{:S(2)}, u32[]{:S(2)}) collective-permute-start(f32[1,192,256]{2,1,0:T(8,128)S(1)} %add_bitcast_fusion), channel_id=1, source_target_pairs={{0,8},{4,12},{8,0},{12,4},{16,24},{20,28},{24,16},{28,20},{1,9},{5... | collective-permute-start | bytes 589832 | tf_op jit(solution)/shard_map/ppermute | solution.py:118
  307.3 11.4 %collective-permute-start.37 = (f32[2,192,256]{2,1,0:T(8,128)S(1)}, f32[2,192,256]{2,1,0:T(8,128)S(1)}, u32[]{:S(2)}, u32[]{:S(2)}) collective-permute-start(f32[2,192,256]{2,1,0:T(8,128)S(1)} %pad_maximum_fusion.12), channel_id=1, source_target_pairs={{0,16},{4,20},{8,24},{12,28},{16,0},{20,4},{24,8},{28,12},{1,17},{... | collective-permute-start | bytes 1179656 | tf_op jit(solution)/shard_map/ppermute | solution.py:118
  318.0 13.1 %collective-permute-start.42 = (f32[192,768]{1,0:T(8,128)S(1)}, f32[192,768]{1,0:T(8,128)S(1)}, u32[]{:S(2)}, u32[]{:S(2)}) collective-permute-start(f32[192,768]{1,0:T(8,128)S(1)} %slice.282), channel_id=1, source_target_pairs={{0,8},{4,12},{8,0},{12,4},{16,24},{20,28},{24,16},{28,20},{1,9},{5... | collective-permute-start | bytes 1769480 | tf_op jit(solution)/shard_map/ppermute | solution.py:118
  318.7 15.8 %collective-permute-start.38 = (f32[4,192,256]{2,1,0:T(8,128)S(1)}, f32[4,192,256]{2,1,0:T(8,128)S(1)}, u32[]{:S(2)}, u32[]{:S(2)}) collective-permute-start(f32[4,192,256]{2,1,0:T(8,128)S(1)} %pad_maximum_fusion.11), channel_id=1, source_target_pairs={{0,4},{4,0},{8,12},{12,8},{16,20},{20,16},{24,28},{28,24},{1,5},{5... | collective-permute-start | bytes 2359304 | tf_op jit(solution)/shard_map/ppermute | solution.py:118
  320.9 40.3 %collective-permute-start.40 = (f32[192,768]{1,0:T(8,128)S(1)}, f32[192,768]{1,0:T(8,128)}, u32[]{:S(2)}, u32[]{:S(2)}) collective-permute-start(f32[192,768]{1,0:T(8,128)S(1)} %slice.280), channel_id=1, source_target_pairs={{0,16},{4,20},{8,24},{12,28},{16,0},{20,4},{24,8},{28,12},{1,17},{... | collective-permute-start | bytes 1769480 | tf_op jit(solution)/shard_map/ppermute | solution.py:118
  331.1 30.1 %collective-permute-start.43 = (f32[192,768]{1,0:T(8,128)S(1)}, f32[192,768]{1,0:T(8,128)}, u32[]{:S(2)}, u32[]{:S(2)}) collective-permute-start(f32[192,768]{1,0:T(8,128)S(1)} %slice_add_fusion.2), channel_id=1, source_target_pairs={{0,2},{1,3},{2,0},{3,1},{4,6},{5,7},{6,4},{7,5},{8,10},{9,11},{10,... | collective-permute-start | bytes 1769480 | tf_op jit(solution)/shard_map/ppermute | solution.py:118
  362.7 6.8 %collective-permute-start.44 = (f32[192,384]{1,0:T(8,128)S(1)}, f32[192,384]{1,0:T(8,128)S(1)}, u32[]{:S(2)}, u32[]{:S(2)}) collective-permute-start(f32[192,384]{1,0:T(8,128)S(1)} %slice.284), channel_id=1, source_target_pairs={{0,1},{1,0},{2,3},{3,2},{4,5},{5,4},{6,7},{7,6},{8,9},{9,8},{10,11... | collective-permute-start | bytes 884744 | tf_op jit(solution)/shard_map/ppermute | solution.py:118
  (41 other events, 358.4 us)

commit v4 on v3

--- a/solution.py
+++ b/solution.py
@@ -133,17 +133,15 @@
         for k, src, dst in chosen:
             groups.setdefault((k, held[src].shape), []).append((src, dst))
         keys = sorted({s for pairs in groups.values() for s, _ in pairs})
-        if gate and keys:
-            tied = lax.optimization_barrier(tuple(held[n] for n in keys) + tuple(held[n] for n in gate))
+        if keys and (gate or sent):
+            tied = lax.optimization_barrier(
+                tuple(held[n] for n in keys) + tuple(held[n] for n in gate) + tuple(own[q] for q in sent)
+            )
             for n, v in zip(keys + gate, tied):
                 held[n] = v
+            for q, v in zip(sent, tied[len(keys) + len(gate) :]):
+                own[q] = v
         gate = []
-        if sent and keys:
-            tied = lax.optimization_barrier(tuple(held[n] for n in keys) + tuple(own[q] for q in sent))
-            for n, v in zip(keys, tied):
-                held[n] = v
-            for q, v in zip(sent, tied[len(keys) :]):
-                own[q] = v
         for q in sent:
             other[q] = permute(own[q], "walk", plan.walk_size, 1)
         sent = []
@@ -166,6 +164,34 @@
     ]
 
 
+def turned_kernel(counts, own, live_ref, f_ref, s_ref, *refs):
+    outs, turned_ref = refs[:-1], refs[-1]
+    done = 0
+    for side, (ref, count) in enumerate(zip((f_ref, s_ref), counts)):
+        turned = ref[...].astype(jnp.float32).T
+        turned_ref[...] = jnp.where(live_ref[...] > 0, turned, 0.0) if side == 0 else turned
+        size = turned.shape[0] // count
+        for rb in range(count):
+            at = pl.multiple_of((own[side] ^ rb) * size, SUB)
+            outs[done + rb][...] = turned_ref[pl.ds(at, size), :]
+        done += count
+
+
+def turned_pieces(own, live, features, signals, counts):
+    rows, width = features.shape
+    whole = pl.BlockSpec(memory_space=pltpu.VMEM)
+    shapes = [jax.ShapeDtypeStruct((width // n, rows), jnp.float32) for n in counts for _ in range(n)]
+    return pl.pallas_call(
+        functools.partial(turned_kernel, counts),
+        out_shape=shapes,
+        in_specs=[pl.BlockSpec(memory_space=pltpu.SMEM), whole, whole, whole],
+        out_specs=[whole] * len(shapes),
+        scratch_shapes=[pltpu.VMEM((width, rows), jnp.float32)],
+        compiler_params=pltpu.CompilerParams(vmem_limit_bytes=VMEM_LIMIT),
+        name="turned_pieces",
+    )(own, live, features, signals)
+
+
 def jacobian_kernel(slots, count, *refs):
     lefts, rights, scale_ref, out_ref = refs[:count], refs[count : 2 * count], refs[2 * count], refs[-1]
     ib = lefts[0].shape[0]
@@ -211,14 +237,21 @@
     return high, (value - high.astype(jnp.float32)).astype(jnp.bfloat16)
 
 
-def gram_kernel(row_block, col_block, orders, count, row_at, col_at, place_at, *refs):
+def product_rows(high_ref, low_ref, at, size, swap):
+    at = pl.ds(at if isinstance(at, int) else pl.multiple_of(at, 16), size)
+    h, l = high_ref[0, at, :], low_ref[0, at, :]
+    return jnp.concatenate([h, l, h] if swap else [h, h, l], axis=1)
+
+
+def centre_kernel(row_block, col_block, orders, count, row_at, col_at, place_at, *refs):
     pieces = refs[:count]
-    hot_ref, hot_t_ref, recip_ref, a_ref, b_ref, value_ref, high_ref, low_ref = refs[count:]
+    hot_ref, hot_t_ref, recip_ref = refs[count : count + 3]
+    far_a, far_b, near_a, near_b, value_ref, high_ref, low_ref = refs[count + 3 :]
 
     @pl.when(pl.program_id(0) == 0)
     def _():
-        a_ref[...] = jnp.zeros_like(a_ref)
-        b_ref[...] = jnp.zeros_like(b_ref)
+        for ref in (far_a, far_b, near_a, near_b):
+            ref[...] = jnp.zeros_like(ref)
 
     members, rows = pieces[0].shape[1:3]
     for a in range(count):
@@ -230,35 +263,33 @@
     means = (dot(hot_t_ref[...], high) + dot(hot_t_ref[...], low)) * recip_ref[...]
     first, second = split_two(means)
     hot = hot_ref[...]
-    high, low = split_two(value - (dot(hot, first) + dot(hot, second)))
-    high_ref[...] = high
-    low_ref[...] = low
+    high_ref[0], low_ref[0] = split_two(value - (dot(hot, first) + dot(hot, second)))
+
     blocks = col_at.shape[0]
-    for half, out in enumerate((a_ref, b_ref)):
-        left = []
-        for s in orders[half]:
-            at = pl.ds(pl.multiple_of(row_at[s], 16), row_block)
-            h, l = high_ref[at, :], low_ref[at, :]
-            left.append(jnp.concatenate([h, h, l], axis=1))
-        left = jnp.concatenate(left, axis=0)
-        right = []
-        for n in range(blocks // 2):
-            at = pl.ds(pl.multiple_of(col_at[half * (blocks // 2) + n], 16), col_block)
-            h, l = high_ref[at, :], low_ref[at, :]
-            right.append(jnp.concatenate([h, l, h], axis=1))
-        right = jnp.concatenate(right, axis=0)
-        out[...] += lax.dot_general(left, right, CONTRACT_LAST, preferred_element_type=jnp.float32)
+    width = blocks // 4 * col_block
+    for h, (far, near) in enumerate(((far_a, near_a), (far_b, near_b))):
+        left = jnp.concatenate(
+            [product_rows(high_ref, low_ref, row_at[s], row_block, False) for s in orders[h]], axis=0
+        )
+        near_cols = list(range(h * blocks // 4, (h + 1) * blocks // 4))
+        far_cols = [n + blocks // 2 for n in near_cols]
+        right = jnp.concatenate(
+            [product_rows(high_ref, low_ref, col_at[n], col_block, True) for n in near_cols + far_cols], axis=0
+        )
+        got = lax.dot_general(left, right, CONTRACT_LAST, preferred_element_type=jnp.float32)
+        near[...] += got[:, :width]
+        far[...] += got[:, width:]
 
 
 def gram_rows(pieces, hot, hot_t, recip, row_at, col_at, place_at, row_block, col_block, orders):
     tiles, members, rows, lanes = pieces[0].shape
     walkers, groups = hot.shape
     slots = len(orders[0])
-    half = jax.ShapeDtypeStruct((slots * row_block, walkers // 2), jnp.float32)
+    quarter = jax.ShapeDtypeStruct((slots * row_block, walkers // 4), jnp.float32)
     fixed = lambda t, *_: (0, 0)
-    return pl.pallas_call(
-        functools.partial(gram_kernel, row_block, col_block, orders, len(pieces)),
-        out_shape=(half, half),
+    parts = pl.pallas_call(
+        functools.partial(centre_kernel, row_block, col_block, orders, len(pieces)),
+        out_shape=(quarter,) * 4,
         grid_spec=pltpu.PrefetchScalarGridSpec(
             num_scalar_prefetch=3,
             grid=(tiles,),
@@ -268,16 +299,17 @@
                 pl.BlockSpec((groups, walkers), fixed),
                 pl.BlockSpec((groups, 1), fixed),
             ],
-            out_specs=(pl.BlockSpec(half.shape, fixed), pl.BlockSpec(half.shape, fixed)),
+            out_specs=(pl.BlockSpec(quarter.shape, fixed),) * 4,
             scratch_shapes=[
                 pltpu.VMEM((walkers, lanes), jnp.float32),
-                pltpu.VMEM((walkers, lanes), jnp.bfloat16),
-                pltpu.VMEM((walkers, lanes), jnp.bfloat16),
+                pltpu.VMEM((1, walkers, lanes), jnp.bfloat16),
+                pltpu.VMEM((1, walkers, lanes), jnp.bfloat16),
             ],
         ),
         compiler_params=pltpu.CompilerParams(vmem_limit_bytes=VMEM_LIMIT),
         name="gram_rows",
     )(row_at, col_at, place_at, *pieces, hot, hot_t, recip)
+    return parts[:2], parts[2:]
 
 
 def inverse_factor(value):
@@ -358,20 +390,24 @@
     own_geometry = lax.dynamic_slice_in_dim(geometry, anchor, per_device)
     own_matches = own_geometry[:, None] == jnp.arange(groups, dtype=jnp.int32)[None, :]
     own_electrons = jnp.sum(jnp.where(own_matches, electrons[None, :], 0), axis=1)
-    live = jnp.arange(slots_count, dtype=jnp.int32)[None, :] < own_electrons[:, None]
-    masked = jnp.where(live[:, :, None], features, jnp.zeros_like(features))
+    live = (jnp.arange(slots_count, dtype=jnp.int32)[None, :] < own_electrons[:, None]).astype(jnp.float32)
 
     own = {"F": 0, "S": 0}
     for k, (axis, bit, kind) in enumerate(plan.dims):
         index = walk_index if axis == "walk" else par_index
         side = "F" if kind == "I" else "S"
         own[side] = own[side] + jnp.where((index & bit) != 0, 1 << plan.place[k], 0)
-    pieces = {}
-    for side, value in (("F", masked), ("S", signals)):
-        flat = value.reshape(per_device * slots_count, width).T.astype(jnp.float32)
-        size = width // plan.blocks[side]
-        for rb in range(plan.blocks[side]):
-            pieces[side, 0, rb] = lax.dynamic_slice_in_dim(flat, (own[side] ^ rb) * size, size, 0)
+    flat = per_device * slots_count
+    counts = (plan.blocks["F"], plan.blocks["S"])
+    turned = turned_pieces(
+        jnp.stack([own["F"], own["S"]]).astype(jnp.int32),
+        live.reshape(1, flat),
+        features.reshape(flat, width),
+        signals.reshape(flat, width),
+        counts,
+    )
+    names = [("F", 0, rb) for rb in range(counts[0])] + [("S", 0, rb) for rb in range(counts[1])]
+    pieces = dict(zip(names, turned))
     ib, jb = width // plan.blocks["F"], width // plan.blocks["S"]
     parts = LANES // jb
     scaling = param_scale * (1.0 / math.sqrt(slots_count * width * width))
@@ -400,58 +436,98 @@
     orders = tuple(
         tuple(sorted(range(slots), key=lambda s, o=o: [s >> b & 1 for b in o])) for o in sweeps
     )
-    halves = list(gram_rows(columns, hot, hot_t, recip, row_at, col_at, place_at, row_block, col_block, orders))
-
-    heads = []
+    far, near = gram_rows(
+        columns, hot, hot_t, recip, row_at, col_at, place_at, row_block, col_block, orders
+    )
+
+    def after(values, *others):
+        tied = lax.optimization_barrier(tuple(values) + others)
+        return list(tied[: len(values)])
+
+    def plane_step(pair, step):
+        mid = pair[0].shape[0] // 2
+        return [permute(pair[h][mid:], "walk", walk_size, 2 << sweeps[h][step]) for h in range(2)]
+
+    def plane_add(pair, moved):
+        return [pair[h][: pair[h].shape[0] // 2] + moved[h] for h in range(2)]
+
+    far, near = list(far), list(near)
+    each = max(par_size // 4, 1)
+    at = (par_index % each) * col_block
+    head_cols = []
     for h in range(2):
-        part = lax.dynamic_slice(
-            halves[h], (0, (par_index % (par_size // 2)) * col_block), (slots * row_block, PB)
-        ).reshape(slots, row_block, PB)
-        heads.append(jnp.stack([part[orders[h].index(s)] for s in range(slots)]))
-    head_rows = jnp.where(par_index < par_size // 2, heads[0], heads[1])
-    sides = [head_rows[:, :, : PB // 2], head_rows[:, :, PB // 2 :]]
-    sides = [jnp.stack([sides[h][s] for s in orders[h]]) for h in range(2)]
-    for step in range(chip_bits):
-        mid = sides[0].shape[0] // 2
-        moved = [permute(sides[h][mid:], "walk", walk_size, 2 << sweeps[h][step]) for h in range(2)]
-        sides = [sides[h][:mid] + moved[h] for h in range(2)]
-    rows_mine = jnp.concatenate([sides[0][0], sides[1][0]], axis=1)
+        picked = None
+        for q, part in enumerate(near + far):
+            cols = lax.dynamic_slice(part, (0, at + h * PB // 2), (slots * row_block, PB // 2))
+            if q % 2 != h:
+                cols = cols.reshape(slots, row_block, PB // 2)
+                cols = jnp.concatenate([cols[orders[q % 2].index(s)] for s in orders[h]], axis=0)
+            picked = cols if picked is None else jnp.where(par_index // each == q, cols, picked)
+        head_cols.append(picked)
+
+    head_cols = plane_add(head_cols, plane_step(head_cols, 0))
+    tied = after([*head_cols, *far, *near])
+    head_cols, far, near = tied[:2], tied[2:4], tied[4:]
+    far_moved = plane_step(far, 0)
+    for step in range(1, chip_bits):
+        head_cols = plane_add(head_cols, plane_step(head_cols, step))
+    rows_mine = jnp.concatenate(head_cols, axis=1)
     bit = par_size // 2
+    rows_mine = rows_mine + permute(rows_mine, "par", par_size, bit)
+    far = plane_add(far, far_moved)
+    rows_mine, far[0], far[1] = after([rows_mine, *far])
+    for step in range(1, chip_bits):
+        far_moved = plane_step(far, step)
+        if step < chip_bits - 1:
+            far = plane_add(far, far_moved)
+    bit //= 2
     while bit:
         rows_mine = rows_mine + permute(rows_mine, "par", par_size, bit)
         bit //= 2
-    all_rows = rows_mine[None]
-    for bit in [2 << b for b in range(chip_bits)] + [1]:
-        all_rows = jnp.concatenate([all_rows, permute(all_rows, "walk", walk_size, bit)], axis=0)
-    flips = [0]
-    for bit in [2 << b for b in range(chip_bits)] + [1]:
-        flips += [f | bit for f in flips]
-    where_flip = np.argsort(np.array(flips))
-
-    def rows_of(block_index):
-        at = jnp.asarray(where_flip)[block_index ^ walk_index]
-        return lax.dynamic_index_in_dim(all_rows, at, 0, keepdims=False)
+
+    chips = walk_size // 2
+    per_col = col_block // row_block
+    top_count = -(-PB // row_block)
+
+    def spread(holder):
+        total = jnp.where(chip == jnp.asarray([holder(z) for z in range(par_size)])[par_index], rows_mine, 0.0)
+        for flip in range(1, chips):
+            pairs = []
+            for z in range(par_size):
+                for c in range(2):
+                    pairs.append(
+                        ((holder(z) * 2 + c) * par_size + z, ((holder(z) ^ flip) * 2 + c) * par_size + z)
+                    )
+            total = total + lax.ppermute(rows_mine, ("walk", "par"), pairs)
+        return total
+
+    both = jnp.stack([spread(lambda z: 0), spread(lambda z: z)])
+    far = plane_add(far, far_moved)
+    both, far[0], far[1] = after([both, *far])
+    far = [permute(part, "par", par_size, par_size // 2) for part in far]
+    near_moved = plane_step(near, 0)
+    swapped = permute(both, "walk", walk_size, 1)
+    near = plane_add(near, near_moved)
+    swapped, near[0], near[1] = after([swapped, *near])
+    for step in range(1, chip_bits):
+        near = plane_add(near, plane_step(near, step))
+    pair = [jnp.where(core == 0, both, swapped), jnp.where(core == 0, swapped, both)]
+    head = jnp.concatenate([pair[0][0], pair[1][0]], axis=0)[:PB]
+    col_rows = jnp.concatenate([pair[0][1], pair[1][1]], axis=0)
 
     def shift_at(first_row, count):
         ids = first_row + jnp.arange(count, dtype=jnp.int32)
         return SHIFT * (ids[:, None] == jnp.arange(PB, dtype=jnp.int32)[None, :]).astype(jnp.float32)
 
-    head = jnp.concatenate([rows_of(b) for b in range(-(-PB // row_block))], axis=0)[:PB]
     inverse = head_inverse(head + shift_at(0, PB))
+    near = [part + got for part, got in zip(near, far)]
+    moved = permute(near[1], "par", par_size, par_size // 4)
+    inverse, near[0], near[1] = after([inverse, *near])
     own_panel = outer_rows(rows_mine + shift_at(walk_index * row_block, row_block), inverse)
-    per_col = col_block // row_block
-    col_rows = jnp.concatenate([rows_of(par_index * per_col + b) for b in range(per_col)], axis=0)
     col_panel = outer_rows(col_rows + shift_at(par_index * col_block, col_block), inverse)
-
-    for step in range(chip_bits):
-        moved = []
-        for h in range(2):
-            mid = halves[h].shape[0] // 2
-            bit = 2 << sweeps[h][step]
-            moved.append(permute(halves[h][mid:], "walk", walk_size, bit))
-        halves = [halves[h][: halves[h].shape[0] // 2] + moved[h] for h in range(2)]
-    gram = halves[0] + permute(halves[1], "par", par_size, par_size // 2)
-    bit = par_size // 4
+    update = outer_rows(own_panel, col_panel)
+    gram = near[0] + moved
+    bit = par_size // 8
     while bit:
         mid = gram.shape[1] // 2
         gram = gram[:, :mid] + permute(gram[:, mid:], "par", par_size, bit)
@@ -459,8 +535,7 @@
     row_ids = walk_index * row_block + jnp.arange(row_block, dtype=jnp.int32)
     col_ids = par_index * col_block + jnp.arange(col_block, dtype=jnp.int32)
     shifted = gram + SHIFT * (row_ids[:, None] == col_ids[None, :]).astype(jnp.float32)
-    trailing = shifted - outer_rows(own_panel, col_panel)
-    return (own_panel, trailing)
+    return (own_panel, shifted - update)
 
 
 def solution(mesh):

time: 372 us -> 350 us (0.941)
  starting transfers between devices: 59 us -> 74.6 us
  local copies, waits for them, and re-layouts: 35 us -> 19.9 us
  waiting for transfers between devices: 130 us -> 116 us
  between operations: 8.61 us -> 1.41 us
    ppermute x45 -> x48, waiting for transfers between devices: 130 us -> 105 us  [permute(): return lax.ppermute(value, axis, xor_pairs(size, bit))]
    ppermute x0 -> x6, waiting for transfers between devices: none -> 11 us  [spread(): total = total + lax.ppermute(rows_mine, ('walk', 'par'), pairs)]
    ppermute x0 -> x6, starting transfers between devices: none -> 10.3 us  [spread(): total = total + lax.ppermute(rows_mine, ('walk', 'par'), pairs)]
    unnamed x96 -> x70, local copies, waits for them, and re-layouts: 9.68 us -> 1.99 us
    ppermute x45 -> x48, starting transfers between devices: 59 us -> 64.3 us  [permute(): return lax.ppermute(value, axis, xor_pairs(size, bit))]
    another operation x2 -> x0, local copies, waits for them, and re-layouts: 4.6 us -> none
    pallas_call x1 -> x2, Pallas kernels: 61.1 us -> 64.5 us  [the longest x1 61.1 us: gram_rows(): pl.pallas_call(functools.partial(centre_kernel, row_block, col_block, ord...]
  transfers between devices with their start and end apart: 45 -> 54, of which waited for: 28 -> 29; matrix products, arithmetic and copies ran while one was open for 10% -> 8% of each run, Pallas kernels for 14% -> 14%
where the time goes in v4:
time: 350 us; the launch traced here: 348 us
  waiting for transfers between devices  116 us (33%)
  Pallas kernels  115 us (33%)
  starting transfers between devices  74.6 us (21%)
  local copies, waits for them, and re-layouts  19.9 us (6%)
  other arithmetic  19.8 us (6%)
    ppermute x48, waiting for transfers between devices, permute(): return lax.ppermute(value, axis, xor_pairs(size, bit))  105 us
    ppermute x48, starting transfers between devices, permute(): return lax.ppermute(value, axis, xor_pairs(size, bit))  64.3 us
    pallas_call x1, Pallas kernels, gram_rows(): pl.pallas_call(functools.partial(centre_kernel, row_block, col_block, ord...  61.1 us
    pallas_call x4, Pallas kernels, jacobian(): pl.pallas_call(functools.partial(jacobian_kernel, slots, count), out_shap...  26.2 us
    pallas_call x1, Pallas kernels, head_inverse(): pl.pallas_call(head_kernel, out_shape=jax.ShapeDtypeStruct(head.shape, jn...  24.2 us
    ppermute x6, waiting for transfers between devices, spread(): total = total + lax.ppermute(rows_mine, ('walk', 'par'), pairs)  11 us
    ppermute x6, starting transfers between devices, spread(): total = total + lax.ppermute(rows_mine, ('walk', 'par'), pairs)  10.3 us
    squeeze x10, local copies, waits for them, and re-layouts, exchange(): held[d] = moved[i]  9.13 us
  transfers between devices with their start and end apart: 54, of which 29 were waited for; matrix products, arithmetic and copies ran while one was open for 8% of the time, Pallas kernels for 14%

profile of v4, /device:TPU:0, one launch (start us, length us, event | category | flops | bytes accessed | tf_op | source)
XLA Modules:
  0.0 348.4 jit_solution(15704958545588933083)
XLA Ops:
  3.6 3.4 turned_pieces.1
  8.2 3.0 collective-permute-start.3
  11.3 1.5 collective-permute-start.2
  12.9 2.6 collective-permute-start
  15.5 1.6 collective-permute-start.1
  17.1 11.8 %collective-permute-done.3 = f32[2,64,1536]{2,1,0:T(8,128)S(1)} collective-permute-done((f32[2,64,1536]{2,1,0:T(8,128)S(1)}, f32[2,64,1536]{2,1,0:T(8,128)S(1)}, u32[]{:S(2)}, u32[]{:S(2)}) %collective-permute-start.3) | collective-permute-done | bytes 786464 | tf_op jit(solution)/shard_map/ppermute | solution.py:118
  34.5 2.2 collective-permute-start.4
  36.7 1.6 collective-permute-start.5
  38.3 12.8 %collective-permute-done.7 = f32[2,64,1536]{2,1,0:T(8,128)S(1)} collective-permute-done((f32[2,64,1536]{2,1,0:T(8,128)S(1)}, f32[2,64,1536]{2,1,0:T(8,128)S(1)}, u32[]{:S(2)}, u32[]{:S(2)}) %collective-permute-start.7) | collective-permute-done | bytes 786464 | tf_op jit(solution)/shard_map/ppermute | solution.py:118
  55.5 1.5 collective-permute-start.10
  58.5 1.4 reshape.114.refs_8_
  60.0 2.3 collective-permute-start.8
  62.3 1.8 collective-permute-start.9
  64.0 6.5 %jacobian.4.refs_0_ = f32[16,4,48,256]{3,2,1,0:T(8,128)} custom-call(f32[64,1536]{1,0:T(8,128)} %get-tuple-element.102.refs_0_, f32[64,1536]{1,0:T(8,128)} %copy-done.4, f32[64,1536]{1,0:T(8,128)} %get-tuple-element.96.refs_2_, f32[64,1536]{1,0:T(8,128)} %get-tuple-element.97.refs_3_, f32[64,1536]{1,0:T(8,128)} %get-tuple-element.101.refs_4_, ...), custom_call_target="tpu_custom_call" | custom-call | tf_op jit(solution)/shard_map/jacobian/pallas_call | solution.py:222
  73.9 4.2 %collective-permute-done.8 = f32[64,1536]{1,0:T(8,128)S(1)} collective-permute-done((f32[64,1536]{1,0:T(8,128)}, f32[64,1536]{1,0:T(8,128)S(1)}, u32[]{:S(2)}, u32[]{:S(2)}) %collective-permute-start.8) | collective-permute-done | bytes 393248 | tf_op jit(solution)/shard_map/ppermute | solution.py:118
  78.2 2.0 collective-permute-start.12
  80.2 1.8 collective-permute-start.13
  84.5 12.3 %collective-permute-done.12.refs_4_ = f32[64,1536]{1,0:T(8,128)S(1)} collective-permute-done((f32[64,1536]{1,0:T(8,128)S(1)}, f32[64,1536]{1,0:T(8,128)S(1)}, u32[]{:S(2)}, u32[]{:S(2)}) %collective-permute-start.12) | collective-permute-done | bytes 393248 | tf_op jit(solution)/shard_map/ppermute | solution.py:118
  99.1 2.5 collective-permute-start.16
  101.6 1.8 collective-permute-start.17
  103.4 10.5 %collective-permute-done.19 = f32[2,64,1536]{2,1,0:T(8,128)S(1)} collective-permute-done((f32[2,64,1536]{2,1,0:T(8,128)S(1)}, f32[2,64,1536]{2,1,0:T(8,128)S(1)}, u32[]{:S(2)}, u32[]{:S(2)}) %collective-permute-start.19) | collective-permute-done | bytes 786464 | tf_op jit(solution)/shard_map/ppermute | solution.py:118
  115.8 1.9 collective-permute-done.16
  117.8 2.5 collective-permute-start.20
  120.3 1.7 collective-permute-start.21
  124.3 6.5 %jacobian.6.refs_2_ = f32[16,4,48,256]{3,2,1,0:T(8,128)} custom-call(f32[64,1536]{1,0:T(8,128)} %copy-done.19, f32[64,1536]{1,0:T(8,128)} %copy-done.21, f32[64,1536]{1,0:T(8,128)} %get-tuple-element.119.refs_2_, f32[64,1536]{1,0:T(8,128)} %get-tuple-element.120.refs_3_, f32[64,1536]{1,0:T(8,128)} %copy-done.13, f32[64,1536]{1,0:T(8,128)} %get-tuple-element.121.refs_5_, ...), custom_call_target="tpu_custom_call" | custom-call | tf_op jit(solution)/shard_map/jacobian/pallas_call | solution.py:222
  130.8 6.6 %jacobian.5.refs_1_ = f32[16,4,48,256]{3,2,1,0:T(8,128)} custom-call(f32[64,1536]{1,0:T(8,128)} %copy-done.12, f32[64,1536]{1,0:T(8,128)} %copy-done.2, f32[64,1536]{1,0:T(8,128)} %get-tuple-element.115.refs_2_, f32[64,1536]{1,0:T(8,128)} %get-tuple-element.116.refs_3_, f32[64,1536]{1,0:T(8,128)} %copy-done.17, f32[64,1536]{1,0:T(8,128)} %get-tuple-element.117.refs_5_, ...), custom_call_target="tpu_custom_call" | custom-call | tf_op jit(solution)/shard_map/jacobian/pallas_call | solution.py:222
  143.2 14.7 %collective-permute-done.25 = f32[2,64,1536]{2,1,0:T(8,128)S(1)} collective-permute-done((f32[2,64,1536]{2,1,0:T(8,128)S(1)}, f32[2,64,1536]{2,1,0:T(8,128)S(1)}, u32[]{:S(2)}, u32[]{:S(2)}) %collective-permute-start.25) | collective-permute-done | bytes 786464 | tf_op jit(solution)/shard_map/ppermute | solution.py:118
  160.4 6.6 %jacobian.7.refs_3_ = f32[16,4,48,256]{3,2,1,0:T(8,128)} custom-call(f32[64,1536]{1,0:T(8,128)} %copy-done.22, f32[64,1536]{1,0:T(8,128)} %copy-done.23, f32[64,1536]{1,0:T(8,128)} %get-tuple-element.171.refs_2_, f32[64,1536]{1,0:T(8,128)} %get-tuple-element.170.refs_3_, f32[64,1536]{1,0:T(8,128)} %copy-done.20, f32[64,1536]{1,0:T(8,128)} %get-tuple-element.169.refs_5_, ...), custom_call_target="tpu_custom_call" | custom-call | tf_op jit(solution)/shard_map/jacobian/pallas_call | solution.py:222
  173.0 61.1 %gram_rows.1 = (f32[768,384]{1,0:T(8,128)}, f32[768,384]{1,0:T(8,128)}, f32[768,384]{1,0:T(8,128)}, f32[768,384]{1,0:T(8,128)}) custom-call(s32[4]{0:T(128)} %pad_add_fusion.row_at, s32[4]{0:T(128)} %pad_add_fusion.1.col_at, s32[32]{0:T(128)} %broadcast_multiply_fusion.place_at, f32[16,4,48,256]{3,2,1,0:T(8,128)} %jacobian.4.refs_0_, ...), custom_call_target="tpu_custom_call" | custom-call | tf_op jit(solution)/shard_map/gram_rows/pallas_call | solution.py:290
  238.7 1.4 collective-permute-start.30
  240.1 4.1 %collective-permute-done.31 = f32[384,128]{1,0:T(8,128)S(1)} collective-permute-done((f32[384,128]{1,0:T(8,128)S(1)}, f32[384,128]{1,0:T(8,128)S(1)}, u32[]{:S(2)}, u32[]{:S(2)}) %collective-permute-start.31) | collective-permute-done | bytes 196640 | tf_op jit(solution)/shard_map/ppermute | solution.py:118
  244.2 1.6 collective-permute-done.30
  249.5 2.2 collective-permute-done.32
  252.8 2.8 collective-permute-start.34
  256.4 6.3 %collective-permute-done.34 = f32[192,256]{1,0:T(8,128)S(1)} collective-permute-done((f32[192,256]{1,0:T(8,128)S(1)}, f32[192,256]{1,0:T(8,128)S(1)}, u32[]{:S(2)}, u32[]{:S(2)}) %collective-permute-start.34) | collective-permute-done | bytes 196640 | tf_op jit(solution)/shard_map/ppermute | solution.py:118
  263.5 4.9 %collective-permute-done.35 = f32[384,384]{1,0:T(8,128)S(1)} collective-permute-done((f32[384,384]{1,0:T(8,128)S(1)}, f32[384,384]{1,0:T(8,128)S(1)}, u32[]{:S(2)}, u32[]{:S(2)}) %collective-permute-start.35) | collective-permute-done | bytes 589856 | tf_op jit(solution)/shard_map/ppermute | solution.py:118
  269.9 2.4 collective-permute-start.37
  277.2 2.9 collective-permute-start.38
  282.8 1.7 slice_add_fusion.4
  284.5 2.2 collective-permute-start.41
  288.0 8.0 %collective-permute-done.39 = f32[192,256]{1,0:T(8,128)S(1)} collective-permute-done((f32[192,256]{1,0:T(8,128)S(1)}, f32[192,256]{1,0:T(8,128)S(1)}, u32[]{:S(2)}, u32[]{:S(2)}) %collective-permute-start.39) | collective-permute-done | bytes 196640 | tf_op jit(solution)/shard_map/ppermute | solution.py:501
  298.4 2.9 collective-permute-done.43
  301.6 7.5 %collective-permute-done.47 = f32[384,384]{1,0:T(8,128)S(1)} collective-permute-done((f32[384,384]{1,0:T(8,128)S(1)}, f32[384,384]{1,0:T(8,128)S(1)}, u32[]{:S(2)}, u32[]{:S(2)}) %collective-permute-start.47) | collective-permute-done | bytes 589856 | tf_op jit(solution)/shard_map/ppermute | solution.py:118
  309.3 2.9 collective-permute-start.50
  312.2 2.3 collective-permute-start.51
  315.4 24.2 %head_inverse.1 = f32[256,256]{1,0:T(8,128)} custom-call(f32[256,256]{1,0:T(8,128)} %fusion.8.a_ref), custom_call_target="tpu_custom_call" | custom-call | tf_op jit(solution)/shard_map/head_inverse/pallas_call | solution.py:366
  340.7 1.9 collective-permute-start.53
  345.2 2.4 collective-permute-done.53
  (217 shorter events, 71.8 us)
Async XLA Ops:
  8.2 20.6 %collective-permute-start.3 = (f32[2,64,1536]{2,1,0:T(8,128)S(1)}, f32[2,64,1536]{2,1,0:T(8,128)S(1)}, u32[]{:S(2)}, u32[]{:S(2)}) collective-permute-start(f32[2,64,1536]{2,1,0:T(8,128)S(1)} %pad_maximum_fusion.1), channel_id=1, source_target_pairs={{0,16},{4,20},{8,24},{12,28},{16,0},{20,4},{24,8},{28,12},{1,17},{... | collective-permute-start | bytes 2359304 | tf_op jit(solution)/shard_map/ppermute | solution.py:118
  11.3 19.1 %collective-permute-start.2 = (f32[2,64,1536]{2,1,0:T(8,128)S(1)}, f32[2,64,1536]{2,1,0:T(8,128)S(1)}, u32[]{:S(2)}, u32[]{:S(2)}) collective-permute-start(f32[2,64,1536]{2,1,0:T(8,128)S(1)} %pad_maximum_fusion), channel_id=1, source_target_pairs={{0,8},{4,12},{8,0},{12,4},{16,24},{20,28},{24,16},{28,20},{1,9},{5... | collective-permute-start | bytes 2359304 | tf_op jit(solution)/shard_map/ppermute | solution.py:118
  12.9 19.7 %collective-permute-start = (f32[64,1536]{1,0:T(8,128)S(1)}, f32[64,1536]{1,0:T(8,128)S(1)}, u32[]{:S(2)}, u32[]{:S(2)}) collective-permute-start(f32[64,1536]{1,0:T(8,128)S(1)} %copy-done.34), channel_id=1, source_target_pairs={{0,2},{1,3},{2,0},{3,1},{4,6},{5,7},{6,4},{7,5},{8,10},{9,11},{10,... | collective-permute-start | bytes 1179656 | tf_op jit(solution)/shard_map/ppermute | solution.py:118
  15.5 17.3 %collective-permute-start.1 = (f32[64,1536]{1,0:T(8,128)S(1)}, f32[64,1536]{1,0:T(8,128)S(1)}, u32[]{:S(2)}, u32[]{:S(2)}) collective-permute-start(f32[64,1536]{1,0:T(8,128)S(1)} %copy-done.33), channel_id=1, source_target_pairs={{0,1},{1,0},{2,3},{3,2},{4,5},{5,4},{6,7},{7,6},{8,9},{9,8},{10,11... | collective-permute-start | bytes 1179656 | tf_op jit(solution)/shard_map/ppermute | solution.py:118
  32.9 18.2 %collective-permute-start.7 = (f32[2,64,1536]{2,1,0:T(8,128)S(1)}, f32[2,64,1536]{2,1,0:T(8,128)S(1)}, u32[]{:S(2)}, u32[]{:S(2)}) collective-permute-start(f32[2,64,1536]{2,1,0:T(8,128)S(1)} %pad_maximum_fusion.3), channel_id=1, source_target_pairs={{0,16},{4,20},{8,24},{12,28},{16,0},{20,4},{24,8},{28,12},{1,17},{... | collective-permute-start | bytes 2359304 | tf_op jit(solution)/shard_map/ppermute | solution.py:118
  33.6 18.3 %collective-permute-start.6 = (f32[2,64,1536]{2,1,0:T(8,128)S(1)}, f32[2,64,1536]{2,1,0:T(8,128)S(1)}, u32[]{:S(2)}, u32[]{:S(2)}) collective-permute-start(f32[2,64,1536]{2,1,0:T(8,128)S(1)} %pad_maximum_fusion.2), channel_id=1, source_target_pairs={{0,8},{4,12},{8,0},{12,4},{16,24},{20,28},{24,16},{28,20},{1,9},{5... | collective-permute-start | bytes 2359304 | tf_op jit(solution)/shard_map/ppermute | solution.py:118
  34.5 18.6 %collective-permute-start.4 = (f32[64,1536]{1,0:T(8,128)S(1)}, f32[64,1536]{1,0:T(8,128)S(1)}, u32[]{:S(2)}, u32[]{:S(2)}) collective-permute-start(f32[64,1536]{1,0:T(8,128)S(1)} %copy-done.32), channel_id=1, source_target_pairs={{0,2},{1,3},{2,0},{3,1},{4,6},{5,7},{6,4},{7,5},{8,10},{9,11},{10,... | collective-permute-start | bytes 1179656 | tf_op jit(solution)/shard_map/ppermute | solution.py:118
  36.7 16.5 %collective-permute-start.5 = (f32[64,1536]{1,0:T(8,128)S(1)}, f32[64,1536]{1,0:T(8,128)S(1)}, u32[]{:S(2)}, u32[]{:S(2)}) collective-permute-start(f32[64,1536]{1,0:T(8,128)S(1)} %copy-done.31), channel_id=1, source_target_pairs={{0,1},{1,0},{2,3},{3,2},{4,5},{5,4},{6,7},{7,6},{8,9},{9,8},{10,11... | collective-permute-start | bytes 1179656 | tf_op jit(solution)/shard_map/ppermute | solution.py:118
  54.3 17.6 %collective-permute-start.11 = (f32[2,64,1536]{2,1,0:T(8,128)}, f32[2,64,1536]{2,1,0:T(8,128)S(1)}, u32[]{:S(2)}, u32[]{:S(2)}) collective-permute-start(f32[2,64,1536]{2,1,0:T(8,128)} %pad_maximum_fusion.5), channel_id=1, source_target_pairs={{0,16},{4,20},{8,24},{12,28},{16,0},{20,4},{24,8},{28,12},{1,17},{... | collective-permute-start | bytes 2359304 | tf_op jit(solution)/shard_map/ppermute | solution.py:118
  55.5 17.3 %collective-permute-start.10 = (f32[2,64,1536]{2,1,0:T(8,128)S(1)}, f32[2,64,1536]{2,1,0:T(8,128)S(1)}, u32[]{:S(2)}, u32[]{:S(2)}) collective-permute-start(f32[2,64,1536]{2,1,0:T(8,128)S(1)} %pad_maximum_fusion.4), channel_id=1, source_target_pairs={{0,8},{4,12},{8,0},{12,4},{16,24},{20,28},{24,16},{28,20},{1,9},{5... | collective-permute-start | bytes 2359304 | tf_op jit(solution)/shard_map/ppermute | solution.py:118
  60.0 18.0 %collective-permute-start.8 = (f32[64,1536]{1,0:T(8,128)}, f32[64,1536]{1,0:T(8,128)S(1)}, u32[]{:S(2)}, u32[]{:S(2)}) collective-permute-start(f32[64,1536]{1,0:T(8,128)} %get-tuple-element.90), channel_id=1, source_target_pairs={{0,2},{1,3},{2,0},{3,1},{4,6},{5,7},{6,4},{7,5},{8,10},{9,11},{10,... | collective-permute-start | bytes 1179656 | tf_op jit(solution)/shard_map/ppermute | solution.py:118
  62.3 15.9 %collective-permute-start.9 = (f32[64,1536]{1,0:T(8,128)}, f32[64,1536]{1,0:T(8,128)}, u32[]{:S(2)}, u32[]{:S(2)}) collective-permute-start(f32[64,1536]{1,0:T(8,128)} %get-tuple-element.91), channel_id=1, source_target_pairs={{0,1},{1,0},{2,3},{3,2},{4,5},{5,4},{6,7},{7,6},{8,9},{9,8},{10,11... | collective-permute-start | bytes 1179656 | tf_op jit(solution)/shard_map/ppermute | solution.py:118
  78.2 18.6 %collective-permute-start.12 = (f32[64,1536]{1,0:T(8,128)S(1)}, f32[64,1536]{1,0:T(8,128)S(1)}, u32[]{:S(2)}, u32[]{:S(2)}) collective-permute-start(f32[64,1536]{1,0:T(8,128)S(1)} %copy-done.16), channel_id=1, source_target_pairs={{0,2},{1,3},{2,0},{3,1},{4,6},{5,7},{6,4},{7,5},{8,10},{9,11},{10,... | collective-permute-start | bytes 1179656 | tf_op jit(solution)/shard_map/ppermute | solution.py:118
  80.2 16.7 %collective-permute-start.13 = (f32[64,1536]{1,0:T(8,128)S(1)}, f32[64,1536]{1,0:T(8,128)S(1)}, u32[]{:S(2)}, u32[]{:S(2)}) collective-permute-start(f32[64,1536]{1,0:T(8,128)S(1)} %copy-done.14), channel_id=1, source_target_pairs={{0,1},{1,0},{2,3},{3,2},{4,5},{5,4},{6,7},{7,6},{8,9},{9,8},{10,11... | collective-permute-start | bytes 1179656 | tf_op jit(solution)/shard_map/ppermute | solution.py:118
  82.0 14.9 %collective-permute-start.14 = (f32[64,1536]{1,0:T(8,128)}, f32[64,1536]{1,0:T(8,128)S(1)}, u32[]{:S(2)}, u32[]{:S(2)}) collective-permute-start(f32[64,1536]{1,0:T(8,128)} %collective-permute-done.9), channel_id=1, source_target_pairs={{0,8},{4,12},{8,0},{12,4},{16,24},{20,28},{24,16},{28,20},{1,9},{5... | collective-permute-start | bytes 1179656 | tf_op jit(solution)/shard_map/ppermute | solution.py:118
  83.2 13.7 %collective-permute-start.15 = (f32[64,1536]{1,0:T(8,128)S(1)}, f32[64,1536]{1,0:T(8,128)S(1)}, u32[]{:S(2)}, u32[]{:S(2)}) collective-permute-start(f32[64,1536]{1,0:T(8,128)S(1)} %collective-permute-done.8), channel_id=1, source_target_pairs={{0,16},{4,20},{8,24},{12,28},{16,0},{20,4},{24,8},{28,12},{1,17},{... | collective-permute-start | bytes 1179656 | tf_op jit(solution)/shard_map/ppermute | solution.py:118
  97.0 16.9 %collective-permute-start.19 = (f32[2,64,1536]{2,1,0:T(8,128)S(1)}, f32[2,64,1536]{2,1,0:T(8,128)S(1)}, u32[]{:S(2)}, u32[]{:S(2)}) collective-permute-start(f32[2,64,1536]{2,1,0:T(8,128)S(1)} %pad_maximum_fusion.7), channel_id=1, source_target_pairs={{0,16},{4,20},{8,24},{12,28},{16,0},{20,4},{24,8},{28,12},{1,17},{... | collective-permute-start | bytes 2359304 | tf_op jit(solution)/shard_map/ppermute | solution.py:118
  98.0 16.9 %collective-permute-start.18 = (f32[2,64,1536]{2,1,0:T(8,128)S(1)}, f32[2,64,1536]{2,1,0:T(8,128)S(1)}, u32[]{:S(2)}, u32[]{:S(2)}) collective-permute-start(f32[2,64,1536]{2,1,0:T(8,128)S(1)} %pad_maximum_fusion.6), channel_id=1, source_target_pairs={{0,8},{4,12},{8,0},{12,4},{16,24},{20,28},{24,16},{28,20},{1,9},{5... | collective-permute-start | bytes 2359304 | tf_op jit(solution)/shard_map/ppermute | solution.py:118
  99.1 18.6 %collective-permute-start.16 = (f32[64,1536]{1,0:T(8,128)S(1)}, f32[64,1536]{1,0:T(8,128)S(1)}, u32[]{:S(2)}, u32[]{:S(2)}) collective-permute-start(f32[64,1536]{1,0:T(8,128)S(1)} %copy-done.28), channel_id=1, source_target_pairs={{0,2},{1,3},{2,0},{3,1},{4,6},{5,7},{6,4},{7,5},{8,10},{9,11},{10,... | collective-permute-start | bytes 1179656 | tf_op jit(solution)/shard_map/ppermute | solution.py:118
  101.6 16.2 %collective-permute-start.17 = (f32[64,1536]{1,0:T(8,128)S(1)}, f32[64,1536]{1,0:T(8,128)S(1)}, u32[]{:S(2)}, u32[]{:S(2)}) collective-permute-start(f32[64,1536]{1,0:T(8,128)S(1)} %collective-permute-done), channel_id=1, source_target_pairs={{0,1},{1,0},{2,3},{3,2},{4,5},{5,4},{6,7},{7,6},{8,9},{9,8},{10,11... | collective-permute-start | bytes 1179656 | tf_op jit(solution)/shard_map/ppermute | solution.py:118
  117.8 19.7 %collective-permute-start.20 = (f32[64,1536]{1,0:T(8,128)S(1)}, f32[64,1536]{1,0:T(8,128)S(1)}, u32[]{:S(2)}, u32[]{:S(2)}) collective-permute-start(f32[64,1536]{1,0:T(8,128)S(1)} %collective-permute-done.5.refs_4_), channel_id=1, source_target_pairs={{0,2},{1,3},{2,0},{3,1},{4,6},{5,7},{6,4},{7,5},{8,10},{9,11},{10,... | collective-permute-start | bytes 1179656 | tf_op jit(solution)/shard_map/ppermute | solution.py:118
  120.3 17.2 %collective-permute-start.21 = (f32[64,1536]{1,0:T(8,128)S(1)}, f32[64,1536]{1,0:T(8,128)S(1)}, u32[]{:S(2)}, u32[]{:S(2)}) collective-permute-start(f32[64,1536]{1,0:T(8,128)S(1)} %collective-permute-done.4.refs_0_), channel_id=1, source_target_pairs={{0,1},{1,0},{2,3},{3,2},{4,5},{5,4},{6,7},{7,6},{8,9},{9,8},{10,11... | collective-permute-start | bytes 1179656 | tf_op jit(solution)/shard_map/ppermute | solution.py:118
  122.0 15.5 %collective-permute-start.22 = (f32[64,1536]{1,0:T(8,128)S(1)}, f32[64,1536]{1,0:T(8,128)S(1)}, u32[]{:S(2)}, u32[]{:S(2)}) collective-permute-start(f32[64,1536]{1,0:T(8,128)S(1)} %collective-permute-done.17), channel_id=1, source_target_pairs={{0,8},{4,12},{8,0},{12,4},{16,24},{20,28},{24,16},{28,20},{1,9},{5... | collective-permute-start | bytes 1179656 | tf_op jit(solution)/shard_map/ppermute | solution.py:118
  123.2 14.3 %collective-permute-start.23 = (f32[64,1536]{1,0:T(8,128)S(1)}, f32[64,1536]{1,0:T(8,128)S(1)}, u32[]{:S(2)}, u32[]{:S(2)}) collective-permute-start(f32[64,1536]{1,0:T(8,128)S(1)} %collective-permute-done.16), channel_id=1, source_target_pairs={{0,16},{4,20},{8,24},{12,28},{16,0},{20,4},{24,8},{28,12},{1,17},{... | collective-permute-start | bytes 1179656 | tf_op jit(solution)/shard_map/ppermute | solution.py:118
  139.7 18.2 %collective-permute-start.25 = (f32[2,64,1536]{2,1,0:T(8,128)S(1)}, f32[2,64,1536]{2,1,0:T(8,128)S(1)}, u32[]{:S(2)}, u32[]{:S(2)}) collective-permute-start(f32[2,64,1536]{2,1,0:T(8,128)S(1)} %pad_maximum_fusion.9), channel_id=1, source_target_pairs={{0,8},{4,12},{8,0},{12,4},{16,24},{20,28},{24,16},{28,20},{1,9},{5... | collective-permute-start | bytes 2359304 | tf_op jit(solution)/shard_map/ppermute | solution.py:118
  141.8 17.6 %collective-permute-start.24 = (f32[2,64,1536]{2,1,0:T(8,128)S(1)}, f32[2,64,1536]{2,1,0:T(8,128)S(1)}, u32[]{:S(2)}, u32[]{:S(2)}) collective-permute-start(f32[2,64,1536]{2,1,0:T(8,128)S(1)} %pad_maximum_fusion.8), channel_id=1, source_target_pairs={{0,16},{4,20},{8,24},{12,28},{16,0},{20,4},{24,8},{28,12},{1,17},{... | collective-permute-start | bytes 2359304 | tf_op jit(solution)/shard_map/ppermute | solution.py:118
  142.7 29.2 %collective-permute-start.26 = (f32[16,4,48,256]{3,2,1,0:T(8,128)S(1)}, f32[16,4,48,256]{3,2,1,0:T(8,128)}, u32[]{:S(2)}, u32[]{:S(2)}) collective-permute-start(f32[16,4,48,256]{3,2,1,0:T(8,128)S(1)} %copy-done), channel_id=1, source_target_pairs={{0,4},{4,0},{8,12},{12,8},{16,20},{20,16},{24,28},{28,24},{1,5},{5... | collective-permute-start | bytes 9437192 | tf_op jit(solution)/shard_map/ppermute | solution.py:118
  142.7 29.2 %collective-permute-start.27 = (f32[16,4,48,256]{3,2,1,0:T(8,128)}, f32[16,4,48,256]{3,2,1,0:T(8,128)}, u32[]{:S(2)}, u32[]{:S(2)}) collective-permute-start(f32[16,4,48,256]{3,2,1,0:T(8,128)} %jacobian.5.refs_1_), channel_id=1, source_target_pairs={{0,4},{4,0},{8,12},{12,8},{16,20},{20,16},{24,28},{28,24},{1,5},{5... | collective-permute-start | bytes 9437192 | tf_op jit(solution)/shard_map/ppermute | solution.py:118
  143.2 28.7 %collective-permute-start.28 = (f32[16,4,48,256]{3,2,1,0:T(8,128)}, f32[16,4,48,256]{3,2,1,0:T(8,128)}, u32[]{:S(2)}, u32[]{:S(2)}) collective-permute-start(f32[16,4,48,256]{3,2,1,0:T(8,128)} %jacobian.6.refs_2_), channel_id=1, source_target_pairs={{0,4},{4,0},{8,12},{12,8},{16,20},{20,16},{24,28},{28,24},{1,5},{5... | collective-permute-start | bytes 9437192 | tf_op jit(solution)/shard_map/ppermute | solution.py:118
  237.1 7.1 %collective-permute-start.31 = (f32[384,128]{1,0:T(8,128)S(1)}, f32[384,128]{1,0:T(8,128)S(1)}, u32[]{:S(2)}, u32[]{:S(2)}) collective-permute-start(f32[384,128]{1,0:T(8,128)S(1)} %slice.323), channel_id=1, source_target_pairs={{0,16},{4,20},{8,24},{12,28},{16,0},{20,4},{24,8},{28,12},{1,17},{... | collective-permute-start | bytes 589832 | tf_op jit(solution)/shard_map/ppermute | solution.py:118
  238.7 7.1 %collective-permute-start.30 = (f32[384,128]{1,0:T(8,128)S(1)}, f32[384,128]{1,0:T(8,128)S(1)}, u32[]{:S(2)}, u32[]{:S(2)}) collective-permute-start(f32[384,128]{1,0:T(8,128)S(1)} %slice.321), channel_id=1, source_target_pairs={{0,8},{4,12},{8,0},{12,4},{16,24},{20,28},{24,16},{28,20},{1,9},{5... | collective-permute-start | bytes 589832 | tf_op jit(solution)/shard_map/ppermute | solution.py:118
  247.0 16.5 %collective-permute-start.36 = (f32[384,384]{1,0:T(8,128)S(1)}, f32[384,384]{1,0:T(8,128)S(1)}, u32[]{:S(2)}, u32[]{:S(2)}) collective-permute-start(f32[384,384]{1,0:T(8,128)S(1)} %slice.282), channel_id=1, source_target_pairs={{0,16},{4,20},{8,24},{12,28},{16,0},{20,4},{24,8},{28,12},{1,17},{... | collective-permute-start | bytes 1769480 | tf_op jit(solution)/shard_map/ppermute | solution.py:118
  252.8 10.0 %collective-permute-start.34 = (f32[192,256]{1,0:T(8,128)S(1)}, f32[192,256]{1,0:T(8,128)S(1)}, u32[]{:S(2)}, u32[]{:S(2)}) collective-permute-start(f32[192,256]{1,0:T(8,128)S(1)} %pad_maximum_fusion.12), channel_id=1, source_target_pairs={{0,2},{1,3},{2,0},{3,1},{4,6},{5,7},{6,4},{7,5},{8,10},{9,11},{10,... | collective-permute-start | bytes 589832 | tf_op jit(solution)/shard_map/ppermute | solution.py:118
  255.6 12.8 %collective-permute-start.35 = (f32[384,384]{1,0:T(8,128)S(1)}, f32[384,384]{1,0:T(8,128)S(1)}, u32[]{:S(2)}, u32[]{:S(2)}) collective-permute-start(f32[384,384]{1,0:T(8,128)S(1)} %slice.280), channel_id=1, source_target_pairs={{0,8},{4,12},{8,0},{12,4},{16,24},{20,28},{24,16},{28,20},{1,9},{5... | collective-permute-start | bytes 1769480 | tf_op jit(solution)/shard_map/ppermute | solution.py:118
  269.2 12.2 %collective-permute-start.45 = (f32[192,384]{1,0:T(8,128)}, f32[192,384]{1,0:T(8,128)}, u32[]{:S(2)}, u32[]{:S(2)}) collective-permute-start(f32[192,384]{1,0:T(8,128)} %slice.286), channel_id=1, source_target_pairs={{0,8},{4,12},{8,0},{12,4},{16,24},{20,28},{24,16},{28,20},{1,9},{5... | collective-permute-start | bytes 884744 | tf_op jit(solution)/shard_map/ppermute | solution.py:118
  273.0 11.4 %collective-permute-start.44 = (f32[192,384]{1,0:T(8,128)}, f32[192,384]{1,0:T(8,128)}, u32[]{:S(2)}, u32[]{:S(2)}) collective-permute-start(f32[192,384]{1,0:T(8,128)} %slice.284), channel_id=1, source_target_pairs={{0,16},{4,20},{8,24},{12,28},{16,0},{20,4},{24,8},{28,12},{1,17},{... | collective-permute-start | bytes 884744 | tf_op jit(solution)/shard_map/ppermute | solution.py:118
  274.3 27.2 %collective-permute-start.48 = (f32[384,384]{1,0:T(8,128)S(1)}, f32[384,384]{1,0:T(8,128)S(1)}, u32[]{:S(2)}, u32[]{:S(2)}) collective-permute-start(f32[384,384]{1,0:T(8,128)S(1)} %slice.290), channel_id=1, source_target_pairs={{0,16},{4,20},{8,24},{12,28},{16,0},{20,4},{24,8},{28,12},{1,17},{... | collective-permute-start | bytes 1769480 | tf_op jit(solution)/shard_map/ppermute | solution.py:118
  277.2 9.4 %collective-permute-start.38 = (f32[192,256]{1,0:T(8,128)S(1)}, f32[192,256]{1,0:T(8,128)S(1)}, u32[]{:S(2)}, u32[]{:S(2)}) collective-permute-start(f32[192,256]{1,0:T(8,128)S(1)} %add.302), channel_id=1, source_target_pairs={{0,8},{4,12},{1,9},{5,13},{2,10},{6,14},{3,11},{7,15}} | collective-permute-start | bytes 589832 | tf_op jit(solution)/shard_map/ppermute | solution.py:501
  280.1 15.9 %collective-permute-start.39 = (f32[192,256]{1,0:T(8,128)S(1)}, f32[192,256]{1,0:T(8,128)S(1)}, u32[]{:S(2)}, u32[]{:S(2)}) collective-permute-start(f32[192,256]{1,0:T(8,128)S(1)} %add.302), channel_id=1, source_target_pairs={{0,16},{4,20},{1,17},{5,21},{2,18},{6,22},{3,19},{7,23}} | collective-permute-start | bytes 589832 | tf_op jit(solution)/shard_map/ppermute | solution.py:501
  281.4 16.8 %collective-permute-start.40 = (f32[192,256]{1,0:T(8,128)S(1)}, f32[192,256]{1,0:T(8,128)S(1)}, u32[]{:S(2)}, u32[]{:S(2)}) collective-permute-start(f32[192,256]{1,0:T(8,128)S(1)} %add.302), channel_id=1, source_target_pairs={{0,24},{4,28},{1,25},{5,29},{2,26},{6,30},{3,27},{7,31}} | collective-permute-start | bytes 589832 | tf_op jit(solution)/shard_map/ppermute | solution.py:501
  284.5 13.9 %collective-permute-start.41 = (f32[192,256]{1,0:T(8,128)S(1)}, f32[192,256]{1,0:T(8,128)S(1)}, u32[]{:S(2)}, u32[]{:S(2)}) collective-permute-start(f32[192,256]{1,0:T(8,128)S(1)} %add.302), channel_id=1, source_target_pairs={{0,8},{4,12},{9,1},{13,5},{18,26},{22,30},{27,19},{31,23}} | collective-permute-start | bytes 589832 | tf_op jit(solution)/shard_map/ppermute | solution.py:501
  286.7 11.7 %collective-permute-start.42 = (f32[192,256]{1,0:T(8,128)S(1)}, f32[192,256]{1,0:T(8,128)S(1)}, u32[]{:S(2)}, u32[]{:S(2)}) collective-permute-start(f32[192,256]{1,0:T(8,128)S(1)} %add.302), channel_id=1, source_target_pairs={{0,16},{4,20},{9,25},{13,29},{18,2},{22,6},{27,11},{31,15}} | collective-permute-start | bytes 589832 | tf_op jit(solution)/shard_map/ppermute | solution.py:501
  298.3 10.8 %collective-permute-start.47 = (f32[384,384]{1,0:T(8,128)S(1)}, f32[384,384]{1,0:T(8,128)S(1)}, u32[]{:S(2)}, u32[]{:S(2)}) collective-permute-start(f32[384,384]{1,0:T(8,128)S(1)} %slice.288), channel_id=1, source_target_pairs={{0,8},{4,12},{8,0},{12,4},{16,24},{20,28},{24,16},{28,20},{1,9},{5... | collective-permute-start | bytes 1769480 | tf_op jit(solution)/shard_map/ppermute | solution.py:118
  301.5 10.7 %collective-permute-start.46 = (f32[2,192,256]{2,1,0:T(8,128)S(1)}, f32[2,192,256]{2,1,0:T(8,128)S(1)}, u32[]{:S(2)}, u32[]{:S(2)}) collective-permute-start(f32[2,192,256]{2,1,0:T(8,128)S(1)} %pad_maximum_fusion.10), channel_id=1, source_target_pairs={{0,4},{4,0},{8,12},{12,8},{16,20},{20,16},{24,28},{28,24},{1,5},{5... | collective-permute-start | bytes 1179656 | tf_op jit(solution)/shard_map/ppermute | solution.py:118
  309.2 30.5 %collective-permute-start.52 = (f32[192,384]{1,0:T(8,128)}, f32[192,384]{1,0:T(8,128)S(1)}, u32[]{:S(2)}, u32[]{:S(2)}) collective-permute-start(f32[192,384]{1,0:T(8,128)} %slice_add_fusion.4), channel_id=1, source_target_pairs={{0,2},{1,3},{2,0},{3,1},{4,6},{5,7},{6,4},{7,5},{8,10},{9,11},{10,... | collective-permute-start | bytes 884744 | tf_op jit(solution)/shard_map/ppermute | solution.py:118
  309.3 33.4 %collective-permute-start.50 = (f32[192,384]{1,0:T(8,128)S(1)}, f32[192,384]{1,0:T(8,128)S(1)}, u32[]{:S(2)}, u32[]{:S(2)}) collective-permute-start(f32[192,384]{1,0:T(8,128)S(1)} %slice_add_fusion.5), channel_id=1, source_target_pairs={{0,2},{1,3},{2,0},{3,1},{4,6},{5,7},{6,4},{7,5},{8,10},{9,11},{10,... | collective-permute-start | bytes 884744 | tf_op jit(solution)/shard_map/ppermute | solution.py:118
  312.2 27.5 %collective-permute-start.51 = (f32[192,384]{1,0:T(8,128)S(1)}, f32[192,384]{1,0:T(8,128)}, u32[]{:S(2)}, u32[]{:S(2)}) collective-permute-start(f32[192,384]{1,0:T(8,128)S(1)} %slice.297), channel_id=1, source_target_pairs={{0,8},{4,12},{8,0},{12,4},{16,24},{20,28},{24,16},{28,20},{1,9},{5... | collective-permute-start | bytes 884744 | tf_op jit(solution)/shard_map/ppermute | solution.py:118
  314.5 28.1 %collective-permute-start.49 = (f32[192,384]{1,0:T(8,128)S(1)}, f32[192,384]{1,0:T(8,128)}, u32[]{:S(2)}, u32[]{:S(2)}) collective-permute-start(f32[192,384]{1,0:T(8,128)S(1)} %slice.295), channel_id=1, source_target_pairs={{0,16},{4,20},{8,24},{12,28},{16,0},{20,4},{24,8},{28,12},{1,17},{... | collective-permute-start | bytes 884744 | tf_op jit(solution)/shard_map/ppermute | solution.py:118
  (41 other events, 289.0 us)

commit v5 on v4

--- a/solution.py
+++ b/solution.py
@@ -14,6 +14,7 @@
 SHIFT = 0.05
 LANES = 256
 SUB = 8
+TOGETHER = 2
 CONTRACT_LAST = (((1,), (1,)), ((), ()))
 VMEM_LIMIT = 60 * 1024 * 1024
 
@@ -239,8 +240,11 @@
 
 def product_rows(high_ref, low_ref, at, size, swap):
     at = pl.ds(at if isinstance(at, int) else pl.multiple_of(at, 16), size)
-    h, l = high_ref[0, at, :], low_ref[0, at, :]
-    return jnp.concatenate([h, l, h] if swap else [h, h, l], axis=1)
+    parts = []
+    for i in range(high_ref.shape[0]):
+        h, l = high_ref[i, at, :], low_ref[i, at, :]
+        parts += [h, l, h] if swap else [h, h, l]
+    return jnp.concatenate(parts, axis=1)
 
 
 def centre_kernel(row_block, col_block, orders, count, row_at, col_at, place_at, *refs):
@@ -254,16 +258,17 @@
             ref[...] = jnp.zeros_like(ref)
 
     members, rows = pieces[0].shape[1:3]
-    for a in range(count):
-        for m in range(members):
-            value_ref[pl.ds(pl.multiple_of(place_at[a * members + m], 8), rows), :] = pieces[a][0, m]
-    value = value_ref[...]
-    high, low = split_two(value)
     dot = functools.partial(jnp.dot, preferred_element_type=jnp.float32)
-    means = (dot(hot_t_ref[...], high) + dot(hot_t_ref[...], low)) * recip_ref[...]
-    first, second = split_two(means)
-    hot = hot_ref[...]
-    high_ref[0], low_ref[0] = split_two(value - (dot(hot, first) + dot(hot, second)))
+    for i in range(high_ref.shape[0]):
+        for a in range(count):
+            for m in range(members):
+                at = pl.multiple_of(place_at[a * members + m], 8)
+                value_ref[i, pl.ds(at, rows), :] = pieces[a][i, m]
+        value = value_ref[i]
+        high, low = split_two(value)
+        means = (dot(hot_t_ref[...], high) + dot(hot_t_ref[...], low)) * recip_ref[...]
+        means = jnp.concatenate(split_two(means), axis=0)
+        high_ref[i], low_ref[i] = split_two(value - dot(hot_ref[...], means))
 
     blocks = col_at.shape[0]
     width = blocks // 4 * col_block
@@ -283,7 +288,8 @@
 
 def gram_rows(pieces, hot, hot_t, recip, row_at, col_at, place_at, row_block, col_block, orders):
     tiles, members, rows, lanes = pieces[0].shape
-    walkers, groups = hot.shape
+    groups, walkers = hot_t.shape
+    hot = jnp.concatenate([hot, hot], axis=1)
     slots = len(orders[0])
     quarter = jax.ShapeDtypeStruct((slots * row_block, walkers // 4), jnp.float32)
     fixed = lambda t, *_: (0, 0)
@@ -292,18 +298,18 @@
         out_shape=(quarter,) * 4,
         grid_spec=pltpu.PrefetchScalarGridSpec(
             num_scalar_prefetch=3,
-            grid=(tiles,),
-            in_specs=[pl.BlockSpec((1, members, rows, lanes), lambda t, *_: (t, 0, 0, 0))] * len(pieces)
+            grid=(tiles // TOGETHER,),
+            in_specs=[pl.BlockSpec((TOGETHER, members, rows, lanes), lambda t, *_: (t, 0, 0, 0))] * len(pieces)
             + [
-                pl.BlockSpec((walkers, groups), fixed),
+                pl.BlockSpec((walkers, 2 * groups), fixed),
                 pl.BlockSpec((groups, walkers), fixed),
                 pl.BlockSpec((groups, 1), fixed),
             ],
             out_specs=(pl.BlockSpec(quarter.shape, fixed),) * 4,
             scratch_shapes=[
-                pltpu.VMEM((walkers, lanes), jnp.float32),
-                pltpu.VMEM((1, walkers, lanes), jnp.bfloat16),
-                pltpu.VMEM((1, walkers, lanes), jnp.bfloat16),
+                pltpu.VMEM((TOGETHER, walkers, lanes), jnp.float32),
+                pltpu.VMEM((TOGETHER, walkers, lanes), jnp.bfloat16),
+                pltpu.VMEM((TOGETHER, walkers, lanes), jnp.bfloat16),
             ],
         ),
         compiler_params=pltpu.CompilerParams(vmem_limit_bytes=VMEM_LIMIT),
@@ -338,40 +344,41 @@
     return unit / jnp.sqrt(diagonal)
 
 
-def head_kernel(a_ref, out_ref, work_ref, below_ref):
-    half = work_ref.shape[0]
-    dot = functools.partial(lax.dot_general, precision=HIGHEST, preferred_element_type=jnp.float32)
-    first = pl.program_id(0) == 0
-    @pl.when(first)
-    def _():
-        work_ref[...] = a_ref[:half, :half]
-    inverse = inverse_factor(work_ref[...])
-    @pl.when(first)
-    def _():
-        out_ref[:half, :half] = inverse
-        out_ref[:half, half:] = jnp.zeros((half, half), jnp.float32)
-        below = dot(a_ref[half:, :half], inverse, CONTRACT_LAST)
-        below_ref[...] = below
-        work_ref[...] = a_ref[half:, half:] - dot(below, below, CONTRACT_LAST)
-    @pl.when(jnp.logical_not(first))
-    def _():
-        out_ref[half:, half:] = inverse
-        plain = (((1,), (0,)), ((), ()))
-        out_ref[half:, :half] = -dot(inverse, dot(below_ref[...], out_ref[:half, :half], plain), plain)
-
-
-def head_inverse(head):
-    size = head.shape[0]
-    fixed = pl.BlockSpec((size, size), lambda i: (0, 0))
+def exact_dot(left, right, dims):
+    return lax.dot_general(left, right, dims, precision=HIGHEST, preferred_element_type=jnp.float32)
+
+
+def top_kernel(a_ref, inverse_ref, below_ref, rest_ref):
+    half = inverse_ref.shape[0]
+    inverse = inverse_factor(a_ref[:half, :half])
+    inverse_ref[...] = inverse
+    below = exact_dot(a_ref[half:, :half], inverse, CONTRACT_LAST)
+    below_ref[...] = below
+    rest_ref[...] = a_ref[half:, half:] - exact_dot(below, below, CONTRACT_LAST)
+
+
+def low_kernel(top_ref, below_ref, rest_ref, out_ref):
+    half = top_ref.shape[0]
+    plain = (((1,), (0,)), ((), ()))
+    inverse = inverse_factor(rest_ref[...])
+    out_ref[:half, :half] = top_ref[...]
+    out_ref[:half, half:] = jnp.zeros((half, half), jnp.float32)
+    out_ref[half:, half:] = inverse
+    out_ref[half:, :half] = -exact_dot(inverse, exact_dot(below_ref[...], top_ref[...], plain), plain)
+
+
+def head_top(head):
+    half = head.shape[0] // 2
     return pl.pallas_call(
-        head_kernel,
-        out_shape=jax.ShapeDtypeStruct(head.shape, jnp.float32),
-        grid=(2,),
-        in_specs=[fixed],
-        out_specs=fixed,
-        scratch_shapes=[pltpu.VMEM((size // 2, size // 2), jnp.float32)] * 2,
-        name="head_inverse",
+        top_kernel, out_shape=[jax.ShapeDtypeStruct((half, half), jnp.float32)] * 3, name="head_top"
     )(head)
+
+
+def head_low(top, below, rest):
+    size = 2 * top.shape[0]
+    return pl.pallas_call(
+        low_kernel, out_shape=jax.ShapeDtypeStruct((size, size), jnp.float32), name="head_low"
+    )(top, below, rest)
 
 
 def on_device(features, signals, param_scale, geometry, electrons):
@@ -505,12 +512,9 @@
     far = plane_add(far, far_moved)
     both, far[0], far[1] = after([both, *far])
     far = [permute(part, "par", par_size, par_size // 2) for part in far]
+    swapped = permute(both, "walk", walk_size, 1)
+    swapped, near[0], near[1] = after([swapped, *near])
     near_moved = plane_step(near, 0)
-    swapped = permute(both, "walk", walk_size, 1)
-    near = plane_add(near, near_moved)
-    swapped, near[0], near[1] = after([swapped, *near])
-    for step in range(1, chip_bits):
-        near = plane_add(near, plane_step(near, step))
     pair = [jnp.where(core == 0, both, swapped), jnp.where(core == 0, swapped, both)]
     head = jnp.concatenate([pair[0][0], pair[1][0]], axis=0)[:PB]
     col_rows = jnp.concatenate([pair[0][1], pair[1][1]], axis=0)
@@ -519,7 +523,13 @@
         ids = first_row + jnp.arange(count, dtype=jnp.int32)
         return SHIFT * (ids[:, None] == jnp.arange(PB, dtype=jnp.int32)[None, :]).astype(jnp.float32)
 
-    inverse = head_inverse(head + shift_at(0, PB))
+    first = head_top(head + shift_at(0, PB))
+    near = plane_add(near, near_moved)
+    tied = after([*first, *near])
+    first, near = tied[:3], tied[3:]
+    for step in range(1, chip_bits):
+        near = plane_add(near, plane_step(near, step))
+    inverse = head_low(*first)
     near = [part + got for part, got in zip(near, far)]
     moved = permute(near[1], "par", par_size, par_size // 4)
     inverse, near[0], near[1] = after([inverse, *near])

time: 350 us -> 338 us (0.966)
  waiting for transfers between devices: 116 us -> 105 us
  Pallas kernels: 115 us -> 110 us
    ppermute x6, waiting for transfers between devices: 11 us -> 2.52 us  [spread(): total = total + lax.ppermute(rows_mine, ('walk', 'par'), pairs)]
    pallas_call x1, Pallas kernels: 61.1 us -> 54.4 us  [gram_rows(): pl.pallas_call(functools.partial(centre_kernel, row_block, col_block, ord...]
    pallas_call x1 -> x2, Pallas kernels: 24.2 us -> 25.5 us  [the longest x1 12.9 us: head_top(): pl.pallas_call(top_kernel, out_shape=[jax.ShapeDtypeStruct((half, half),...]
  transfers between devices with their start and end apart: 54 -> 54, of which waited for: 29 -> 29; matrix products, arithmetic and copies ran while one was open for 8% -> 10% of each run, Pallas kernels for 14% -> 15%
where the time goes in v5:
time: 338 us; the launch traced here: 335 us
  Pallas kernels  110 us (33%)
  waiting for transfers between devices  105 us (31%)
  starting transfers between devices  74.6 us (22%)
  other arithmetic  22.2 us (7%)
  local copies, waits for them, and re-layouts  21.4 us (6%)
    ppermute x48, waiting for transfers between devices, permute(): return lax.ppermute(value, axis, xor_pairs(size, bit))  102 us
    ppermute x48, starting transfers between devices, permute(): return lax.ppermute(value, axis, xor_pairs(size, bit))  64.7 us
    pallas_call x1, Pallas kernels, gram_rows(): pl.pallas_call(functools.partial(centre_kernel, row_block, col_block, ord...  54.4 us
    pallas_call x4, Pallas kernels, jacobian(): pl.pallas_call(functools.partial(jacobian_kernel, slots, count), out_shap...  26.2 us
    pallas_call x1, Pallas kernels, head_top(): pl.pallas_call(top_kernel, out_shape=[jax.ShapeDtypeStruct((half, half),...  12.9 us
    pallas_call x1, Pallas kernels, head_low(): pl.pallas_call(low_kernel, out_shape=jax.ShapeDtypeStruct((size, size), j...  12.5 us
    ppermute x6, starting transfers between devices, spread(): total = total + lax.ppermute(rows_mine, ('walk', 'par'), pairs)  9.93 us
    squeeze x10, local copies, waits for them, and re-layouts, exchange(): held[d] = moved[i]  9.18 us
  transfers between devices with their start and end apart: 54, of which 29 were waited for; matrix products, arithmetic and copies ran while one was open for 10% of the time, Pallas kernels for 15%

profile of v5, /device:TPU:0, one launch (start us, length us, event | category | flops | bytes accessed | tf_op | source)
XLA Modules:
  0.0 335.4 jit_solution(15176486805097036849)
XLA Ops:
  3.6 3.4 %turned_pieces.1 = (f32[64,1536]{1,0:T(8,128)}, f32[64,1536]{1,0:T(8,128)}, f32[64,1536]{1,0:T(8,128)}, f32[64,1536]{1,0:T(8,128)}, f32[64,1536]{1,0:T(8,128)}, ...) custom-call(s32[2]{0:T(128)} %pad_add_fusion.2.own, f32[1,1536]{1,0:T(1,128)} %reshape.117.live_ref, ...), custom_call_target="tpu_custom_call" | custom-call | tf_op jit(solution)/shard_map/turned_pieces/pallas_call | solution.py:185
  8.3 3.0 collective-permute-start.3
  11.4 1.5 collective-permute-start.2
  12.9 2.6 collective-permute-start
  15.5 1.6 collective-permute-start.1
  17.1 11.8 %collective-permute-done.3 = f32[2,64,1536]{2,1,0:T(8,128)S(1)} collective-permute-done((f32[2,64,1536]{2,1,0:T(8,128)S(1)}, f32[2,64,1536]{2,1,0:T(8,128)S(1)}, u32[]{:S(2)}, u32[]{:S(2)}) %collective-permute-start.3) | collective-permute-done | bytes 786464 | tf_op jit(solution)/shard_map/ppermute | solution.py:119
  34.5 2.2 collective-permute-start.4
  36.7 1.6 collective-permute-start.5
  38.3 12.8 %collective-permute-done.7 = f32[2,64,1536]{2,1,0:T(8,128)S(1)} collective-permute-done((f32[2,64,1536]{2,1,0:T(8,128)S(1)}, f32[2,64,1536]{2,1,0:T(8,128)S(1)}, u32[]{:S(2)}, u32[]{:S(2)}) %collective-permute-start.7) | collective-permute-done | bytes 786464 | tf_op jit(solution)/shard_map/ppermute | solution.py:119
  55.6 1.5 collective-permute-start.10
  58.6 1.4 reshape.114.refs_8_
  60.0 2.3 collective-permute-start.8
  62.3 1.8 collective-permute-start.9
  64.1 6.5 %jacobian.4.refs_0_ = f32[16,4,48,256]{3,2,1,0:T(8,128)} custom-call(f32[64,1536]{1,0:T(8,128)} %get-tuple-element.110.refs_0_, f32[64,1536]{1,0:T(8,128)} %copy-done.4, f32[64,1536]{1,0:T(8,128)} %get-tuple-element.104.refs_2_, f32[64,1536]{1,0:T(8,128)} %get-tuple-element.105.refs_3_, f32[64,1536]{1,0:T(8,128)} %get-tuple-element.109.refs_4_, ...), custom_call_target="tpu_custom_call" | custom-call | tf_op jit(solution)/shard_map/jacobian/pallas_call | solution.py:223
  73.9 4.1 %collective-permute-done.8 = f32[64,1536]{1,0:T(8,128)S(1)} collective-permute-done((f32[64,1536]{1,0:T(8,128)}, f32[64,1536]{1,0:T(8,128)S(1)}, u32[]{:S(2)}, u32[]{:S(2)}) %collective-permute-start.8) | collective-permute-done | bytes 393248 | tf_op jit(solution)/shard_map/ppermute | solution.py:119
  78.2 2.0 collective-permute-start.12
  80.2 1.8 collective-permute-start.13
  84.5 12.3 %collective-permute-done.12.refs_4_ = f32[64,1536]{1,0:T(8,128)S(1)} collective-permute-done((f32[64,1536]{1,0:T(8,128)S(1)}, f32[64,1536]{1,0:T(8,128)S(1)}, u32[]{:S(2)}, u32[]{:S(2)}) %collective-permute-start.12) | collective-permute-done | bytes 393248 | tf_op jit(solution)/shard_map/ppermute | solution.py:119
  99.1 2.5 collective-permute-start.16
  101.6 1.8 collective-permute-start.17
  103.4 10.6 %collective-permute-done.19 = f32[2,64,1536]{2,1,0:T(8,128)S(1)} collective-permute-done((f32[2,64,1536]{2,1,0:T(8,128)S(1)}, f32[2,64,1536]{2,1,0:T(8,128)S(1)}, u32[]{:S(2)}, u32[]{:S(2)}) %collective-permute-start.19) | collective-permute-done | bytes 786464 | tf_op jit(solution)/shard_map/ppermute | solution.py:119
  115.9 1.9 collective-permute-done.16
  117.8 2.4 collective-permute-start.20
  120.3 1.7 collective-permute-start.21
  124.4 6.6 %jacobian.6.refs_2_ = f32[16,4,48,256]{3,2,1,0:T(8,128)} custom-call(f32[64,1536]{1,0:T(8,128)} %copy-done.19, f32[64,1536]{1,0:T(8,128)} %copy-done.21, f32[64,1536]{1,0:T(8,128)} %get-tuple-element.127.refs_2_, f32[64,1536]{1,0:T(8,128)} %get-tuple-element.128.refs_3_, f32[64,1536]{1,0:T(8,128)} %copy-done.13, f32[64,1536]{1,0:T(8,128)} %get-tuple-element.129.refs_5_, ...), custom_call_target="tpu_custom_call" | custom-call | tf_op jit(solution)/shard_map/jacobian/pallas_call | solution.py:223
  130.9 6.6 %jacobian.5.refs_1_ = f32[16,4,48,256]{3,2,1,0:T(8,128)} custom-call(f32[64,1536]{1,0:T(8,128)} %copy-done.12, f32[64,1536]{1,0:T(8,128)} %copy-done.2, f32[64,1536]{1,0:T(8,128)} %get-tuple-element.123.refs_2_, f32[64,1536]{1,0:T(8,128)} %get-tuple-element.124.refs_3_, f32[64,1536]{1,0:T(8,128)} %copy-done.17, f32[64,1536]{1,0:T(8,128)} %get-tuple-element.125.refs_5_, ...), custom_call_target="tpu_custom_call" | custom-call | tf_op jit(solution)/shard_map/jacobian/pallas_call | solution.py:223
  143.3 14.6 %collective-permute-done.25 = f32[2,64,1536]{2,1,0:T(8,128)S(1)} collective-permute-done((f32[2,64,1536]{2,1,0:T(8,128)S(1)}, f32[2,64,1536]{2,1,0:T(8,128)S(1)}, u32[]{:S(2)}, u32[]{:S(2)}) %collective-permute-start.25) | collective-permute-done | bytes 786464 | tf_op jit(solution)/shard_map/ppermute | solution.py:119
  160.4 6.6 %jacobian.7.refs_3_ = f32[16,4,48,256]{3,2,1,0:T(8,128)} custom-call(f32[64,1536]{1,0:T(8,128)} %copy-done.22, f32[64,1536]{1,0:T(8,128)} %copy-done.23, f32[64,1536]{1,0:T(8,128)} %get-tuple-element.187.refs_2_, f32[64,1536]{1,0:T(8,128)} %get-tuple-element.186.refs_3_, f32[64,1536]{1,0:T(8,128)} %copy-done.20, f32[64,1536]{1,0:T(8,128)} %get-tuple-element.185.refs_5_, ...), custom_call_target="tpu_custom_call" | custom-call | tf_op jit(solution)/shard_map/jacobian/pallas_call | solution.py:223
  173.0 54.4 %gram_rows.1 = (f32[768,384]{1,0:T(8,128)}, f32[768,384]{1,0:T(8,128)}, f32[768,384]{1,0:T(8,128)}, f32[768,384]{1,0:T(8,128)}) custom-call(s32[4]{0:T(128)} %pad_add_fusion.row_at, s32[4]{0:T(128)} %pad_add_fusion.1.col_at, s32[32]{0:T(128)} %broadcast_multiply_fusion.place_at, f32[16,4,48,256]{3,2,1,0:T(8,128)} %jacobian.4.refs_0_, ...), custom_call_target="tpu_custom_call" | custom-call | tf_op jit(solution)/shard_map/gram_rows/pallas_call | solution.py:296
  233.5 4.0 %collective-permute-done.31 = f32[384,128]{1,0:T(8,128)S(1)} collective-permute-done((f32[384,128]{1,0:T(8,128)S(1)}, f32[384,128]{1,0:T(8,128)S(1)}, u32[]{:S(2)}, u32[]{:S(2)}) %collective-permute-start.31) | collective-permute-done | bytes 196640 | tf_op jit(solution)/shard_map/ppermute | solution.py:119
  237.5 1.6 collective-permute-done.30
  242.7 2.2 collective-permute-done.32
  246.0 2.9 collective-permute-start.34
  249.8 6.3 %collective-permute-done.34 = f32[192,256]{1,0:T(8,128)S(1)} collective-permute-done((f32[192,256]{1,0:T(8,128)S(1)}, f32[192,256]{1,0:T(8,128)S(1)}, u32[]{:S(2)}, u32[]{:S(2)}) %collective-permute-start.34) | collective-permute-done | bytes 196640 | tf_op jit(solution)/shard_map/ppermute | solution.py:119
  256.9 5.0 %collective-permute-done.35 = f32[384,384]{1,0:T(8,128)S(1)} collective-permute-done((f32[384,384]{1,0:T(8,128)S(1)}, f32[384,384]{1,0:T(8,128)S(1)}, u32[]{:S(2)}, u32[]{:S(2)}) %collective-permute-start.35) | collective-permute-done | bytes 589856 | tf_op jit(solution)/shard_map/ppermute | solution.py:119
  263.4 2.0 collective-permute-start.37
  267.5 1.9 collective-permute-done.37
  270.5 3.2 collective-permute-start.38
  277.6 1.7 slice_add_fusion.4
  280.6 1.5 collective-permute-start.43
  282.2 1.7 slice_add_fusion.5
  284.3 2.1 collective-permute-done.43
  286.8 1.5 collective-permute-done.46
  290.0 3.9 %collective-permute-start.47 = (f32[384,384]{1,0:T(8,128)}, f32[384,384]{1,0:T(8,128)}, u32[]{:S(2)}, u32[]{:S(2)}) collective-permute-start(f32[384,384]{1,0:T(8,128)} %slice.291), channel_id=1, source_target_pairs={{0,8},{4,12},{8,0},{12,4},{16,24},{20,28},{24,16},{28,20},{1,9},{5... | collective-permute-start | bytes 1769480 | tf_op jit(solution)/shard_map/ppermute | solution.py:119
  294.9 12.9 %head_top.1 = (f32[128,128]{1,0:T(8,128)}, f32[128,128]{1,0:T(8,128)}, f32[128,128]{1,0:T(8,128)}) custom-call(f32[256,256]{1,0:T(8,128)} %fusion.7.a_ref), custom_call_target="tpu_custom_call" | custom-call | tf_op jit(solution)/shard_map/head_top/pallas_call | solution.py:372
  312.6 12.5 %head_low.1 = f32[256,256]{1,0:T(8,128)} custom-call(f32[128,128]{1,0:T(8,128)} %get-tuple-element.157.top_ref, f32[128,128]{1,0:T(8,128)} %get-tuple-element.158.below_ref, f32[128,128]{1,0:T(8,128)} %get-tuple-element.159.rest_ref), custom_call_target="tpu_custom_call" | custom-call | tf_op jit(solution)/shard_map/head_low/pallas_call | solution.py:379
  326.3 2.0 collective-permute-start.53
  329.9 4.6 %collective-permute-done.53 = f32[192,384]{1,0:T(8,128)S(1)} collective-permute-done((f32[192,384]{1,0:T(8,128)S(1)}, f32[192,384]{1,0:T(8,128)S(1)}, u32[]{:S(2)}, u32[]{:S(2)}) %collective-permute-start.53) | collective-permute-done | bytes 294944 | tf_op jit(solution)/shard_map/ppermute | solution.py:119
  (219 shorter events, 76.5 us)
Async XLA Ops:
  8.3 20.6 %collective-permute-start.3 = (f32[2,64,1536]{2,1,0:T(8,128)S(1)}, f32[2,64,1536]{2,1,0:T(8,128)S(1)}, u32[]{:S(2)}, u32[]{:S(2)}) collective-permute-start(f32[2,64,1536]{2,1,0:T(8,128)S(1)} %pad_maximum_fusion.1), channel_id=1, source_target_pairs={{0,16},{4,20},{8,24},{12,28},{16,0},{20,4},{24,8},{28,12},{1,17},{... | collective-permute-start | bytes 2359304 | tf_op jit(solution)/shard_map/ppermute | solution.py:119
  11.4 19.1 %collective-permute-start.2 = (f32[2,64,1536]{2,1,0:T(8,128)S(1)}, f32[2,64,1536]{2,1,0:T(8,128)S(1)}, u32[]{:S(2)}, u32[]{:S(2)}) collective-permute-start(f32[2,64,1536]{2,1,0:T(8,128)S(1)} %pad_maximum_fusion), channel_id=1, source_target_pairs={{0,8},{4,12},{8,0},{12,4},{16,24},{20,28},{24,16},{28,20},{1,9},{5... | collective-permute-start | bytes 2359304 | tf_op jit(solution)/shard_map/ppermute | solution.py:119
  12.9 19.7 %collective-permute-start = (f32[64,1536]{1,0:T(8,128)S(1)}, f32[64,1536]{1,0:T(8,128)S(1)}, u32[]{:S(2)}, u32[]{:S(2)}) collective-permute-start(f32[64,1536]{1,0:T(8,128)S(1)} %copy-done.34), channel_id=1, source_target_pairs={{0,2},{1,3},{2,0},{3,1},{4,6},{5,7},{6,4},{7,5},{8,10},{9,11},{10,... | collective-permute-start | bytes 1179656 | tf_op jit(solution)/shard_map/ppermute | solution.py:119
  15.5 17.3 %collective-permute-start.1 = (f32[64,1536]{1,0:T(8,128)S(1)}, f32[64,1536]{1,0:T(8,128)S(1)}, u32[]{:S(2)}, u32[]{:S(2)}) collective-permute-start(f32[64,1536]{1,0:T(8,128)S(1)} %copy-done.33), channel_id=1, source_target_pairs={{0,1},{1,0},{2,3},{3,2},{4,5},{5,4},{6,7},{7,6},{8,9},{9,8},{10,11... | collective-permute-start | bytes 1179656 | tf_op jit(solution)/shard_map/ppermute | solution.py:119
  32.9 18.2 %collective-permute-start.7 = (f32[2,64,1536]{2,1,0:T(8,128)S(1)}, f32[2,64,1536]{2,1,0:T(8,128)S(1)}, u32[]{:S(2)}, u32[]{:S(2)}) collective-permute-start(f32[2,64,1536]{2,1,0:T(8,128)S(1)} %pad_maximum_fusion.3), channel_id=1, source_target_pairs={{0,16},{4,20},{8,24},{12,28},{16,0},{20,4},{24,8},{28,12},{1,17},{... | collective-permute-start | bytes 2359304 | tf_op jit(solution)/shard_map/ppermute | solution.py:119
  33.6 18.3 %collective-permute-start.6 = (f32[2,64,1536]{2,1,0:T(8,128)S(1)}, f32[2,64,1536]{2,1,0:T(8,128)S(1)}, u32[]{:S(2)}, u32[]{:S(2)}) collective-permute-start(f32[2,64,1536]{2,1,0:T(8,128)S(1)} %pad_maximum_fusion.2), channel_id=1, source_target_pairs={{0,8},{4,12},{8,0},{12,4},{16,24},{20,28},{24,16},{28,20},{1,9},{5... | collective-permute-start | bytes 2359304 | tf_op jit(solution)/shard_map/ppermute | solution.py:119
  34.5 18.6 %collective-permute-start.4 = (f32[64,1536]{1,0:T(8,128)S(1)}, f32[64,1536]{1,0:T(8,128)S(1)}, u32[]{:S(2)}, u32[]{:S(2)}) collective-permute-start(f32[64,1536]{1,0:T(8,128)S(1)} %copy-done.32), channel_id=1, source_target_pairs={{0,2},{1,3},{2,0},{3,1},{4,6},{5,7},{6,4},{7,5},{8,10},{9,11},{10,... | collective-permute-start | bytes 1179656 | tf_op jit(solution)/shard_map/ppermute | solution.py:119
  36.7 16.5 %collective-permute-start.5 = (f32[64,1536]{1,0:T(8,128)S(1)}, f32[64,1536]{1,0:T(8,128)S(1)}, u32[]{:S(2)}, u32[]{:S(2)}) collective-permute-start(f32[64,1536]{1,0:T(8,128)S(1)} %copy-done.31), channel_id=1, source_target_pairs={{0,1},{1,0},{2,3},{3,2},{4,5},{5,4},{6,7},{7,6},{8,9},{9,8},{10,11... | collective-permute-start | bytes 1179656 | tf_op jit(solution)/shard_map/ppermute | solution.py:119
  54.3 17.6 %collective-permute-start.11 = (f32[2,64,1536]{2,1,0:T(8,128)}, f32[2,64,1536]{2,1,0:T(8,128)S(1)}, u32[]{:S(2)}, u32[]{:S(2)}) collective-permute-start(f32[2,64,1536]{2,1,0:T(8,128)} %pad_maximum_fusion.5), channel_id=1, source_target_pairs={{0,16},{4,20},{8,24},{12,28},{16,0},{20,4},{24,8},{28,12},{1,17},{... | collective-permute-start | bytes 2359304 | tf_op jit(solution)/shard_map/ppermute | solution.py:119
  55.6 17.3 %collective-permute-start.10 = (f32[2,64,1536]{2,1,0:T(8,128)S(1)}, f32[2,64,1536]{2,1,0:T(8,128)S(1)}, u32[]{:S(2)}, u32[]{:S(2)}) collective-permute-start(f32[2,64,1536]{2,1,0:T(8,128)S(1)} %pad_maximum_fusion.4), channel_id=1, source_target_pairs={{0,8},{4,12},{8,0},{12,4},{16,24},{20,28},{24,16},{28,20},{1,9},{5... | collective-permute-start | bytes 2359304 | tf_op jit(solution)/shard_map/ppermute | solution.py:119
  60.0 18.0 %collective-permute-start.8 = (f32[64,1536]{1,0:T(8,128)}, f32[64,1536]{1,0:T(8,128)S(1)}, u32[]{:S(2)}, u32[]{:S(2)}) collective-permute-start(f32[64,1536]{1,0:T(8,128)} %get-tuple-element.98), channel_id=1, source_target_pairs={{0,2},{1,3},{2,0},{3,1},{4,6},{5,7},{6,4},{7,5},{8,10},{9,11},{10,... | collective-permute-start | bytes 1179656 | tf_op jit(solution)/shard_map/ppermute | solution.py:119
  62.3 15.9 %collective-permute-start.9 = (f32[64,1536]{1,0:T(8,128)}, f32[64,1536]{1,0:T(8,128)}, u32[]{:S(2)}, u32[]{:S(2)}) collective-permute-start(f32[64,1536]{1,0:T(8,128)} %get-tuple-element.99), channel_id=1, source_target_pairs={{0,1},{1,0},{2,3},{3,2},{4,5},{5,4},{6,7},{7,6},{8,9},{9,8},{10,11... | collective-permute-start | bytes 1179656 | tf_op jit(solution)/shard_map/ppermute | solution.py:119
  78.2 18.6 %collective-permute-start.12 = (f32[64,1536]{1,0:T(8,128)S(1)}, f32[64,1536]{1,0:T(8,128)S(1)}, u32[]{:S(2)}, u32[]{:S(2)}) collective-permute-start(f32[64,1536]{1,0:T(8,128)S(1)} %copy-done.16), channel_id=1, source_target_pairs={{0,2},{1,3},{2,0},{3,1},{4,6},{5,7},{6,4},{7,5},{8,10},{9,11},{10,... | collective-permute-start | bytes 1179656 | tf_op jit(solution)/shard_map/ppermute | solution.py:119
  80.2 16.7 %collective-permute-start.13 = (f32[64,1536]{1,0:T(8,128)S(1)}, f32[64,1536]{1,0:T(8,128)S(1)}, u32[]{:S(2)}, u32[]{:S(2)}) collective-permute-start(f32[64,1536]{1,0:T(8,128)S(1)} %copy-done.14), channel_id=1, source_target_pairs={{0,1},{1,0},{2,3},{3,2},{4,5},{5,4},{6,7},{7,6},{8,9},{9,8},{10,11... | collective-permute-start | bytes 1179656 | tf_op jit(solution)/shard_map/ppermute | solution.py:119
  82.0 14.9 %collective-permute-start.14 = (f32[64,1536]{1,0:T(8,128)}, f32[64,1536]{1,0:T(8,128)S(1)}, u32[]{:S(2)}, u32[]{:S(2)}) collective-permute-start(f32[64,1536]{1,0:T(8,128)} %collective-permute-done.9), channel_id=1, source_target_pairs={{0,8},{4,12},{8,0},{12,4},{16,24},{20,28},{24,16},{28,20},{1,9},{5... | collective-permute-start | bytes 1179656 | tf_op jit(solution)/shard_map/ppermute | solution.py:119
  83.3 13.7 %collective-permute-start.15 = (f32[64,1536]{1,0:T(8,128)S(1)}, f32[64,1536]{1,0:T(8,128)S(1)}, u32[]{:S(2)}, u32[]{:S(2)}) collective-permute-start(f32[64,1536]{1,0:T(8,128)S(1)} %collective-permute-done.8), channel_id=1, source_target_pairs={{0,16},{4,20},{8,24},{12,28},{16,0},{20,4},{24,8},{28,12},{1,17},{... | collective-permute-start | bytes 1179656 | tf_op jit(solution)/shard_map/ppermute | solution.py:119
  97.0 16.9 %collective-permute-start.19 = (f32[2,64,1536]{2,1,0:T(8,128)S(1)}, f32[2,64,1536]{2,1,0:T(8,128)S(1)}, u32[]{:S(2)}, u32[]{:S(2)}) collective-permute-start(f32[2,64,1536]{2,1,0:T(8,128)S(1)} %pad_maximum_fusion.7), channel_id=1, source_target_pairs={{0,16},{4,20},{8,24},{12,28},{16,0},{20,4},{24,8},{28,12},{1,17},{... | collective-permute-start | bytes 2359304 | tf_op jit(solution)/shard_map/ppermute | solution.py:119
  98.0 16.9 %collective-permute-start.18 = (f32[2,64,1536]{2,1,0:T(8,128)S(1)}, f32[2,64,1536]{2,1,0:T(8,128)S(1)}, u32[]{:S(2)}, u32[]{:S(2)}) collective-permute-start(f32[2,64,1536]{2,1,0:T(8,128)S(1)} %pad_maximum_fusion.6), channel_id=1, source_target_pairs={{0,8},{4,12},{8,0},{12,4},{16,24},{20,28},{24,16},{28,20},{1,9},{5... | collective-permute-start | bytes 2359304 | tf_op jit(solution)/shard_map/ppermute | solution.py:119
  99.1 18.7 %collective-permute-start.16 = (f32[64,1536]{1,0:T(8,128)S(1)}, f32[64,1536]{1,0:T(8,128)S(1)}, u32[]{:S(2)}, u32[]{:S(2)}) collective-permute-start(f32[64,1536]{1,0:T(8,128)S(1)} %copy-done.27), channel_id=1, source_target_pairs={{0,2},{1,3},{2,0},{3,1},{4,6},{5,7},{6,4},{7,5},{8,10},{9,11},{10,... | collective-permute-start | bytes 1179656 | tf_op jit(solution)/shard_map/ppermute | solution.py:119
  101.6 16.2 %collective-permute-start.17 = (f32[64,1536]{1,0:T(8,128)S(1)}, f32[64,1536]{1,0:T(8,128)S(1)}, u32[]{:S(2)}, u32[]{:S(2)}) collective-permute-start(f32[64,1536]{1,0:T(8,128)S(1)} %collective-permute-done), channel_id=1, source_target_pairs={{0,1},{1,0},{2,3},{3,2},{4,5},{5,4},{6,7},{7,6},{8,9},{9,8},{10,11... | collective-permute-start | bytes 1179656 | tf_op jit(solution)/shard_map/ppermute | solution.py:119
  117.8 19.7 %collective-permute-start.20 = (f32[64,1536]{1,0:T(8,128)S(1)}, f32[64,1536]{1,0:T(8,128)S(1)}, u32[]{:S(2)}, u32[]{:S(2)}) collective-permute-start(f32[64,1536]{1,0:T(8,128)S(1)} %collective-permute-done.5.refs_4_), channel_id=1, source_target_pairs={{0,2},{1,3},{2,0},{3,1},{4,6},{5,7},{6,4},{7,5},{8,10},{9,11},{10,... | collective-permute-start | bytes 1179656 | tf_op jit(solution)/shard_map/ppermute | solution.py:119
  120.3 17.2 %collective-permute-start.21 = (f32[64,1536]{1,0:T(8,128)S(1)}, f32[64,1536]{1,0:T(8,128)S(1)}, u32[]{:S(2)}, u32[]{:S(2)}) collective-permute-start(f32[64,1536]{1,0:T(8,128)S(1)} %collective-permute-done.4.refs_0_), channel_id=1, source_target_pairs={{0,1},{1,0},{2,3},{3,2},{4,5},{5,4},{6,7},{7,6},{8,9},{9,8},{10,11... | collective-permute-start | bytes 1179656 | tf_op jit(solution)/shard_map/ppermute | solution.py:119
  122.0 15.6 %collective-permute-start.22 = (f32[64,1536]{1,0:T(8,128)S(1)}, f32[64,1536]{1,0:T(8,128)S(1)}, u32[]{:S(2)}, u32[]{:S(2)}) collective-permute-start(f32[64,1536]{1,0:T(8,128)S(1)} %collective-permute-done.17), channel_id=1, source_target_pairs={{0,8},{4,12},{8,0},{12,4},{16,24},{20,28},{24,16},{28,20},{1,9},{5... | collective-permute-start | bytes 1179656 | tf_op jit(solution)/shard_map/ppermute | solution.py:119
  123.3 14.3 %collective-permute-start.23 = (f32[64,1536]{1,0:T(8,128)S(1)}, f32[64,1536]{1,0:T(8,128)S(1)}, u32[]{:S(2)}, u32[]{:S(2)}) collective-permute-start(f32[64,1536]{1,0:T(8,128)S(1)} %collective-permute-done.16), channel_id=1, source_target_pairs={{0,16},{4,20},{8,24},{12,28},{16,0},{20,4},{24,8},{28,12},{1,17},{... | collective-permute-start | bytes 1179656 | tf_op jit(solution)/shard_map/ppermute | solution.py:119
  139.7 18.2 %collective-permute-start.25 = (f32[2,64,1536]{2,1,0:T(8,128)S(1)}, f32[2,64,1536]{2,1,0:T(8,128)S(1)}, u32[]{:S(2)}, u32[]{:S(2)}) collective-permute-start(f32[2,64,1536]{2,1,0:T(8,128)S(1)} %pad_maximum_fusion.9), channel_id=1, source_target_pairs={{0,8},{4,12},{8,0},{12,4},{16,24},{20,28},{24,16},{28,20},{1,9},{5... | collective-permute-start | bytes 2359304 | tf_op jit(solution)/shard_map/ppermute | solution.py:119
  141.9 17.5 %collective-permute-start.24 = (f32[2,64,1536]{2,1,0:T(8,128)S(1)}, f32[2,64,1536]{2,1,0:T(8,128)S(1)}, u32[]{:S(2)}, u32[]{:S(2)}) collective-permute-start(f32[2,64,1536]{2,1,0:T(8,128)S(1)} %pad_maximum_fusion.8), channel_id=1, source_target_pairs={{0,16},{4,20},{8,24},{12,28},{16,0},{20,4},{24,8},{28,12},{1,17},{... | collective-permute-start | bytes 2359304 | tf_op jit(solution)/shard_map/ppermute | solution.py:119
  142.8 29.4 %collective-permute-start.26 = (f32[16,4,48,256]{3,2,1,0:T(8,128)S(1)}, f32[16,4,48,256]{3,2,1,0:T(8,128)}, u32[]{:S(2)}, u32[]{:S(2)}) collective-permute-start(f32[16,4,48,256]{3,2,1,0:T(8,128)S(1)} %copy-done), channel_id=1, source_target_pairs={{0,4},{4,0},{8,12},{12,8},{16,20},{20,16},{24,28},{28,24},{1,5},{5... | collective-permute-start | bytes 9437192 | tf_op jit(solution)/shard_map/ppermute | solution.py:119
  142.8 29.4 %collective-permute-start.27 = (f32[16,4,48,256]{3,2,1,0:T(8,128)}, f32[16,4,48,256]{3,2,1,0:T(8,128)}, u32[]{:S(2)}, u32[]{:S(2)}) collective-permute-start(f32[16,4,48,256]{3,2,1,0:T(8,128)} %jacobian.5.refs_1_), channel_id=1, source_target_pairs={{0,4},{4,0},{8,12},{12,8},{16,20},{20,16},{24,28},{28,24},{1,5},{5... | collective-permute-start | bytes 9437192 | tf_op jit(solution)/shard_map/ppermute | solution.py:119
  143.3 28.8 %collective-permute-start.28 = (f32[16,4,48,256]{3,2,1,0:T(8,128)}, f32[16,4,48,256]{3,2,1,0:T(8,128)}, u32[]{:S(2)}, u32[]{:S(2)}) collective-permute-start(f32[16,4,48,256]{3,2,1,0:T(8,128)} %jacobian.6.refs_2_), channel_id=1, source_target_pairs={{0,4},{4,0},{8,12},{12,8},{16,20},{20,16},{24,28},{28,24},{1,5},{5... | collective-permute-start | bytes 9437192 | tf_op jit(solution)/shard_map/ppermute | solution.py:119
  167.0 6.0 %collective-permute-start.29 = (f32[16,4,48,256]{3,2,1,0:T(8,128)}, f32[16,4,48,256]{3,2,1,0:T(8,128)}, u32[]{:S(2)}, u32[]{:S(2)}) collective-permute-start(f32[16,4,48,256]{3,2,1,0:T(8,128)} %jacobian.7.refs_3_), channel_id=1, source_target_pairs={{0,4},{4,0},{8,12},{12,8},{16,20},{20,16},{24,28},{28,24},{1,5},{5... | collective-permute-start | bytes 9437192 | tf_op jit(solution)/shard_map/ppermute | solution.py:119
  230.5 7.0 %collective-permute-start.31 = (f32[384,128]{1,0:T(8,128)S(1)}, f32[384,128]{1,0:T(8,128)S(1)}, u32[]{:S(2)}, u32[]{:S(2)}) collective-permute-start(f32[384,128]{1,0:T(8,128)S(1)} %slice.323), channel_id=1, source_target_pairs={{0,16},{4,20},{8,24},{12,28},{16,0},{20,4},{24,8},{28,12},{1,17},{... | collective-permute-start | bytes 589832 | tf_op jit(solution)/shard_map/ppermute | solution.py:119
  232.1 7.0 %collective-permute-start.30 = (f32[384,128]{1,0:T(8,128)S(1)}, f32[384,128]{1,0:T(8,128)S(1)}, u32[]{:S(2)}, u32[]{:S(2)}) collective-permute-start(f32[384,128]{1,0:T(8,128)S(1)} %slice.321), channel_id=1, source_target_pairs={{0,8},{4,12},{8,0},{12,4},{16,24},{20,28},{24,16},{28,20},{1,9},{5... | collective-permute-start | bytes 589832 | tf_op jit(solution)/shard_map/ppermute | solution.py:119
  240.2 16.6 %collective-permute-start.36 = (f32[384,384]{1,0:T(8,128)S(1)}, f32[384,384]{1,0:T(8,128)S(1)}, u32[]{:S(2)}, u32[]{:S(2)}) collective-permute-start(f32[384,384]{1,0:T(8,128)S(1)} %slice.282), channel_id=1, source_target_pairs={{0,16},{4,20},{8,24},{12,28},{16,0},{20,4},{24,8},{28,12},{1,17},{... | collective-permute-start | bytes 1769480 | tf_op jit(solution)/shard_map/ppermute | solution.py:119
  246.0 10.1 %collective-permute-start.34 = (f32[192,256]{1,0:T(8,128)S(1)}, f32[192,256]{1,0:T(8,128)S(1)}, u32[]{:S(2)}, u32[]{:S(2)}) collective-permute-start(f32[192,256]{1,0:T(8,128)S(1)} %pad_maximum_fusion.12), channel_id=1, source_target_pairs={{0,2},{1,3},{2,0},{3,1},{4,6},{5,7},{6,4},{7,5},{8,10},{9,11},{10,... | collective-permute-start | bytes 589832 | tf_op jit(solution)/shard_map/ppermute | solution.py:119
  249.0 12.9 %collective-permute-start.35 = (f32[384,384]{1,0:T(8,128)S(1)}, f32[384,384]{1,0:T(8,128)S(1)}, u32[]{:S(2)}, u32[]{:S(2)}) collective-permute-start(f32[384,384]{1,0:T(8,128)S(1)} %slice.280), channel_id=1, source_target_pairs={{0,8},{4,12},{8,0},{12,4},{16,24},{20,28},{24,16},{28,20},{1,9},{5... | collective-permute-start | bytes 1769480 | tf_op jit(solution)/shard_map/ppermute | solution.py:119
  262.7 13.6 %collective-permute-start.45 = (f32[192,384]{1,0:T(8,128)}, f32[192,384]{1,0:T(8,128)}, u32[]{:S(2)}, u32[]{:S(2)}) collective-permute-start(f32[192,384]{1,0:T(8,128)} %slice.286), channel_id=1, source_target_pairs={{0,8},{4,12},{8,0},{12,4},{16,24},{20,28},{24,16},{28,20},{1,9},{5... | collective-permute-start | bytes 884744 | tf_op jit(solution)/shard_map/ppermute | solution.py:119
  266.1 13.2 %collective-permute-start.44 = (f32[192,384]{1,0:T(8,128)}, f32[192,384]{1,0:T(8,128)}, u32[]{:S(2)}, u32[]{:S(2)}) collective-permute-start(f32[192,384]{1,0:T(8,128)} %slice.284), channel_id=1, source_target_pairs={{0,16},{4,20},{8,24},{12,28},{16,0},{20,4},{24,8},{28,12},{1,17},{... | collective-permute-start | bytes 884744 | tf_op jit(solution)/shard_map/ppermute | solution.py:119
  270.5 10.2 %collective-permute-start.38 = (f32[192,256]{1,0:T(8,128)S(1)}, f32[192,256]{1,0:T(8,128)S(1)}, u32[]{:S(2)}, u32[]{:S(2)}) collective-permute-start(f32[192,256]{1,0:T(8,128)S(1)} %add.302), channel_id=1, source_target_pairs={{0,8},{4,12},{1,9},{5,13},{2,10},{6,14},{3,11},{7,15}} | collective-permute-start | bytes 589832 | tf_op jit(solution)/shard_map/ppermute | solution.py:508
  273.7 10.2 %collective-permute-start.39 = (f32[192,256]{1,0:T(8,128)S(1)}, f32[192,256]{1,0:T(8,128)S(1)}, u32[]{:S(2)}, u32[]{:S(2)}) collective-permute-start(f32[192,256]{1,0:T(8,128)S(1)} %add.302), channel_id=1, source_target_pairs={{0,16},{4,20},{1,17},{5,21},{2,18},{6,22},{3,19},{7,23}} | collective-permute-start | bytes 589832 | tf_op jit(solution)/shard_map/ppermute | solution.py:508
  275.0 8.9 %collective-permute-start.40 = (f32[192,256]{1,0:T(8,128)S(1)}, f32[192,256]{1,0:T(8,128)S(1)}, u32[]{:S(2)}, u32[]{:S(2)}) collective-permute-start(f32[192,256]{1,0:T(8,128)S(1)} %add.302), channel_id=1, source_target_pairs={{0,24},{4,28},{1,25},{5,29},{2,26},{6,30},{3,27},{7,31}} | collective-permute-start | bytes 589832 | tf_op jit(solution)/shard_map/ppermute | solution.py:508
  276.3 8.0 %collective-permute-start.41 = (f32[192,256]{1,0:T(8,128)S(1)}, f32[192,256]{1,0:T(8,128)S(1)}, u32[]{:S(2)}, u32[]{:S(2)}) collective-permute-start(f32[192,256]{1,0:T(8,128)S(1)} %add.302), channel_id=1, source_target_pairs={{0,8},{4,12},{9,1},{13,5},{18,26},{22,30},{27,19},{31,23}} | collective-permute-start | bytes 589832 | tf_op jit(solution)/shard_map/ppermute | solution.py:508
  286.6 38.6 %collective-permute-start.52 = (f32[192,384]{1,0:T(8,128)}, f32[192,384]{1,0:T(8,128)}, u32[]{:S(2)}, u32[]{:S(2)}) collective-permute-start(f32[192,384]{1,0:T(8,128)} %slice_add_fusion.4), channel_id=1, source_target_pairs={{0,2},{1,3},{2,0},{3,1},{4,6},{5,7},{6,4},{7,5},{8,10},{9,11},{10,... | collective-permute-start | bytes 884744 | tf_op jit(solution)/shard_map/ppermute | solution.py:119
  289.2 18.6 %collective-permute-start.48 = (f32[384,384]{1,0:T(8,128)}, f32[384,384]{1,0:T(8,128)}, u32[]{:S(2)}, u32[]{:S(2)}) collective-permute-start(f32[384,384]{1,0:T(8,128)} %slice.293), channel_id=1, source_target_pairs={{0,16},{4,20},{8,24},{12,28},{16,0},{20,4},{24,8},{28,12},{1,17},{... | collective-permute-start | bytes 1769480 | tf_op jit(solution)/shard_map/ppermute | solution.py:119
  290.0 18.9 %collective-permute-start.47 = (f32[384,384]{1,0:T(8,128)}, f32[384,384]{1,0:T(8,128)}, u32[]{:S(2)}, u32[]{:S(2)}) collective-permute-start(f32[384,384]{1,0:T(8,128)} %slice.291), channel_id=1, source_target_pairs={{0,8},{4,12},{8,0},{12,4},{16,24},{20,28},{24,16},{28,20},{1,9},{5... | collective-permute-start | bytes 1769480 | tf_op jit(solution)/shard_map/ppermute | solution.py:119
  310.2 15.0 %collective-permute-start.51 = (f32[192,384]{1,0:T(8,128)S(1)}, f32[192,384]{1,0:T(8,128)}, u32[]{:S(2)}, u32[]{:S(2)}) collective-permute-start(f32[192,384]{1,0:T(8,128)S(1)} %slice.297), channel_id=1, source_target_pairs={{0,8},{4,12},{8,0},{12,4},{16,24},{20,28},{24,16},{28,20},{1,9},{5... | collective-permute-start | bytes 884744 | tf_op jit(solution)/shard_map/ppermute | solution.py:119
  310.6 17.7 %collective-permute-start.50 = (f32[192,384]{1,0:T(8,128)S(1)}, f32[192,384]{1,0:T(8,128)S(1)}, u32[]{:S(2)}, u32[]{:S(2)}) collective-permute-start(f32[192,384]{1,0:T(8,128)S(1)} %copy-done.29), channel_id=1, source_target_pairs={{0,2},{1,3},{2,0},{3,1},{4,6},{5,7},{6,4},{7,5},{8,10},{9,11},{10,... | collective-permute-start | bytes 884744 | tf_op jit(solution)/shard_map/ppermute | solution.py:119
  312.0 16.4 %collective-permute-start.49 = (f32[192,384]{1,0:T(8,128)S(1)}, f32[192,384]{1,0:T(8,128)S(1)}, u32[]{:S(2)}, u32[]{:S(2)}) collective-permute-start(f32[192,384]{1,0:T(8,128)S(1)} %slice.295), channel_id=1, source_target_pairs={{0,16},{4,20},{8,24},{12,28},{16,0},{20,4},{24,8},{28,12},{1,17},{... | collective-permute-start | bytes 884744 | tf_op jit(solution)/shard_map/ppermute | solution.py:119
  326.3 8.2 %collective-permute-start.53 = (f32[192,384]{1,0:T(8,128)S(1)}, f32[192,384]{1,0:T(8,128)S(1)}, u32[]{:S(2)}, u32[]{:S(2)}) collective-permute-start(f32[192,384]{1,0:T(8,128)S(1)} %add_add_fusion), channel_id=1, source_target_pairs={{0,1},{1,0},{2,3},{3,2},{4,5},{5,4},{6,7},{7,6},{8,9},{9,8},{10,11... | collective-permute-start | bytes 884744 | tf_op jit(solution)/shard_map/ppermute | solution.py:119
  (41 other events, 275.4 us)

commit v6 on v5

--- a/solution.py
+++ b/solution.py
@@ -203,15 +203,18 @@
     row = lax.broadcasted_iota(jnp.int32, (together, LANES), 0)
     mine = (lane >= row * slots) & (lane < row * slots + slots)
     for n in range(count):
-        left = lefts[n][...]
-        right = rights[n][...].astype(jnp.bfloat16)
-        spread = jnp.where(mine[None], left[:, None, :], 0.0).reshape(ib * together, LANES)
-        block = lax.dot_general(
-            spread.astype(jnp.bfloat16), right, CONTRACT_LAST, preferred_element_type=jnp.float32
-        )
-        block = block.reshape(parts, ib // parts, together, jb)
-        for b in range(parts):
-            out_ref[:, n, :, b * jb : (b + 1) * jb] = block[b] * scale_ref[:, b * jb : (b + 1) * jb][:, None, :]
+        for g in range(lefts[n].shape[1] // LANES):
+            left = lefts[n][:, g * LANES : (g + 1) * LANES]
+            right = rights[n][:, g * LANES : (g + 1) * LANES].astype(jnp.bfloat16)
+            spread = jnp.where(mine[None], left[:, None, :], 0.0).reshape(ib * together, LANES)
+            block = lax.dot_general(
+                spread.astype(jnp.bfloat16), right, CONTRACT_LAST, preferred_element_type=jnp.float32
+            )
+            block = block.reshape(parts, ib // parts, together, jb)
+            for b in range(parts):
+                out_ref[:, n, g * together : (g + 1) * together, b * jb : (b + 1) * jb] = (
+                    block[b] * scale_ref[:, b * jb : (b + 1) * jb][:, None, :]
+                )
 
 
 def jacobian(lefts, rights, scaling, slots):
@@ -220,14 +223,15 @@
     jb = rights[0].shape[0]
     tiles = ib * jb // LANES
     together = LANES // slots
+    chunk = LANES * math.gcd(lanes // LANES, 3)
     return pl.pallas_call(
         functools.partial(jacobian_kernel, slots, count),
         out_shape=jax.ShapeDtypeStruct((tiles, count, lanes // slots, LANES), jnp.float32),
-        grid=(lanes // LANES,),
-        in_specs=[pl.BlockSpec((ib, LANES), lambda g: (0, g))] * count
-        + [pl.BlockSpec((jb, LANES), lambda g: (0, g))] * count
+        grid=(lanes // chunk,),
+        in_specs=[pl.BlockSpec((ib, chunk), lambda g: (0, g))] * count
+        + [pl.BlockSpec((jb, chunk), lambda g: (0, g))] * count
         + [pl.BlockSpec((tiles, LANES), lambda g: (0, 0))],
-        out_specs=pl.BlockSpec((tiles, count, together, LANES), lambda g: (0, 0, g, 0)),
+        out_specs=pl.BlockSpec((tiles, count, chunk // slots, LANES), lambda g: (0, 0, g, 0)),
         compiler_params=pltpu.CompilerParams(vmem_limit_bytes=VMEM_LIMIT),
         name="jacobian",
     )(*lefts, *rights, scaling)
@@ -493,22 +497,19 @@
         bit //= 2
 
     chips = walk_size // 2
-    per_col = col_block // row_block
-    top_count = -(-PB // row_block)
-
-    def spread(holder):
-        total = jnp.where(chip == jnp.asarray([holder(z) for z in range(par_size)])[par_index], rows_mine, 0.0)
-        for flip in range(1, chips):
-            pairs = []
-            for z in range(par_size):
+    assert chips == par_size and col_block == 2 * row_block and row_block < PB <= 2 * row_block
+    landed = [rows_mine]
+    for flip in range(1, chips):
+        pairs = []
+        for z in range(par_size):
+            for holder in sorted({0, z}):
                 for c in range(2):
-                    pairs.append(
-                        ((holder(z) * 2 + c) * par_size + z, ((holder(z) ^ flip) * 2 + c) * par_size + z)
-                    )
-            total = total + lax.ppermute(rows_mine, ("walk", "par"), pairs)
-        return total
-
-    both = jnp.stack([spread(lambda z: 0), spread(lambda z: z)])
+                    pairs.append(((holder * 2 + c) * par_size + z, ((holder ^ flip) * 2 + c) * par_size + z))
+        landed.append(lax.ppermute(rows_mine, ("walk", "par"), pairs))
+    landed = jnp.stack(landed)
+    both = jnp.stack(
+        [lax.dynamic_index_in_dim(landed, n, 0, keepdims=False) for n in (chip, chip ^ par_index)]
+    )
     far = plane_add(far, far_moved)
     both, far[0], far[1] = after([both, *far])
     far = [permute(part, "par", par_size, par_size // 2) for part in far]

time: 338 us -> 329 us (0.973)
  Pallas kernels: 110 us -> 103 us
    pallas_call x4, Pallas kernels: 26.2 us -> 19.5 us  [jacobian(): pl.pallas_call(functools.partial(jacobian_kernel, slots, count), out_shap...]
    ppermute x6 -> x3, starting transfers between devices: 9.93 us -> 5.8 us  [on_device(): landed.append(lax.ppermute(rows_mine, ('walk', 'par'), pairs))]
    ppermute x48, waiting for transfers between devices: 102 us -> 106 us  [permute(): return lax.ppermute(value, axis, xor_pairs(size, bit))]
  transfers between devices with their start and end apart: 54 -> 51, of which waited for: 29 -> 28; matrix products, arithmetic and copies ran while one was open for 10% -> 10% of each run, Pallas kernels for 15% -> 14%
where the time goes in v6:
time: 329 us; the launch traced here: 328 us
  waiting for transfers between devices  106 us (32%)
  Pallas kernels  103 us (31%)
  starting transfers between devices  72.8 us (22%)
  other arithmetic  22.1 us (7%)
  local copies, waits for them, and re-layouts  21.9 us (7%)
    ppermute x48, waiting for transfers between devices, permute(): return lax.ppermute(value, axis, xor_pairs(size, bit))  106 us
    ppermute x48, starting transfers between devices, permute(): return lax.ppermute(value, axis, xor_pairs(size, bit))  67 us
    pallas_call x1, Pallas kernels, gram_rows(): pl.pallas_call(functools.partial(centre_kernel, row_block, col_block, ord...  54.4 us
    pallas_call x4, Pallas kernels, jacobian(): pl.pallas_call(functools.partial(jacobian_kernel, slots, count), out_shap...  19.5 us
    pallas_call x1, Pallas kernels, head_top(): pl.pallas_call(top_kernel, out_shape=[jax.ShapeDtypeStruct((half, half),...  12.9 us
    pallas_call x1, Pallas kernels, head_low(): pl.pallas_call(low_kernel, out_shape=jax.ShapeDtypeStruct((size, size), j...  12.5 us
    squeeze x10, local copies, waits for them, and re-layouts, exchange(): held[d] = moved[i]  9.13 us
  transfers between devices with their start and end apart: 51, of which 28 were waited for; matrix products, arithmetic and copies ran while one was open for 10% of the time, Pallas kernels for 14%

profile of v6, /device:TPU:0, one launch (start us, length us, event | category | flops | bytes accessed | tf_op | source)
XLA Modules:
  0.0 328.5 jit_solution(7388100904270855157)
XLA Ops:
  3.6 3.4 %turned_pieces.1 = (f32[64,1536]{1,0:T(8,128)}, f32[64,1536]{1,0:T(8,128)}, f32[64,1536]{1,0:T(8,128)}, f32[64,1536]{1,0:T(8,128)}, f32[64,1536]{1,0:T(8,128)}, ...) custom-call(s32[2]{0:T(128)} %pad_add_fusion.2.own, f32[1,1536]{1,0:T(1,128)} %reshape.115.live_ref, ...), custom_call_target="tpu_custom_call" | custom-call | tf_op jit(solution)/shard_map/turned_pieces/pallas_call | solution.py:185
  8.2 3.0 collective-permute-start.3
  12.8 2.6 collective-permute-start
  15.4 1.6 collective-permute-start.1
  17.0 11.8 %collective-permute-done.3 = f32[2,64,1536]{2,1,0:T(8,128)S(1)} collective-permute-done((f32[2,64,1536]{2,1,0:T(8,128)S(1)}, f32[2,64,1536]{2,1,0:T(8,128)S(1)}, u32[]{:S(2)}, u32[]{:S(2)}) %collective-permute-start.3) | collective-permute-done | bytes 786464 | tf_op jit(solution)/shard_map/ppermute | solution.py:119
  34.4 2.2 collective-permute-start.4
  36.6 1.6 collective-permute-start.5
  38.2 12.8 %collective-permute-done.7 = f32[2,64,1536]{2,1,0:T(8,128)S(1)} collective-permute-done((f32[2,64,1536]{2,1,0:T(8,128)S(1)}, f32[2,64,1536]{2,1,0:T(8,128)S(1)}, u32[]{:S(2)}, u32[]{:S(2)}) %collective-permute-start.7) | collective-permute-done | bytes 786464 | tf_op jit(solution)/shard_map/ppermute | solution.py:119
  60.0 2.3 collective-permute-start.8
  62.2 1.8 collective-permute-start.9
  64.0 4.9 %jacobian.4.refs_0_ = f32[16,4,48,256]{3,2,1,0:T(8,128)} custom-call(f32[64,1536]{1,0:T(8,128)} %get-tuple-element.110.refs_0_, f32[64,1536]{1,0:T(8,128)} %copy-done.4, f32[64,1536]{1,0:T(8,128)} %get-tuple-element.104.refs_2_, f32[64,1536]{1,0:T(8,128)} %get-tuple-element.105.refs_3_, f32[64,1536]{1,0:T(8,128)} %get-tuple-element.109.refs_4_, ...), custom_call_target="tpu_custom_call" | custom-call | tf_op jit(solution)/shard_map/jacobian/pallas_call | solution.py:227
  68.9 3.0 collective-permute-done.11
  73.8 4.2 %collective-permute-done.8 = f32[64,1536]{1,0:T(8,128)S(1)} collective-permute-done((f32[64,1536]{1,0:T(8,128)}, f32[64,1536]{1,0:T(8,128)S(1)}, u32[]{:S(2)}, u32[]{:S(2)}) %collective-permute-start.8) | collective-permute-done | bytes 393248 | tf_op jit(solution)/shard_map/ppermute | solution.py:119
  78.2 1.9 collective-permute-start.12
  80.1 1.8 collective-permute-start.13
  84.5 12.4 %collective-permute-done.12.refs_4_ = f32[64,1536]{1,0:T(8,128)S(1)} collective-permute-done((f32[64,1536]{1,0:T(8,128)S(1)}, f32[64,1536]{1,0:T(8,128)S(1)}, u32[]{:S(2)}, u32[]{:S(2)}) %collective-permute-start.12) | collective-permute-done | bytes 393248 | tf_op jit(solution)/shard_map/ppermute | solution.py:119
  99.0 2.5 collective-permute-start.16
  101.6 1.8 collective-permute-start.17
  103.3 10.6 %collective-permute-done.19 = f32[2,64,1536]{2,1,0:T(8,128)S(1)} collective-permute-done((f32[2,64,1536]{2,1,0:T(8,128)S(1)}, f32[2,64,1536]{2,1,0:T(8,128)S(1)}, u32[]{:S(2)}, u32[]{:S(2)}) %collective-permute-start.19) | collective-permute-done | bytes 786464 | tf_op jit(solution)/shard_map/ppermute | solution.py:119
  115.9 1.8 collective-permute-done.16
  117.7 2.5 collective-permute-start.20
  120.2 1.7 collective-permute-start.21
  124.3 4.9 %jacobian.6.refs_2_ = f32[16,4,48,256]{3,2,1,0:T(8,128)} custom-call(f32[64,1536]{1,0:T(8,128)} %copy-done.19, f32[64,1536]{1,0:T(8,128)} %copy-done.21, f32[64,1536]{1,0:T(8,128)} %get-tuple-element.127.refs_2_, f32[64,1536]{1,0:T(8,128)} %get-tuple-element.128.refs_3_, f32[64,1536]{1,0:T(8,128)} %copy-done.13, f32[64,1536]{1,0:T(8,128)} %get-tuple-element.129.refs_5_, ...), custom_call_target="tpu_custom_call" | custom-call | tf_op jit(solution)/shard_map/jacobian/pallas_call | solution.py:227
  129.2 4.9 %jacobian.5.refs_1_ = f32[16,4,48,256]{3,2,1,0:T(8,128)} custom-call(f32[64,1536]{1,0:T(8,128)} %copy-done.12, f32[64,1536]{1,0:T(8,128)} %copy-done.2, f32[64,1536]{1,0:T(8,128)} %get-tuple-element.123.refs_2_, f32[64,1536]{1,0:T(8,128)} %get-tuple-element.124.refs_3_, f32[64,1536]{1,0:T(8,128)} %copy-done.17, f32[64,1536]{1,0:T(8,128)} %get-tuple-element.125.refs_5_, ...), custom_call_target="tpu_custom_call" | custom-call | tf_op jit(solution)/shard_map/jacobian/pallas_call | solution.py:227
  134.1 2.3 collective-permute-done.20.refs_4_
  138.6 2.1 collective-permute-start.25
  143.2 13.1 %collective-permute-done.25 = f32[2,64,1536]{2,1,0:T(8,128)S(1)} collective-permute-done((f32[2,64,1536]{2,1,0:T(8,128)S(1)}, f32[2,64,1536]{2,1,0:T(8,128)S(1)}, u32[]{:S(2)}, u32[]{:S(2)}) %collective-permute-start.25) | collective-permute-done | bytes 786464 | tf_op jit(solution)/shard_map/ppermute | solution.py:119
  157.2 1.7 collective-permute-done.24
  159.8 4.9 %jacobian.7.refs_3_ = f32[16,4,48,256]{3,2,1,0:T(8,128)} custom-call(f32[64,1536]{1,0:T(8,128)} %copy-done.22, f32[64,1536]{1,0:T(8,128)} %copy-done.23, f32[64,1536]{1,0:T(8,128)} %get-tuple-element.189.refs_2_, f32[64,1536]{1,0:T(8,128)} %get-tuple-element.188.refs_3_, f32[64,1536]{1,0:T(8,128)} %copy-done.20, f32[64,1536]{1,0:T(8,128)} %get-tuple-element.187.refs_5_, ...), custom_call_target="tpu_custom_call" | custom-call | tf_op jit(solution)/shard_map/jacobian/pallas_call | solution.py:227
  170.7 54.4 %gram_rows.1 = (f32[768,384]{1,0:T(8,128)}, f32[768,384]{1,0:T(8,128)}, f32[768,384]{1,0:T(8,128)}, f32[768,384]{1,0:T(8,128)}) custom-call(s32[4]{0:T(128)} %pad_add_fusion.row_at, s32[4]{0:T(128)} %pad_add_fusion.1.col_at, s32[32]{0:T(128)} %broadcast_multiply_fusion.place_at, f32[16,4,48,256]{3,2,1,0:T(8,128)} %jacobian.4.refs_0_, ...), custom_call_target="tpu_custom_call" | custom-call | tf_op jit(solution)/shard_map/gram_rows/pallas_call | solution.py:300
  230.1 5.0 %collective-permute-done.31 = f32[384,128]{1,0:T(8,128)S(1)} collective-permute-done((f32[384,128]{1,0:T(8,128)S(1)}, f32[384,128]{1,0:T(8,128)S(1)}, u32[]{:S(2)}, u32[]{:S(2)}) %collective-permute-start.31) | collective-permute-done | bytes 196640 | tf_op jit(solution)/shard_map/ppermute | solution.py:119
  235.1 1.6 collective-permute-done.30
  239.3 3.2 collective-permute-done.32
  243.7 3.4 %collective-permute-start.34 = (f32[192,256]{1,0:T(8,128)S(1)}, f32[192,256]{1,0:T(8,128)S(1)}, u32[]{:S(2)}, u32[]{:S(2)}) collective-permute-start(f32[192,256]{1,0:T(8,128)S(1)} %pad_maximum_fusion.13), channel_id=1, source_target_pairs={{0,2},{1,3},{2,0},{3,1},{4,6},{5,7},{6,4},{7,5},{8,10},{9,11},{10,... | collective-permute-start | bytes 589832 | tf_op jit(solution)/shard_map/ppermute | solution.py:119
  248.0 6.3 %collective-permute-done.34 = f32[192,256]{1,0:T(8,128)S(1)} collective-permute-done((f32[192,256]{1,0:T(8,128)S(1)}, f32[192,256]{1,0:T(8,128)S(1)}, u32[]{:S(2)}, u32[]{:S(2)}) %collective-permute-start.34) | collective-permute-done | bytes 196640 | tf_op jit(solution)/shard_map/ppermute | solution.py:119
  255.0 5.0 %collective-permute-done.35 = f32[384,384]{1,0:T(8,128)S(1)} collective-permute-done((f32[384,384]{1,0:T(8,128)S(1)}, f32[384,384]{1,0:T(8,128)S(1)}, u32[]{:S(2)}, u32[]{:S(2)}) %collective-permute-start.35) | collective-permute-done | bytes 589856 | tf_op jit(solution)/shard_map/ppermute | solution.py:119
  261.6 2.0 collective-permute-start.37
  265.6 1.9 collective-permute-done.37
  268.6 3.2 collective-permute-start.38
  274.5 1.7 slice_add_fusion.4
  276.2 1.7 slice_add_fusion.5
  278.1 2.0 collective-permute-start.49
  282.9 2.7 collective-permute-start.44
  286.4 12.9 %head_top.1 = (f32[128,128]{1,0:T(8,128)}, f32[128,128]{1,0:T(8,128)}, f32[128,128]{1,0:T(8,128)}) custom-call(f32[256,256]{1,0:T(8,128)} %fusion.7.a_ref), custom_call_target="tpu_custom_call" | custom-call | tf_op jit(solution)/shard_map/head_top/pallas_call | solution.py:376
  302.2 1.6 collective-permute-start.47
  304.9 12.5 %head_low.1 = f32[256,256]{1,0:T(8,128)} custom-call(f32[128,128]{1,0:T(8,128)} %get-tuple-element.157.top_ref, f32[128,128]{1,0:T(8,128)} %get-tuple-element.158.below_ref, f32[128,128]{1,0:T(8,128)} %get-tuple-element.159.rest_ref), custom_call_target="tpu_custom_call" | custom-call | tf_op jit(solution)/shard_map/head_low/pallas_call | solution.py:383
  318.6 3.2 collective-permute-start.50
  323.4 4.3 %collective-permute-done.50 = f32[192,384]{1,0:T(8,128)S(1)} collective-permute-done((f32[192,384]{1,0:T(8,128)S(1)}, f32[192,384]{1,0:T(8,128)S(1)}, u32[]{:S(2)}, u32[]{:S(2)}) %collective-permute-start.50) | collective-permute-done | bytes 294944 | tf_op jit(solution)/shard_map/ppermute | solution.py:119
  (214 shorter events, 72.7 us)
Async XLA Ops:
  8.2 20.6 %collective-permute-start.3 = (f32[2,64,1536]{2,1,0:T(8,128)S(1)}, f32[2,64,1536]{2,1,0:T(8,128)S(1)}, u32[]{:S(2)}, u32[]{:S(2)}) collective-permute-start(f32[2,64,1536]{2,1,0:T(8,128)S(1)} %pad_maximum_fusion.1), channel_id=1, source_target_pairs={{0,16},{4,20},{8,24},{12,28},{16,0},{20,4},{24,8},{28,12},{1,17},{... | collective-permute-start | bytes 2359304 | tf_op jit(solution)/shard_map/ppermute | solution.py:119
  11.3 19.1 %collective-permute-start.2 = (f32[2,64,1536]{2,1,0:T(8,128)S(1)}, f32[2,64,1536]{2,1,0:T(8,128)S(1)}, u32[]{:S(2)}, u32[]{:S(2)}) collective-permute-start(f32[2,64,1536]{2,1,0:T(8,128)S(1)} %pad_maximum_fusion), channel_id=1, source_target_pairs={{0,8},{4,12},{8,0},{12,4},{16,24},{20,28},{24,16},{28,20},{1,9},{5... | collective-permute-start | bytes 2359304 | tf_op jit(solution)/shard_map/ppermute | solution.py:119
  12.8 19.7 %collective-permute-start = (f32[64,1536]{1,0:T(8,128)S(1)}, f32[64,1536]{1,0:T(8,128)S(1)}, u32[]{:S(2)}, u32[]{:S(2)}) collective-permute-start(f32[64,1536]{1,0:T(8,128)S(1)} %copy-done.34), channel_id=1, source_target_pairs={{0,2},{1,3},{2,0},{3,1},{4,6},{5,7},{6,4},{7,5},{8,10},{9,11},{10,... | collective-permute-start | bytes 1179656 | tf_op jit(solution)/shard_map/ppermute | solution.py:119
  15.4 17.3 %collective-permute-start.1 = (f32[64,1536]{1,0:T(8,128)S(1)}, f32[64,1536]{1,0:T(8,128)S(1)}, u32[]{:S(2)}, u32[]{:S(2)}) collective-permute-start(f32[64,1536]{1,0:T(8,128)S(1)} %copy-done.33), channel_id=1, source_target_pairs={{0,1},{1,0},{2,3},{3,2},{4,5},{5,4},{6,7},{7,6},{8,9},{9,8},{10,11... | collective-permute-start | bytes 1179656 | tf_op jit(solution)/shard_map/ppermute | solution.py:119
  32.8 18.2 %collective-permute-start.7 = (f32[2,64,1536]{2,1,0:T(8,128)S(1)}, f32[2,64,1536]{2,1,0:T(8,128)S(1)}, u32[]{:S(2)}, u32[]{:S(2)}) collective-permute-start(f32[2,64,1536]{2,1,0:T(8,128)S(1)} %pad_maximum_fusion.3), channel_id=1, source_target_pairs={{0,16},{4,20},{8,24},{12,28},{16,0},{20,4},{24,8},{28,12},{1,17},{... | collective-permute-start | bytes 2359304 | tf_op jit(solution)/shard_map/ppermute | solution.py:119
  33.5 18.3 %collective-permute-start.6 = (f32[2,64,1536]{2,1,0:T(8,128)S(1)}, f32[2,64,1536]{2,1,0:T(8,128)S(1)}, u32[]{:S(2)}, u32[]{:S(2)}) collective-permute-start(f32[2,64,1536]{2,1,0:T(8,128)S(1)} %pad_maximum_fusion.2), channel_id=1, source_target_pairs={{0,8},{4,12},{8,0},{12,4},{16,24},{20,28},{24,16},{28,20},{1,9},{5... | collective-permute-start | bytes 2359304 | tf_op jit(solution)/shard_map/ppermute | solution.py:119
  34.4 18.6 %collective-permute-start.4 = (f32[64,1536]{1,0:T(8,128)S(1)}, f32[64,1536]{1,0:T(8,128)S(1)}, u32[]{:S(2)}, u32[]{:S(2)}) collective-permute-start(f32[64,1536]{1,0:T(8,128)S(1)} %copy-done.32), channel_id=1, source_target_pairs={{0,2},{1,3},{2,0},{3,1},{4,6},{5,7},{6,4},{7,5},{8,10},{9,11},{10,... | collective-permute-start | bytes 1179656 | tf_op jit(solution)/shard_map/ppermute | solution.py:119
  36.6 16.5 %collective-permute-start.5 = (f32[64,1536]{1,0:T(8,128)S(1)}, f32[64,1536]{1,0:T(8,128)S(1)}, u32[]{:S(2)}, u32[]{:S(2)}) collective-permute-start(f32[64,1536]{1,0:T(8,128)S(1)} %copy-done.31), channel_id=1, source_target_pairs={{0,1},{1,0},{2,3},{3,2},{4,5},{5,4},{6,7},{7,6},{8,9},{9,8},{10,11... | collective-permute-start | bytes 1179656 | tf_op jit(solution)/shard_map/ppermute | solution.py:119
  54.3 17.6 %collective-permute-start.11 = (f32[2,64,1536]{2,1,0:T(8,128)}, f32[2,64,1536]{2,1,0:T(8,128)S(1)}, u32[]{:S(2)}, u32[]{:S(2)}) collective-permute-start(f32[2,64,1536]{2,1,0:T(8,128)} %pad_maximum_fusion.5), channel_id=1, source_target_pairs={{0,16},{4,20},{8,24},{12,28},{16,0},{20,4},{24,8},{28,12},{1,17},{... | collective-permute-start | bytes 2359304 | tf_op jit(solution)/shard_map/ppermute | solution.py:119
  55.5 17.3 %collective-permute-start.10 = (f32[2,64,1536]{2,1,0:T(8,128)S(1)}, f32[2,64,1536]{2,1,0:T(8,128)S(1)}, u32[]{:S(2)}, u32[]{:S(2)}) collective-permute-start(f32[2,64,1536]{2,1,0:T(8,128)S(1)} %pad_maximum_fusion.4), channel_id=1, source_target_pairs={{0,8},{4,12},{8,0},{12,4},{16,24},{20,28},{24,16},{28,20},{1,9},{5... | collective-permute-start | bytes 2359304 | tf_op jit(solution)/shard_map/ppermute | solution.py:119
  60.0 18.0 %collective-permute-start.8 = (f32[64,1536]{1,0:T(8,128)}, f32[64,1536]{1,0:T(8,128)S(1)}, u32[]{:S(2)}, u32[]{:S(2)}) collective-permute-start(f32[64,1536]{1,0:T(8,128)} %get-tuple-element.98), channel_id=1, source_target_pairs={{0,2},{1,3},{2,0},{3,1},{4,6},{5,7},{6,4},{7,5},{8,10},{9,11},{10,... | collective-permute-start | bytes 1179656 | tf_op jit(solution)/shard_map/ppermute | solution.py:119
  62.2 15.9 %collective-permute-start.9 = (f32[64,1536]{1,0:T(8,128)}, f32[64,1536]{1,0:T(8,128)}, u32[]{:S(2)}, u32[]{:S(2)}) collective-permute-start(f32[64,1536]{1,0:T(8,128)} %get-tuple-element.99), channel_id=1, source_target_pairs={{0,1},{1,0},{2,3},{3,2},{4,5},{5,4},{6,7},{7,6},{8,9},{9,8},{10,11... | collective-permute-start | bytes 1179656 | tf_op jit(solution)/shard_map/ppermute | solution.py:119
  78.2 18.7 %collective-permute-start.12 = (f32[64,1536]{1,0:T(8,128)S(1)}, f32[64,1536]{1,0:T(8,128)S(1)}, u32[]{:S(2)}, u32[]{:S(2)}) collective-permute-start(f32[64,1536]{1,0:T(8,128)S(1)} %copy-done.16), channel_id=1, source_target_pairs={{0,2},{1,3},{2,0},{3,1},{4,6},{5,7},{6,4},{7,5},{8,10},{9,11},{10,... | collective-permute-start | bytes 1179656 | tf_op jit(solution)/shard_map/ppermute | solution.py:119
  80.1 16.8 %collective-permute-start.13 = (f32[64,1536]{1,0:T(8,128)S(1)}, f32[64,1536]{1,0:T(8,128)S(1)}, u32[]{:S(2)}, u32[]{:S(2)}) collective-permute-start(f32[64,1536]{1,0:T(8,128)S(1)} %copy-done.14), channel_id=1, source_target_pairs={{0,1},{1,0},{2,3},{3,2},{4,5},{5,4},{6,7},{7,6},{8,9},{9,8},{10,11... | collective-permute-start | bytes 1179656 | tf_op jit(solution)/shard_map/ppermute | solution.py:119
  82.0 15.0 %collective-permute-start.14 = (f32[64,1536]{1,0:T(8,128)}, f32[64,1536]{1,0:T(8,128)S(1)}, u32[]{:S(2)}, u32[]{:S(2)}) collective-permute-start(f32[64,1536]{1,0:T(8,128)} %collective-permute-done.9), channel_id=1, source_target_pairs={{0,8},{4,12},{8,0},{12,4},{16,24},{20,28},{24,16},{28,20},{1,9},{5... | collective-permute-start | bytes 1179656 | tf_op jit(solution)/shard_map/ppermute | solution.py:119
  83.2 13.8 %collective-permute-start.15 = (f32[64,1536]{1,0:T(8,128)S(1)}, f32[64,1536]{1,0:T(8,128)S(1)}, u32[]{:S(2)}, u32[]{:S(2)}) collective-permute-start(f32[64,1536]{1,0:T(8,128)S(1)} %collective-permute-done.8), channel_id=1, source_target_pairs={{0,16},{4,20},{8,24},{12,28},{16,0},{20,4},{24,8},{28,12},{1,17},{... | collective-permute-start | bytes 1179656 | tf_op jit(solution)/shard_map/ppermute | solution.py:119
  97.0 17.0 %collective-permute-start.19 = (f32[2,64,1536]{2,1,0:T(8,128)S(1)}, f32[2,64,1536]{2,1,0:T(8,128)S(1)}, u32[]{:S(2)}, u32[]{:S(2)}) collective-permute-start(f32[2,64,1536]{2,1,0:T(8,128)S(1)} %pad_maximum_fusion.7), channel_id=1, source_target_pairs={{0,16},{4,20},{8,24},{12,28},{16,0},{20,4},{24,8},{28,12},{1,17},{... | collective-permute-start | bytes 2359304 | tf_op jit(solution)/shard_map/ppermute | solution.py:119
  98.0 17.0 %collective-permute-start.18 = (f32[2,64,1536]{2,1,0:T(8,128)S(1)}, f32[2,64,1536]{2,1,0:T(8,128)S(1)}, u32[]{:S(2)}, u32[]{:S(2)}) collective-permute-start(f32[2,64,1536]{2,1,0:T(8,128)S(1)} %pad_maximum_fusion.6), channel_id=1, source_target_pairs={{0,8},{4,12},{8,0},{12,4},{16,24},{20,28},{24,16},{28,20},{1,9},{5... | collective-permute-start | bytes 2359304 | tf_op jit(solution)/shard_map/ppermute | solution.py:119
  99.0 18.7 %collective-permute-start.16 = (f32[64,1536]{1,0:T(8,128)S(1)}, f32[64,1536]{1,0:T(8,128)S(1)}, u32[]{:S(2)}, u32[]{:S(2)}) collective-permute-start(f32[64,1536]{1,0:T(8,128)S(1)} %copy-done.27), channel_id=1, source_target_pairs={{0,2},{1,3},{2,0},{3,1},{4,6},{5,7},{6,4},{7,5},{8,10},{9,11},{10,... | collective-permute-start | bytes 1179656 | tf_op jit(solution)/shard_map/ppermute | solution.py:119
  101.6 16.2 %collective-permute-start.17 = (f32[64,1536]{1,0:T(8,128)S(1)}, f32[64,1536]{1,0:T(8,128)S(1)}, u32[]{:S(2)}, u32[]{:S(2)}) collective-permute-start(f32[64,1536]{1,0:T(8,128)S(1)} %collective-permute-done), channel_id=1, source_target_pairs={{0,1},{1,0},{2,3},{3,2},{4,5},{5,4},{6,7},{7,6},{8,9},{9,8},{10,11... | collective-permute-start | bytes 1179656 | tf_op jit(solution)/shard_map/ppermute | solution.py:119
  117.7 18.6 %collective-permute-start.20 = (f32[64,1536]{1,0:T(8,128)S(1)}, f32[64,1536]{1,0:T(8,128)S(1)}, u32[]{:S(2)}, u32[]{:S(2)}) collective-permute-start(f32[64,1536]{1,0:T(8,128)S(1)} %collective-permute-done.5.refs_4_), channel_id=1, source_target_pairs={{0,2},{1,3},{2,0},{3,1},{4,6},{5,7},{6,4},{7,5},{8,10},{9,11},{10,... | collective-permute-start | bytes 1179656 | tf_op jit(solution)/shard_map/ppermute | solution.py:119
  120.2 16.2 %collective-permute-start.21 = (f32[64,1536]{1,0:T(8,128)S(1)}, f32[64,1536]{1,0:T(8,128)S(1)}, u32[]{:S(2)}, u32[]{:S(2)}) collective-permute-start(f32[64,1536]{1,0:T(8,128)S(1)} %collective-permute-done.4.refs_0_), channel_id=1, source_target_pairs={{0,1},{1,0},{2,3},{3,2},{4,5},{5,4},{6,7},{7,6},{8,9},{9,8},{10,11... | collective-permute-start | bytes 1179656 | tf_op jit(solution)/shard_map/ppermute | solution.py:119
  121.9 14.5 %collective-permute-start.22 = (f32[64,1536]{1,0:T(8,128)S(1)}, f32[64,1536]{1,0:T(8,128)S(1)}, u32[]{:S(2)}, u32[]{:S(2)}) collective-permute-start(f32[64,1536]{1,0:T(8,128)S(1)} %collective-permute-done.17), channel_id=1, source_target_pairs={{0,8},{4,12},{8,0},{12,4},{16,24},{20,28},{24,16},{28,20},{1,9},{5... | collective-permute-start | bytes 1179656 | tf_op jit(solution)/shard_map/ppermute | solution.py:119
  123.2 13.2 %collective-permute-start.23 = (f32[64,1536]{1,0:T(8,128)S(1)}, f32[64,1536]{1,0:T(8,128)S(1)}, u32[]{:S(2)}, u32[]{:S(2)}) collective-permute-start(f32[64,1536]{1,0:T(8,128)S(1)} %collective-permute-done.16), channel_id=1, source_target_pairs={{0,16},{4,20},{8,24},{12,28},{16,0},{20,4},{24,8},{28,12},{1,17},{... | collective-permute-start | bytes 1179656 | tf_op jit(solution)/shard_map/ppermute | solution.py:119
  138.6 17.6 %collective-permute-start.25 = (f32[2,64,1536]{2,1,0:T(8,128)S(1)}, f32[2,64,1536]{2,1,0:T(8,128)S(1)}, u32[]{:S(2)}, u32[]{:S(2)}) collective-permute-start(f32[2,64,1536]{2,1,0:T(8,128)S(1)} %pad_maximum_fusion.9), channel_id=1, source_target_pairs={{0,8},{4,12},{8,0},{12,4},{16,24},{20,28},{24,16},{28,20},{1,9},{5... | collective-permute-start | bytes 2359304 | tf_op jit(solution)/shard_map/ppermute | solution.py:119
  141.8 17.1 %collective-permute-start.24 = (f32[2,64,1536]{2,1,0:T(8,128)S(1)}, f32[2,64,1536]{2,1,0:T(8,128)S(1)}, u32[]{:S(2)}, u32[]{:S(2)}) collective-permute-start(f32[2,64,1536]{2,1,0:T(8,128)S(1)} %pad_maximum_fusion.8), channel_id=1, source_target_pairs={{0,16},{4,20},{8,24},{12,28},{16,0},{20,4},{24,8},{28,12},{1,17},{... | collective-permute-start | bytes 2359304 | tf_op jit(solution)/shard_map/ppermute | solution.py:119
  142.7 27.1 %collective-permute-start.26 = (f32[16,4,48,256]{3,2,1,0:T(8,128)S(1)}, f32[16,4,48,256]{3,2,1,0:T(8,128)}, u32[]{:S(2)}, u32[]{:S(2)}) collective-permute-start(f32[16,4,48,256]{3,2,1,0:T(8,128)S(1)} %copy-done), channel_id=1, source_target_pairs={{0,4},{4,0},{8,12},{12,8},{16,20},{20,16},{24,28},{28,24},{1,5},{5... | collective-permute-start | bytes 9437192 | tf_op jit(solution)/shard_map/ppermute | solution.py:119
  142.7 27.1 %collective-permute-start.27 = (f32[16,4,48,256]{3,2,1,0:T(8,128)}, f32[16,4,48,256]{3,2,1,0:T(8,128)}, u32[]{:S(2)}, u32[]{:S(2)}) collective-permute-start(f32[16,4,48,256]{3,2,1,0:T(8,128)} %jacobian.5.refs_1_), channel_id=1, source_target_pairs={{0,4},{4,0},{8,12},{12,8},{16,20},{20,16},{24,28},{28,24},{1,5},{5... | collective-permute-start | bytes 9437192 | tf_op jit(solution)/shard_map/ppermute | solution.py:119
  143.2 26.6 %collective-permute-start.28 = (f32[16,4,48,256]{3,2,1,0:T(8,128)}, f32[16,4,48,256]{3,2,1,0:T(8,128)}, u32[]{:S(2)}, u32[]{:S(2)}) collective-permute-start(f32[16,4,48,256]{3,2,1,0:T(8,128)} %jacobian.6.refs_2_), channel_id=1, source_target_pairs={{0,4},{4,0},{8,12},{12,8},{16,20},{20,16},{24,28},{28,24},{1,5},{5... | collective-permute-start | bytes 9437192 | tf_op jit(solution)/shard_map/ppermute | solution.py:119
  164.7 6.0 %collective-permute-start.29 = (f32[16,4,48,256]{3,2,1,0:T(8,128)}, f32[16,4,48,256]{3,2,1,0:T(8,128)}, u32[]{:S(2)}, u32[]{:S(2)}) collective-permute-start(f32[16,4,48,256]{3,2,1,0:T(8,128)} %jacobian.7.refs_3_), channel_id=1, source_target_pairs={{0,4},{4,0},{8,12},{12,8},{16,20},{20,16},{24,28},{28,24},{1,5},{5... | collective-permute-start | bytes 9437192 | tf_op jit(solution)/shard_map/ppermute | solution.py:119
  228.1 7.0 %collective-permute-start.31 = (f32[384,128]{1,0:T(8,128)S(1)}, f32[384,128]{1,0:T(8,128)S(1)}, u32[]{:S(2)}, u32[]{:S(2)}) collective-permute-start(f32[384,128]{1,0:T(8,128)S(1)} %slice.323), channel_id=1, source_target_pairs={{0,16},{4,20},{8,24},{12,28},{16,0},{20,4},{24,8},{28,12},{1,17},{... | collective-permute-start | bytes 589832 | tf_op jit(solution)/shard_map/ppermute | solution.py:119
  229.7 7.0 %collective-permute-start.30 = (f32[384,128]{1,0:T(8,128)S(1)}, f32[384,128]{1,0:T(8,128)S(1)}, u32[]{:S(2)}, u32[]{:S(2)}) collective-permute-start(f32[384,128]{1,0:T(8,128)S(1)} %slice.321), channel_id=1, source_target_pairs={{0,8},{4,12},{8,0},{12,4},{16,24},{20,28},{24,16},{28,20},{1,9},{5... | collective-permute-start | bytes 589832 | tf_op jit(solution)/shard_map/ppermute | solution.py:119
  236.8 5.8 %collective-permute-start.32 = (f32[192,128]{1,0:T(8,128)S(1)}, f32[192,128]{1,0:T(8,128)S(1)}, u32[]{:S(2)}, u32[]{:S(2)}) collective-permute-start(f32[192,128]{1,0:T(8,128)S(1)} %slice.276), channel_id=1, source_target_pairs={{0,16},{4,20},{8,24},{12,28},{16,0},{20,4},{24,8},{28,12},{1,17},{... | collective-permute-start | bytes 294920 | tf_op jit(solution)/shard_map/ppermute | solution.py:119
  237.5 17.5 %collective-permute-start.36 = (f32[384,384]{1,0:T(8,128)S(1)}, f32[384,384]{1,0:T(8,128)S(1)}, u32[]{:S(2)}, u32[]{:S(2)}) collective-permute-start(f32[384,384]{1,0:T(8,128)S(1)} %slice.282), channel_id=1, source_target_pairs={{0,16},{4,20},{8,24},{12,28},{16,0},{20,4},{24,8},{28,12},{1,17},{... | collective-permute-start | bytes 1769480 | tf_op jit(solution)/shard_map/ppermute | solution.py:119
  243.7 10.6 %collective-permute-start.34 = (f32[192,256]{1,0:T(8,128)S(1)}, f32[192,256]{1,0:T(8,128)S(1)}, u32[]{:S(2)}, u32[]{:S(2)}) collective-permute-start(f32[192,256]{1,0:T(8,128)S(1)} %pad_maximum_fusion.13), channel_id=1, source_target_pairs={{0,2},{1,3},{2,0},{3,1},{4,6},{5,7},{6,4},{7,5},{8,10},{9,11},{10,... | collective-permute-start | bytes 589832 | tf_op jit(solution)/shard_map/ppermute | solution.py:119
  247.1 12.9 %collective-permute-start.35 = (f32[384,384]{1,0:T(8,128)S(1)}, f32[384,384]{1,0:T(8,128)S(1)}, u32[]{:S(2)}, u32[]{:S(2)}) collective-permute-start(f32[384,384]{1,0:T(8,128)S(1)} %slice.280), channel_id=1, source_target_pairs={{0,8},{4,12},{8,0},{12,4},{16,24},{20,28},{24,16},{28,20},{1,9},{5... | collective-permute-start | bytes 1769480 | tf_op jit(solution)/shard_map/ppermute | solution.py:119
  260.8 13.6 %collective-permute-start.42 = (f32[192,384]{1,0:T(8,128)}, f32[192,384]{1,0:T(8,128)}, u32[]{:S(2)}, u32[]{:S(2)}) collective-permute-start(f32[192,384]{1,0:T(8,128)} %slice.286), channel_id=1, source_target_pairs={{0,8},{4,12},{8,0},{12,4},{16,24},{20,28},{24,16},{28,20},{1,9},{5... | collective-permute-start | bytes 884744 | tf_op jit(solution)/shard_map/ppermute | solution.py:119
  261.6 6.0 %collective-permute-start.37 = (f32[192,256]{1,0:T(8,128)}, f32[192,256]{1,0:T(8,128)}, u32[]{:S(2)}, u32[]{:S(2)}) collective-permute-start(f32[192,256]{1,0:T(8,128)} %fusion.23), channel_id=1, source_target_pairs={{0,1},{1,0},{2,3},{3,2},{4,5},{5,4},{6,7},{7,6},{8,9},{9,8},{10,11... | collective-permute-start | bytes 589832 | tf_op jit(solution)/shard_map/ppermute | solution.py:119
  264.3 11.8 %collective-permute-start.41 = (f32[192,384]{1,0:T(8,128)}, f32[192,384]{1,0:T(8,128)}, u32[]{:S(2)}, u32[]{:S(2)}) collective-permute-start(f32[192,384]{1,0:T(8,128)} %slice.284), channel_id=1, source_target_pairs={{0,16},{4,20},{8,24},{12,28},{16,0},{20,4},{24,8},{28,12},{1,17},{... | collective-permute-start | bytes 884744 | tf_op jit(solution)/shard_map/ppermute | solution.py:119
  268.6 9.2 %collective-permute-start.38 = (f32[192,256]{1,0:T(8,128)S(1)}, f32[192,256]{1,0:T(8,128)S(1)}, u32[]{:S(2)}, u32[]{:S(2)}) collective-permute-start(f32[192,256]{1,0:T(8,128)S(1)} %add.287), channel_id=1, source_target_pairs={{0,8},{4,12},{1,9},{5,13},{9,1},{13,5},{2,10},{6,14},{18,26},{22,3... | collective-permute-start | bytes 589832 | tf_op jit(solution)/shard_map/ppermute | solution.py:508
  271.8 6.0 %collective-permute-start.39 = (f32[192,256]{1,0:T(8,128)S(1)}, f32[192,256]{1,0:T(8,128)S(1)}, u32[]{:S(2)}, u32[]{:S(2)}) collective-permute-start(f32[192,256]{1,0:T(8,128)S(1)} %add.287), channel_id=1, source_target_pairs={{0,16},{4,20},{1,17},{5,21},{9,25},{13,29},{2,18},{6,22},{18,2},{2... | collective-permute-start | bytes 589832 | tf_op jit(solution)/shard_map/ppermute | solution.py:508
  278.1 39.3 %collective-permute-start.49 = (f32[192,384]{1,0:T(8,128)}, f32[192,384]{1,0:T(8,128)}, u32[]{:S(2)}, u32[]{:S(2)}) collective-permute-start(f32[192,384]{1,0:T(8,128)} %slice_add_fusion.4), channel_id=1, source_target_pairs={{0,2},{1,3},{2,0},{3,1},{4,6},{5,7},{6,4},{7,5},{8,10},{9,11},{10,... | collective-permute-start | bytes 884744 | tf_op jit(solution)/shard_map/ppermute | solution.py:119
  281.0 18.3 %collective-permute-start.45 = (f32[384,384]{1,0:T(8,128)}, f32[384,384]{1,0:T(8,128)}, u32[]{:S(2)}, u32[]{:S(2)}) collective-permute-start(f32[384,384]{1,0:T(8,128)} %slice.293), channel_id=1, source_target_pairs={{0,16},{4,20},{8,24},{12,28},{16,0},{20,4},{24,8},{28,12},{1,17},{... | collective-permute-start | bytes 1769480 | tf_op jit(solution)/shard_map/ppermute | solution.py:119
  282.9 17.6 %collective-permute-start.44 = (f32[384,384]{1,0:T(8,128)}, f32[384,384]{1,0:T(8,128)}, u32[]{:S(2)}, u32[]{:S(2)}) collective-permute-start(f32[384,384]{1,0:T(8,128)} %slice.291), channel_id=1, source_target_pairs={{0,8},{4,12},{8,0},{12,4},{16,24},{20,28},{24,16},{28,20},{1,9},{5... | collective-permute-start | bytes 1769480 | tf_op jit(solution)/shard_map/ppermute | solution.py:119
  301.7 15.7 %collective-permute-start.48 = (f32[192,384]{1,0:T(8,128)S(1)}, f32[192,384]{1,0:T(8,128)}, u32[]{:S(2)}, u32[]{:S(2)}) collective-permute-start(f32[192,384]{1,0:T(8,128)S(1)} %slice.297), channel_id=1, source_target_pairs={{0,8},{4,12},{8,0},{12,4},{16,24},{20,28},{24,16},{28,20},{1,9},{5... | collective-permute-start | bytes 884744 | tf_op jit(solution)/shard_map/ppermute | solution.py:119
  302.2 19.6 %collective-permute-start.47 = (f32[192,384]{1,0:T(8,128)S(1)}, f32[192,384]{1,0:T(8,128)S(1)}, u32[]{:S(2)}, u32[]{:S(2)}) collective-permute-start(f32[192,384]{1,0:T(8,128)S(1)} %copy-done.29), channel_id=1, source_target_pairs={{0,2},{1,3},{2,0},{3,1},{4,6},{5,7},{6,4},{7,5},{8,10},{9,11},{10,... | collective-permute-start | bytes 884744 | tf_op jit(solution)/shard_map/ppermute | solution.py:119
  303.8 17.9 %collective-permute-start.46 = (f32[192,384]{1,0:T(8,128)S(1)}, f32[192,384]{1,0:T(8,128)S(1)}, u32[]{:S(2)}, u32[]{:S(2)}) collective-permute-start(f32[192,384]{1,0:T(8,128)S(1)} %slice.295), channel_id=1, source_target_pairs={{0,16},{4,20},{8,24},{12,28},{16,0},{20,4},{24,8},{28,12},{1,17},{... | collective-permute-start | bytes 884744 | tf_op jit(solution)/shard_map/ppermute | solution.py:119
  318.6 9.1 %collective-permute-start.50 = (f32[192,384]{1,0:T(8,128)S(1)}, f32[192,384]{1,0:T(8,128)S(1)}, u32[]{:S(2)}, u32[]{:S(2)}) collective-permute-start(f32[192,384]{1,0:T(8,128)S(1)} %add_add_fusion), channel_id=1, source_target_pairs={{0,1},{1,0},{2,3},{3,2},{4,5},{5,4},{6,7},{7,6},{8,9},{9,8},{10,11... | collective-permute-start | bytes 884744 | tf_op jit(solution)/shard_map/ppermute | solution.py:119
  (38 other events, 254.6 us)

commit v7 on v6

--- a/solution.py
+++ b/solution.py
@@ -254,7 +254,7 @@
 def centre_kernel(row_block, col_block, orders, count, row_at, col_at, place_at, *refs):
     pieces = refs[:count]
     hot_ref, hot_t_ref, recip_ref = refs[count : count + 3]
-    far_a, far_b, near_a, near_b, value_ref, high_ref, low_ref = refs[count + 3 :]
+    head_a, head_b, far_a, far_b, near_a, near_b, value_ref, high_ref, low_ref = refs[count + 3 :]
 
     @pl.when(pl.program_id(0) == 0)
     def _():
@@ -289,6 +289,19 @@
         near[...] += got[:, :width]
         far[...] += got[:, width:]
 
+    for n in range(blocks):
+        part, own_order = ((near_a, 0), (near_b, 1), (far_a, 0), (far_b, 1))[n // (blocks // 4)]
+        at = n % (blocks // 4) * col_block
+
+        @pl.when((pl.program_id(0) == pl.num_programs(0) - 1) & (col_at[n] == 0))
+        def _(part=part, own_order=own_order, at=at):
+            for h, head in enumerate((head_a, head_b)):
+                for i, s in enumerate(orders[h]):
+                    j = orders[own_order].index(s)
+                    head[i * row_block : (i + 1) * row_block, :] = part[
+                        j * row_block : (j + 1) * row_block, at + h * PB // 2 : at + (h + 1) * PB // 2
+                    ]
+
 
 def gram_rows(pieces, hot, hot_t, recip, row_at, col_at, place_at, row_block, col_block, orders):
     tiles, members, rows, lanes = pieces[0].shape
@@ -296,10 +309,11 @@
     hot = jnp.concatenate([hot, hot], axis=1)
     slots = len(orders[0])
     quarter = jax.ShapeDtypeStruct((slots * row_block, walkers // 4), jnp.float32)
+    head = jax.ShapeDtypeStruct((slots * row_block, PB // 2), jnp.float32)
     fixed = lambda t, *_: (0, 0)
     parts = pl.pallas_call(
         functools.partial(centre_kernel, row_block, col_block, orders, len(pieces)),
-        out_shape=(quarter,) * 4,
+        out_shape=(head, head) + (quarter,) * 4,
         grid_spec=pltpu.PrefetchScalarGridSpec(
             num_scalar_prefetch=3,
             grid=(tiles // TOGETHER,),
@@ -309,7 +323,7 @@
                 pl.BlockSpec((groups, walkers), fixed),
                 pl.BlockSpec((groups, 1), fixed),
             ],
-            out_specs=(pl.BlockSpec(quarter.shape, fixed),) * 4,
+            out_specs=(pl.BlockSpec(head.shape, fixed),) * 2 + (pl.BlockSpec(quarter.shape, fixed),) * 4,
             scratch_shapes=[
                 pltpu.VMEM((TOGETHER, walkers, lanes), jnp.float32),
                 pltpu.VMEM((TOGETHER, walkers, lanes), jnp.bfloat16),
@@ -319,7 +333,7 @@
         compiler_params=pltpu.CompilerParams(vmem_limit_bytes=VMEM_LIMIT),
         name="gram_rows",
     )(row_at, col_at, place_at, *pieces, hot, hot_t, recip)
-    return parts[:2], parts[2:]
+    return parts[:2], parts[2:4], parts[4:]
 
 
 def inverse_factor(value):
@@ -447,7 +461,7 @@
     orders = tuple(
         tuple(sorted(range(slots), key=lambda s, o=o: [s >> b & 1 for b in o])) for o in sweeps
     )
-    far, near = gram_rows(
+    head_cols, far, near = gram_rows(
         columns, hot, hot_t, recip, row_at, col_at, place_at, row_block, col_block, orders
     )
 
@@ -463,19 +477,6 @@
         return [pair[h][: pair[h].shape[0] // 2] + moved[h] for h in range(2)]
 
     far, near = list(far), list(near)
-    each = max(par_size // 4, 1)
-    at = (par_index % each) * col_block
-    head_cols = []
-    for h in range(2):
-        picked = None
-        for q, part in enumerate(near + far):
-            cols = lax.dynamic_slice(part, (0, at + h * PB // 2), (slots * row_block, PB // 2))
-            if q % 2 != h:
-                cols = cols.reshape(slots, row_block, PB // 2)
-                cols = jnp.concatenate([cols[orders[q % 2].index(s)] for s in orders[h]], axis=0)
-            picked = cols if picked is None else jnp.where(par_index // each == q, cols, picked)
-        head_cols.append(picked)
-
     head_cols = plane_add(head_cols, plane_step(head_cols, 0))
     tied = after([*head_cols, *far, *near])
     head_cols, far, near = tied[:2], tied[2:4], tied[4:]
@@ -534,8 +535,17 @@
     near = [part + got for part, got in zip(near, far)]
     moved = permute(near[1], "par", par_size, par_size // 4)
     inverse, near[0], near[1] = after([inverse, *near])
-    own_panel = outer_rows(rows_mine + shift_at(walk_index * row_block, row_block), inverse)
-    col_panel = outer_rows(col_rows + shift_at(par_index * col_block, col_block), inverse)
+    panels = outer_rows(
+        jnp.concatenate(
+            [
+                rows_mine + shift_at(walk_index * row_block, row_block),
+                col_rows + shift_at(par_index * col_block, col_block),
+            ],
+            axis=0,
+        ),
+        inverse,
+    )
+    own_panel, col_panel = panels[:row_block], panels[row_block:]
     update = outer_rows(own_panel, col_panel)
     gram = near[0] + moved
     bit = par_size // 8

time: 329 us -> 329 us (level)
  transfers between devices with their start and end apart: 51 -> 51, of which waited for: 28 -> 28; matrix products, arithmetic and copies ran while one was open for 10% -> 11% of each run, Pallas kernels for 14% -> 14%
where the time goes in v7:
time: 329 us; the launch traced here: 328 us
  waiting for transfers between devices  105 us (32%)
  Pallas kernels  104 us (32%)
  starting transfers between devices  72.7 us (22%)
  other arithmetic  24.5 us (7%)
  local copies, waits for them, and re-layouts  18.9 us (6%)
    ppermute x48, waiting for transfers between devices, permute(): return lax.ppermute(value, axis, xor_pairs(size, bit))  104 us
    ppermute x48, starting transfers between devices, permute(): return lax.ppermute(value, axis, xor_pairs(size, bit))  67.2 us
    pallas_call x1, Pallas kernels, gram_rows(): pl.pallas_call(functools.partial(centre_kernel, row_block, col_block, ord...  55.5 us
    pallas_call x4, Pallas kernels, jacobian(): pl.pallas_call(functools.partial(jacobian_kernel, slots, count), out_shap...  19.6 us
    pallas_call x1, Pallas kernels, head_top(): pl.pallas_call(top_kernel, out_shape=[jax.ShapeDtypeStruct((half, half),...  12.9 us
    pallas_call x1, Pallas kernels, head_low(): pl.pallas_call(low_kernel, out_shape=jax.ShapeDtypeStruct((size, size), j...  12.6 us
    squeeze x10, local copies, waits for them, and re-layouts, exchange(): held[d] = moved[i]  9.18 us
    another operation x10, other arithmetic, exchange(): jnp.stack([held[s] for s, _ in pairs])  7.98 us
  transfers between devices with their start and end apart: 51, of which 28 were waited for; matrix products, arithmetic and copies ran while one was open for 11% of the time, Pallas kernels for 14%

profile of v7, /device:TPU:0, one launch (start us, length us, event | category | flops | bytes accessed | tf_op | source)
XLA Modules:
  0.0 328.2 jit_solution(9319591626222738396)
XLA Ops:
  3.7 3.4 %turned_pieces.1 = (f32[64,1536]{1,0:T(8,128)}, f32[64,1536]{1,0:T(8,128)}, f32[64,1536]{1,0:T(8,128)}, f32[64,1536]{1,0:T(8,128)}, f32[64,1536]{1,0:T(8,128)}, ...) custom-call(s32[2]{0:T(128)} %pad_add_fusion.2.own, f32[1,1536]{1,0:T(1,128)} %reshape.79.live_ref, ...), custom_call_target="tpu_custom_call" | custom-call | tf_op jit(solution)/shard_map/turned_pieces/pallas_call | solution.py:185
  8.3 3.0 collective-permute-start.3
  14.0 2.6 collective-permute-start
  18.2 10.6 %collective-permute-done.3 = f32[2,64,1536]{2,1,0:T(8,128)S(1)} collective-permute-done((f32[2,64,1536]{2,1,0:T(8,128)S(1)}, f32[2,64,1536]{2,1,0:T(8,128)S(1)}, u32[]{:S(2)}, u32[]{:S(2)}) %collective-permute-start.3) | collective-permute-done | bytes 786464 | tf_op jit(solution)/shard_map/ppermute | solution.py:119
  29.7 1.9 collective-permute-done.2
  36.0 2.0 collective-permute-start.4
  38.0 1.8 collective-permute-start.5
  39.8 13.2 %collective-permute-done.7 = f32[2,64,1536]{2,1,0:T(8,128)S(1)} collective-permute-done((f32[2,64,1536]{2,1,0:T(8,128)S(1)}, f32[2,64,1536]{2,1,0:T(8,128)S(1)}, u32[]{:S(2)}, u32[]{:S(2)}) %collective-permute-start.7) | collective-permute-done | bytes 786464 | tf_op jit(solution)/shard_map/ppermute | solution.py:119
  57.3 1.9 pad_maximum_fusion.4
  62.3 2.3 collective-permute-start.8
  64.6 1.8 collective-permute-start.9
  66.4 4.8 %jacobian.4.refs_0_ = f32[16,4,48,256]{3,2,1,0:T(8,128)} custom-call(f32[64,1536]{1,0:T(8,128)} %get-tuple-element.112.refs_0_, f32[64,1536]{1,0:T(8,128)} %copy-done.4, f32[64,1536]{1,0:T(8,128)} %get-tuple-element.106.refs_2_, f32[64,1536]{1,0:T(8,128)} %get-tuple-element.107.refs_3_, f32[64,1536]{1,0:T(8,128)} %get-tuple-element.111.refs_4_, ...), custom_call_target="tpu_custom_call" | custom-call | tf_op jit(solution)/shard_map/jacobian/pallas_call | solution.py:227
  71.3 2.0 collective-permute-done.11
  74.3 2.3 collective-permute-done.10
  77.5 2.8 collective-permute-done.8
  80.5 1.8 collective-permute-start.12
  82.3 2.0 collective-permute-start.13
  86.9 12.4 %collective-permute-done.12.refs_4_ = f32[64,1536]{1,0:T(8,128)S(1)} collective-permute-done((f32[64,1536]{1,0:T(8,128)S(1)}, f32[64,1536]{1,0:T(8,128)S(1)}, u32[]{:S(2)}, u32[]{:S(2)}) %collective-permute-start.12) | collective-permute-done | bytes 393248 | tf_op jit(solution)/shard_map/ppermute | solution.py:119
  99.8 1.6 collective-permute-start.18
  101.5 2.0 collective-permute-start.16
  103.5 1.9 collective-permute-start.17
  105.4 11.1 %collective-permute-done.19 = f32[2,64,1536]{2,1,0:T(8,128)S(1)} collective-permute-done((f32[2,64,1536]{2,1,0:T(8,128)S(1)}, f32[2,64,1536]{2,1,0:T(8,128)S(1)}, u32[]{:S(2)}, u32[]{:S(2)}) %collective-permute-start.19) | collective-permute-done | bytes 786464 | tf_op jit(solution)/shard_map/ppermute | solution.py:119
  119.8 2.9 collective-permute-start.20
  122.7 1.8 collective-permute-start.21
  126.8 4.9 %jacobian.6.refs_2_ = f32[16,4,48,256]{3,2,1,0:T(8,128)} custom-call(f32[64,1536]{1,0:T(8,128)} %copy-done.10, f32[64,1536]{1,0:T(8,128)} %copy-done.12, f32[64,1536]{1,0:T(8,128)} %get-tuple-element.129.refs_2_, f32[64,1536]{1,0:T(8,128)} %get-tuple-element.130.refs_3_, f32[64,1536]{1,0:T(8,128)} %collective-permute-done.5.refs_4_, ...), custom_call_target="tpu_custom_call" | custom-call | tf_op jit(solution)/shard_map/jacobian/pallas_call | solution.py:227
  131.7 5.0 %jacobian.5.refs_1_ = f32[16,4,48,256]{3,2,1,0:T(8,128)} custom-call(f32[64,1536]{1,0:T(8,128)} %copy-done.5, f32[64,1536]{1,0:T(8,128)} %copy-done.2, f32[64,1536]{1,0:T(8,128)} %get-tuple-element.125.refs_2_, f32[64,1536]{1,0:T(8,128)} %get-tuple-element.126.refs_3_, f32[64,1536]{1,0:T(8,128)} %copy-done.8, f32[64,1536]{1,0:T(8,128)} %get-tuple-element.127.refs_5_, ...), custom_call_target="tpu_custom_call" | custom-call | tf_op jit(solution)/shard_map/jacobian/pallas_call | solution.py:227
  136.7 2.2 collective-permute-done.20.refs_4_
  142.5 2.0 collective-permute-start.24
  145.0 12.6 %collective-permute-done.25 = f32[2,64,1536]{2,1,0:T(8,128)S(1)} collective-permute-done((f32[2,64,1536]{2,1,0:T(8,128)S(1)}, f32[2,64,1536]{2,1,0:T(8,128)S(1)}, u32[]{:S(2)}, u32[]{:S(2)}) %collective-permute-start.25) | collective-permute-done | bytes 786464 | tf_op jit(solution)/shard_map/ppermute | solution.py:119
  160.9 4.9 %jacobian.7.refs_3_ = f32[16,4,48,256]{3,2,1,0:T(8,128)} custom-call(f32[64,1536]{1,0:T(8,128)} %collective-permute-done.21.refs_0_, f32[64,1536]{1,0:T(8,128)} %collective-permute-done.22.refs_1_, f32[64,1536]{1,0:T(8,128)} %get-tuple-element.179.refs_2_, f32[64,1536]{1,0:T(8,128)} %get-tuple-element.178.refs_3_, f32[64,1536]{1,0:T(8,128)} %copy-done.11, ...), custom_call_target="tpu_custom_call" | custom-call | tf_op jit(solution)/shard_map/jacobian/pallas_call | solution.py:227
  171.8 55.5 %gram_rows.1 = (f32[768,128]{1,0:T(8,128)}, f32[768,128]{1,0:T(8,128)}, f32[768,384]{1,0:T(8,128)}, f32[768,384]{1,0:T(8,128)}, f32[768,384]{1,0:T(8,128)}, /*index=5*/f32[768,384]{1,0:T(8,128)}) custom-call(s32[4]{0:T(128)} %get-tuple-element.200.row_at, s32[4]{0:T(128)} %get-tuple-element.201.col_at, s32[32]{0:T(128)} %broadcast_multiply_fusion.place_at, ...), custom_call_target="tpu_custom_call" | custom-call | tf_op jit(solution)/shard_map/gram_rows/pallas_call | solution.py:314
  228.4 1.8 collective-permute-start.31
  231.5 3.9 %collective-permute-done.31 = f32[384,128]{1,0:T(8,128)S(1)} collective-permute-done((f32[384,128]{1,0:T(8,128)S(1)}, f32[384,128]{1,0:T(8,128)S(1)}, u32[]{:S(2)}, u32[]{:S(2)}) %collective-permute-start.31) | collective-permute-done | bytes 196640 | tf_op jit(solution)/shard_map/ppermute | solution.py:119
  240.3 1.8 collective-permute-start.36
  242.5 2.0 collective-permute-done.32
  244.5 2.3 collective-permute-done.33
  246.8 3.4 %collective-permute-start.34 = (f32[192,256]{1,0:T(8,128)S(1)}, f32[192,256]{1,0:T(8,128)S(1)}, u32[]{:S(2)}, u32[]{:S(2)}) collective-permute-start(f32[192,256]{1,0:T(8,128)S(1)} %pad_maximum_fusion.13), channel_id=1, source_target_pairs={{0,2},{1,3},{2,0},{3,1},{4,6},{5,7},{6,4},{7,5},{8,10},{9,11},{10,... | collective-permute-start | bytes 589832 | tf_op jit(solution)/shard_map/ppermute | solution.py:119
  251.0 6.1 %collective-permute-done.34 = f32[192,256]{1,0:T(8,128)S(1)} collective-permute-done((f32[192,256]{1,0:T(8,128)S(1)}, f32[192,256]{1,0:T(8,128)S(1)}, u32[]{:S(2)}, u32[]{:S(2)}) %collective-permute-start.34) | collective-permute-done | bytes 196640 | tf_op jit(solution)/shard_map/ppermute | solution.py:119
  257.2 5.7 %collective-permute-done.35 = f32[384,384]{1,0:T(8,128)S(1)} collective-permute-done((f32[384,384]{1,0:T(8,128)S(1)}, f32[384,384]{1,0:T(8,128)S(1)}, u32[]{:S(2)}, u32[]{:S(2)}) %collective-permute-start.35) | collective-permute-done | bytes 589856 | tf_op jit(solution)/shard_map/ppermute | solution.py:119
  265.8 1.8 collective-permute-start.41
  269.5 2.7 collective-permute-start.38
  275.0 1.7 slice_add_fusion.4
  283.1 3.1 collective-permute-start.44
  287.1 12.9 %head_top.1 = (f32[128,128]{1,0:T(8,128)}, f32[128,128]{1,0:T(8,128)}, f32[128,128]{1,0:T(8,128)}) custom-call(f32[256,256]{1,0:T(8,128)} %fusion.7.a_ref), custom_call_target="tpu_custom_call" | custom-call | tf_op jit(solution)/shard_map/head_top/pallas_call | solution.py:390
  305.3 12.6 %head_low.1 = f32[256,256]{1,0:T(8,128)} custom-call(f32[128,128]{1,0:T(8,128)} %get-tuple-element.161.top_ref, f32[128,128]{1,0:T(8,128)} %get-tuple-element.162.below_ref, f32[128,128]{1,0:T(8,128)} %get-tuple-element.163.rest_ref), custom_call_target="tpu_custom_call" | custom-call | tf_op jit(solution)/shard_map/head_low/pallas_call | solution.py:397
  319.0 2.5 collective-permute-start.50
  321.5 1.6 fusion
  323.7 3.6 %collective-permute-done.50 = f32[192,384]{1,0:T(8,128)S(1)} collective-permute-done((f32[192,384]{1,0:T(8,128)S(1)}, f32[192,384]{1,0:T(8,128)S(1)}, u32[]{:S(2)}, u32[]{:S(2)}) %collective-permute-start.50) | collective-permute-done | bytes 294944 | tf_op jit(solution)/shard_map/ppermute | solution.py:119
  (196 shorter events, 76.1 us)
Async XLA Ops:
  8.3 20.6 %collective-permute-start.3 = (f32[2,64,1536]{2,1,0:T(8,128)S(1)}, f32[2,64,1536]{2,1,0:T(8,128)S(1)}, u32[]{:S(2)}, u32[]{:S(2)}) collective-permute-start(f32[2,64,1536]{2,1,0:T(8,128)S(1)} %pad_maximum_fusion.1), channel_id=1, source_target_pairs={{0,16},{4,20},{8,24},{12,28},{16,0},{20,4},{24,8},{28,12},{1,17},{... | collective-permute-start | bytes 2359304 | tf_op jit(solution)/shard_map/ppermute | solution.py:119
  12.5 19.1 %collective-permute-start.2 = (f32[2,64,1536]{2,1,0:T(8,128)S(1)}, f32[2,64,1536]{2,1,0:T(8,128)S(1)}, u32[]{:S(2)}, u32[]{:S(2)}) collective-permute-start(f32[2,64,1536]{2,1,0:T(8,128)S(1)} %pad_maximum_fusion), channel_id=1, source_target_pairs={{0,8},{4,12},{8,0},{12,4},{16,24},{20,28},{24,16},{28,20},{1,9},{5... | collective-permute-start | bytes 2359304 | tf_op jit(solution)/shard_map/ppermute | solution.py:119
  14.0 19.7 %collective-permute-start = (f32[64,1536]{1,0:T(8,128)S(1)}, f32[64,1536]{1,0:T(8,128)S(1)}, u32[]{:S(2)}, u32[]{:S(2)}) collective-permute-start(f32[64,1536]{1,0:T(8,128)S(1)} %copy-done.27), channel_id=1, source_target_pairs={{0,2},{1,3},{2,0},{3,1},{4,6},{5,7},{6,4},{7,5},{8,10},{9,11},{10,... | collective-permute-start | bytes 1179656 | tf_op jit(solution)/shard_map/ppermute | solution.py:119
  16.6 17.3 %collective-permute-start.1 = (f32[64,1536]{1,0:T(8,128)S(1)}, f32[64,1536]{1,0:T(8,128)S(1)}, u32[]{:S(2)}, u32[]{:S(2)}) collective-permute-start(f32[64,1536]{1,0:T(8,128)S(1)} %copy-done.26), channel_id=1, source_target_pairs={{0,1},{1,0},{2,3},{3,2},{4,5},{5,4},{6,7},{7,6},{8,9},{9,8},{10,11... | collective-permute-start | bytes 1179656 | tf_op jit(solution)/shard_map/ppermute | solution.py:119
  34.8 18.2 %collective-permute-start.7 = (f32[2,64,1536]{2,1,0:T(8,128)S(1)}, f32[2,64,1536]{2,1,0:T(8,128)S(1)}, u32[]{:S(2)}, u32[]{:S(2)}) collective-permute-start(f32[2,64,1536]{2,1,0:T(8,128)S(1)} %pad_maximum_fusion.3), channel_id=1, source_target_pairs={{0,16},{4,20},{8,24},{12,28},{16,0},{20,4},{24,8},{28,12},{1,17},{... | collective-permute-start | bytes 2359304 | tf_op jit(solution)/shard_map/ppermute | solution.py:119
  35.4 18.4 %collective-permute-start.6 = (f32[2,64,1536]{2,1,0:T(8,128)S(1)}, f32[2,64,1536]{2,1,0:T(8,128)S(1)}, u32[]{:S(2)}, u32[]{:S(2)}) collective-permute-start(f32[2,64,1536]{2,1,0:T(8,128)S(1)} %pad_maximum_fusion.2), channel_id=1, source_target_pairs={{0,8},{4,12},{8,0},{12,4},{16,24},{20,28},{24,16},{28,20},{1,9},{5... | collective-permute-start | bytes 2359304 | tf_op jit(solution)/shard_map/ppermute | solution.py:119
  36.0 18.7 %collective-permute-start.4 = (f32[64,1536]{1,0:T(8,128)S(1)}, f32[64,1536]{1,0:T(8,128)S(1)}, u32[]{:S(2)}, u32[]{:S(2)}) collective-permute-start(f32[64,1536]{1,0:T(8,128)S(1)} %copy-done.25), channel_id=1, source_target_pairs={{0,2},{1,3},{2,0},{3,1},{4,6},{5,7},{6,4},{7,5},{8,10},{9,11},{10,... | collective-permute-start | bytes 1179656 | tf_op jit(solution)/shard_map/ppermute | solution.py:119
  38.0 16.7 %collective-permute-start.5 = (f32[64,1536]{1,0:T(8,128)S(1)}, f32[64,1536]{1,0:T(8,128)}, u32[]{:S(2)}, u32[]{:S(2)}) collective-permute-start(f32[64,1536]{1,0:T(8,128)S(1)} %copy-done.24), channel_id=1, source_target_pairs={{0,1},{1,0},{2,3},{3,2},{4,5},{5,4},{6,7},{7,6},{8,9},{9,8},{10,11... | collective-permute-start | bytes 1179656 | tf_op jit(solution)/shard_map/ppermute | solution.py:119
  55.8 17.5 %collective-permute-start.11 = (f32[2,64,1536]{2,1,0:T(8,128)}, f32[2,64,1536]{2,1,0:T(8,128)S(1)}, u32[]{:S(2)}, u32[]{:S(2)}) collective-permute-start(f32[2,64,1536]{2,1,0:T(8,128)} %pad_maximum_fusion.5), channel_id=1, source_target_pairs={{0,16},{4,20},{8,24},{12,28},{16,0},{20,4},{24,8},{28,12},{1,17},{... | collective-permute-start | bytes 2359304 | tf_op jit(solution)/shard_map/ppermute | solution.py:119
  59.3 17.3 %collective-permute-start.10 = (f32[2,64,1536]{2,1,0:T(8,128)}, f32[2,64,1536]{2,1,0:T(8,128)S(1)}, u32[]{:S(2)}, u32[]{:S(2)}) collective-permute-start(f32[2,64,1536]{2,1,0:T(8,128)} %pad_maximum_fusion.4), channel_id=1, source_target_pairs={{0,8},{4,12},{8,0},{12,4},{16,24},{20,28},{24,16},{28,20},{1,9},{5... | collective-permute-start | bytes 2359304 | tf_op jit(solution)/shard_map/ppermute | solution.py:119
  62.3 18.1 %collective-permute-start.8 = (f32[64,1536]{1,0:T(8,128)}, f32[64,1536]{1,0:T(8,128)S(1)}, u32[]{:S(2)}, u32[]{:S(2)}) collective-permute-start(f32[64,1536]{1,0:T(8,128)} %get-tuple-element.100), channel_id=1, source_target_pairs={{0,2},{1,3},{2,0},{3,1},{4,6},{5,7},{6,4},{7,5},{8,10},{9,11},{10,... | collective-permute-start | bytes 1179656 | tf_op jit(solution)/shard_map/ppermute | solution.py:119
  64.6 15.9 %collective-permute-start.9 = (f32[64,1536]{1,0:T(8,128)}, f32[64,1536]{1,0:T(8,128)}, u32[]{:S(2)}, u32[]{:S(2)}) collective-permute-start(f32[64,1536]{1,0:T(8,128)} %get-tuple-element.101), channel_id=1, source_target_pairs={{0,1},{1,0},{2,3},{3,2},{4,5},{5,4},{6,7},{7,6},{8,9},{9,8},{10,11... | collective-permute-start | bytes 1179656 | tf_op jit(solution)/shard_map/ppermute | solution.py:119
  80.5 18.8 %collective-permute-start.12 = (f32[64,1536]{1,0:T(8,128)S(1)}, f32[64,1536]{1,0:T(8,128)S(1)}, u32[]{:S(2)}, u32[]{:S(2)}) collective-permute-start(f32[64,1536]{1,0:T(8,128)S(1)} %copy-done.7), channel_id=1, source_target_pairs={{0,2},{1,3},{2,0},{3,1},{4,6},{5,7},{6,4},{7,5},{8,10},{9,11},{10,... | collective-permute-start | bytes 1179656 | tf_op jit(solution)/shard_map/ppermute | solution.py:119
  82.3 17.1 %collective-permute-start.13 = (f32[64,1536]{1,0:T(8,128)S(1)}, f32[64,1536]{1,0:T(8,128)S(1)}, u32[]{:S(2)}, u32[]{:S(2)}) collective-permute-start(f32[64,1536]{1,0:T(8,128)S(1)} %copy-done.6), channel_id=1, source_target_pairs={{0,1},{1,0},{2,3},{3,2},{4,5},{5,4},{6,7},{7,6},{8,9},{9,8},{10,11... | collective-permute-start | bytes 1179656 | tf_op jit(solution)/shard_map/ppermute | solution.py:119
  84.4 15.1 %collective-permute-start.14 = (f32[64,1536]{1,0:T(8,128)}, f32[64,1536]{1,0:T(8,128)S(1)}, u32[]{:S(2)}, u32[]{:S(2)}) collective-permute-start(f32[64,1536]{1,0:T(8,128)} %collective-permute-done.9), channel_id=1, source_target_pairs={{0,8},{4,12},{8,0},{12,4},{16,24},{20,28},{24,16},{28,20},{1,9},{5... | collective-permute-start | bytes 1179656 | tf_op jit(solution)/shard_map/ppermute | solution.py:119
  85.5 13.9 %collective-permute-start.15 = (f32[64,1536]{1,0:T(8,128)S(1)}, f32[64,1536]{1,0:T(8,128)S(1)}, u32[]{:S(2)}, u32[]{:S(2)}) collective-permute-start(f32[64,1536]{1,0:T(8,128)S(1)} %collective-permute-done.8), channel_id=1, source_target_pairs={{0,16},{4,20},{8,24},{12,28},{16,0},{20,4},{24,8},{28,12},{1,17},{... | collective-permute-start | bytes 1179656 | tf_op jit(solution)/shard_map/ppermute | solution.py:119
  99.5 17.1 %collective-permute-start.19 = (f32[2,64,1536]{2,1,0:T(8,128)S(1)}, f32[2,64,1536]{2,1,0:T(8,128)S(1)}, u32[]{:S(2)}, u32[]{:S(2)}) collective-permute-start(f32[2,64,1536]{2,1,0:T(8,128)S(1)} %pad_maximum_fusion.7), channel_id=1, source_target_pairs={{0,16},{4,20},{8,24},{12,28},{16,0},{20,4},{24,8},{28,12},{1,17},{... | collective-permute-start | bytes 2359304 | tf_op jit(solution)/shard_map/ppermute | solution.py:119
  99.8 17.7 %collective-permute-start.18 = (f32[2,64,1536]{2,1,0:T(8,128)S(1)}, f32[2,64,1536]{2,1,0:T(8,128)S(1)}, u32[]{:S(2)}, u32[]{:S(2)}) collective-permute-start(f32[2,64,1536]{2,1,0:T(8,128)S(1)} %pad_maximum_fusion.6), channel_id=1, source_target_pairs={{0,8},{4,12},{8,0},{12,4},{16,24},{20,28},{24,16},{28,20},{1,9},{5... | collective-permute-start | bytes 2359304 | tf_op jit(solution)/shard_map/ppermute | solution.py:119
  101.5 18.2 %collective-permute-start.16 = (f32[64,1536]{1,0:T(8,128)S(1)}, f32[64,1536]{1,0:T(8,128)}, u32[]{:S(2)}, u32[]{:S(2)}) collective-permute-start(f32[64,1536]{1,0:T(8,128)S(1)} %copy-done.22), channel_id=1, source_target_pairs={{0,2},{1,3},{2,0},{3,1},{4,6},{5,7},{6,4},{7,5},{8,10},{9,11},{10,... | collective-permute-start | bytes 1179656 | tf_op jit(solution)/shard_map/ppermute | solution.py:119
  103.5 16.3 %collective-permute-start.17 = (f32[64,1536]{1,0:T(8,128)S(1)}, f32[64,1536]{1,0:T(8,128)}, u32[]{:S(2)}, u32[]{:S(2)}) collective-permute-start(f32[64,1536]{1,0:T(8,128)S(1)} %copy-done.20), channel_id=1, source_target_pairs={{0,1},{1,0},{2,3},{3,2},{4,5},{5,4},{6,7},{7,6},{8,9},{9,8},{10,11... | collective-permute-start | bytes 1179656 | tf_op jit(solution)/shard_map/ppermute | solution.py:119
  119.8 19.1 %collective-permute-start.20 = (f32[64,1536]{1,0:T(8,128)}, f32[64,1536]{1,0:T(8,128)S(1)}, u32[]{:S(2)}, u32[]{:S(2)}) collective-permute-start(f32[64,1536]{1,0:T(8,128)} %collective-permute-done.5.refs_4_), channel_id=1, source_target_pairs={{0,2},{1,3},{2,0},{3,1},{4,6},{5,7},{6,4},{7,5},{8,10},{9,11},{10,... | collective-permute-start | bytes 1179656 | tf_op jit(solution)/shard_map/ppermute | solution.py:119
  122.7 16.2 %collective-permute-start.21 = (f32[64,1536]{1,0:T(8,128)S(1)}, f32[64,1536]{1,0:T(8,128)}, u32[]{:S(2)}, u32[]{:S(2)}) collective-permute-start(f32[64,1536]{1,0:T(8,128)S(1)} %collective-permute-done.4.refs_0_), channel_id=1, source_target_pairs={{0,1},{1,0},{2,3},{3,2},{4,5},{5,4},{6,7},{7,6},{8,9},{9,8},{10,11... | collective-permute-start | bytes 1179656 | tf_op jit(solution)/shard_map/ppermute | solution.py:119
  124.5 14.4 %collective-permute-start.22 = (f32[64,1536]{1,0:T(8,128)}, f32[64,1536]{1,0:T(8,128)}, u32[]{:S(2)}, u32[]{:S(2)}) collective-permute-start(f32[64,1536]{1,0:T(8,128)} %collective-permute-done.17), channel_id=1, source_target_pairs={{0,8},{4,12},{8,0},{12,4},{16,24},{20,28},{24,16},{28,20},{1,9},{5... | collective-permute-start | bytes 1179656 | tf_op jit(solution)/shard_map/ppermute | solution.py:119
  125.7 13.3 %collective-permute-start.23 = (f32[64,1536]{1,0:T(8,128)}, f32[64,1536]{1,0:T(8,128)}, u32[]{:S(2)}, u32[]{:S(2)}) collective-permute-start(f32[64,1536]{1,0:T(8,128)} %collective-permute-done.16), channel_id=1, source_target_pairs={{0,16},{4,20},{8,24},{12,28},{16,0},{20,4},{24,8},{28,12},{1,17},{... | collective-permute-start | bytes 1179656 | tf_op jit(solution)/shard_map/ppermute | solution.py:119
  140.1 17.5 %collective-permute-start.25 = (f32[2,64,1536]{2,1,0:T(8,128)S(1)}, f32[2,64,1536]{2,1,0:T(8,128)S(1)}, u32[]{:S(2)}, u32[]{:S(2)}) collective-permute-start(f32[2,64,1536]{2,1,0:T(8,128)S(1)} %pad_maximum_fusion.9), channel_id=1, source_target_pairs={{0,8},{4,12},{8,0},{12,4},{16,24},{20,28},{24,16},{28,20},{1,9},{5... | collective-permute-start | bytes 2359304 | tf_op jit(solution)/shard_map/ppermute | solution.py:119
  142.5 17.5 %collective-permute-start.24 = (f32[2,64,1536]{2,1,0:T(8,128)S(1)}, f32[2,64,1536]{2,1,0:T(8,128)S(1)}, u32[]{:S(2)}, u32[]{:S(2)}) collective-permute-start(f32[2,64,1536]{2,1,0:T(8,128)S(1)} %pad_maximum_fusion.8), channel_id=1, source_target_pairs={{0,16},{4,20},{8,24},{12,28},{16,0},{20,4},{24,8},{28,12},{1,17},{... | collective-permute-start | bytes 2359304 | tf_op jit(solution)/shard_map/ppermute | solution.py:119
  144.5 25.8 %collective-permute-start.26 = (f32[16,4,48,256]{3,2,1,0:T(8,128)S(1)}, f32[16,4,48,256]{3,2,1,0:T(8,128)}, u32[]{:S(2)}, u32[]{:S(2)}) collective-permute-start(f32[16,4,48,256]{3,2,1,0:T(8,128)S(1)} %copy-done), channel_id=1, source_target_pairs={{0,4},{4,0},{8,12},{12,8},{16,20},{20,16},{24,28},{28,24},{1,5},{5... | collective-permute-start | bytes 9437192 | tf_op jit(solution)/shard_map/ppermute | solution.py:119
  144.5 25.8 %collective-permute-start.27 = (f32[16,4,48,256]{3,2,1,0:T(8,128)}, f32[16,4,48,256]{3,2,1,0:T(8,128)}, u32[]{:S(2)}, u32[]{:S(2)}) collective-permute-start(f32[16,4,48,256]{3,2,1,0:T(8,128)} %jacobian.5.refs_1_), channel_id=1, source_target_pairs={{0,4},{4,0},{8,12},{12,8},{16,20},{20,16},{24,28},{28,24},{1,5},{5... | collective-permute-start | bytes 9437192 | tf_op jit(solution)/shard_map/ppermute | solution.py:119
  145.0 25.3 %collective-permute-start.28 = (f32[16,4,48,256]{3,2,1,0:T(8,128)}, f32[16,4,48,256]{3,2,1,0:T(8,128)}, u32[]{:S(2)}, u32[]{:S(2)}) collective-permute-start(f32[16,4,48,256]{3,2,1,0:T(8,128)} %jacobian.6.refs_2_), channel_id=1, source_target_pairs={{0,4},{4,0},{8,12},{12,8},{16,20},{20,16},{24,28},{28,24},{1,5},{5... | collective-permute-start | bytes 9437192 | tf_op jit(solution)/shard_map/ppermute | solution.py:119
  165.8 6.0 %collective-permute-start.29 = (f32[16,4,48,256]{3,2,1,0:T(8,128)}, f32[16,4,48,256]{3,2,1,0:T(8,128)}, u32[]{:S(2)}, u32[]{:S(2)}) collective-permute-start(f32[16,4,48,256]{3,2,1,0:T(8,128)} %jacobian.7.refs_3_), channel_id=1, source_target_pairs={{0,4},{4,0},{8,12},{12,8},{16,20},{20,16},{24,28},{28,24},{1,5},{5... | collective-permute-start | bytes 9437192 | tf_op jit(solution)/shard_map/ppermute | solution.py:119
  228.4 7.0 %collective-permute-start.31 = (f32[384,128]{1,0:T(8,128)S(1)}, f32[384,128]{1,0:T(8,128)S(1)}, u32[]{:S(2)}, u32[]{:S(2)}) collective-permute-start(f32[384,128]{1,0:T(8,128)S(1)} %slice.176), channel_id=1, source_target_pairs={{0,16},{4,20},{8,24},{12,28},{16,0},{20,4},{24,8},{28,12},{1,17},{... | collective-permute-start | bytes 589832 | tf_op jit(solution)/shard_map/ppermute | solution.py:119
  231.2 6.7 %collective-permute-start.30 = (f32[384,128]{1,0:T(8,128)S(1)}, f32[384,128]{1,0:T(8,128)S(1)}, u32[]{:S(2)}, u32[]{:S(2)}) collective-permute-start(f32[384,128]{1,0:T(8,128)S(1)} %slice.174), channel_id=1, source_target_pairs={{0,8},{4,12},{8,0},{12,4},{16,24},{20,28},{24,16},{28,20},{1,9},{5... | collective-permute-start | bytes 589832 | tf_op jit(solution)/shard_map/ppermute | solution.py:119
  238.9 5.7 %collective-permute-start.32 = (f32[192,128]{1,0:T(8,128)S(1)}, f32[192,128]{1,0:T(8,128)S(1)}, u32[]{:S(2)}, u32[]{:S(2)}) collective-permute-start(f32[192,128]{1,0:T(8,128)S(1)} %slice.178), channel_id=1, source_target_pairs={{0,16},{4,20},{8,24},{12,28},{16,0},{20,4},{24,8},{28,12},{1,17},{... | collective-permute-start | bytes 294920 | tf_op jit(solution)/shard_map/ppermute | solution.py:119
  240.3 16.8 %collective-permute-start.36 = (f32[384,384]{1,0:T(8,128)S(1)}, f32[384,384]{1,0:T(8,128)S(1)}, u32[]{:S(2)}, u32[]{:S(2)}) collective-permute-start(f32[384,384]{1,0:T(8,128)S(1)} %slice.184), channel_id=1, source_target_pairs={{0,16},{4,20},{8,24},{12,28},{16,0},{20,4},{24,8},{28,12},{1,17},{... | collective-permute-start | bytes 1769480 | tf_op jit(solution)/shard_map/ppermute | solution.py:119
  246.8 10.3 %collective-permute-start.34 = (f32[192,256]{1,0:T(8,128)S(1)}, f32[192,256]{1,0:T(8,128)S(1)}, u32[]{:S(2)}, u32[]{:S(2)}) collective-permute-start(f32[192,256]{1,0:T(8,128)S(1)} %pad_maximum_fusion.13), channel_id=1, source_target_pairs={{0,2},{1,3},{2,0},{3,1},{4,6},{5,7},{6,4},{7,5},{8,10},{9,11},{10,... | collective-permute-start | bytes 589832 | tf_op jit(solution)/shard_map/ppermute | solution.py:119
  250.3 12.6 %collective-permute-start.35 = (f32[384,384]{1,0:T(8,128)S(1)}, f32[384,384]{1,0:T(8,128)S(1)}, u32[]{:S(2)}, u32[]{:S(2)}) collective-permute-start(f32[384,384]{1,0:T(8,128)S(1)} %slice.182), channel_id=1, source_target_pairs={{0,8},{4,12},{8,0},{12,4},{16,24},{20,28},{24,16},{28,20},{1,9},{5... | collective-permute-start | bytes 1769480 | tf_op jit(solution)/shard_map/ppermute | solution.py:119
  263.0 5.7 %collective-permute-start.37 = (f32[192,256]{1,0:T(8,128)S(1)}, f32[192,256]{1,0:T(8,128)S(1)}, u32[]{:S(2)}, u32[]{:S(2)}) collective-permute-start(f32[192,256]{1,0:T(8,128)S(1)} %fusion.10), channel_id=1, source_target_pairs={{0,1},{1,0},{2,3},{3,2},{4,5},{5,4},{6,7},{7,6},{8,9},{9,8},{10,11... | collective-permute-start | bytes 589832 | tf_op jit(solution)/shard_map/ppermute | solution.py:119
  265.1 9.9 %collective-permute-start.42 = (f32[192,384]{1,0:T(8,128)}, f32[192,384]{1,0:T(8,128)}, u32[]{:S(2)}, u32[]{:S(2)}) collective-permute-start(f32[192,384]{1,0:T(8,128)} %slice.188), channel_id=1, source_target_pairs={{0,8},{4,12},{8,0},{12,4},{16,24},{20,28},{24,16},{28,20},{1,9},{5... | collective-permute-start | bytes 884744 | tf_op jit(solution)/shard_map/ppermute | solution.py:119
  265.8 11.0 %collective-permute-start.41 = (f32[192,384]{1,0:T(8,128)S(1)}, f32[192,384]{1,0:T(8,128)S(1)}, u32[]{:S(2)}, u32[]{:S(2)}) collective-permute-start(f32[192,384]{1,0:T(8,128)S(1)} %slice.186), channel_id=1, source_target_pairs={{0,16},{4,20},{8,24},{12,28},{16,0},{20,4},{24,8},{28,12},{1,17},{... | collective-permute-start | bytes 884744 | tf_op jit(solution)/shard_map/ppermute | solution.py:119
  269.5 8.0 %collective-permute-start.38 = (f32[192,256]{1,0:T(8,128)S(1)}, f32[192,256]{1,0:T(8,128)S(1)}, u32[]{:S(2)}, u32[]{:S(2)}) collective-permute-start(f32[192,256]{1,0:T(8,128)S(1)} %get-tuple-element.171), channel_id=1, source_target_pairs={{0,8},{4,12},{1,9},{5,13},{9,1},{13,5},{2,10},{6,14},{18,26},{22,3... | collective-permute-start | bytes 589832 | tf_op jit(solution)/shard_map/ppermute | solution.py:509
  272.1 5.3 %collective-permute-start.39 = (f32[192,256]{1,0:T(8,128)S(1)}, f32[192,256]{1,0:T(8,128)S(1)}, u32[]{:S(2)}, u32[]{:S(2)}) collective-permute-start(f32[192,256]{1,0:T(8,128)S(1)} %get-tuple-element.171), channel_id=1, source_target_pairs={{0,16},{4,20},{1,17},{5,21},{9,25},{13,29},{2,18},{6,22},{18,2},{2... | collective-permute-start | bytes 589832 | tf_op jit(solution)/shard_map/ppermute | solution.py:509
  278.9 39.0 %collective-permute-start.49 = (f32[192,384]{1,0:T(8,128)}, f32[192,384]{1,0:T(8,128)}, u32[]{:S(2)}, u32[]{:S(2)}) collective-permute-start(f32[192,384]{1,0:T(8,128)} %slice_add_fusion.4), channel_id=1, source_target_pairs={{0,2},{1,3},{2,0},{3,1},{4,6},{5,7},{6,4},{7,5},{8,10},{9,11},{10,... | collective-permute-start | bytes 884744 | tf_op jit(solution)/shard_map/ppermute | solution.py:119
  281.4 18.6 %collective-permute-start.45 = (f32[384,384]{1,0:T(8,128)}, f32[384,384]{1,0:T(8,128)}, u32[]{:S(2)}, u32[]{:S(2)}) collective-permute-start(f32[384,384]{1,0:T(8,128)} %slice.197), channel_id=1, source_target_pairs={{0,16},{4,20},{8,24},{12,28},{16,0},{20,4},{24,8},{28,12},{1,17},{... | collective-permute-start | bytes 1769480 | tf_op jit(solution)/shard_map/ppermute | solution.py:119
  283.1 18.0 %collective-permute-start.44 = (f32[384,384]{1,0:T(8,128)}, f32[384,384]{1,0:T(8,128)}, u32[]{:S(2)}, u32[]{:S(2)}) collective-permute-start(f32[384,384]{1,0:T(8,128)} %slice.195), channel_id=1, source_target_pairs={{0,8},{4,12},{8,0},{12,4},{16,24},{20,28},{24,16},{28,20},{1,9},{5... | collective-permute-start | bytes 1769480 | tf_op jit(solution)/shard_map/ppermute | solution.py:119
  302.4 15.5 %collective-permute-start.48 = (f32[192,384]{1,0:T(8,128)S(1)}, f32[192,384]{1,0:T(8,128)}, u32[]{:S(2)}, u32[]{:S(2)}) collective-permute-start(f32[192,384]{1,0:T(8,128)S(1)} %slice.201), channel_id=1, source_target_pairs={{0,8},{4,12},{8,0},{12,4},{16,24},{20,28},{24,16},{28,20},{1,9},{5... | collective-permute-start | bytes 884744 | tf_op jit(solution)/shard_map/ppermute | solution.py:119
  302.9 18.6 %collective-permute-start.47 = (f32[192,384]{1,0:T(8,128)}, f32[192,384]{1,0:T(8,128)S(1)}, u32[]{:S(2)}, u32[]{:S(2)}) collective-permute-start(f32[192,384]{1,0:T(8,128)} %slice_add_fusion.5), channel_id=1, source_target_pairs={{0,2},{1,3},{2,0},{3,1},{4,6},{5,7},{6,4},{7,5},{8,10},{9,11},{10,... | collective-permute-start | bytes 884744 | tf_op jit(solution)/shard_map/ppermute | solution.py:119
  304.2 17.3 %collective-permute-start.46 = (f32[192,384]{1,0:T(8,128)S(1)}, f32[192,384]{1,0:T(8,128)S(1)}, u32[]{:S(2)}, u32[]{:S(2)}) collective-permute-start(f32[192,384]{1,0:T(8,128)S(1)} %slice.199), channel_id=1, source_target_pairs={{0,16},{4,20},{8,24},{12,28},{16,0},{20,4},{24,8},{28,12},{1,17},{... | collective-permute-start | bytes 884744 | tf_op jit(solution)/shard_map/ppermute | solution.py:119
  319.0 8.4 %collective-permute-start.50 = (f32[192,384]{1,0:T(8,128)S(1)}, f32[192,384]{1,0:T(8,128)S(1)}, u32[]{:S(2)}, u32[]{:S(2)}) collective-permute-start(f32[192,384]{1,0:T(8,128)S(1)} %add_add_fusion), channel_id=1, source_target_pairs={{0,1},{1,0},{2,3},{3,2},{4,5},{5,4},{6,7},{7,6},{8,9},{9,8},{10,11... | collective-permute-start | bytes 884744 | tf_op jit(solution)/shard_map/ppermute | solution.py:119
  (31 other events, 539.2 us)

commit v8 on v7

--- a/solution.py
+++ b/solution.py
@@ -487,7 +487,9 @@
     bit = par_size // 2
     rows_mine = rows_mine + permute(rows_mine, "par", par_size, bit)
     far = plane_add(far, far_moved)
-    rows_mine, far[0], far[1] = after([rows_mine, *far])
+    tied = after([rows_mine, *far, *near])
+    rows_mine, far, near = tied[0], tied[1:3], tied[3:]
+    near_moved = plane_step(near, 0)
     for step in range(1, chip_bits):
         far_moved = plane_step(far, step)
         if step < chip_bits - 1:
@@ -515,8 +517,12 @@
     both, far[0], far[1] = after([both, *far])
     far = [permute(part, "par", par_size, par_size // 2) for part in far]
     swapped = permute(both, "walk", walk_size, 1)
+    near = plane_add(near, near_moved)
     swapped, near[0], near[1] = after([swapped, *near])
-    near_moved = plane_step(near, 0)
+    for step in range(1, chip_bits):
+        near_moved = plane_step(near, step)
+        if step < chip_bits - 1:
+            near = plane_add(near, near_moved)
     pair = [jnp.where(core == 0, both, swapped), jnp.where(core == 0, swapped, both)]
     head = jnp.concatenate([pair[0][0], pair[1][0]], axis=0)[:PB]
     col_rows = jnp.concatenate([pair[0][1], pair[1][1]], axis=0)
@@ -529,8 +535,6 @@
     near = plane_add(near, near_moved)
     tied = after([*first, *near])
     first, near = tied[:3], tied[3:]
-    for step in range(1, chip_bits):
-        near = plane_add(near, plane_step(near, step))
     inverse = head_low(*first)
     near = [part + got for part, got in zip(near, far)]
     moved = permute(near[1], "par", par_size, par_size // 4)

time: 329 us -> 338 us (1.027)
  starting transfers between devices: 72.7 us -> 77.4 us
    ppermute x3, starting transfers between devices: 5.5 us -> 9.43 us  [on_device(): landed.append(lax.ppermute(rows_mine, ('walk', 'par'), pairs))]
    add x10 -> x12, other arithmetic: 6.83 us -> 7.43 us  [plane_add(): return [pair[h][:pair[h].shape[0] // 2] + moved[h] for h in range(2)]]
  transfers between devices with their start and end apart: 51 -> 51, of which waited for: 28 -> 32; matrix products, arithmetic and copies ran while one was open for 11% -> 11% of each run, Pallas kernels for 14% -> 13%
where the time goes in v8:
time: 338 us; the launch traced here: 337 us
  waiting for transfers between devices  107 us (32%)
  Pallas kernels  104 us (31%)
  starting transfers between devices  77.4 us (23%)
  other arithmetic  26.6 us (8%)
  local copies, waits for them, and re-layouts  18.7 us (6%)
    ppermute x48, waiting for transfers between devices, permute(): return lax.ppermute(value, axis, xor_pairs(size, bit))  104 us
    ppermute x48, starting transfers between devices, permute(): return lax.ppermute(value, axis, xor_pairs(size, bit))  67.9 us
    pallas_call x1, Pallas kernels, gram_rows(): pl.pallas_call(functools.partial(centre_kernel, row_block, col_block, ord...  55.5 us
    pallas_call x4, Pallas kernels, jacobian(): pl.pallas_call(functools.partial(jacobian_kernel, slots, count), out_shap...  19.7 us
    pallas_call x1, Pallas kernels, head_top(): pl.pallas_call(top_kernel, out_shape=[jax.ShapeDtypeStruct((half, half),...  12.9 us
    pallas_call x1, Pallas kernels, head_low(): pl.pallas_call(low_kernel, out_shape=jax.ShapeDtypeStruct((size, size), j...  12.5 us
    ppermute x3, starting transfers between devices, on_device(): landed.append(lax.ppermute(rows_mine, ('walk', 'par'), pairs))  9.43 us
    squeeze x10, local copies, waits for them, and re-layouts, exchange(): held[d] = moved[i]  9.17 us
  transfers between devices with their start and end apart: 51, of which 32 were waited for; matrix products, arithmetic and copies ran while one was open for 11% of the time, Pallas kernels for 13%

profile of v8, /device:TPU:0, one launch (start us, length us, event | category | flops | bytes accessed | tf_op | source)
XLA Modules:
  0.0 337.0 jit_solution(3647400343415424054)
XLA Ops:
  3.6 3.4 turned_pieces.1
  8.2 3.0 collective-permute-start.3
  14.0 2.6 collective-permute-start
  18.2 10.6 %collective-permute-done.3 = f32[2,64,1536]{2,1,0:T(8,128)S(1)} collective-permute-done((f32[2,64,1536]{2,1,0:T(8,128)S(1)}, f32[2,64,1536]{2,1,0:T(8,128)S(1)}, u32[]{:S(2)}, u32[]{:S(2)}) %collective-permute-start.3) | collective-permute-done | bytes 786464 | tf_op jit(solution)/shard_map/ppermute | solution.py:119
  29.7 1.9 collective-permute-done.2
  35.2 2.1 collective-permute-start.4
  37.3 1.8 collective-permute-start.5
  39.1 13.1 %collective-permute-done.7 = f32[2,64,1536]{2,1,0:T(8,128)S(1)} collective-permute-done((f32[2,64,1536]{2,1,0:T(8,128)S(1)}, f32[2,64,1536]{2,1,0:T(8,128)S(1)}, u32[]{:S(2)}, u32[]{:S(2)}) %collective-permute-start.7) | collective-permute-done | bytes 786464 | tf_op jit(solution)/shard_map/ppermute | solution.py:119
  56.5 1.9 pad_maximum_fusion.4
  61.5 2.3 collective-permute-start.8
  63.8 1.8 collective-permute-start.9
  65.5 4.9 %jacobian.4.refs_0_ = f32[16,4,48,256]{3,2,1,0:T(8,128)} custom-call(f32[64,1536]{1,0:T(8,128)} %get-tuple-element.114.refs_0_, f32[64,1536]{1,0:T(8,128)} %copy-done.4, f32[64,1536]{1,0:T(8,128)} %get-tuple-element.108.refs_2_, f32[64,1536]{1,0:T(8,128)} %get-tuple-element.109.refs_3_, f32[64,1536]{1,0:T(8,128)} %get-tuple-element.113.refs_4_, ...), custom_call_target="tpu_custom_call" | custom-call | tf_op jit(solution)/shard_map/jacobian/pallas_call | solution.py:227
  70.5 2.4 collective-permute-done.11
  73.9 1.8 collective-permute-done.10
  76.7 2.8 collective-permute-done.8
  79.7 1.8 collective-permute-start.12
  81.5 2.0 collective-permute-start.13
  86.0 12.4 %collective-permute-done.12.refs_4_ = f32[64,1536]{1,0:T(8,128)S(1)} collective-permute-done((f32[64,1536]{1,0:T(8,128)S(1)}, f32[64,1536]{1,0:T(8,128)S(1)}, u32[]{:S(2)}, u32[]{:S(2)}) %collective-permute-start.12) | collective-permute-done | bytes 393248 | tf_op jit(solution)/shard_map/ppermute | solution.py:119
  100.6 2.9 collective-permute-start.16
  103.5 1.8 collective-permute-start.17
  105.3 10.4 %collective-permute-done.19 = f32[2,64,1536]{2,1,0:T(8,128)S(1)} collective-permute-done((f32[2,64,1536]{2,1,0:T(8,128)S(1)}, f32[2,64,1536]{2,1,0:T(8,128)S(1)}, u32[]{:S(2)}, u32[]{:S(2)}) %collective-permute-start.19) | collective-permute-done | bytes 786464 | tf_op jit(solution)/shard_map/ppermute | solution.py:119
  117.8 1.8 collective-permute-done.16
  119.7 2.2 collective-permute-start.20
  121.9 1.8 collective-permute-start.21
  126.0 4.9 %jacobian.6.refs_2_ = f32[16,4,48,256]{3,2,1,0:T(8,128)} custom-call(f32[64,1536]{1,0:T(8,128)} %copy-done.10, f32[64,1536]{1,0:T(8,128)} %copy-done.12, f32[64,1536]{1,0:T(8,128)} %get-tuple-element.131.refs_2_, f32[64,1536]{1,0:T(8,128)} %get-tuple-element.132.refs_3_, f32[64,1536]{1,0:T(8,128)} %collective-permute-done.5.refs_4_, ...), custom_call_target="tpu_custom_call" | custom-call | tf_op jit(solution)/shard_map/jacobian/pallas_call | solution.py:227
  130.9 4.9 %jacobian.5.refs_1_ = f32[16,4,48,256]{3,2,1,0:T(8,128)} custom-call(f32[64,1536]{1,0:T(8,128)} %copy-done.5, f32[64,1536]{1,0:T(8,128)} %copy-done.2, f32[64,1536]{1,0:T(8,128)} %get-tuple-element.127.refs_2_, f32[64,1536]{1,0:T(8,128)} %get-tuple-element.128.refs_3_, f32[64,1536]{1,0:T(8,128)} %copy-done.8, f32[64,1536]{1,0:T(8,128)} %get-tuple-element.129.refs_5_, ...), custom_call_target="tpu_custom_call" | custom-call | tf_op jit(solution)/shard_map/jacobian/pallas_call | solution.py:227
  135.8 2.4 collective-permute-done.20.refs_4_
  139.5 2.2 collective-permute-start.25
  144.2 13.3 %collective-permute-done.25 = f32[2,64,1536]{2,1,0:T(8,128)S(1)} collective-permute-done((f32[2,64,1536]{2,1,0:T(8,128)S(1)}, f32[2,64,1536]{2,1,0:T(8,128)S(1)}, u32[]{:S(2)}, u32[]{:S(2)}) %collective-permute-start.25) | collective-permute-done | bytes 786464 | tf_op jit(solution)/shard_map/ppermute | solution.py:119
  161.1 5.0 %jacobian.7.refs_3_ = f32[16,4,48,256]{3,2,1,0:T(8,128)} custom-call(f32[64,1536]{1,0:T(8,128)} %collective-permute-done.21.refs_0_, f32[64,1536]{1,0:T(8,128)} %collective-permute-done.22.refs_1_, f32[64,1536]{1,0:T(8,128)} %get-tuple-element.183.refs_2_, f32[64,1536]{1,0:T(8,128)} %get-tuple-element.182.refs_3_, f32[64,1536]{1,0:T(8,128)} %copy-done.11, ...), custom_call_target="tpu_custom_call" | custom-call | tf_op jit(solution)/shard_map/jacobian/pallas_call | solution.py:227
  172.1 55.5 %gram_rows.1 = (f32[768,128]{1,0:T(8,128)}, f32[768,128]{1,0:T(8,128)}, f32[768,384]{1,0:T(8,128)}, f32[768,384]{1,0:T(8,128)}, f32[768,384]{1,0:T(8,128)}, /*index=5*/f32[768,384]{1,0:T(8,128)}) custom-call(s32[4]{0:T(128)} %get-tuple-element.204.row_at, s32[4]{0:T(128)} %get-tuple-element.205.col_at, s32[32]{0:T(128)} %broadcast_multiply_fusion.place_at, ...), custom_call_target="tpu_custom_call" | custom-call | tf_op jit(solution)/shard_map/gram_rows/pallas_call | solution.py:314
  230.7 5.0 %collective-permute-done.31 = f32[384,128]{1,0:T(8,128)S(1)} collective-permute-done((f32[384,128]{1,0:T(8,128)S(1)}, f32[384,128]{1,0:T(8,128)S(1)}, u32[]{:S(2)}, u32[]{:S(2)}) %collective-permute-start.31) | collective-permute-done | bytes 196640 | tf_op jit(solution)/shard_map/ppermute | solution.py:119
  241.6 1.9 collective-permute-done.32
  243.5 2.5 collective-permute-done.33
  246.0 3.4 %collective-permute-start.34 = (f32[192,256]{1,0:T(8,128)S(1)}, f32[192,256]{1,0:T(8,128)S(1)}, u32[]{:S(2)}, u32[]{:S(2)}) collective-permute-start(f32[192,256]{1,0:T(8,128)S(1)} %pad_maximum_fusion.13), channel_id=1, source_target_pairs={{0,2},{1,3},{2,0},{3,1},{4,6},{5,7},{6,4},{7,5},{8,10},{9,11},{10,... | collective-permute-start | bytes 589832 | tf_op jit(solution)/shard_map/ppermute | solution.py:119
  250.9 5.3 %collective-permute-done.34 = f32[192,256]{1,0:T(8,128)S(1)} collective-permute-done((f32[192,256]{1,0:T(8,128)S(1)}, f32[192,256]{1,0:T(8,128)S(1)}, u32[]{:S(2)}, u32[]{:S(2)}) %collective-permute-start.34) | collective-permute-done | bytes 196640 | tf_op jit(solution)/shard_map/ppermute | solution.py:119
  258.2 4.8 %collective-permute-done.35 = f32[384,384]{1,0:T(8,128)} collective-permute-done((f32[384,384]{1,0:T(8,128)}, f32[384,384]{1,0:T(8,128)}, u32[]{:S(2)}, u32[]{:S(2)}) %collective-permute-start.35) | collective-permute-done | bytes 589856 | tf_op jit(solution)/shard_map/ppermute | solution.py:119
  270.8 1.8 select_add_fusion
  272.6 3.2 collective-permute-start.38
  276.7 3.3 collective-permute-start.39
  281.8 4.3 %collective-permute-done.41 = f32[192,384]{1,0:T(8,128)S(1)} collective-permute-done((f32[192,384]{1,0:T(8,128)S(1)}, f32[192,384]{1,0:T(8,128)S(1)}, u32[]{:S(2)}, u32[]{:S(2)}) %collective-permute-start.41) | collective-permute-done | bytes 294944 | tf_op jit(solution)/shard_map/ppermute | solution.py:119
  286.1 2.8 collective-permute-start.40
  289.5 2.4 collective-permute-done.40
  292.8 2.3 collective-permute-start.48
  297.7 3.1 collective-permute-start.46
  301.7 12.9 %head_top.1 = (f32[128,128]{1,0:T(8,128)}, f32[128,128]{1,0:T(8,128)}, f32[128,128]{1,0:T(8,128)}) custom-call(f32[256,256]{1,0:T(8,128)} %fusion.7.a_ref), custom_call_target="tpu_custom_call" | custom-call | tf_op jit(solution)/shard_map/head_top/pallas_call | solution.py:390
  316.8 4.5 %collective-permute-start.50 = (f32[192,384]{1,0:T(8,128)S(1)}, f32[192,384]{1,0:T(8,128)S(1)}, u32[]{:S(2)}, u32[]{:S(2)}) collective-permute-start(f32[192,384]{1,0:T(8,128)S(1)} %add.287), channel_id=1, source_target_pairs={{0,1},{1,0},{2,3},{3,2},{4,5},{5,4},{6,7},{7,6},{8,9},{9,8},{10,11... | collective-permute-start | bytes 884744 | tf_op jit(solution)/shard_map/ppermute | solution.py:119
  321.3 12.5 %head_low.1 = f32[256,256]{1,0:T(8,128)} custom-call(f32[128,128]{1,0:T(8,128)} %get-tuple-element.165.top_ref, f32[128,128]{1,0:T(8,128)} %get-tuple-element.166.below_ref, f32[128,128]{1,0:T(8,128)} %get-tuple-element.167.rest_ref), custom_call_target="tpu_custom_call" | custom-call | tf_op jit(solution)/shard_map/head_low/pallas_call | solution.py:397
  (196 shorter events, 77.9 us)
Async XLA Ops:
  8.2 20.6 %collective-permute-start.3 = (f32[2,64,1536]{2,1,0:T(8,128)S(1)}, f32[2,64,1536]{2,1,0:T(8,128)S(1)}, u32[]{:S(2)}, u32[]{:S(2)}) collective-permute-start(f32[2,64,1536]{2,1,0:T(8,128)S(1)} %pad_maximum_fusion.1), channel_id=1, source_target_pairs={{0,16},{4,20},{8,24},{12,28},{16,0},{20,4},{24,8},{28,12},{1,17},{... | collective-permute-start | bytes 2359304 | tf_op jit(solution)/shard_map/ppermute | solution.py:119
  12.4 19.1 %collective-permute-start.2 = (f32[2,64,1536]{2,1,0:T(8,128)S(1)}, f32[2,64,1536]{2,1,0:T(8,128)S(1)}, u32[]{:S(2)}, u32[]{:S(2)}) collective-permute-start(f32[2,64,1536]{2,1,0:T(8,128)S(1)} %pad_maximum_fusion), channel_id=1, source_target_pairs={{0,8},{4,12},{8,0},{12,4},{16,24},{20,28},{24,16},{28,20},{1,9},{5... | collective-permute-start | bytes 2359304 | tf_op jit(solution)/shard_map/ppermute | solution.py:119
  14.0 19.7 %collective-permute-start = (f32[64,1536]{1,0:T(8,128)S(1)}, f32[64,1536]{1,0:T(8,128)S(1)}, u32[]{:S(2)}, u32[]{:S(2)}) collective-permute-start(f32[64,1536]{1,0:T(8,128)S(1)} %copy-done.26), channel_id=1, source_target_pairs={{0,2},{1,3},{2,0},{3,1},{4,6},{5,7},{6,4},{7,5},{8,10},{9,11},{10,... | collective-permute-start | bytes 1179656 | tf_op jit(solution)/shard_map/ppermute | solution.py:119
  16.6 17.3 %collective-permute-start.1 = (f32[64,1536]{1,0:T(8,128)S(1)}, f32[64,1536]{1,0:T(8,128)S(1)}, u32[]{:S(2)}, u32[]{:S(2)}) collective-permute-start(f32[64,1536]{1,0:T(8,128)S(1)} %copy-done.25), channel_id=1, source_target_pairs={{0,1},{1,0},{2,3},{3,2},{4,5},{5,4},{6,7},{7,6},{8,9},{9,8},{10,11... | collective-permute-start | bytes 1179656 | tf_op jit(solution)/shard_map/ppermute | solution.py:119
  34.0 18.2 %collective-permute-start.7 = (f32[2,64,1536]{2,1,0:T(8,128)S(1)}, f32[2,64,1536]{2,1,0:T(8,128)S(1)}, u32[]{:S(2)}, u32[]{:S(2)}) collective-permute-start(f32[2,64,1536]{2,1,0:T(8,128)S(1)} %pad_maximum_fusion.3), channel_id=1, source_target_pairs={{0,16},{4,20},{8,24},{12,28},{16,0},{20,4},{24,8},{28,12},{1,17},{... | collective-permute-start | bytes 2359304 | tf_op jit(solution)/shard_map/ppermute | solution.py:119
  34.6 18.4 %collective-permute-start.6 = (f32[2,64,1536]{2,1,0:T(8,128)S(1)}, f32[2,64,1536]{2,1,0:T(8,128)S(1)}, u32[]{:S(2)}, u32[]{:S(2)}) collective-permute-start(f32[2,64,1536]{2,1,0:T(8,128)S(1)} %pad_maximum_fusion.2), channel_id=1, source_target_pairs={{0,8},{4,12},{8,0},{12,4},{16,24},{20,28},{24,16},{28,20},{1,9},{5... | collective-permute-start | bytes 2359304 | tf_op jit(solution)/shard_map/ppermute | solution.py:119
  35.2 19.0 %collective-permute-start.4 = (f32[64,1536]{1,0:T(8,128)S(1)}, f32[64,1536]{1,0:T(8,128)S(1)}, u32[]{:S(2)}, u32[]{:S(2)}) collective-permute-start(f32[64,1536]{1,0:T(8,128)S(1)} %copy-done.24), channel_id=1, source_target_pairs={{0,2},{1,3},{2,0},{3,1},{4,6},{5,7},{6,4},{7,5},{8,10},{9,11},{10,... | collective-permute-start | bytes 1179656 | tf_op jit(solution)/shard_map/ppermute | solution.py:119
  37.3 17.1 %collective-permute-start.5 = (f32[64,1536]{1,0:T(8,128)S(1)}, f32[64,1536]{1,0:T(8,128)}, u32[]{:S(2)}, u32[]{:S(2)}) collective-permute-start(f32[64,1536]{1,0:T(8,128)S(1)} %copy-done.23), channel_id=1, source_target_pairs={{0,1},{1,0},{2,3},{3,2},{4,5},{5,4},{6,7},{7,6},{8,9},{9,8},{10,11... | collective-permute-start | bytes 1179656 | tf_op jit(solution)/shard_map/ppermute | solution.py:119
  55.4 17.5 %collective-permute-start.11 = (f32[2,64,1536]{2,1,0:T(8,128)}, f32[2,64,1536]{2,1,0:T(8,128)S(1)}, u32[]{:S(2)}, u32[]{:S(2)}) collective-permute-start(f32[2,64,1536]{2,1,0:T(8,128)} %pad_maximum_fusion.5), channel_id=1, source_target_pairs={{0,16},{4,20},{8,24},{12,28},{16,0},{20,4},{24,8},{28,12},{1,17},{... | collective-permute-start | bytes 2359304 | tf_op jit(solution)/shard_map/ppermute | solution.py:119
  58.4 17.3 %collective-permute-start.10 = (f32[2,64,1536]{2,1,0:T(8,128)}, f32[2,64,1536]{2,1,0:T(8,128)S(1)}, u32[]{:S(2)}, u32[]{:S(2)}) collective-permute-start(f32[2,64,1536]{2,1,0:T(8,128)} %pad_maximum_fusion.4), channel_id=1, source_target_pairs={{0,8},{4,12},{8,0},{12,4},{16,24},{20,28},{24,16},{28,20},{1,9},{5... | collective-permute-start | bytes 2359304 | tf_op jit(solution)/shard_map/ppermute | solution.py:119
  61.5 18.0 %collective-permute-start.8 = (f32[64,1536]{1,0:T(8,128)}, f32[64,1536]{1,0:T(8,128)S(1)}, u32[]{:S(2)}, u32[]{:S(2)}) collective-permute-start(f32[64,1536]{1,0:T(8,128)} %get-tuple-element.102), channel_id=1, source_target_pairs={{0,2},{1,3},{2,0},{3,1},{4,6},{5,7},{6,4},{7,5},{8,10},{9,11},{10,... | collective-permute-start | bytes 1179656 | tf_op jit(solution)/shard_map/ppermute | solution.py:119
  63.8 15.9 %collective-permute-start.9 = (f32[64,1536]{1,0:T(8,128)}, f32[64,1536]{1,0:T(8,128)}, u32[]{:S(2)}, u32[]{:S(2)}) collective-permute-start(f32[64,1536]{1,0:T(8,128)} %get-tuple-element.103), channel_id=1, source_target_pairs={{0,1},{1,0},{2,3},{3,2},{4,5},{5,4},{6,7},{7,6},{8,9},{9,8},{10,11... | collective-permute-start | bytes 1179656 | tf_op jit(solution)/shard_map/ppermute | solution.py:119
  79.7 18.8 %collective-permute-start.12 = (f32[64,1536]{1,0:T(8,128)S(1)}, f32[64,1536]{1,0:T(8,128)S(1)}, u32[]{:S(2)}, u32[]{:S(2)}) collective-permute-start(f32[64,1536]{1,0:T(8,128)S(1)} %copy-done.7), channel_id=1, source_target_pairs={{0,2},{1,3},{2,0},{3,1},{4,6},{5,7},{6,4},{7,5},{8,10},{9,11},{10,... | collective-permute-start | bytes 1179656 | tf_op jit(solution)/shard_map/ppermute | solution.py:119
  81.5 17.0 %collective-permute-start.13 = (f32[64,1536]{1,0:T(8,128)S(1)}, f32[64,1536]{1,0:T(8,128)S(1)}, u32[]{:S(2)}, u32[]{:S(2)}) collective-permute-start(f32[64,1536]{1,0:T(8,128)S(1)} %copy-done.6), channel_id=1, source_target_pairs={{0,1},{1,0},{2,3},{3,2},{4,5},{5,4},{6,7},{7,6},{8,9},{9,8},{10,11... | collective-permute-start | bytes 1179656 | tf_op jit(solution)/shard_map/ppermute | solution.py:119
  83.5 15.0 %collective-permute-start.14 = (f32[64,1536]{1,0:T(8,128)}, f32[64,1536]{1,0:T(8,128)S(1)}, u32[]{:S(2)}, u32[]{:S(2)}) collective-permute-start(f32[64,1536]{1,0:T(8,128)} %collective-permute-done.9), channel_id=1, source_target_pairs={{0,8},{4,12},{8,0},{12,4},{16,24},{20,28},{24,16},{28,20},{1,9},{5... | collective-permute-start | bytes 1179656 | tf_op jit(solution)/shard_map/ppermute | solution.py:119
  84.7 13.8 %collective-permute-start.15 = (f32[64,1536]{1,0:T(8,128)S(1)}, f32[64,1536]{1,0:T(8,128)S(1)}, u32[]{:S(2)}, u32[]{:S(2)}) collective-permute-start(f32[64,1536]{1,0:T(8,128)S(1)} %collective-permute-done.8), channel_id=1, source_target_pairs={{0,16},{4,20},{8,24},{12,28},{16,0},{20,4},{24,8},{28,12},{1,17},{... | collective-permute-start | bytes 1179656 | tf_op jit(solution)/shard_map/ppermute | solution.py:119
  98.6 17.0 %collective-permute-start.19 = (f32[2,64,1536]{2,1,0:T(8,128)S(1)}, f32[2,64,1536]{2,1,0:T(8,128)S(1)}, u32[]{:S(2)}, u32[]{:S(2)}) collective-permute-start(f32[2,64,1536]{2,1,0:T(8,128)S(1)} %pad_maximum_fusion.7), channel_id=1, source_target_pairs={{0,16},{4,20},{8,24},{12,28},{16,0},{20,4},{24,8},{28,12},{1,17},{... | collective-permute-start | bytes 2359304 | tf_op jit(solution)/shard_map/ppermute | solution.py:119
  100.1 16.8 %collective-permute-start.18 = (f32[2,64,1536]{2,1,0:T(8,128)S(1)}, f32[2,64,1536]{2,1,0:T(8,128)S(1)}, u32[]{:S(2)}, u32[]{:S(2)}) collective-permute-start(f32[2,64,1536]{2,1,0:T(8,128)S(1)} %pad_maximum_fusion.6), channel_id=1, source_target_pairs={{0,8},{4,12},{8,0},{12,4},{16,24},{20,28},{24,16},{28,20},{1,9},{5... | collective-permute-start | bytes 2359304 | tf_op jit(solution)/shard_map/ppermute | solution.py:119
  100.6 19.0 %collective-permute-start.16 = (f32[64,1536]{1,0:T(8,128)S(1)}, f32[64,1536]{1,0:T(8,128)}, u32[]{:S(2)}, u32[]{:S(2)}) collective-permute-start(f32[64,1536]{1,0:T(8,128)S(1)} %copy-done.21), channel_id=1, source_target_pairs={{0,2},{1,3},{2,0},{3,1},{4,6},{5,7},{6,4},{7,5},{8,10},{9,11},{10,... | collective-permute-start | bytes 1179656 | tf_op jit(solution)/shard_map/ppermute | solution.py:119
  103.5 16.2 %collective-permute-start.17 = (f32[64,1536]{1,0:T(8,128)S(1)}, f32[64,1536]{1,0:T(8,128)}, u32[]{:S(2)}, u32[]{:S(2)}) collective-permute-start(f32[64,1536]{1,0:T(8,128)S(1)} %copy-done.19), channel_id=1, source_target_pairs={{0,1},{1,0},{2,3},{3,2},{4,5},{5,4},{6,7},{7,6},{8,9},{9,8},{10,11... | collective-permute-start | bytes 1179656 | tf_op jit(solution)/shard_map/ppermute | solution.py:119
  119.7 18.6 %collective-permute-start.20 = (f32[64,1536]{1,0:T(8,128)}, f32[64,1536]{1,0:T(8,128)S(1)}, u32[]{:S(2)}, u32[]{:S(2)}) collective-permute-start(f32[64,1536]{1,0:T(8,128)} %collective-permute-done.5.refs_4_), channel_id=1, source_target_pairs={{0,2},{1,3},{2,0},{3,1},{4,6},{5,7},{6,4},{7,5},{8,10},{9,11},{10,... | collective-permute-start | bytes 1179656 | tf_op jit(solution)/shard_map/ppermute | solution.py:119
  121.9 16.4 %collective-permute-start.21 = (f32[64,1536]{1,0:T(8,128)S(1)}, f32[64,1536]{1,0:T(8,128)}, u32[]{:S(2)}, u32[]{:S(2)}) collective-permute-start(f32[64,1536]{1,0:T(8,128)S(1)} %collective-permute-done.4.refs_0_), channel_id=1, source_target_pairs={{0,1},{1,0},{2,3},{3,2},{4,5},{5,4},{6,7},{7,6},{8,9},{9,8},{10,11... | collective-permute-start | bytes 1179656 | tf_op jit(solution)/shard_map/ppermute | solution.py:119
  123.7 14.6 %collective-permute-start.22 = (f32[64,1536]{1,0:T(8,128)}, f32[64,1536]{1,0:T(8,128)}, u32[]{:S(2)}, u32[]{:S(2)}) collective-permute-start(f32[64,1536]{1,0:T(8,128)} %collective-permute-done.17), channel_id=1, source_target_pairs={{0,8},{4,12},{8,0},{12,4},{16,24},{20,28},{24,16},{28,20},{1,9},{5... | collective-permute-start | bytes 1179656 | tf_op jit(solution)/shard_map/ppermute | solution.py:119
  125.0 13.3 %collective-permute-start.23 = (f32[64,1536]{1,0:T(8,128)}, f32[64,1536]{1,0:T(8,128)}, u32[]{:S(2)}, u32[]{:S(2)}) collective-permute-start(f32[64,1536]{1,0:T(8,128)} %collective-permute-done.16), channel_id=1, source_target_pairs={{0,16},{4,20},{8,24},{12,28},{16,0},{20,4},{24,8},{28,12},{1,17},{... | collective-permute-start | bytes 1179656 | tf_op jit(solution)/shard_map/ppermute | solution.py:119
  139.5 17.9 %collective-permute-start.25 = (f32[2,64,1536]{2,1,0:T(8,128)S(1)}, f32[2,64,1536]{2,1,0:T(8,128)S(1)}, u32[]{:S(2)}, u32[]{:S(2)}) collective-permute-start(f32[2,64,1536]{2,1,0:T(8,128)S(1)} %pad_maximum_fusion.9), channel_id=1, source_target_pairs={{0,8},{4,12},{8,0},{12,4},{16,24},{20,28},{24,16},{28,20},{1,9},{5... | collective-permute-start | bytes 2359304 | tf_op jit(solution)/shard_map/ppermute | solution.py:119
  142.9 17.2 %collective-permute-start.24 = (f32[2,64,1536]{2,1,0:T(8,128)S(1)}, f32[2,64,1536]{2,1,0:T(8,128)S(1)}, u32[]{:S(2)}, u32[]{:S(2)}) collective-permute-start(f32[2,64,1536]{2,1,0:T(8,128)S(1)} %pad_maximum_fusion.8), channel_id=1, source_target_pairs={{0,16},{4,20},{8,24},{12,28},{16,0},{20,4},{24,8},{28,12},{1,17},{... | collective-permute-start | bytes 2359304 | tf_op jit(solution)/shard_map/ppermute | solution.py:119
  143.6 26.9 %collective-permute-start.26 = (f32[16,4,48,256]{3,2,1,0:T(8,128)S(1)}, f32[16,4,48,256]{3,2,1,0:T(8,128)}, u32[]{:S(2)}, u32[]{:S(2)}) collective-permute-start(f32[16,4,48,256]{3,2,1,0:T(8,128)S(1)} %copy-done), channel_id=1, source_target_pairs={{0,4},{4,0},{8,12},{12,8},{16,20},{20,16},{24,28},{28,24},{1,5},{5... | collective-permute-start | bytes 9437192 | tf_op jit(solution)/shard_map/ppermute | solution.py:119
  143.6 26.9 %collective-permute-start.27 = (f32[16,4,48,256]{3,2,1,0:T(8,128)}, f32[16,4,48,256]{3,2,1,0:T(8,128)}, u32[]{:S(2)}, u32[]{:S(2)}) collective-permute-start(f32[16,4,48,256]{3,2,1,0:T(8,128)} %jacobian.5.refs_1_), channel_id=1, source_target_pairs={{0,4},{4,0},{8,12},{12,8},{16,20},{20,16},{24,28},{28,24},{1,5},{5... | collective-permute-start | bytes 9437192 | tf_op jit(solution)/shard_map/ppermute | solution.py:119
  144.2 26.4 %collective-permute-start.28 = (f32[16,4,48,256]{3,2,1,0:T(8,128)}, f32[16,4,48,256]{3,2,1,0:T(8,128)}, u32[]{:S(2)}, u32[]{:S(2)}) collective-permute-start(f32[16,4,48,256]{3,2,1,0:T(8,128)} %jacobian.6.refs_2_), channel_id=1, source_target_pairs={{0,4},{4,0},{8,12},{12,8},{16,20},{20,16},{24,28},{28,24},{1,5},{5... | collective-permute-start | bytes 9437192 | tf_op jit(solution)/shard_map/ppermute | solution.py:119
  166.1 6.0 %collective-permute-start.29 = (f32[16,4,48,256]{3,2,1,0:T(8,128)}, f32[16,4,48,256]{3,2,1,0:T(8,128)}, u32[]{:S(2)}, u32[]{:S(2)}) collective-permute-start(f32[16,4,48,256]{3,2,1,0:T(8,128)} %jacobian.7.refs_3_), channel_id=1, source_target_pairs={{0,4},{4,0},{8,12},{12,8},{16,20},{20,16},{24,28},{28,24},{1,5},{5... | collective-permute-start | bytes 9437192 | tf_op jit(solution)/shard_map/ppermute | solution.py:119
  228.6 7.0 %collective-permute-start.31 = (f32[384,128]{1,0:T(8,128)S(1)}, f32[384,128]{1,0:T(8,128)S(1)}, u32[]{:S(2)}, u32[]{:S(2)}) collective-permute-start(f32[384,128]{1,0:T(8,128)S(1)} %slice.176), channel_id=1, source_target_pairs={{0,16},{4,20},{8,24},{12,28},{16,0},{20,4},{24,8},{28,12},{1,17},{... | collective-permute-start | bytes 589832 | tf_op jit(solution)/shard_map/ppermute | solution.py:119
  230.3 6.7 %collective-permute-start.30 = (f32[384,128]{1,0:T(8,128)S(1)}, f32[384,128]{1,0:T(8,128)S(1)}, u32[]{:S(2)}, u32[]{:S(2)}) collective-permute-start(f32[384,128]{1,0:T(8,128)S(1)} %slice.174), channel_id=1, source_target_pairs={{0,8},{4,12},{8,0},{12,4},{16,24},{20,28},{24,16},{28,20},{1,9},{5... | collective-permute-start | bytes 589832 | tf_op jit(solution)/shard_map/ppermute | solution.py:119
  240.5 16.4 %collective-permute-start.36 = (f32[384,384]{1,0:T(8,128)S(1)}, f32[384,384]{1,0:T(8,128)}, u32[]{:S(2)}, u32[]{:S(2)}) collective-permute-start(f32[384,384]{1,0:T(8,128)S(1)} %slice.184), channel_id=1, source_target_pairs={{0,16},{4,20},{8,24},{12,28},{16,0},{20,4},{24,8},{28,12},{1,17},{... | collective-permute-start | bytes 1769480 | tf_op jit(solution)/shard_map/ppermute | solution.py:119
  246.0 10.2 %collective-permute-start.34 = (f32[192,256]{1,0:T(8,128)S(1)}, f32[192,256]{1,0:T(8,128)S(1)}, u32[]{:S(2)}, u32[]{:S(2)}) collective-permute-start(f32[192,256]{1,0:T(8,128)S(1)} %pad_maximum_fusion.13), channel_id=1, source_target_pairs={{0,2},{1,3},{2,0},{3,1},{4,6},{5,7},{6,4},{7,5},{8,10},{9,11},{10,... | collective-permute-start | bytes 589832 | tf_op jit(solution)/shard_map/ppermute | solution.py:119
  250.3 12.8 %collective-permute-start.35 = (f32[384,384]{1,0:T(8,128)}, f32[384,384]{1,0:T(8,128)}, u32[]{:S(2)}, u32[]{:S(2)}) collective-permute-start(f32[384,384]{1,0:T(8,128)} %slice.182), channel_id=1, source_target_pairs={{0,8},{4,12},{8,0},{12,4},{16,24},{20,28},{24,16},{28,20},{1,9},{5... | collective-permute-start | bytes 1769480 | tf_op jit(solution)/shard_map/ppermute | solution.py:119
  264.4 6.4 %collective-permute-start.37 = (f32[192,256]{1,0:T(8,128)}, f32[192,256]{1,0:T(8,128)}, u32[]{:S(2)}, u32[]{:S(2)}) collective-permute-start(f32[192,256]{1,0:T(8,128)} %fusion.10), channel_id=1, source_target_pairs={{0,1},{1,0},{2,3},{3,2},{4,5},{5,4},{6,7},{7,6},{8,9},{9,8},{10,11... | collective-permute-start | bytes 589832 | tf_op jit(solution)/shard_map/ppermute | solution.py:119
  266.5 10.3 %collective-permute-start.42 = (f32[192,384]{1,0:T(8,128)}, f32[192,384]{1,0:T(8,128)}, u32[]{:S(2)}, u32[]{:S(2)}) collective-permute-start(f32[192,384]{1,0:T(8,128)} %slice.188), channel_id=1, source_target_pairs={{0,8},{4,12},{8,0},{12,4},{16,24},{20,28},{24,16},{28,20},{1,9},{5... | collective-permute-start | bytes 884744 | tf_op jit(solution)/shard_map/ppermute | solution.py:119
  267.8 27.3 %collective-permute-start.45 = (f32[384,384]{1,0:T(8,128)S(1)}, f32[384,384]{1,0:T(8,128)S(1)}, u32[]{:S(2)}, u32[]{:S(2)}) collective-permute-start(f32[384,384]{1,0:T(8,128)S(1)} %slice.192), channel_id=1, source_target_pairs={{0,16},{4,20},{8,24},{12,28},{16,0},{20,4},{24,8},{28,12},{1,17},{... | collective-permute-start | bytes 1769480 | tf_op jit(solution)/shard_map/ppermute | solution.py:119
  269.2 26.0 %collective-permute-start.44 = (f32[384,384]{1,0:T(8,128)S(1)}, f32[384,384]{1,0:T(8,128)S(1)}, u32[]{:S(2)}, u32[]{:S(2)}) collective-permute-start(f32[384,384]{1,0:T(8,128)S(1)} %slice.190), channel_id=1, source_target_pairs={{0,8},{4,12},{8,0},{12,4},{16,24},{20,28},{24,16},{28,20},{1,9},{5... | collective-permute-start | bytes 1769480 | tf_op jit(solution)/shard_map/ppermute | solution.py:119
  270.2 16.0 %collective-permute-start.41 = (f32[192,384]{1,0:T(8,128)S(1)}, f32[192,384]{1,0:T(8,128)S(1)}, u32[]{:S(2)}, u32[]{:S(2)}) collective-permute-start(f32[192,384]{1,0:T(8,128)S(1)} %slice.186), channel_id=1, source_target_pairs={{0,16},{4,20},{8,24},{12,28},{16,0},{20,4},{24,8},{28,12},{1,17},{... | collective-permute-start | bytes 884744 | tf_op jit(solution)/shard_map/ppermute | solution.py:119
  272.6 16.9 %collective-permute-start.38 = (f32[192,256]{1,0:T(8,128)S(1)}, f32[192,256]{1,0:T(8,128)S(1)}, u32[]{:S(2)}, u32[]{:S(2)}) collective-permute-start(f32[192,256]{1,0:T(8,128)S(1)} %get-tuple-element.175), channel_id=1, source_target_pairs={{0,8},{4,12},{1,9},{5,13},{9,1},{13,5},{2,10},{6,14},{18,26},{22,3... | collective-permute-start | bytes 589832 | tf_op jit(solution)/shard_map/ppermute | solution.py:511
  276.7 12.8 %collective-permute-start.39 = (f32[192,256]{1,0:T(8,128)S(1)}, f32[192,256]{1,0:T(8,128)S(1)}, u32[]{:S(2)}, u32[]{:S(2)}) collective-permute-start(f32[192,256]{1,0:T(8,128)S(1)} %get-tuple-element.175), channel_id=1, source_target_pairs={{0,16},{4,20},{1,17},{5,21},{9,25},{13,29},{2,18},{6,22},{18,2},{2... | collective-permute-start | bytes 589832 | tf_op jit(solution)/shard_map/ppermute | solution.py:511
  286.1 5.8 %collective-permute-start.40 = (f32[192,256]{1,0:T(8,128)S(1)}, f32[192,256]{1,0:T(8,128)S(1)}, u32[]{:S(2)}, u32[]{:S(2)}) collective-permute-start(f32[192,256]{1,0:T(8,128)S(1)} %get-tuple-element.175), channel_id=1, source_target_pairs={{0,24},{4,28},{1,25},{5,29},{9,17},{13,21},{2,26},{6,30},{18,10},{... | collective-permute-start | bytes 589832 | tf_op jit(solution)/shard_map/ppermute | solution.py:511
  292.1 23.7 %collective-permute-start.49 = (f32[192,384]{1,0:T(8,128)}, f32[192,384]{1,0:T(8,128)}, u32[]{:S(2)}, u32[]{:S(2)}) collective-permute-start(f32[192,384]{1,0:T(8,128)} %slice_add_fusion.6), channel_id=1, source_target_pairs={{0,2},{1,3},{2,0},{3,1},{4,6},{5,7},{6,4},{7,5},{8,10},{9,11},{10,... | collective-permute-start | bytes 884744 | tf_op jit(solution)/shard_map/ppermute | solution.py:119
  292.8 41.1 %collective-permute-start.48 = (f32[192,384]{1,0:T(8,128)S(1)}, f32[192,384]{1,0:T(8,128)S(1)}, u32[]{:S(2)}, u32[]{:S(2)}) collective-permute-start(f32[192,384]{1,0:T(8,128)S(1)} %slice_add_fusion.7), channel_id=1, source_target_pairs={{0,2},{1,3},{2,0},{3,1},{4,6},{5,7},{6,4},{7,5},{8,10},{9,11},{10,... | collective-permute-start | bytes 884744 | tf_op jit(solution)/shard_map/ppermute | solution.py:119
  296.2 18.5 %collective-permute-start.47 = (f32[192,384]{1,0:T(8,128)}, f32[192,384]{1,0:T(8,128)}, u32[]{:S(2)}, u32[]{:S(2)}) collective-permute-start(f32[192,384]{1,0:T(8,128)} %slice.201), channel_id=1, source_target_pairs={{0,8},{4,12},{8,0},{12,4},{16,24},{20,28},{24,16},{28,20},{1,9},{5... | collective-permute-start | bytes 884744 | tf_op jit(solution)/shard_map/ppermute | solution.py:119
  297.7 17.9 %collective-permute-start.46 = (f32[192,384]{1,0:T(8,128)}, f32[192,384]{1,0:T(8,128)S(1)}, u32[]{:S(2)}, u32[]{:S(2)}) collective-permute-start(f32[192,384]{1,0:T(8,128)} %slice.199), channel_id=1, source_target_pairs={{0,16},{4,20},{8,24},{12,28},{16,0},{20,4},{24,8},{28,12},{1,17},{... | collective-permute-start | bytes 884744 | tf_op jit(solution)/shard_map/ppermute | solution.py:119
  316.8 19.3 %collective-permute-start.50 = (f32[192,384]{1,0:T(8,128)S(1)}, f32[192,384]{1,0:T(8,128)S(1)}, u32[]{:S(2)}, u32[]{:S(2)}) collective-permute-start(f32[192,384]{1,0:T(8,128)S(1)} %add.287), channel_id=1, source_target_pairs={{0,1},{1,0},{2,3},{3,2},{4,5},{5,4},{6,7},{7,6},{8,9},{9,8},{10,11... | collective-permute-start | bytes 884744 | tf_op jit(solution)/shard_map/ppermute | solution.py:119
  (30 other events, 534.8 us)
